TPU v7x, 32 devices: a whole 2x2x4 slice. The times are simulated.
32 devices in a mesh: req: 8 (over z, x), head: 4 (over y, core).
Axes of the slice: x: 2, y: 2, z: 4, core: 2. Of those that a mesh axis runs over, the one named last changes fastest.
Arguments:
- resid: bfloat16 [32, 4, 2048], P('req'), may hold values from -6 to 6
- proj: bfloat16 [32, 4, 3, 2048], P('req', None, None, 'head'), may hold values from -6 to 6
- conv_cache: bfloat16 [32, 3, 3, 2048], P('req', None, None, 'head'), may hold values from -6 to 6
- conv_weight: bfloat16 [4, 3, 2048], P(None, None, 'head'), may hold values from -3 to 3
- forget_bias: float32 [2048], P('head'), may hold values from -2 to 6
- owner: int32 [32], replicated, may hold values from 0 to 31, each once
- lengths: int32 [32], replicated, may hold values from 0 to 4096, as said below
- old_state: bfloat16 [32, 16, 128, 128], P('req', 'head'), may hold values from -6 to 6
- norm_gain: float32 [2048], P('head'), may hold values from 0.5 to 1.5
- out_weight: bfloat16 [2048, 2048], P('head'), may hold values from -0.125 to 0.125
Outputs:
- mixed: bfloat16 [32, 4, 2048], P('req')
- new_state: bfloat16 [32, 16, 128, 128], P('req', 'head')
Inputs may be any that keep to these rules, and one draw needn't show every extreme that they name: `lengths`: short requests (below 3) and long ones are mixed; some request has length 0 and some 4096.
All inputs are finite; a program needn't handle non-finite values.
Results may differ from a plain program's by a relative error of at most 0.015.
Values may be sent and summed in bfloat16 or wider, within the bound.
No kernel may reach another device: no remote copies, remote signals or barrier semaphores. Data moves between devices by JAX's collectives and lax.ppermute only.
A program may use at most 64 MiB of HBM per device.

v0:
```python
import jax
import jax.numpy as jnp
from jax import lax
from jax.sharding import PartitionSpec as P


def convolve(proj, conv_cache, conv_weight, lens):
    taps = conv_weight.shape[0]
    new_tokens = proj.shape[1]
    joined = jnp.concatenate([conv_cache, proj], axis=1).astype(jnp.float32)
    places = lens[:, None] + jnp.arange(-(taps - 1), new_tokens, dtype=jnp.int32)[None, :]
    joined = jnp.where((places >= 0)[:, :, None, None], joined, jnp.float32(0.0))
    summed = jnp.zeros(proj.shape, jnp.float32)
    for offset in range(taps):
        begin_at = taps - 1 - offset
        summed = summed + joined[:, begin_at : begin_at + new_tokens] * conv_weight[offset].astype(
            jnp.float32
        )
    return jax.nn.silu(summed).astype(jnp.bfloat16)


def recurrence(convolved, relocated, lens, forget_bias, norm_gain, head_size):
    local_reqs, new_tokens, _, channels = convolved.shape
    head_count = channels // head_size
    values = convolved.astype(jnp.float32).reshape(local_reqs, new_tokens, 3, head_count, head_size)
    queries = values[:, :, 0]
    keep_rate = jax.nn.sigmoid(values[:, :, 1] + forget_bias.reshape(head_count, head_size))
    inputs = values[:, :, 2]
    current = relocated.astype(jnp.float32) * (lens > 0).astype(jnp.float32)[:, None, None, None]
    outputs = []
    for position in range(new_tokens):
        rate_now = keep_rate[:, position]
        current = (
            rate_now[..., None] * current
            + (1.0 - rate_now)[..., None] * inputs[:, position][:, :, None, :]
        )
        outputs.append(jnp.einsum("rhk,rhkv->rhv", queries[:, position], current))
    stacked = jnp.stack(outputs, axis=1)
    inverse_rms = lax.rsqrt(jnp.mean(stacked * stacked, axis=-1, keepdims=True) + 1e-06)
    normed = (stacked * inverse_rms).reshape(local_reqs, new_tokens, channels) * norm_gain
    return (normed.astype(jnp.bfloat16), current.astype(jnp.bfloat16))


def body(
    resid,
    proj,
    conv_cache,
    conv_weight,
    forget_bias,
    owner,
    lengths,
    old_state,
    norm_gain,
    out_weight,
):
    local_reqs = resid.shape[0]
    new_tokens = resid.shape[1]
    devices = lax.axis_size("req")
    own_index = lax.axis_index("req")
    total_reqs = owner.shape[0]
    head_size = old_state.shape[-1]
    inverse = (
        jnp.zeros((total_reqs,), jnp.int32).at[owner].set(jnp.arange(total_reqs, dtype=jnp.int32))
    )
    local_lens = lax.dynamic_slice_in_dim(lengths, own_index * local_reqs, local_reqs)
    convolved = convolve(proj, conv_cache, conv_weight, local_lens)
    pieces = old_state.reshape(local_reqs, devices, -1)
    spread = lax.all_to_all(pieces, "req", split_axis=1, concat_axis=0, tiled=True).reshape(
        total_reqs, -1
    )
    picked = jnp.take(spread, inverse, axis=0).reshape(devices, local_reqs, 1, -1)
    routed = lax.all_to_all(picked, "req", split_axis=0, concat_axis=2, tiled=True)
    relocated = routed.reshape(old_state.shape)
    normed, new_state = recurrence(
        convolved, relocated, local_lens, forget_bias, norm_gain, head_size
    )
    flat_normed = normed.reshape(local_reqs * new_tokens, -1)
    flat_resid = resid.reshape(local_reqs * new_tokens, -1)
    partial_value = jnp.dot(flat_normed, out_weight, preferred_element_type=jnp.float32)
    summed = lax.psum(partial_value, "head")
    mixed = (flat_resid.astype(jnp.float32) + summed).astype(jnp.bfloat16).reshape(resid.shape)
    return (mixed, new_state)


def solution(mesh):
    in_specs = (
        P("req", None, None),
        P("req", None, None, "head"),
        P("req", None, None, "head"),
        P(None, None, "head"),
        P("head"),
        P(),
        P(),
        P("req", "head", None, None),
        P("head"),
        P("head", None),
    )
    out_specs = (P("req", None, None), P("req", "head", None, None))
    return jax.shard_map(body, mesh=mesh, in_specs=in_specs, out_specs=out_specs, check_vma=False)
```

profile of v0, /device:TPU:0, one launch (start us, length us, event | category | flops | bytes accessed | tf_op | source)
XLA Modules:
  0.0 103.1 jit_solution(8104832526261652992)
XLA Ops:
  7.2 1.4 %reshape.167 = bf16[4,8,8192]{2,1,0:T(8,128)(2,1)S(1)} reshape(bf16[4,4,128,128]{3,2,1,0:T(8,128)(2,1)} %param.17) | data formatting | bytes 1048576 | tf_op jit(solution)/shard_map/reshape | solution.py:67
  8.6 1.2 %copy.27 = bf16[4,8,8192]{2,0,1:T(4,128)(2,1)} copy(bf16[4,8,8192]{2,1,0:T(8,128)(2,1)S(1)} %reshape.167) | data formatting | bytes 1048576 | tf_op jit(solution)/shard_map/reshape | solution.py:67
  9.8 7.3 %all-to-all-start = ((bf16[4,8,8192]{2,0,1:T(4,128)(2,1)}), bf16[4,8,8192]{2,0,1:T(4,128)(2,1)S(1)}, u32[]{:S(2)}, u32[]{:S(2)}) async-start(bf16[4,8,8192]{2,0,1:T(4,128)(2,1)} %copy.27), calls=%async_computation | async-start | bytes 1048576 | tf_op jit(solution)/shard_map/all_to_all | solution.py:68
  17.2 0.1 compare_convert_fusion
  17.3 0.1 add_compare_fusion
  17.4 0.1 convert_select_fusion
  17.5 0.1 fusion.21
  17.7 0.7 scatter_custom_fusion
  18.4 0.1 broadcast_in_dim.46
  18.6 13.0 %all-to-all-done = bf16[4,8,8192]{2,0,1:T(4,128)(2,1)S(1)} async-done(((bf16[4,8,8192]{2,0,1:T(4,128)(2,1)}), bf16[4,8,8192]{2,0,1:T(4,128)(2,1)S(1)}, u32[]{:S(2)}, u32[]{:S(2)}) %all-to-all-start) | async-done | bytes 524320 | tf_op jit(solution)/shard_map/all_to_all | solution.py:68
  31.6 0.1 reshape.168
  31.7 0.9 gather_fusion
  32.6 0.2 gather.7
  32.8 1.1 %bitcast_select_fusion = bf16[8,4,1,8192]{3,1,2,0:T(4,128)(2,1)} fusion(bf16[8,4,1,8192]{3,1,0,2:T(4,128)(2,1)S(1)} %gather.7, pred[8,4]{1,0:T(8,128)(4,1)S(1)} %broadcast_in_dim.46), kind=kLoop, calls=%fused_computation.11 | loop fusion | flops 262144 | bytes 1048608 | tf_op jit(solution)/shard_map/jit(_take)/select_n | solution.py:71
  33.9 3.6 %all-to-all-start.1 = ((bf16[8,4,1,8192]{3,1,2,0:T(4,128)(2,1)}), bf16[8,4,1,8192]{3,1,2,0:T(4,128)(2,1)S(1)}, u32[]{:S(2)}, u32[]{:S(2)}) async-start(bf16[8,4,1,8192]{3,1,2,0:T(4,128)(2,1)} %bitcast_select_fusion), calls=%async_computation.1 | async-start | bytes 1048576 | tf_op jit(solution)/shard_map/all_to_all | solution.py:72
  37.5 0.0 all-reduce.2.cloned.1.call-start
  37.7 14.5 %all-to-all-done.1 = bf16[8,4,1,8192]{3,1,2,0:T(4,128)(2,1)S(1)} async-done(((bf16[8,4,1,8192]{3,1,2,0:T(4,128)(2,1)}), bf16[8,4,1,8192]{3,1,2,0:T(4,128)(2,1)S(1)}, u32[]{:S(2)}, u32[]{:S(2)}) %all-to-all-start.1) | async-done | bytes 524320 | tf_op jit(solution)/shard_map/all_to_all | solution.py:72
  52.2 0.1 convert_bitcast_fusion
  52.3 1.6 %copy.29 = f32[1,4,8,1,8192]{4,2,1,3,0:T(8,128)} copy(f32[1,4,8,1,8192]{4,1,2,3,0:T(4,128)S(1)} %convert_bitcast_fusion) | data formatting | bytes 2097152 | tf_op jit(solution)/shard_map/convert_element_type | solution.py:29
  53.9 1.4 %reshape.175 = f32[4,4,128,128]{3,2,1,0:T(8,128)S(1)} reshape(f32[1,4,8,1,8192]{4,2,1,3,0:T(8,128)} %copy.29) | data formatting | bytes 2097152 | tf_op jit(solution)/shard_map/convert_element_type | solution.py:29
  55.2 0.7 fusion.3
  56.0 1.5 %fusion = f32[4,4,1,128]{3,2,1,0:T(1,128)S(1)} fusion(f32[4,4,128,128]{3,2,1,0:T(8,128)S(1)} %reshape.175, f32[4,4,128]{2,1,0:T(4,128)S(1)} %get-tuple-element.15, f32[4,4,128]{2,1,0:T(4,128)S(1)} %get-tuple-element.11, f32[4,4,128]{2,1,0:T(4,128)S(1)} %get-tuple-element.7, f32[4,4,128]{2,1,0:T(4,128)S(1)} %get-tuple-element.12, ...), kind=kOutput, calls=%fused_computation.7 | convolution fusion | flops 2359296 | bytes 1110032 | tf_op jit(solution)/shard_map/rhk,rhkv->rhv/dot_general | solution.py:37
  57.4 2.4 %fusion.34 = f32[4,4,1,128]{3,2,1,0:T(1,128)S(1)} fusion(bf16[4,4,128,1]{2,1,0,3:T(4,128)(2,1)S(1)} %get-tuple-element.18, f32[4,4,128,128]{3,2,1,0:T(8,128)S(1)} %reshape.175, f32[4,4,128]{2,1,0:T(4,128)S(1)} %get-tuple-element.14, f32[4,4,128]{2,1,0:T(4,128)S(1)} %get-tuple-element.10, f32[4,4,128]{2,1,0:T(4,128)S(1)} %get-tuple-element.6, ...), kind=kOutput, calls=%fused_computation.67 | convolution fusion | flops 3145728 | bytes 1134608 | tf_op jit(solution)/shard_map/rhk,rhkv->rhv/dot_general | solution.py:37
  59.8 2.9 %fusion.2 = f32[4,4,1,128]{3,2,1,0:T(1,128)S(1)} fusion(f32[4,4,128]{2,1,0:T(4,128)S(1)} %get-tuple-element.13, f32[4,4,128]{2,1,0:T(4,128)S(1)} %get-tuple-element.9, f32[4,4,128]{2,1,0:T(4,128)S(1)} %get-tuple-element.5, bf16[4,4,128,1]{2,1,0,3:T(4,128)(2,1)S(1)} %get-tuple-element.17, f32[4,4,128,128]{3,2,1,0:T(8,128)S(1)} %reshape.175, ...), kind=kOutput, calls=%fused_computation.9 | convolution fusion | flops 3932160 | bytes 1159184 | tf_op jit(solution)/shard_map/rhk,rhkv->rhv/dot_general | solution.py:37
  62.7 0.1 fusion.29
  62.9 0.1 mul.212
  63.0 1.0 %fusion.30 = f32[16,2048]{1,0:T(8,128)} fusion(bf16[512,2048]{1,0:T(8,128)(2,1)S(1)} %copy-done, f32[16,512]{1,0:T(8,128)S(1)} %stack.32, f32[2,8,4,128]{3,2,1,0:T(4,128)S(1)} %bitcast.112, f32[512]{0:T(512)S(1)} %copy-done.6), kind=kOutput, calls=%fused_computation.51 | convolution fusion | flops 33579008 | bytes 2295808 | tf_op jit(solution)/shard_map/dot_general | solution.py:79
  64.0 0.0 all-reduce.2.cloned.1.call-update
  64.1 3.2 %fusion.1 = bf16[4,4,128,128]{3,2,1,0:T(8,128)(2,1)} fusion(f32[4,4,128]{2,1,0:T(4,128)S(1)} %get-tuple-element.13, f32[4,4,128]{2,1,0:T(4,128)S(1)} %get-tuple-element.9, f32[4,4,128]{2,1,0:T(4,128)S(1)} %get-tuple-element.5, f32[4,4,128]{2,1,0:T(4,128)S(1)} %get-tuple-element.14, f32[4,4,128]{2,1,0:T(4,128)S(1)} %get-tuple-element.10, ...), kind=kLoop, calls=%fused_computation.8 | loop fusion | flops 3670016 | bytes 1671184 | tf_op jit(solution)/shard_map/convert_element_type | solution.py:41
  67.3 27.5 %all-reduce.2.cloned.1.call-done = f32[16,2048]{1,0:T(8,128)} async-done(((f32[16,2048]{1,0:T(8,128)}), f32[16,2048]{1,0:T(8,128)}) %all-reduce.2.cloned.1.call-update) | async-done | bytes 131088 | tf_op jit(solution)/shard_map/psum | solution.py:80
  94.7 0.9 add_convert_fusion
  95.6 0.7 reshape.169
  (42 shorter events, 0.3 us)
Async XLA Ops:
  7.2 55.8 %copy-start = (bf16[512,2048]{1,0:T(8,128)(2,1)S(1)}, bf16[512,2048]{1,0:T(8,128)(2,1)}, u32[]{:S(2)}) copy-start(bf16[512,2048]{1,0:T(8,128)(2,1)} %param.19) | copy-start | bytes 6291460
  7.2 9.9 %copy-start.4 = (bf16[4,3,3,512]{3,0,2,1:T(4,128)(2,1)S(1)}, bf16[4,3,3,512]{3,0,2,1:T(4,128)(2,1)}, u32[]{:S(2)}) copy-start(bf16[4,3,3,512]{3,0,2,1:T(4,128)(2,1)} %param.12) | copy-start | bytes 110596
  7.2 10.0 %copy-start.3 = (bf16[4,3,512]{2,0,1:T(4,128)(2,1)S(1)}, bf16[4,3,512]{2,0,1:T(4,128)(2,1)}, u32[]{:S(2)}) copy-start(bf16[4,3,512]{2,0,1:T(4,128)(2,1)} %param.13) | copy-start | bytes 36868
  7.2 10.0 %copy-start.7 = (s32[32]{0:T(128)S(1)}, s32[32]{0:T(128)}, u32[]{:S(2)}) copy-start(s32[32]{0:T(128)} %param.16) | copy-start | bytes 388
  7.2 10.2 %copy-start.2 = (bf16[4,4,3,512]{3,1,2,0:T(4,128)(2,1)S(1)}, bf16[4,4,3,512]{3,1,2,0:T(4,128)(2,1)}, u32[]{:S(2)}) copy-start(bf16[4,4,3,512]{3,1,2,0:T(4,128)(2,1)} %param.11) | copy-start | bytes 147460
  7.2 10.4 %copy-start.8 = (s32[32]{0:T(128)S(1)}, s32[32]{0:T(128)}, u32[]{:S(2)}) copy-start(s32[32]{0:T(128)} %param.15) | copy-start | bytes 388
  7.2 11.3 %copy-start.5 = (f32[512]{0:T(512)S(1)}, f32[512]{0:T(512)}, u32[]{:S(2)}) copy-start(f32[512]{0:T(512)} %param.14) | copy-start | bytes 6148
  9.8 21.7 %all-to-all-start = ((bf16[4,8,8192]{2,0,1:T(4,128)(2,1)}), bf16[4,8,8192]{2,0,1:T(4,128)(2,1)S(1)}, u32[]{:S(2)}, u32[]{:S(2)}) async-start(bf16[4,8,8192]{2,0,1:T(4,128)(2,1)} %copy.27), calls=%async_computation | async-start | bytes 1048576 | tf_op jit(solution)/shard_map/all_to_all | solution.py:68
  32.6 5.0 %copy-start.1 = (bf16[4,4,2048]{2,1,0:T(4,128)(2,1)S(1)}, bf16[4,4,2048]{2,1,0:T(4,128)(2,1)}, u32[]{:S(2)}) copy-start(bf16[4,4,2048]{2,1,0:T(4,128)(2,1)} %param.10) | copy-start | bytes 196612
  33.9 18.3 %all-to-all-start.1 = ((bf16[8,4,1,8192]{3,1,2,0:T(4,128)(2,1)}), bf16[8,4,1,8192]{3,1,2,0:T(4,128)(2,1)S(1)}, u32[]{:S(2)}, u32[]{:S(2)}) async-start(bf16[8,4,1,8192]{3,1,2,0:T(4,128)(2,1)} %bitcast_select_fusion), calls=%async_computation.1 | async-start | bytes 1048576 | tf_op jit(solution)/shard_map/all_to_all | solution.py:72
  37.5 57.2 %all-reduce.2.cloned.1.call-start = ((), (), s32[]{:S(2)}) async-start(), calls=%async_computation.2 | async-start | bytes 262144 | tf_op jit(solution)/shard_map/psum | solution.py:80
  59.8 3.2 %copy-start.6 = (f32[512]{0:T(512)S(1)}, f32[512]{0:T(512)}, u32[]{:S(2)}) copy-start(f32[512]{0:T(512)} %param.18) | copy-start | bytes 6148
Sparse Core Ops, SparseCore 0:
  64.2 30.4 all-reduce.1
where the time goes:
time: 103 us
  waiting for transfers between devices  55 us (53%)
  between operations  14.4 us (14%)
  starting transfers between devices  10.9 us (11%)
  matrix products  8.49 us (8%)
  local copies, waits for them, and re-layouts  8.43 us (8%)
  other arithmetic  5.91 us (6%)
    psum x1, waiting for transfers between devices, body(): summed = lax.psum(partial_value, 'head')  27.5 us
    all_to_all x1, waiting for transfers between devices, body(): lax.all_to_all(picked, 'req', split_axis=0, concat_axis=2, tiled=True)  14.5 us
    all_to_all x1, waiting for transfers between devices, body(): lax.all_to_all(pieces, 'req', split_axis=1, concat_axis=0, tiled=True)  13 us
    dot_general x4, matrix products, recurrence(): outputs.append(jnp.einsum('rhk,rhkv->rhv', queries[:, position], current))  7.46 us
    all_to_all x1, starting transfers between devices, body(): lax.all_to_all(pieces, 'req', split_axis=1, concat_axis=0, tiled=True)  7.25 us
    all_to_all x1, starting transfers between devices, body(): lax.all_to_all(picked, 'req', split_axis=0, concat_axis=2, tiled=True)  3.64 us
    convert_element_type x1, other arithmetic, recurrence(): return (normed.astype(jnp.bfloat16), current.astype(jnp.bfloat16))  3.19 us
    convert_element_type x2, local copies, waits for them, and re-layouts, recurrence(): relocated.astype(jnp.float32)  2.97 us
  transfers between devices with their start and end apart: 3, of which 3 were waited for; matrix products, arithmetic and copies ran while one was open for 4% of the time, Pallas kernels for 0%

commit v1 on v0

v1 whole, which is shorter than its diff:
```python
import functools

import jax
import jax.numpy as jnp
from jax import lax
from jax.experimental import pallas as pl
from jax.experimental.pallas import tpu as pltpu
from jax.sharding import PartitionSpec as P

BF16 = jnp.bfloat16
F32 = jnp.float32
VMEM = pltpu.VMEM


def convolve(proj, conv_cache, conv_weight, lens):
    taps = conv_weight.shape[0]
    new_tokens = proj.shape[1]
    joined = jnp.concatenate([conv_cache, proj], axis=1).astype(F32)
    places = lens[:, None] + jnp.arange(-(taps - 1), new_tokens, dtype=jnp.int32)[None, :]
    joined = jnp.where((places >= 0)[:, :, None, None], joined, F32(0.0))
    summed = jnp.zeros(proj.shape, F32)
    for offset in range(taps):
        begin_at = taps - 1 - offset
        summed = summed + joined[:, begin_at : begin_at + new_tokens] * conv_weight[offset].astype(F32)
    return jax.nn.silu(summed).astype(BF16)


def recurrence(convolved, relocated, lens, forget_bias, norm_gain, head_size):
    local_reqs, new_tokens, _, channels = convolved.shape
    head_count = channels // head_size
    values = convolved.astype(F32).reshape(local_reqs, new_tokens, 3, head_count, head_size)
    queries = values[:, :, 0]
    keep_rate = jax.nn.sigmoid(values[:, :, 1] + forget_bias.reshape(head_count, head_size))
    inputs = values[:, :, 2]
    current = relocated.astype(F32) * (lens > 0).astype(F32)[:, None, None, None]
    outputs = []
    for position in range(new_tokens):
        rate_now = keep_rate[:, position]
        current = (
            rate_now[..., None] * current
            + (1.0 - rate_now)[..., None] * inputs[:, position][:, :, None, :]
        )
        outputs.append(jnp.einsum("rhk,rhkv->rhv", queries[:, position], current))
    stacked = jnp.stack(outputs, axis=1)
    inverse_rms = lax.rsqrt(jnp.mean(stacked * stacked, axis=-1, keepdims=True) + 1e-06)
    normed = (stacked * inverse_rms).reshape(local_reqs, new_tokens, channels) * norm_gain
    return (normed.astype(BF16), current.astype(BF16))


def generic_body(
    resid, proj, conv_cache, conv_weight, forget_bias, owner, lengths, old_state, norm_gain, out_weight
):
    local_reqs, new_tokens = resid.shape[:2]
    devices = lax.axis_size("req")
    own_index = lax.axis_index("req")
    total_reqs = owner.shape[0]
    head_size = old_state.shape[-1]
    inverse = (
        jnp.zeros((total_reqs,), jnp.int32).at[owner].set(jnp.arange(total_reqs, dtype=jnp.int32))
    )
    local_lens = lax.dynamic_slice_in_dim(lengths, own_index * local_reqs, local_reqs)
    convolved = convolve(proj, conv_cache, conv_weight, local_lens)
    pieces = old_state.reshape(local_reqs, devices, -1)
    spread = lax.all_to_all(pieces, "req", split_axis=1, concat_axis=0, tiled=True)
    spread = spread.reshape(total_reqs, -1)
    picked = jnp.take(spread, inverse, axis=0).reshape(devices, local_reqs, 1, -1)
    routed = lax.all_to_all(picked, "req", split_axis=0, concat_axis=2, tiled=True)
    relocated = routed.reshape(old_state.shape)
    normed, new_state = recurrence(
        convolved, relocated, local_lens, forget_bias, norm_gain, head_size
    )
    flat_normed = normed.reshape(local_reqs * new_tokens, -1)
    flat_resid = resid.reshape(local_reqs * new_tokens, -1)
    partial_value = jnp.dot(flat_normed, out_weight, preferred_element_type=F32)
    summed = lax.psum(partial_value, "head")
    mixed = (flat_resid.astype(F32) + summed).astype(BF16).reshape(resid.shape)
    return (mixed, new_state)


def middle_kernel(blocks, reqs, steps, index_ref, *refs):
    own = refs[:blocks]
    sib = refs[blocks : 2 * blocks]
    packs = refs[2 * blocks : 3 * blocks]
    params_ref, live_ref = refs[3 * blocks : 3 * blocks + 2]
    at = 3 * blocks + 2
    states_out = refs[at : at + blocks]
    normed_out = refs[at + blocks : at + 2 * blocks]
    pool, flat, gathered, columns, lefts, local_out, state_out = refs[at + 2 * blocks :]
    count = blocks * reqs

    for s in range(blocks):
        pool[pl.ds(s * reqs, reqs)] = own[s][...]
        pool[pl.ds((blocks + s) * reqs, reqs)] = sib[s][...]
        flat[...] = packs[s][...].astype(F32)
        for row in range(3 * steps):
            gathered[row, pl.ds(s * reqs, reqs), :] = flat[pl.ds(row * reqs, reqs), :]

    bias = params_ref[0:1, :]
    gain = params_ref[1:2, :]
    live = live_ref[...]
    query = [gathered[t] for t in range(steps)]
    keep = [jax.nn.sigmoid(gathered[steps + t] + bias) for t in range(steps)]
    inputs = [gathered[2 * steps + t] for t in range(steps)]

    weights = []
    decay = live
    for t in range(steps):
        weights = [w * keep[t] for w in weights] + [1.0 - keep[t]]
        decay = decay * keep[t]
        lefts[pl.ds(t * count, count), :] = query[t] * decay
        out = jnp.zeros_like(query[t])
        for earlier in range(t + 1):
            score = jnp.sum(query[t] * weights[earlier], axis=-1, keepdims=True)
            out = out + score * inputs[earlier]
        local_out[pl.ds(t, count, stride=steps), :] = out

    columns[...] = jnp.zeros_like(columns)
    columns[pl.ds(0, count), :] = decay
    for t in range(steps):
        columns[pl.ds((1 + t) * count, count), :] = weights[t]
    turned = columns[...].T

    for i in range(count):
        old = pool[index_ref[i]]
        left = lefts[pl.ds(i, steps, stride=count), :].astype(BF16)
        state_out[pl.ds(i * steps, steps), :] = jnp.dot(left, old, preferred_element_type=F32)
        current = turned[:, i : i + 1] * old.astype(F32)
        for t in range(steps):
            column = (1 + t) * count + i
            current = current + turned[:, column : column + 1] * inputs[t][i : i + 1, :]
        states_out[i // reqs][i % reqs] = current.astype(BF16)

    head_out = state_out[...] + local_out[...]
    scale = lax.rsqrt(jnp.mean(head_out * head_out, axis=-1, keepdims=True) + 1e-06)
    normed = (head_out * scale * gain).astype(BF16)
    for s in range(blocks):
        normed_out[s][...] = normed[s * reqs * steps : (s + 1) * reqs * steps]


def middle(index, own, sib, packs, params, live, steps):
    blocks = len(own)
    reqs, head_size, _ = own[0].shape
    count = blocks * reqs
    spec = pl.BlockSpec(memory_space=VMEM)
    columns = -(-count * (1 + steps) // 128) * 128
    outs = pl.pallas_call(
        functools.partial(middle_kernel, blocks, reqs, steps),
        out_shape=[jax.ShapeDtypeStruct(own[0].shape, BF16)] * blocks
        + [jax.ShapeDtypeStruct((reqs * steps, head_size), BF16)] * blocks,
        in_specs=[pl.BlockSpec(memory_space=pltpu.SMEM)] + [spec] * (3 * blocks + 2),
        out_specs=[spec] * (2 * blocks),
        scratch_shapes=[
            VMEM((2 * count, head_size, head_size), BF16),
            VMEM((3 * steps * reqs, head_size), F32),
            VMEM((3 * steps, count, head_size), F32),
            VMEM((columns, head_size), F32),
            VMEM((steps * count, head_size), F32),
            VMEM((steps * count, head_size), F32),
            VMEM((steps * count, head_size), F32),
        ],
        name="middle",
    )(index, *own, *sib, *packs, params, live)
    return outs[:blocks], outs[blocks:]


def swapped_body(
    resid, proj, conv_cache, conv_weight, forget_bias, owner, lengths, old_state, norm_gain, out_weight
):
    local_reqs, steps, width = resid.shape
    blocks = old_state.shape[1]
    head_size = old_state.shape[-1]
    n_head = lax.axis_size("head")
    own_req = lax.axis_index("req")
    own_head = lax.axis_index("head")
    z, x, core = own_req // 2, own_req % 2, own_head % 2

    both = ("req", "head")
    sibling = [(i, i ^ 1) for i in range(n_head)]
    planes = range(n_head // 2)

    def swap(value, s):
        pairs = [
            ((a * 2 + b) * n_head + y * 2 + c, ((a ^ s) * 2 + c) * n_head + y * 2 + b)
            for a in range(blocks)
            for b in range(2)
            for y in planes
            for c in range(2)
        ]
        return lax.ppermute(value, both, pairs)

    def head_of(value, s, axis):
        return lax.dynamic_index_in_dim(value, z ^ s, axis, keepdims=False)

    order = [s for s in range(blocks - 1, -1, -1)]
    own = [None] * blocks
    for s in order:
        own[s] = swap(head_of(old_state, s, 1), s)

    params = jnp.stack([forget_bias, norm_gain]).reshape(2, blocks, head_size)
    other_params = lax.ppermute(params, "head", sibling)
    params = head_of(jnp.where(core == x, params, other_params), 0, 1)

    local_lens = lax.dynamic_slice_in_dim(lengths, own_req * local_reqs, local_reqs)
    convolved = convolve(proj, conv_cache, conv_weight, local_lens)
    convolved = convolved.reshape(local_reqs, steps, 3, blocks, head_size).transpose(3, 2, 1, 0, 4)
    convolved = convolved.reshape(blocks, 3 * steps * local_reqs, head_size)
    packs = [None] * blocks
    for s in order:
        packs[s] = swap(head_of(convolved, s, 0), s)
    sib = [None] * blocks
    for s in order:
        sib[s] = lax.ppermute(own[s], "head", sibling)

    zs = z ^ jnp.arange(blocks, dtype=jnp.int32)
    slots = ((zs * 2 + core) * local_reqs)[:, None] + jnp.arange(local_reqs, dtype=jnp.int32)[None, :]
    slots = slots.reshape(-1)
    total = owner.shape[0]
    hit = owner[None, :] == slots[:, None]
    source = jnp.sum(jnp.where(hit, jnp.arange(total, dtype=jnp.int32)[None, :], 0), axis=1)
    device, place = source // local_reqs, source % local_reqs
    away = (device % 2 != core).astype(jnp.int32)
    index = (away * blocks + ((device // 2) ^ z)) * local_reqs + place
    lens = jnp.sum(
        jnp.where(jnp.arange(total, dtype=jnp.int32)[None, :] == slots[:, None], lengths[None, :], 0),
        axis=1,
    )
    live = jnp.broadcast_to((lens > 0).astype(F32)[:, None], (slots.shape[0], head_size))

    states, normed = middle(index, own, sib, packs, params, live, steps)

    rows = [None] * blocks
    for s in order:
        rows[s] = swap(normed[s], s)
    back = [None] * blocks
    for s in order:
        back[s] = swap(states[s], s)

    flat = jnp.zeros((local_reqs * steps, blocks * head_size), BF16)
    for s in range(blocks):
        flat = lax.dynamic_update_slice(flat, rows[s], (0, (z ^ s) * head_size))
    part = jnp.dot(flat, out_weight, preferred_element_type=F32)
    part = part + lax.ppermute(part, "head", sibling)
    part = part.astype(BF16)
    part = part.astype(F32) + lax.ppermute(
        part, "head", [(i, (i + 2) % n_head) for i in range(n_head)]
    ).astype(F32)
    mixed = (resid.reshape(-1, width).astype(F32) + part).astype(BF16).reshape(resid.shape)

    new_state = jnp.zeros(old_state.shape, BF16)
    for s in range(blocks):
        new_state = lax.dynamic_update_slice(new_state, back[s][:, None], (0, z ^ s, 0, 0))
    return (mixed, new_state)


def solution(mesh):
    in_specs = (
        P("req", None, None),
        P("req", None, None, "head"),
        P("req", None, None, "head"),
        P(None, None, "head"),
        P("head"),
        P(),
        P(),
        P("req", "head", None, None),
        P("head"),
        P("head", None),
    )
    out_specs = (P("req", None, None), P("req", "head", None, None))

    def body(*args):
        heads = args[7].shape[1]
        swapped = (
            mesh.shape["req"] == 2 * heads and heads & (heads - 1) == 0 and mesh.shape["head"] == 4
        )
        return (swapped_body if swapped else generic_body)(*args)

    return jax.shard_map(body, mesh=mesh, in_specs=in_specs, out_specs=out_specs, check_vma=False)
```

time: 103 us -> 73.3 us (0.71)
  waiting for transfers between devices: 55 us -> 19.6 us
  starting transfers between devices: 10.9 us -> 40 us
  between operations: 14.4 us -> 1.06 us
  matrix products: 8.49 us -> 0.38 us
  Pallas kernels: 0 us -> 3.95 us
  local copies, waits for them, and re-layouts: 8.43 us -> 4.64 us
  other arithmetic: 5.91 us -> 3.39 us
    ppermute x0 -> x23, starting transfers between devices: none -> 40 us  [the longest x16 28.4 us: swap(): return lax.ppermute(value, both, pairs)]
    all_to_all x2 -> x0, waiting for transfers between devices: 27.6 us -> none  [the longest x1 14.5 us: body(): lax.all_to_all(picked, 'req', split_axis=0, concat_axis=2, tiled=True)]
    psum x1 -> x0, waiting for transfers between devices: 27.5 us -> none  [body(): summed = lax.psum(partial_value, 'head')]
    ppermute x0 -> x23, waiting for transfers between devices: none -> 19.6 us  [the longest x16 15.5 us: swap(): return lax.ppermute(value, both, pairs)]
    all_to_all x2 -> x0, starting transfers between devices: 10.9 us -> none  [the longest x1 7.25 us: body(): lax.all_to_all(pieces, 'req', split_axis=1, concat_axis=0, tiled=True)]
    dot_general x5 -> x1, matrix products: 8.49 us -> 0.38 us  [swapped_body(): part = jnp.dot(flat, out_weight, preferred_element_type=F32)]
    pallas_call x0 -> x1, Pallas kernels: none -> 3.95 us  [middle(): pl.pallas_call(functools.partial(middle_kernel, blocks, reqs, steps), out...]
    convert_element_type x6 -> x5, other arithmetic: 4.42 us -> 1.07 us  [the longest x1 0.88 us: convolve(): conv_weight[offset].astype(F32)]
  transfers between devices with their start and end apart: 3 -> 23, of which waited for: 3 -> 8; matrix products, arithmetic and copies ran while one was open for 4% -> 4% of each run, Pallas kernels for 0% -> 0%
where the time goes in v1:
time: 73.3 us; the launch traced here: 73 us
  starting transfers between devices  40 us (55%)
  waiting for transfers between devices  19.6 us (27%)
  local copies, waits for them, and re-layouts  4.64 us (6%)
  Pallas kernels  3.95 us (5%)
  other arithmetic  3.39 us (5%)
  between operations  1.06 us (1%)
    ppermute x16, starting transfers between devices, swap(): return lax.ppermute(value, both, pairs)  28.4 us
    ppermute x16, waiting for transfers between devices, swap(): return lax.ppermute(value, both, pairs)  15.5 us
    ppermute x4, starting transfers between devices, swapped_body(): sib[s] = lax.ppermute(own[s], 'head', sibling)  4.58 us
    pallas_call x1, Pallas kernels, middle(): pl.pallas_call(functools.partial(middle_kernel, blocks, reqs, steps), out...  3.95 us
    ppermute x1, starting transfers between devices, swapped_body(): other_params = lax.ppermute(params, 'head', sibling)  3.53 us
    ppermute x1, waiting for transfers between devices, swapped_body(): lax.ppermute(part, 'head', [(i, (i + 2) % n_head) for i in range(n_head)])  2.79 us
    ppermute x1, starting transfers between devices, swapped_body(): part = part + lax.ppermute(part, 'head', sibling)  1.89 us
    ppermute x1, starting transfers between devices, swapped_body(): lax.ppermute(part, 'head', [(i, (i + 2) % n_head) for i in range(n_head)])  1.6 us
  transfers between devices with their start and end apart: 23, of which 8 were waited for; matrix products, arithmetic and copies ran while one was open for 4% of the time, Pallas kernels for 0%

profile of v1, /device:TPU:0, one launch (start us, length us, event | category | flops | bytes accessed | tf_op | source)
XLA Modules:
  0.0 73.0 jit_solution(12918057789494780268)
XLA Ops:
  0.7 0.9 %copy.24 = bf16[4,3,3,512]{3,1,2,0:T(4,128)(2,1)S(1)} copy(bf16[4,3,3,512]{3,0,2,1:T(4,128)(2,1)} %param.12) | data formatting | bytes 73728 | tf_op args[2]
  1.7 0.9 %slice_convert_fusion.3 = (f32[1,3,512]{2,0,1:T(1,128)S(1)}, f32[1,3,512]{2,0,1:T(1,128)S(1)}, f32[1,3,512]{2,0,1:T(1,128)S(1)}, f32[1,3,512]{2,0,1:T(1,128)S(1)}) fusion(bf16[4,3,512]{2,0,1:T(4,128)(2,1)} %param.13), kind=kLoop, calls=%fused_computation.34 | loop fusion | flops 6144 | bytes 36864 | tf_op jit(solution)/shard_map/convert_element_type | solution.py:24
  2.5 0.7 %dynamic_slice.37 = s32[4]{0:T(128)S(1)} dynamic-slice(s32[32]{0:T(128)} %param.16, s32[]{:T(128)S(6)} %select_n.102), dynamic_slice_sizes={4} | dynamic-slice | bytes 36 | tf_op jit(solution)/shard_map/dynamic_slice | solution.py:203
  3.4 0.9 %convert_select_fusion = f32[4,7,3,512]{3,1,2,0:T(8,128)S(1)} fusion(bf16[4,4,3,512]{3,1,2,0:T(4,128)(2,1)} %param.11, bf16[4,3,3,512]{3,1,2,0:T(4,128)(2,1)S(1)} %copy.24, pred[4,7]{1,0:T(4,128)(4,1)S(1)} %add_compare_fusion), kind=kLoop, calls=%fused_computation | loop fusion | flops 215040 | bytes 258076 | tf_op jit(solution)/shard_map/jit(_where)/select_n | solution.py:20
  4.5 4.1 %collective-permute-start.10 = (bf16[48,128]{1,0:T(8,128)(2,1)S(1)}, bf16[48,128]{1,0:T(8,128)(2,1)S(1)}, u32[]{:S(2)}, u32[]{:S(2)}) collective-permute-start(bf16[48,128]{1,0:T(8,128)(2,1)S(1)} %get-tuple-element.25), channel_id=1, source_target_pairs={{0,16},{1,20},{2,18},{3,22},{4,17},{5,21},{6,19},{7,23},{8,24},{9,... | collective-permute-start | bytes 36872 | tf_op jit(solution)/shard_map/ppermute | solution.py:189
  8.6 1.3 %collective-permute-start.11 = (bf16[48,128]{1,0:T(8,128)(2,1)S(1)}, bf16[48,128]{1,0:T(8,128)(2,1)S(1)}, u32[]{:S(2)}, u32[]{:S(2)}) collective-permute-start(bf16[48,128]{1,0:T(8,128)(2,1)S(1)} %get-tuple-element.24), channel_id=1, source_target_pairs={{0,24},{1,28},{2,26},{3,30},{4,25},{5,29},{6,27},{7,31},{8,16},{9,... | collective-permute-start | bytes 36872 | tf_op jit(solution)/shard_map/ppermute | solution.py:189
  10.0 1.1 %dynamic-slice_bitcast_fusion = (bf16[4,128,128]{2,1,0:T(8,128)(2,1)S(1)}, bf16[4,128,128]{2,1,0:T(8,128)(2,1)S(1)}, bf16[4,128,128]{2,1,0:T(8,128)(2,1)S(1)}, bf16[4,128,128]{2,1,0:T(8,128)(2,1)S(1)}) fusion(bf16[4,4,128,128]{3,2,1,0:T(8,128)(2,1)} %param.17, s32[]{:T(128)S(6)} %select_n.101, s32[]{:T(128)S(6)} %select_n.99, s32[]{:T(128)S(6)} %select_n.98, ...), kind=kLoop, calls=%fused_computation.7 | loop fusion | bytes 1048592 | tf_op jit(solution)/shard_map/jit(dynamic_index_in_dim)/squeeze | solution.py:192
  11.1 0.7 collective-permute-start
  12.1 3.5 %collective-permute-start.12 = (f32[2,4,128]{2,0,1:T(2,128)S(1)}, f32[2,4,128]{2,0,1:T(2,128)S(1)}, u32[]{:S(2)}, u32[]{:S(2)}) collective-permute-start(f32[2,4,128]{2,0,1:T(2,128)S(1)} %pad_maximum_fusion), channel_id=1, source_target_pairs={{0,1},{1,0},{2,3},{3,2},{4,5},{5,4},{6,7},{7,6},{8,9},{9,8},{10,11... | collective-permute-start | bytes 12296 | tf_op jit(solution)/shard_map/ppermute | solution.py:200
  16.4 2.3 %collective-permute-start.2 = (bf16[4,128,128]{2,1,0:T(8,128)(2,1)S(1)}, bf16[4,128,128]{2,1,0:T(8,128)(2,1)S(1)}, u32[]{:S(2)}, u32[]{:S(2)}) collective-permute-start(bf16[4,128,128]{2,1,0:T(8,128)(2,1)S(1)} %get-tuple-element.23), channel_id=1, source_target_pairs={{0,16},{1,20},{2,18},{3,22},{4,17},{5,21},{6,19},{7,23},{8,24},{9,... | collective-permute-start | bytes 393224 | tf_op jit(solution)/shard_map/ppermute | solution.py:189
  18.7 1.6 %collective-permute-start.3 = (bf16[4,128,128]{2,1,0:T(8,128)(2,1)S(1)}, bf16[4,128,128]{2,1,0:T(8,128)(2,1)S(1)}, u32[]{:S(2)}, u32[]{:S(2)}) collective-permute-start(bf16[4,128,128]{2,1,0:T(8,128)(2,1)S(1)} %get-tuple-element.20), channel_id=1, source_target_pairs={{0,24},{1,28},{2,26},{3,30},{4,25},{5,29},{6,27},{7,31},{8,16},{9,... | collective-permute-start | bytes 393224 | tf_op jit(solution)/shard_map/ppermute | solution.py:189
  21.5 3.7 %collective-permute-start.4 = (bf16[4,128,128]{2,1,0:T(8,128)(2,1)S(1)}, bf16[4,128,128]{2,1,0:T(8,128)(2,1)S(1)}, u32[]{:S(2)}, u32[]{:S(2)}) collective-permute-start(bf16[4,128,128]{2,1,0:T(8,128)(2,1)S(1)} %collective-permute-done.refs_0_), channel_id=1, source_target_pairs={{0,1},{1,0},{2,3},{3,2},{4,5},{5,4},{6,7},{7,6},{8,9},{9,8},{10,11... | collective-permute-start | bytes 393224 | tf_op jit(solution)/shard_map/ppermute | solution.py:212
  25.4 3.9 %collective-permute-done.2.refs_2_ = bf16[4,128,128]{2,1,0:T(8,128)(2,1)S(1)} collective-permute-done((bf16[4,128,128]{2,1,0:T(8,128)(2,1)S(1)}, bf16[4,128,128]{2,1,0:T(8,128)(2,1)S(1)}, u32[]{:S(2)}, u32[]{:S(2)}) %collective-permute-start.2) | collective-permute-done | bytes 131104 | tf_op jit(solution)/shard_map/ppermute | solution.py:189
  29.2 0.7 collective-permute-start.6
  30.0 2.8 %collective-permute-start.9 = (bf16[48,128]{1,0:T(8,128)(2,1)S(1)}, bf16[48,128]{1,0:T(8,128)(2,1)S(1)}, u32[]{:S(2)}, u32[]{:S(2)}) collective-permute-start(bf16[48,128]{1,0:T(8,128)(2,1)S(1)} %get-tuple-element.26), channel_id=1, source_target_pairs={{0,8},{1,12},{2,10},{3,14},{4,9},{5,13},{6,11},{7,15},{8,0},{9,4},... | collective-permute-start | bytes 36872 | tf_op jit(solution)/shard_map/ppermute | solution.py:189
  33.4 1.1 %collective-permute-done.9.refs_9_ = bf16[48,128]{1,0:T(8,128)(2,1)S(1)} collective-permute-done((bf16[48,128]{1,0:T(8,128)(2,1)S(1)}, bf16[48,128]{1,0:T(8,128)(2,1)S(1)}, u32[]{:S(2)}, u32[]{:S(2)}) %collective-permute-start.9) | collective-permute-done | bytes 12320 | tf_op jit(solution)/shard_map/ppermute | solution.py:189
  34.6 0.7 broadcast_in_dim.76.refs_13_
  35.4 4.0 %middle.1 = (bf16[4,128,128]{2,1,0:T(8,128)(2,1)}, bf16[4,128,128]{2,1,0:T(8,128)(2,1)}, bf16[4,128,128]{2,1,0:T(8,128)(2,1)}, bf16[4,128,128]{2,1,0:T(8,128)(2,...) custom-call(s32[16]{0:T(128)} %fusion.7.index_ref, ...), custom_call_target="tpu_custom_call" | custom-call | tf_op jit(solution)/shard_map/middle/pallas_call | solution.py:146
  39.3 1.3 %collective-permute-start.13 = (bf16[16,128]{1,0:T(8,128)(2,1)}, bf16[16,128]{1,0:T(8,128)(2,1)S(1)}, u32[]{:S(2)}, u32[]{:S(2)}) collective-permute-start(bf16[16,128]{1,0:T(8,128)(2,1)} %get-tuple-element.10), channel_id=1, source_target_pairs={{0,0},{1,4},{2,2},{3,6},{4,1},{5,5},{6,3},{7,7},{8,8},{9,12},{10,1... | collective-permute-start | bytes 12296 | tf_op jit(solution)/shard_map/ppermute | solution.py:189
  40.7 1.6 %collective-permute-start.19 = (bf16[4,128,128]{2,1,0:T(8,128)(2,1)}, bf16[4,128,128]{2,1,0:T(8,128)(2,1)S(1)}, u32[]{:S(2)}, u32[]{:S(2)}) collective-permute-start(bf16[4,128,128]{2,1,0:T(8,128)(2,1)} %get-tuple-element.14), channel_id=1, source_target_pairs={{0,0},{1,4},{2,2},{3,6},{4,1},{5,5},{6,3},{7,7},{8,8},{9,12},{10,1... | collective-permute-start | bytes 393224 | tf_op jit(solution)/shard_map/ppermute | solution.py:189
  42.3 2.0 %collective-permute-start.20 = (bf16[4,128,128]{2,1,0:T(8,128)(2,1)}, bf16[4,128,128]{2,1,0:T(8,128)(2,1)S(1)}, u32[]{:S(2)}, u32[]{:S(2)}) collective-permute-start(bf16[4,128,128]{2,1,0:T(8,128)(2,1)} %get-tuple-element.15), channel_id=1, source_target_pairs={{0,8},{1,12},{2,10},{3,14},{4,9},{5,13},{6,11},{7,15},{8,0},{9,4},... | collective-permute-start | bytes 393224 | tf_op jit(solution)/shard_map/ppermute | solution.py:189
  44.3 1.4 %collective-permute-start.21 = (bf16[4,128,128]{2,1,0:T(8,128)(2,1)}, bf16[4,128,128]{2,1,0:T(8,128)(2,1)S(1)}, u32[]{:S(2)}, u32[]{:S(2)}) collective-permute-start(bf16[4,128,128]{2,1,0:T(8,128)(2,1)} %get-tuple-element.16), channel_id=1, source_target_pairs={{0,16},{1,20},{2,18},{3,22},{4,17},{5,21},{6,19},{7,23},{8,24},{9,... | collective-permute-start | bytes 393224 | tf_op jit(solution)/shard_map/ppermute | solution.py:189
  45.7 1.5 %collective-permute-start.22 = (bf16[4,128,128]{2,1,0:T(8,128)(2,1)}, bf16[4,128,128]{2,1,0:T(8,128)(2,1)S(1)}, u32[]{:S(2)}, u32[]{:S(2)}) collective-permute-start(bf16[4,128,128]{2,1,0:T(8,128)(2,1)} %get-tuple-element.17), channel_id=1, source_target_pairs={{0,24},{1,28},{2,26},{3,30},{4,25},{5,29},{6,27},{7,31},{8,16},{9,... | collective-permute-start | bytes 393224 | tf_op jit(solution)/shard_map/ppermute | solution.py:189
  47.8 3.5 %collective-permute-done.14 = bf16[16,128]{1,0:T(8,128)(2,1)S(1)} collective-permute-done((bf16[16,128]{1,0:T(8,128)(2,1)}, bf16[16,128]{1,0:T(8,128)(2,1)S(1)}, u32[]{:S(2)}, u32[]{:S(2)}) %collective-permute-start.14) | collective-permute-done | bytes 4128 | tf_op jit(solution)/shard_map/ppermute | solution.py:189
  51.3 3.6 %collective-permute-start.15 = (bf16[16,128]{1,0:T(8,128)(2,1)}, bf16[16,128]{1,0:T(8,128)(2,1)S(1)}, u32[]{:S(2)}, u32[]{:S(2)}) collective-permute-start(bf16[16,128]{1,0:T(8,128)(2,1)} %get-tuple-element.12), channel_id=1, source_target_pairs={{0,16},{1,20},{2,18},{3,22},{4,17},{5,21},{6,19},{7,23},{8,24},{9,... | collective-permute-start | bytes 12296 | tf_op jit(solution)/shard_map/ppermute | solution.py:189
  54.9 4.0 %collective-permute-done.15 = bf16[16,128]{1,0:T(8,128)(2,1)S(1)} collective-permute-done((bf16[16,128]{1,0:T(8,128)(2,1)}, bf16[16,128]{1,0:T(8,128)(2,1)S(1)}, u32[]{:S(2)}, u32[]{:S(2)}) %collective-permute-start.15) | collective-permute-done | bytes 4128 | tf_op jit(solution)/shard_map/ppermute | solution.py:189
  58.9 2.6 %collective-permute-start.16 = (bf16[16,128]{1,0:T(8,128)(2,1)}, bf16[16,128]{1,0:T(8,128)(2,1)S(1)}, u32[]{:S(2)}, u32[]{:S(2)}) collective-permute-start(bf16[16,128]{1,0:T(8,128)(2,1)} %get-tuple-element.13), channel_id=1, source_target_pairs={{0,24},{1,28},{2,26},{3,30},{4,25},{5,29},{6,27},{7,31},{8,16},{9,... | collective-permute-start | bytes 12296 | tf_op jit(solution)/shard_map/ppermute | solution.py:189
  61.6 3.0 %collective-permute-done.16 = bf16[16,128]{1,0:T(8,128)(2,1)S(1)} collective-permute-done((bf16[16,128]{1,0:T(8,128)(2,1)}, bf16[16,128]{1,0:T(8,128)(2,1)S(1)}, u32[]{:S(2)}, u32[]{:S(2)}) %collective-permute-start.16) | collective-permute-done | bytes 4128 | tf_op jit(solution)/shard_map/ppermute | solution.py:189
  65.0 1.9 %collective-permute-start.17 = (f32[16,2048]{1,0:T(8,128)S(1)}, f32[16,2048]{1,0:T(8,128)S(1)}, u32[]{:S(2)}, u32[]{:S(2)}) collective-permute-start(f32[16,2048]{1,0:T(8,128)S(1)} %fusion.9), channel_id=1, source_target_pairs={{0,1},{1,0},{2,3},{3,2},{4,5},{5,4},{6,7},{7,6},{8,9},{9,8},{10,11... | collective-permute-start | bytes 393224 | tf_op jit(solution)/shard_map/ppermute | solution.py:242
  67.1 0.8 %collective-permute-done.17 = f32[16,2048]{1,0:T(8,128)S(1)} collective-permute-done((f32[16,2048]{1,0:T(8,128)S(1)}, f32[16,2048]{1,0:T(8,128)S(1)}, u32[]{:S(2)}, u32[]{:S(2)}) %collective-permute-start.17) | collective-permute-done | bytes 131104 | tf_op jit(solution)/shard_map/ppermute | solution.py:242
  67.9 1.6 %collective-permute-start.18 = (bf16[16,2048]{1,0:T(8,128)(2,1)S(1)}, bf16[16,2048]{1,0:T(8,128)(2,1)S(1)}, u32[]{:S(2)}, u32[]{:S(2)}) collective-permute-start(bf16[16,2048]{1,0:T(8,128)(2,1)S(1)} %add_convert_fusion.1), channel_id=1, source_target_pairs={{0,2},{1,3},{2,0},{3,1},{4,6},{5,7},{6,4},{7,5},{8,10},{9,11},{10,... | collective-permute-start | bytes 196616 | tf_op jit(solution)/shard_map/ppermute | solution.py:244
  69.5 2.8 %collective-permute-done.18 = bf16[16,2048]{1,0:T(8,128)(2,1)S(1)} collective-permute-done((bf16[16,2048]{1,0:T(8,128)(2,1)S(1)}, bf16[16,2048]{1,0:T(8,128)(2,1)S(1)}, u32[]{:S(2)}, u32[]{:S(2)}) %collective-permute-start.18) | collective-permute-done | bytes 65568 | tf_op jit(solution)/shard_map/ppermute | solution.py:244
  (90 shorter events, 5.4 us)
Async XLA Ops:
  0.6 63.9 %copy-start = (bf16[512,2048]{1,0:T(8,128)(2,1)S(1)}, bf16[512,2048]{1,0:T(8,128)(2,1)}, u32[]{:S(2)}) copy-start(bf16[512,2048]{1,0:T(8,128)(2,1)} %param.19) | copy-start | bytes 6291460
  0.6 15.1 %copy-start.17 = (s32[32]{0:T(128)S(1)}, s32[32]{0:T(128)}, u32[]{:S(2)}) copy-start(s32[32]{0:T(128)} %param.16) | copy-start | bytes 388
  0.7 11.4 %copy-start.16 = (f32[512]{0:T(512)S(1)}, f32[512]{0:T(512)}, u32[]{:S(2)}) copy-start(f32[512]{0:T(512)} %param.14) | copy-start | bytes 6148
  0.7 11.4 %copy-start.15 = (f32[512]{0:T(512)S(1)}, f32[512]{0:T(512)}, u32[]{:S(2)}) copy-start(f32[512]{0:T(512)} %param.18) | copy-start | bytes 6148
  0.7 15.1 %copy-start.18 = (s32[32]{0:T(128)S(1)}, s32[32]{0:T(128)}, u32[]{:S(2)}) copy-start(s32[32]{0:T(128)} %param.15) | copy-start | bytes 388
  0.7 40.0 %copy-start.10 = (bf16[4,4,2048]{2,1,0:T(4,128)(2,1)S(1)}, bf16[4,4,2048]{2,1,0:T(4,128)(2,1)}, u32[]{:S(2)}) copy-start(bf16[4,4,2048]{2,1,0:T(4,128)(2,1)} %param.10) | copy-start | bytes 196612
  4.5 14.2 %collective-permute-start.10 = (bf16[48,128]{1,0:T(8,128)(2,1)S(1)}, bf16[48,128]{1,0:T(8,128)(2,1)S(1)}, u32[]{:S(2)}, u32[]{:S(2)}) collective-permute-start(bf16[48,128]{1,0:T(8,128)(2,1)S(1)} %get-tuple-element.25), channel_id=1, source_target_pairs={{0,16},{1,20},{2,18},{3,22},{4,17},{5,21},{6,19},{7,23},{8,24},{9,... | collective-permute-start | bytes 36872 | tf_op jit(solution)/shard_map/ppermute | solution.py:189
  8.6 12.2 %collective-permute-start.11 = (bf16[48,128]{1,0:T(8,128)(2,1)S(1)}, bf16[48,128]{1,0:T(8,128)(2,1)S(1)}, u32[]{:S(2)}, u32[]{:S(2)}) collective-permute-start(bf16[48,128]{1,0:T(8,128)(2,1)S(1)} %get-tuple-element.24), channel_id=1, source_target_pairs={{0,24},{1,28},{2,26},{3,30},{4,25},{5,29},{6,27},{7,31},{8,16},{9,... | collective-permute-start | bytes 36872 | tf_op jit(solution)/shard_map/ppermute | solution.py:189
  11.1 10.4 %collective-permute-start = (bf16[4,128,128]{2,1,0:T(8,128)(2,1)S(1)}, bf16[4,128,128]{2,1,0:T(8,128)(2,1)S(1)}, u32[]{:S(2)}, u32[]{:S(2)}) collective-permute-start(bf16[4,128,128]{2,1,0:T(8,128)(2,1)S(1)} %get-tuple-element.22), channel_id=1, source_target_pairs={{0,0},{1,4},{2,2},{3,6},{4,1},{5,5},{6,3},{7,7},{8,8},{9,12},{10,1... | collective-permute-start | bytes 393224 | tf_op jit(solution)/shard_map/ppermute | solution.py:189
  11.8 13.5 %collective-permute-start.1 = (bf16[4,128,128]{2,1,0:T(8,128)(2,1)S(1)}, bf16[4,128,128]{2,1,0:T(8,128)(2,1)S(1)}, u32[]{:S(2)}, u32[]{:S(2)}) collective-permute-start(bf16[4,128,128]{2,1,0:T(8,128)(2,1)S(1)} %get-tuple-element.21), channel_id=1, source_target_pairs={{0,8},{1,12},{2,10},{3,14},{4,9},{5,13},{6,11},{7,15},{8,0},{9,4},... | collective-permute-start | bytes 393224 | tf_op jit(solution)/shard_map/ppermute | solution.py:189
  12.1 4.4 %collective-permute-start.12 = (f32[2,4,128]{2,0,1:T(2,128)S(1)}, f32[2,4,128]{2,0,1:T(2,128)S(1)}, u32[]{:S(2)}, u32[]{:S(2)}) collective-permute-start(f32[2,4,128]{2,0,1:T(2,128)S(1)} %pad_maximum_fusion), channel_id=1, source_target_pairs={{0,1},{1,0},{2,3},{3,2},{4,5},{5,4},{6,7},{7,6},{8,9},{9,8},{10,11... | collective-permute-start | bytes 12296 | tf_op jit(solution)/shard_map/ppermute | solution.py:200
  16.4 12.8 %collective-permute-start.2 = (bf16[4,128,128]{2,1,0:T(8,128)(2,1)S(1)}, bf16[4,128,128]{2,1,0:T(8,128)(2,1)S(1)}, u32[]{:S(2)}, u32[]{:S(2)}) collective-permute-start(bf16[4,128,128]{2,1,0:T(8,128)(2,1)S(1)} %get-tuple-element.23), channel_id=1, source_target_pairs={{0,16},{1,20},{2,18},{3,22},{4,17},{5,21},{6,19},{7,23},{8,24},{9,... | collective-permute-start | bytes 393224 | tf_op jit(solution)/shard_map/ppermute | solution.py:189
  18.7 16.6 %copy-start.11 = (bf16[48,128]{1,0:T(8,128)(2,1)}, bf16[48,128]{1,0:T(8,128)(2,1)S(1)}, u32[]{:S(2)}) copy-start(bf16[48,128]{1,0:T(8,128)(2,1)S(1)} %collective-permute-done.10.refs_10_) | copy-start | bytes 36868
  18.7 11.2 %collective-permute-start.3 = (bf16[4,128,128]{2,1,0:T(8,128)(2,1)S(1)}, bf16[4,128,128]{2,1,0:T(8,128)(2,1)S(1)}, u32[]{:S(2)}, u32[]{:S(2)}) collective-permute-start(bf16[4,128,128]{2,1,0:T(8,128)(2,1)S(1)} %get-tuple-element.20), channel_id=1, source_target_pairs={{0,24},{1,28},{2,26},{3,30},{4,25},{5,29},{6,27},{7,31},{8,16},{9,... | collective-permute-start | bytes 393224 | tf_op jit(solution)/shard_map/ppermute | solution.py:189
  20.9 14.4 %copy-start.12 = (bf16[48,128]{1,0:T(8,128)(2,1)}, bf16[48,128]{1,0:T(8,128)(2,1)S(1)}, u32[]{:S(2)}) copy-start(bf16[48,128]{1,0:T(8,128)(2,1)S(1)} %collective-permute-done.11.refs_11_) | copy-start | bytes 36868
  20.9 9.2 %collective-permute-start.8 = (bf16[48,128]{1,0:T(8,128)(2,1)S(1)}, bf16[48,128]{1,0:T(8,128)(2,1)S(1)}, u32[]{:S(2)}, u32[]{:S(2)}) collective-permute-start(bf16[48,128]{1,0:T(8,128)(2,1)S(1)} %get-tuple-element.27), channel_id=1, source_target_pairs={{0,0},{1,4},{2,2},{3,6},{4,1},{5,5},{6,3},{7,7},{8,8},{9,12},{10,1... | collective-permute-start | bytes 36872 | tf_op jit(solution)/shard_map/ppermute | solution.py:189
  21.5 13.8 %copy-start.2 = (bf16[4,128,128]{2,1,0:T(8,128)(2,1)}, bf16[4,128,128]{2,1,0:T(8,128)(2,1)S(1)}, u32[]{:S(2)}) copy-start(bf16[4,128,128]{2,1,0:T(8,128)(2,1)S(1)} %collective-permute-done.refs_0_) | copy-start | bytes 393220
  21.5 13.0 %collective-permute-start.4 = (bf16[4,128,128]{2,1,0:T(8,128)(2,1)S(1)}, bf16[4,128,128]{2,1,0:T(8,128)(2,1)S(1)}, u32[]{:S(2)}, u32[]{:S(2)}) collective-permute-start(bf16[4,128,128]{2,1,0:T(8,128)(2,1)S(1)} %collective-permute-done.refs_0_), channel_id=1, source_target_pairs={{0,1},{1,0},{2,3},{3,2},{4,5},{5,4},{6,7},{7,6},{8,9},{9,8},{10,11... | collective-permute-start | bytes 393224 | tf_op jit(solution)/shard_map/ppermute | solution.py:212
  25.3 9.2 %collective-permute-start.5 = (bf16[4,128,128]{2,1,0:T(8,128)(2,1)S(1)}, bf16[4,128,128]{2,1,0:T(8,128)(2,1)S(1)}, u32[]{:S(2)}, u32[]{:S(2)}) collective-permute-start(bf16[4,128,128]{2,1,0:T(8,128)(2,1)S(1)} %collective-permute-done.1.refs_1_), channel_id=1, source_target_pairs={{0,1},{1,0},{2,3},{3,2},{4,5},{5,4},{6,7},{7,6},{8,9},{9,8},{10,11... | collective-permute-start | bytes 393224 | tf_op jit(solution)/shard_map/ppermute | solution.py:212
  29.2 5.3 %collective-permute-start.6 = (bf16[4,128,128]{2,1,0:T(8,128)(2,1)S(1)}, bf16[4,128,128]{2,1,0:T(8,128)(2,1)S(1)}, u32[]{:S(2)}, u32[]{:S(2)}) collective-permute-start(bf16[4,128,128]{2,1,0:T(8,128)(2,1)S(1)} %collective-permute-done.2.refs_2_), channel_id=1, source_target_pairs={{0,1},{1,0},{2,3},{3,2},{4,5},{5,4},{6,7},{7,6},{8,9},{9,8},{10,11... | collective-permute-start | bytes 393224 | tf_op jit(solution)/shard_map/ppermute | solution.py:212
  29.9 4.6 %collective-permute-start.7 = (bf16[4,128,128]{2,1,0:T(8,128)(2,1)S(1)}, bf16[4,128,128]{2,1,0:T(8,128)(2,1)S(1)}, u32[]{:S(2)}, u32[]{:S(2)}) collective-permute-start(bf16[4,128,128]{2,1,0:T(8,128)(2,1)S(1)} %collective-permute-done.3.refs_3_), channel_id=1, source_target_pairs={{0,1},{1,0},{2,3},{3,2},{4,5},{5,4},{6,7},{7,6},{8,9},{9,8},{10,11... | collective-permute-start | bytes 393224 | tf_op jit(solution)/shard_map/ppermute | solution.py:212
  30.0 4.5 %collective-permute-start.9 = (bf16[48,128]{1,0:T(8,128)(2,1)S(1)}, bf16[48,128]{1,0:T(8,128)(2,1)S(1)}, u32[]{:S(2)}, u32[]{:S(2)}) collective-permute-start(bf16[48,128]{1,0:T(8,128)(2,1)S(1)} %get-tuple-element.26), channel_id=1, source_target_pairs={{0,8},{1,12},{2,10},{3,14},{4,9},{5,13},{6,11},{7,15},{8,0},{9,4},... | collective-permute-start | bytes 36872 | tf_op jit(solution)/shard_map/ppermute | solution.py:189
  39.3 7.8 %collective-permute-start.13 = (bf16[16,128]{1,0:T(8,128)(2,1)}, bf16[16,128]{1,0:T(8,128)(2,1)S(1)}, u32[]{:S(2)}, u32[]{:S(2)}) collective-permute-start(bf16[16,128]{1,0:T(8,128)(2,1)} %get-tuple-element.10), channel_id=1, source_target_pairs={{0,0},{1,4},{2,2},{3,6},{4,1},{5,5},{6,3},{7,7},{8,8},{9,12},{10,1... | collective-permute-start | bytes 12296 | tf_op jit(solution)/shard_map/ppermute | solution.py:189
  40.7 26.1 %collective-permute-start.19 = (bf16[4,128,128]{2,1,0:T(8,128)(2,1)}, bf16[4,128,128]{2,1,0:T(8,128)(2,1)S(1)}, u32[]{:S(2)}, u32[]{:S(2)}) collective-permute-start(bf16[4,128,128]{2,1,0:T(8,128)(2,1)} %get-tuple-element.14), channel_id=1, source_target_pairs={{0,0},{1,4},{2,2},{3,6},{4,1},{5,5},{6,3},{7,7},{8,8},{9,12},{10,1... | collective-permute-start | bytes 393224 | tf_op jit(solution)/shard_map/ppermute | solution.py:189
  42.3 24.7 %collective-permute-start.20 = (bf16[4,128,128]{2,1,0:T(8,128)(2,1)}, bf16[4,128,128]{2,1,0:T(8,128)(2,1)S(1)}, u32[]{:S(2)}, u32[]{:S(2)}) collective-permute-start(bf16[4,128,128]{2,1,0:T(8,128)(2,1)} %get-tuple-element.15), channel_id=1, source_target_pairs={{0,8},{1,12},{2,10},{3,14},{4,9},{5,13},{6,11},{7,15},{8,0},{9,4},... | collective-permute-start | bytes 393224 | tf_op jit(solution)/shard_map/ppermute | solution.py:189
  44.3 22.7 %collective-permute-start.21 = (bf16[4,128,128]{2,1,0:T(8,128)(2,1)}, bf16[4,128,128]{2,1,0:T(8,128)(2,1)S(1)}, u32[]{:S(2)}, u32[]{:S(2)}) collective-permute-start(bf16[4,128,128]{2,1,0:T(8,128)(2,1)} %get-tuple-element.16), channel_id=1, source_target_pairs={{0,16},{1,20},{2,18},{3,22},{4,17},{5,21},{6,19},{7,23},{8,24},{9,... | collective-permute-start | bytes 393224 | tf_op jit(solution)/shard_map/ppermute | solution.py:189
  45.7 23.8 %collective-permute-start.22 = (bf16[4,128,128]{2,1,0:T(8,128)(2,1)}, bf16[4,128,128]{2,1,0:T(8,128)(2,1)S(1)}, u32[]{:S(2)}, u32[]{:S(2)}) collective-permute-start(bf16[4,128,128]{2,1,0:T(8,128)(2,1)} %get-tuple-element.17), channel_id=1, source_target_pairs={{0,24},{1,28},{2,26},{3,30},{4,25},{5,29},{6,27},{7,31},{8,16},{9,... | collective-permute-start | bytes 393224 | tf_op jit(solution)/shard_map/ppermute | solution.py:189
  47.1 4.2 %collective-permute-start.14 = (bf16[16,128]{1,0:T(8,128)(2,1)}, bf16[16,128]{1,0:T(8,128)(2,1)S(1)}, u32[]{:S(2)}, u32[]{:S(2)}) collective-permute-start(bf16[16,128]{1,0:T(8,128)(2,1)} %get-tuple-element.11), channel_id=1, source_target_pairs={{0,8},{1,12},{2,10},{3,14},{4,9},{5,13},{6,11},{7,15},{8,0},{9,4},... | collective-permute-start | bytes 12296 | tf_op jit(solution)/shard_map/ppermute | solution.py:189
  51.3 7.6 %collective-permute-start.15 = (bf16[16,128]{1,0:T(8,128)(2,1)}, bf16[16,128]{1,0:T(8,128)(2,1)S(1)}, u32[]{:S(2)}, u32[]{:S(2)}) collective-permute-start(bf16[16,128]{1,0:T(8,128)(2,1)} %get-tuple-element.12), channel_id=1, source_target_pairs={{0,16},{1,20},{2,18},{3,22},{4,17},{5,21},{6,19},{7,23},{8,24},{9,... | collective-permute-start | bytes 12296 | tf_op jit(solution)/shard_map/ppermute | solution.py:189
  58.9 5.6 %collective-permute-start.16 = (bf16[16,128]{1,0:T(8,128)(2,1)}, bf16[16,128]{1,0:T(8,128)(2,1)S(1)}, u32[]{:S(2)}, u32[]{:S(2)}) collective-permute-start(bf16[16,128]{1,0:T(8,128)(2,1)} %get-tuple-element.13), channel_id=1, source_target_pairs={{0,24},{1,28},{2,26},{3,30},{4,25},{5,29},{6,27},{7,31},{8,16},{9,... | collective-permute-start | bytes 12296 | tf_op jit(solution)/shard_map/ppermute | solution.py:189
  65.0 2.9 %collective-permute-start.17 = (f32[16,2048]{1,0:T(8,128)S(1)}, f32[16,2048]{1,0:T(8,128)S(1)}, u32[]{:S(2)}, u32[]{:S(2)}) collective-permute-start(f32[16,2048]{1,0:T(8,128)S(1)} %fusion.9), channel_id=1, source_target_pairs={{0,1},{1,0},{2,3},{3,2},{4,5},{5,4},{6,7},{7,6},{8,9},{9,8},{10,11... | collective-permute-start | bytes 393224 | tf_op jit(solution)/shard_map/ppermute | solution.py:242
  67.9 4.4 %collective-permute-start.18 = (bf16[16,2048]{1,0:T(8,128)(2,1)S(1)}, bf16[16,2048]{1,0:T(8,128)(2,1)S(1)}, u32[]{:S(2)}, u32[]{:S(2)}) collective-permute-start(bf16[16,2048]{1,0:T(8,128)(2,1)S(1)} %add_convert_fusion.1), channel_id=1, source_target_pairs={{0,2},{1,3},{2,0},{3,1},{4,6},{5,7},{6,4},{7,5},{8,10},{9,11},{10,... | collective-permute-start | bytes 196616 | tf_op jit(solution)/shard_map/ppermute | solution.py:244
  (10 other events, 34.3 us)

commit v2 on v1

v2 whole, which is shorter than its diff:
```python
import functools

import jax
import jax.numpy as jnp
from jax import lax
from jax.experimental import pallas as pl
from jax.experimental.pallas import tpu as pltpu
from jax.sharding import PartitionSpec as P

BF16 = jnp.bfloat16
F32 = jnp.float32
VMEM = pltpu.VMEM


def convolve(proj, conv_cache, conv_weight, lens):
    taps = conv_weight.shape[0]
    new_tokens = proj.shape[1]
    joined = jnp.concatenate([conv_cache, proj], axis=1).astype(F32)
    places = lens[:, None] + jnp.arange(-(taps - 1), new_tokens, dtype=jnp.int32)[None, :]
    joined = jnp.where((places >= 0)[:, :, None, None], joined, F32(0.0))
    summed = jnp.zeros(proj.shape, F32)
    for offset in range(taps):
        begin_at = taps - 1 - offset
        summed = summed + joined[:, begin_at : begin_at + new_tokens] * conv_weight[offset].astype(F32)
    return jax.nn.silu(summed).astype(BF16)


def recurrence(convolved, relocated, lens, forget_bias, norm_gain, head_size):
    local_reqs, new_tokens, _, channels = convolved.shape
    head_count = channels // head_size
    values = convolved.astype(F32).reshape(local_reqs, new_tokens, 3, head_count, head_size)
    queries = values[:, :, 0]
    keep_rate = jax.nn.sigmoid(values[:, :, 1] + forget_bias.reshape(head_count, head_size))
    inputs = values[:, :, 2]
    current = relocated.astype(F32) * (lens > 0).astype(F32)[:, None, None, None]
    outputs = []
    for position in range(new_tokens):
        rate_now = keep_rate[:, position]
        current = (
            rate_now[..., None] * current
            + (1.0 - rate_now)[..., None] * inputs[:, position][:, :, None, :]
        )
        outputs.append(jnp.einsum("rhk,rhkv->rhv", queries[:, position], current))
    stacked = jnp.stack(outputs, axis=1)
    inverse_rms = lax.rsqrt(jnp.mean(stacked * stacked, axis=-1, keepdims=True) + 1e-06)
    normed = (stacked * inverse_rms).reshape(local_reqs, new_tokens, channels) * norm_gain
    return (normed.astype(BF16), current.astype(BF16))


def generic_body(
    resid, proj, conv_cache, conv_weight, forget_bias, owner, lengths, old_state, norm_gain, out_weight
):
    local_reqs, new_tokens = resid.shape[:2]
    devices = lax.axis_size("req")
    own_index = lax.axis_index("req")
    total_reqs = owner.shape[0]
    head_size = old_state.shape[-1]
    inverse = (
        jnp.zeros((total_reqs,), jnp.int32).at[owner].set(jnp.arange(total_reqs, dtype=jnp.int32))
    )
    local_lens = lax.dynamic_slice_in_dim(lengths, own_index * local_reqs, local_reqs)
    convolved = convolve(proj, conv_cache, conv_weight, local_lens)
    pieces = old_state.reshape(local_reqs, devices, -1)
    spread = lax.all_to_all(pieces, "req", split_axis=1, concat_axis=0, tiled=True)
    spread = spread.reshape(total_reqs, -1)
    picked = jnp.take(spread, inverse, axis=0).reshape(devices, local_reqs, 1, -1)
    routed = lax.all_to_all(picked, "req", split_axis=0, concat_axis=2, tiled=True)
    relocated = routed.reshape(old_state.shape)
    normed, new_state = recurrence(
        convolved, relocated, local_lens, forget_bias, norm_gain, head_size
    )
    flat_normed = normed.reshape(local_reqs * new_tokens, -1)
    flat_resid = resid.reshape(local_reqs * new_tokens, -1)
    partial_value = jnp.dot(flat_normed, out_weight, preferred_element_type=F32)
    summed = lax.psum(partial_value, "head")
    mixed = (flat_resid.astype(F32) + summed).astype(BF16).reshape(resid.shape)
    return (mixed, new_state)


def pack_kernel(blocks, taps, lens_ref, *refs):
    proj_ref, cache_ref, weight_ref, bias_ref, gain_ref, state_ref = refs[:6]
    outs = refs[6 : 6 + blocks]
    joined, conv, tail, sems = refs[6 + blocks :]
    reqs, _, steps, _ = proj_ref.shape
    head_size = state_ref.shape[-1]
    req = lax.axis_index("req")
    z = req // 2
    rows = reqs * head_size
    copies = []
    for s in range(blocks - 1, -1, -1):
        for r in range(reqs):
            copy = pltpu.make_async_copy(
                state_ref.at[r, z ^ s],
                outs[s].at[pl.ds(r * head_size, head_size), :],
                sems.at[s * reqs + r],
            )
            copy.start()
            copies.append(copy)

    past = taps - 1
    for p in range(3):
        weight = weight_ref[p].astype(F32)
        old = [cache_ref[j, p].astype(F32) for j in range(past)]
        for r in range(reqs):
            length = lens_ref[req * reqs + r]
            for j in range(past):
                seen = (length >= past - j).astype(F32)
                joined[j : j + 1, :] = old[j][r : r + 1, :] * seen
            joined[past : past + steps, :] = proj_ref[r, p].astype(F32)
            total = joined[past : past + steps, :] * weight[0:1, :]
            for tap in range(1, taps):
                total = total + joined[past - tap : past - tap + steps, :] * weight[tap : tap + 1, :]
            at = (p * reqs + r) * steps
            conv[at : at + steps, :] = total / (1.0 + jnp.exp(-total))

    count = 3 * reqs * steps
    tail[...] = jnp.zeros_like(tail)
    for s in range(blocks):
        head = z ^ s
        lanes = pl.ds(pl.multiple_of(head * head_size, head_size), head_size)
        tail[0:count, :] = conv[:, lanes]
        for k, ref in enumerate((bias_ref, gain_ref)):
            rest = ref[pl.ds(head, 1), :]
            for piece in range(3):
                value = rest.astype(BF16).astype(F32)
                tail[count + 3 * k + piece : count + 3 * k + piece + 1, :] = value
                rest = rest - value
        outs[s][rows:, :] = tail[...].astype(BF16)
    for copy in copies:
        copy.wait()


def pack(lengths, proj, conv_cache, conv_weight, forget_bias, norm_gain, old_state):
    reqs, blocks, head_size, _ = old_state.shape
    taps = conv_weight.shape[0]
    steps, width = proj.shape[1], proj.shape[-1]
    extra = 3 * reqs * steps + 6
    extra += -extra % 8
    spec = pl.BlockSpec(memory_space=VMEM)
    return pl.pallas_call(
        functools.partial(pack_kernel, blocks, taps),
        out_shape=[VMEM((reqs * head_size + extra, head_size), BF16)] * blocks,
        in_specs=[pl.BlockSpec(memory_space=pltpu.SMEM)]
        + [spec] * 5
        + [pl.BlockSpec(memory_space=pl.ANY)],
        out_specs=[spec] * blocks,
        scratch_shapes=[
            VMEM((taps - 1 + steps + 1, width), F32),
            VMEM((3 * reqs * steps, width), F32),
            VMEM((extra, head_size), F32),
            pltpu.SemaphoreType.DMA((blocks * reqs,)),
        ],
        name="pack",
    )(
        lengths,
        proj.transpose(0, 2, 1, 3),
        conv_cache.transpose(1, 2, 0, 3),
        conv_weight.transpose(1, 0, 2),
        forget_bias.reshape(blocks, head_size),
        norm_gain.reshape(blocks, head_size),
        old_state,
    )


def rows_kernel(blocks, reqs, steps, index_ref, *refs):
    own = refs[:blocks][::-1]
    sib = refs[blocks : 2 * blocks][::-1]
    live_ref = refs[2 * blocks]
    normed_out = refs[2 * blocks + 1 : 3 * blocks + 1]
    pool, turned, values = refs[3 * blocks + 1 : 3 * blocks + 4]
    flat, gathered, columns, lefts, local_out, state_out = refs[3 * blocks + 4 :]
    count = blocks * reqs
    head_size = pool.shape[-1]
    rows = reqs * head_size

    for s in range(blocks):
        flat[...] = own[s][rows:, :].astype(F32)
        for part in range(3):
            for t in range(steps):
                gathered[part * steps + t, pl.ds(s * reqs, reqs), :] = flat[
                    pl.ds(part * reqs * steps + t, reqs, stride=steps), :
                ]
        for r in range(reqs):
            here = slice(r * head_size, (r + 1) * head_size)
            pool[s * reqs + r] = own[s][here, :]
            pool[(blocks + s) * reqs + r] = sib[s][here, :]

    base = 3 * steps * reqs
    bias = flat[base : base + 1, :] + flat[base + 1 : base + 2, :] + flat[base + 2 : base + 3, :]
    gain = flat[base + 3 : base + 4, :] + flat[base + 4 : base + 5, :] + flat[base + 5 : base + 6, :]
    live = live_ref[...]
    query = [gathered[t] for t in range(steps)]
    keep = [jax.nn.sigmoid(gathered[steps + t] + bias) for t in range(steps)]
    inputs = [gathered[2 * steps + t] for t in range(steps)]

    weights = []
    decay = live
    for t in range(steps):
        weights = [w * keep[t] for w in weights] + [1.0 - keep[t]]
        decay = decay * keep[t]
        lefts[pl.ds(t * count, count), :] = query[t] * decay
        values[pl.ds(t * count, count), :] = inputs[t]
        out = jnp.zeros_like(query[t])
        for earlier in range(t + 1):
            score = jnp.sum(query[t] * weights[earlier], axis=-1, keepdims=True)
            out = out + score * inputs[earlier]
        local_out[pl.ds(t, count, stride=steps), :] = out

    for i in range(count):
        left = lefts[pl.ds(i, steps, stride=count), :].astype(BF16)
        state_out[pl.ds(i * steps, steps), :] = jnp.dot(
            left, pool[index_ref[i]], preferred_element_type=F32
        )
    head_out = state_out[...] + local_out[...]
    scale = lax.rsqrt(jnp.mean(head_out * head_out, axis=-1, keepdims=True) + 1e-06)
    normed = (head_out * scale * gain).astype(BF16)
    for s in range(blocks):
        normed_out[s][...] = normed[s * reqs * steps : (s + 1) * reqs * steps]

    columns[...] = jnp.zeros_like(columns)
    columns[pl.ds(0, count), :] = decay
    for t in range(steps):
        columns[pl.ds((1 + t) * count, count), :] = weights[t]
    turned[...] = columns[...].T


def states_kernel(blocks, reqs, steps, apart, index_ref, pool, turned_ref, values, *refs):
    riders = refs[: blocks - len(apart)]
    outs = refs[blocks - len(apart) :]
    head_size = pool.shape[-1]
    count = blocks * reqs
    turned = turned_ref[...]
    for i in range(count):
        current = turned[:, i : i + 1] * pool[index_ref[i]].astype(F32)
        for t in range(steps):
            column = (1 + t) * count + i
            value = values[t * count + i : t * count + i + 1, :]
            current = current + turned[:, column : column + 1] * value
        row = i % reqs * head_size
        outs[i // reqs][row : row + head_size, :] = current.astype(BF16)
    for k, s in enumerate(s for s in range(blocks) if s not in apart):
        outs[s][reqs * head_size :, :] = riders[k][...]


def place_kernel(blocks, *refs):
    parts, out, sems = refs[:blocks], refs[blocks], refs[blocks + 1]
    reqs, _, head_size, _ = out.shape
    z = lax.axis_index("req") // 2
    copies = []
    for s in range(blocks):
        for r in range(reqs):
            copy = pltpu.make_async_copy(
                parts[blocks - 1 - s].at[pl.ds(r * head_size, head_size), :],
                out.at[r, z ^ s],
                sems.at[s * reqs + r],
            )
            copy.start()
            copies.append(copy)
    for copy in copies:
        copy.wait()


def place(back, reqs):
    blocks = len(back)
    head_size = back[0].shape[-1]
    return pl.pallas_call(
        functools.partial(place_kernel, blocks),
        out_shape=jax.ShapeDtypeStruct((reqs, blocks, head_size, head_size), BF16),
        in_specs=[pl.BlockSpec(memory_space=VMEM)] * blocks,
        out_specs=pl.BlockSpec(memory_space=pl.ANY),
        scratch_shapes=[pltpu.SemaphoreType.DMA((blocks * reqs,))],
        name="place",
    )(*on_chip(*back[::-1]))


def on_chip(*arrays):
    return [pltpu.with_memory_space_constraint(value, VMEM) for value in arrays]


def middle_rows(index, own, sib, live, reqs, steps):
    blocks = len(own)
    count = blocks * reqs
    head_size = own[0].shape[-1]
    extra = own[0].shape[0] - reqs * head_size
    columns = -(-count * (1 + steps) // 128) * 128
    spec = pl.BlockSpec(memory_space=VMEM)
    outs = pl.pallas_call(
        functools.partial(rows_kernel, blocks, reqs, steps),
        out_shape=[VMEM((reqs * steps, head_size), BF16)] * blocks
        + [
            VMEM((2 * count, head_size, head_size), BF16),
            VMEM((head_size, columns), F32),
            VMEM((steps * count, head_size), F32),
        ],
        in_specs=[pl.BlockSpec(memory_space=pltpu.SMEM)] + [spec] * (2 * blocks + 1),
        out_specs=[spec] * (blocks + 3),
        scratch_shapes=[
            VMEM((extra, head_size), F32),
            VMEM((3 * steps, count, head_size), F32),
            VMEM((columns, head_size), F32),
            VMEM((steps * count, head_size), F32),
            VMEM((steps * count, head_size), F32),
            VMEM((steps * count, head_size), F32),
        ],
        name="rows",
    )(index, *on_chip(*own[::-1], *sib[::-1], live))
    return outs[:blocks], outs[blocks:]


def middle_states(index, kept, riders, blocks, reqs, steps, apart):
    head_size = kept[0].shape[-1]
    spec = pl.BlockSpec(memory_space=VMEM)
    rows = [reqs * head_size + (0 if s in apart else reqs * steps) for s in range(blocks)]
    return pl.pallas_call(
        functools.partial(states_kernel, blocks, reqs, steps, apart),
        out_shape=[VMEM((r, head_size), BF16) for r in rows],
        in_specs=[pl.BlockSpec(memory_space=pltpu.SMEM)] + [spec] * (3 + len(riders)),
        out_specs=[spec] * blocks,
        name="states",
    )(index, *on_chip(*kept, *riders))


def swapped_body(
    resid, proj, conv_cache, conv_weight, forget_bias, owner, lengths, old_state, norm_gain, out_weight
):
    local_reqs, steps, width = resid.shape
    blocks = old_state.shape[1]
    head_size = old_state.shape[-1]
    n_head = lax.axis_size("head")
    own_req = lax.axis_index("req")
    own_head = lax.axis_index("head")
    z, core = own_req // 2, own_head % 2
    state_rows = local_reqs * head_size

    both = ("req", "head")
    sibling = [(i, i ^ 1) for i in range(n_head)]
    across = [(i, (i + 2) % n_head) for i in range(n_head)]

    def swap(value, s):
        pairs = [
            ((a * 2 + b) * n_head + y * 2 + c, ((a ^ s) * 2 + c) * n_head + y * 2 + b)
            for a in range(blocks)
            for b in range(2)
            for y in range(n_head // 2)
            for c in range(2)
        ]
        return lax.ppermute(value, both, pairs)

    packs = pack(lengths, proj, conv_cache, conv_weight, forget_bias, norm_gain, old_state)
    own = [swap(packs[s], s) for s in range(blocks)]
    sib = [lax.ppermute(own[s][:state_rows], "head", sibling) for s in range(blocks)]

    zs = z ^ jnp.arange(blocks, dtype=jnp.int32)
    slots = ((zs * 2 + core) * local_reqs)[:, None] + jnp.arange(local_reqs, dtype=jnp.int32)[None, :]
    slots = slots.reshape(-1)
    every = jnp.arange(owner.shape[0], dtype=jnp.int32)[None, :]
    source = jnp.sum(jnp.where(owner[None, :] == slots[:, None], every, 0), axis=1)
    device, pos = source // local_reqs, source % local_reqs
    away = (device % 2 != core).astype(jnp.int32)
    index = (away * blocks + ((device // 2) ^ z)) * local_reqs + pos
    lens = jnp.sum(jnp.where(every == slots[:, None], lengths[None, :], 0), axis=1)
    live = jnp.broadcast_to((lens > 0).astype(F32)[:, None], (slots.shape[0], head_size))

    apart = tuple(range(blocks // 2, blocks))
    normed, kept = middle_rows(index, own, sib, live, local_reqs, steps)
    rows = [swap(normed[s], s) if s in apart else None for s in range(blocks)]
    riders = [normed[s] for s in range(blocks) if s not in apart]
    states = middle_states(index, kept, riders, blocks, local_reqs, steps, apart)
    held = lax.optimization_barrier((*states, *[rows[s] for s in apart]))
    states, far = held[:blocks], held[blocks:]
    for s, value in zip(apart, far):
        rows[s] = value
    back = [swap(states[s], s) for s in range(blocks)]

    flat = jnp.zeros((local_reqs * steps, blocks * head_size), BF16)
    for s in range(blocks):
        if s not in apart:
            rows[s] = back[s][state_rows:]
        flat = lax.dynamic_update_slice(flat, rows[s], (0, (z ^ s) * head_size))
    new_state = place(back, local_reqs)
    part = jnp.dot(flat, out_weight, preferred_element_type=F32)
    part = part + lax.ppermute(part, "head", sibling)
    part = part.astype(BF16)
    part = part.astype(F32) + lax.ppermute(part, "head", across).astype(F32)
    mixed = (resid.reshape(-1, width).astype(F32) + part).astype(BF16).reshape(resid.shape)
    return (mixed, new_state)


def solution(mesh):
    in_specs = (
        P("req", None, None),
        P("req", None, None, "head"),
        P("req", None, None, "head"),
        P(None, None, "head"),
        P("head"),
        P(),
        P(),
        P("req", "head", None, None),
        P("head"),
        P("head", None),
    )
    out_specs = (P("req", None, None), P("req", "head", None, None))

    def body(*args):
        heads = args[7].shape[1]
        swapped = (
            mesh.shape["req"] == 2 * heads and heads & (heads - 1) == 0 and mesh.shape["head"] == 4
        )
        return (swapped_body if swapped else generic_body)(*args)

    return jax.shard_map(body, mesh=mesh, in_specs=in_specs, out_specs=out_specs, check_vma=False)
```

time: 73.3 us -> 58.5 us (0.80)
  starting transfers between devices: 40 us -> 21.6 us
  waiting for transfers between devices: 19.6 us -> 25.1 us
  local copies, waits for them, and re-layouts: 4.64 us -> 0.91 us
  Pallas kernels: 3.95 us -> 6.26 us
  other arithmetic: 3.39 us -> 1.52 us
  matrix products: 0.38 us -> 1.97 us
    ppermute x16 -> x10, starting transfers between devices: 28.4 us -> 13.5 us  [swap(): return lax.ppermute(value, both, pairs)]
    ppermute x16 -> x10, waiting for transfers between devices: 15.5 us -> 23.8 us  [swap(): return lax.ppermute(value, both, pairs)]
    ppermute x6 -> x5, starting transfers between devices: 9.71 us -> 4.4 us  [the longest x4 2.82 us: swapped_body(): lax.ppermute(own[s][:state_rows], 'head', sibling)]
    pallas_call x1 -> x4, Pallas kernels: 3.95 us -> 6.26 us  [the longest x1 2.21 us: middle_states(): pl.pallas_call(functools.partial(states_kernel, blocks, reqs, steps, apar...]
    ppermute x6 -> x5, waiting for transfers between devices: 3.27 us -> 1.32 us  [the longest x4 1.31 us: swapped_body(): lax.ppermute(own[s][:state_rows], 'head', sibling)]
    ppermute x1, starting transfers between devices: 1.89 us -> 3.73 us  [swapped_body(): part = part + lax.ppermute(part, 'head', sibling)]
    dot_general x1, matrix products: 0.38 us -> 1.97 us  [swapped_body(): part = jnp.dot(flat, out_weight, preferred_element_type=F32)]
    squeeze x2 -> x0, local copies, waits for them, and re-layouts: 1.15 us -> none  [head_of(): return lax.dynamic_index_in_dim(value, z ^ s, axis, keepdims=False)]
  transfers between devices with their start and end apart: 23 -> 16, of which waited for: 8 -> 9; matrix products, arithmetic and copies ran while one was open for 4% -> 3% of each run, Pallas kernels for 0% -> 5%
where the time goes in v2:
time: 58.5 us; the launch traced here: 58.2 us
  waiting for transfers between devices  25.1 us (43%)
  starting transfers between devices  21.6 us (37%)
  Pallas kernels  6.26 us (11%)
  matrix products  1.97 us (3%)
  other arithmetic  1.52 us (3%)
  local copies, waits for them, and re-layouts  0.91 us (2%)
  between operations  0.83 us (1%)
    ppermute x10, waiting for transfers between devices, swap(): return lax.ppermute(value, both, pairs)  23.8 us
    ppermute x10, starting transfers between devices, swap(): return lax.ppermute(value, both, pairs)  13.5 us
    ppermute x1, starting transfers between devices, swapped_body(): part = part + lax.ppermute(part, 'head', sibling)  3.73 us
    ppermute x4, starting transfers between devices, swapped_body(): lax.ppermute(own[s][:state_rows], 'head', sibling)  2.82 us
    pallas_call x1, Pallas kernels, middle_states(): pl.pallas_call(functools.partial(states_kernel, blocks, reqs, steps, apar...  2.21 us
    pallas_call x1, Pallas kernels, pack(): pl.pallas_call(functools.partial(pack_kernel, blocks, taps), out_shape=[V...  2.01 us
    dot_general x1, matrix products, swapped_body(): part = jnp.dot(flat, out_weight, preferred_element_type=F32)  1.97 us
    ppermute x1, starting transfers between devices, swapped_body(): part = part.astype(F32) + lax.ppermute(part, 'head', across).astype(F32)  1.58 us
  transfers between devices with their start and end apart: 16, of which 9 were waited for; matrix products, arithmetic and copies ran while one was open for 3% of the time, Pallas kernels for 5%

profile of v2, /device:TPU:0, one launch (start us, length us, event | category | flops | bytes accessed | tf_op | source)
XLA Modules:
  0.0 58.2 jit_solution(16482850725939193000)
XLA Ops:
  0.6 2.0 %pack.1 = (bf16[568,128]{1,0:T(8,128)(2,1)S(1)}, bf16[568,128]{1,0:T(8,128)(2,1)S(1)}, bf16[568,128]{1,0:T(8,128)(2,1)S(1)}, bf16[568,128]{1,0:T(8,128)(2,1)S(1)}) custom-call(s32[32]{0:T(128)} %lens_ref.1, bf16[4,3,4,512]{3,2,1,0:T(4,128)(2,1)} %bitcast.7, bf16[3,3,4,512]{3,2,1,0:T(4,128)(2,1)} %bitcast.8, bf16[3,4,512]{2,1,0:T(4,128)(2,1)} %bitcast.9, ...), custom_call_target="tpu_custom_call" | custom-call | tf_op jit(solution)/shard_map/pack/pallas_call | solution.py:140
  2.6 5.1 %collective-permute-start = (bf16[568,128]{1,0:T(8,128)(2,1)S(1)}, bf16[568,128]{1,0:T(8,128)(2,1)S(1)}, u32[]{:S(2)}, u32[]{:S(2)}) collective-permute-start(bf16[568,128]{1,0:T(8,128)(2,1)S(1)} %get-tuple-element.23), channel_id=1, source_target_pairs={{0,24},{1,28},{2,26},{3,30},{4,25},{5,29},{6,27},{7,31},{8,16},{9,... | collective-permute-start | bytes 436232 | tf_op jit(solution)/shard_map/ppermute | solution.py:347
  7.8 0.6 %collective-permute-start.2 = (bf16[568,128]{1,0:T(8,128)(2,1)S(1)}, bf16[568,128]{1,0:T(8,128)(2,1)S(1)}, u32[]{:S(2)}, u32[]{:S(2)}) collective-permute-start(bf16[568,128]{1,0:T(8,128)(2,1)S(1)} %get-tuple-element.25), channel_id=1, source_target_pairs={{0,8},{1,12},{2,10},{3,14},{4,9},{5,13},{6,11},{7,15},{8,0},{9,4},... | collective-permute-start | bytes 436232 | tf_op jit(solution)/shard_map/ppermute | solution.py:347
  8.4 0.7 %collective-permute-start.3 = (bf16[568,128]{1,0:T(8,128)(2,1)S(1)}, bf16[568,128]{1,0:T(8,128)(2,1)S(1)}, u32[]{:S(2)}, u32[]{:S(2)}) collective-permute-start(bf16[568,128]{1,0:T(8,128)(2,1)S(1)} %get-tuple-element.26), channel_id=1, source_target_pairs={{0,0},{1,4},{2,2},{3,6},{4,1},{5,5},{6,3},{7,7},{8,8},{9,12},{10,1... | collective-permute-start | bytes 436232 | tf_op jit(solution)/shard_map/ppermute | solution.py:347
  9.1 0.1 iota_add_fusion
  9.2 0.1 add.80
  9.3 0.9 %select_reduce_fusion = (s32[16]{0:T(128)S(1)}, s32[16]{0:T(128)S(1)}) fusion(s32[32]{0:T(128)} %lens_ref.1, s32[16]{0:T(128)S(1)} %add.80, s32[32]{0:T(128)} %param.15), kind=kLoop, calls=%fused_computation.2 | loop fusion | flops 3040 | bytes 448 | tf_op jit(solution)/shard_map/reduce_sum | solution.py:361
  10.1 0.5 fusion.index_ref
  10.7 1.4 %collective-permute-done.refs_0_ = bf16[568,128]{1,0:T(8,128)(2,1)S(1)} collective-permute-done((bf16[568,128]{1,0:T(8,128)(2,1)S(1)}, bf16[568,128]{1,0:T(8,128)(2,1)S(1)}, u32[]{:S(2)}, u32[]{:S(2)}) %collective-permute-start) | collective-permute-done | bytes 145440 | tf_op jit(solution)/shard_map/ppermute | solution.py:347
  12.1 2.1 %collective-permute-start.4 = (bf16[512,128]{1,0:T(8,128)(2,1)S(1)}, bf16[512,128]{1,0:T(8,128)(2,1)S(1)}, u32[]{:S(2)}, u32[]{:S(2)}) collective-permute-start(bf16[512,128]{1,0:T(8,128)(2,1)S(1)} %slice.24), channel_id=1, source_target_pairs={{0,1},{1,0},{2,3},{3,2},{4,5},{5,4},{6,7},{7,6},{8,9},{9,8},{10,11... | collective-permute-start | bytes 393224 | tf_op jit(solution)/shard_map/ppermute | solution.py:351
  14.2 6.7 %collective-permute-done.1.refs_1_ = bf16[568,128]{1,0:T(8,128)(2,1)S(1)} collective-permute-done((bf16[568,128]{1,0:T(8,128)(2,1)S(1)}, bf16[568,128]{1,0:T(8,128)(2,1)S(1)}, u32[]{:S(2)}, u32[]{:S(2)}) %collective-permute-start.1) | collective-permute-done | bytes 145440 | tf_op jit(solution)/shard_map/ppermute | solution.py:347
  20.9 0.1 collective-permute-start.5
  21.1 0.6 collective-permute-start.6
  21.6 0.1 collective-permute-start.7
  21.7 0.6 %collective-permute-done.5.refs_5_ = bf16[512,128]{1,0:T(8,128)(2,1)S(1)} collective-permute-done((bf16[512,128]{1,0:T(8,128)(2,1)S(1)}, bf16[512,128]{1,0:T(8,128)(2,1)S(1)}, u32[]{:S(2)}, u32[]{:S(2)}) %collective-permute-start.5) | collective-permute-done | bytes 131104 | tf_op jit(solution)/shard_map/ppermute | solution.py:351
  22.4 0.2 collective-permute-done.6.refs_6_
  22.6 0.4 collective-permute-done.7.refs_7_
  23.1 1.1 %rows.1 = (bf16[16,128]{1,0:T(8,128)(2,1)S(1)}, bf16[16,128]{1,0:T(8,128)(2,1)S(1)}, bf16[16,128]{1,0:T(8,128)(2,1)S(1)}, bf16[16,128]{1,0:T(8,128)(2,1)S(1)}, b...) custom-call(s32[16]{0:T(128)} %fusion.index_ref, ...), custom_call_target="tpu_custom_call" | custom-call | tf_op jit(solution)/shard_map/rows/pallas_call | solution.py:287
  24.3 2.5 %collective-permute-start.9 = (bf16[16,128]{1,0:T(8,128)(2,1)S(1)}, bf16[16,128]{1,0:T(8,128)(2,1)S(1)}, u32[]{:S(2)}, u32[]{:S(2)}) collective-permute-start(bf16[16,128]{1,0:T(8,128)(2,1)S(1)} %get-tuple-element.37), channel_id=1, source_target_pairs={{0,24},{1,28},{2,26},{3,30},{4,25},{5,29},{6,27},{7,31},{8,16},{9,... | collective-permute-start | bytes 12296 | tf_op jit(solution)/shard_map/ppermute | solution.py:347
  26.9 2.2 %states.1 = (bf16[528,128]{1,0:T(8,128)(2,1)S(1)}, bf16[528,128]{1,0:T(8,128)(2,1)S(1)}, bf16[512,128]{1,0:T(8,128)(2,1)S(1)}, bf16[512,128]{1,0:T(8,128)(2,1)S(1)}) custom-call(s32[16]{0:T(128)} %fusion.index_ref, bf16[32,128,128]{2,1,0:T(8,128)(2,1)S(1)} %get-tuple-element.27.pool, f32[128,128]{1,0:T(8,128)S(1)} %get-tuple-element.28.turned_ref, ...), custom_call_target="tpu_custom_call" | custom-call | tf_op jit(solution)/shard_map/states/pallas_call | solution.py:314
  29.1 0.7 %collective-permute-done.9 = bf16[16,128]{1,0:T(8,128)(2,1)S(1)} collective-permute-done((bf16[16,128]{1,0:T(8,128)(2,1)S(1)}, bf16[16,128]{1,0:T(8,128)(2,1)S(1)}, u32[]{:S(2)}, u32[]{:S(2)}) %collective-permute-start.9) | collective-permute-done | bytes 4128 | tf_op jit(solution)/shard_map/ppermute | solution.py:347
  29.8 0.7 %collective-permute-start.10 = (bf16[528,128]{1,0:T(8,128)(2,1)S(1)}, bf16[528,128]{1,0:T(8,128)(2,1)S(1)}, u32[]{:S(2)}, u32[]{:S(2)}) collective-permute-start(bf16[528,128]{1,0:T(8,128)(2,1)S(1)} %get-tuple-element.38), channel_id=1, source_target_pairs={{0,0},{1,4},{2,2},{3,6},{4,1},{5,5},{6,3},{7,7},{8,8},{9,12},{10,1... | collective-permute-start | bytes 405512 | tf_op jit(solution)/shard_map/ppermute | solution.py:347
  30.5 1.3 %collective-permute-start.11 = (bf16[528,128]{1,0:T(8,128)(2,1)S(1)}, bf16[528,128]{1,0:T(8,128)(2,1)S(1)}, u32[]{:S(2)}, u32[]{:S(2)}) collective-permute-start(bf16[528,128]{1,0:T(8,128)(2,1)S(1)} %get-tuple-element.39), channel_id=1, source_target_pairs={{0,8},{1,12},{2,10},{3,14},{4,9},{5,13},{6,11},{7,15},{8,0},{9,4},... | collective-permute-start | bytes 405512 | tf_op jit(solution)/shard_map/ppermute | solution.py:347
  31.8 3.8 %collective-permute-done.11.refs_2_ = bf16[528,128]{1,0:T(8,128)(2,1)S(1)} collective-permute-done((bf16[528,128]{1,0:T(8,128)(2,1)S(1)}, bf16[528,128]{1,0:T(8,128)(2,1)S(1)}, u32[]{:S(2)}, u32[]{:S(2)}) %collective-permute-start.11) | collective-permute-done | bytes 135200 | tf_op jit(solution)/shard_map/ppermute | solution.py:347
  35.6 2.0 %fusion.2 = f32[16,2048]{1,0:T(8,128)S(1)} fusion(bf16[16,512]{1,0:T(8,128)(2,1)S(1)} %constant_dynamic-update-slice_fusion.1, bf16[512,2048]{1,0:T(8,128)(2,1)} %param.19), kind=kOutput, calls=%fused_computation.25 | convolution fusion | flops 33554432 | bytes 2244608 | tf_op jit(solution)/shard_map/dot_general | solution.py:381
  37.6 3.7 %collective-permute-start.12 = (f32[16,2048]{1,0:T(8,128)S(1)}, f32[16,2048]{1,0:T(8,128)S(1)}, u32[]{:S(2)}, u32[]{:S(2)}) collective-permute-start(f32[16,2048]{1,0:T(8,128)S(1)} %fusion.2), channel_id=1, source_target_pairs={{0,1},{1,0},{2,3},{3,2},{4,5},{5,4},{6,7},{7,6},{8,9},{9,8},{10,11... | collective-permute-start | bytes 393224 | tf_op jit(solution)/shard_map/ppermute | solution.py:382
  41.3 2.5 %collective-permute-start.14 = (bf16[512,128]{1,0:T(8,128)(2,1)S(1)}, bf16[512,128]{1,0:T(8,128)(2,1)S(1)}, u32[]{:S(2)}, u32[]{:S(2)}) collective-permute-start(bf16[512,128]{1,0:T(8,128)(2,1)S(1)} %get-tuple-element.42), channel_id=1, source_target_pairs={{0,24},{1,28},{2,26},{3,30},{4,25},{5,29},{6,27},{7,31},{8,16},{9,... | collective-permute-start | bytes 393224 | tf_op jit(solution)/shard_map/ppermute | solution.py:347
  43.9 1.6 %collective-permute-start.13 = (bf16[16,2048]{1,0:T(8,128)(2,1)S(1)}, bf16[16,2048]{1,0:T(8,128)(2,1)S(1)}, u32[]{:S(2)}, u32[]{:S(2)}) collective-permute-start(bf16[16,2048]{1,0:T(8,128)(2,1)S(1)} %add_convert_fusion.1), channel_id=1, source_target_pairs={{0,2},{1,3},{2,0},{3,1},{4,6},{5,7},{6,4},{7,5},{8,10},{9,11},{10,... | collective-permute-start | bytes 196616 | tf_op jit(solution)/shard_map/ppermute | solution.py:384
  45.5 4.1 %collective-permute-done.14.refs_0_ = bf16[512,128]{1,0:T(8,128)(2,1)S(1)} collective-permute-done((bf16[512,128]{1,0:T(8,128)(2,1)S(1)}, bf16[512,128]{1,0:T(8,128)(2,1)S(1)}, u32[]{:S(2)}, u32[]{:S(2)}) %collective-permute-start.14) | collective-permute-done | bytes 131104 | tf_op jit(solution)/shard_map/ppermute | solution.py:347
  49.5 7.0 %collective-permute-done.15.refs_1_ = bf16[512,128]{1,0:T(8,128)(2,1)S(1)} collective-permute-done((bf16[512,128]{1,0:T(8,128)(2,1)S(1)}, bf16[512,128]{1,0:T(8,128)(2,1)S(1)}, u32[]{:S(2)}, u32[]{:S(2)}) %collective-permute-start.15) | collective-permute-done | bytes 131104 | tf_op jit(solution)/shard_map/ppermute | solution.py:347
  56.6 0.9 %place.1 = bf16[4,4,128,128]{3,2,1,0:T(8,128)(2,1)} custom-call(bf16[512,128]{1,0:T(8,128)(2,1)S(1)} %collective-permute-done.14.refs_0_, bf16[512,128]{1,0:T(8,128)(2,1)S(1)} %collective-permute-done.15.refs_1_, bf16[528,128]{1,0:T(8,128)(2,1)S(1)} %collective-permute-done.11.refs_2_, bf16[528,128]{1,0:T(8,128)(2,1)S(1)} %collective-permute-done.10.refs_3_), custom_call_target="tpu_custom_call" | custom-call | tf_op jit(solution)/shard_map/place/pallas_call | solution.py:266
  57.5 0.7 %reshape.45 = bf16[4,4,2048]{2,1,0:T(4,128)(2,1)} reshape(bf16[16,2048]{1,0:T(8,128)(2,1)S(1)} %add_convert_fusion) | data formatting | bytes 131072 | tf_op jit(solution)/shard_map/reshape | solution.py:385
  (27 shorter events, 0.4 us)
Async XLA Ops:
  2.6 9.4 %collective-permute-start = (bf16[568,128]{1,0:T(8,128)(2,1)S(1)}, bf16[568,128]{1,0:T(8,128)(2,1)S(1)}, u32[]{:S(2)}, u32[]{:S(2)}) collective-permute-start(bf16[568,128]{1,0:T(8,128)(2,1)S(1)} %get-tuple-element.23), channel_id=1, source_target_pairs={{0,24},{1,28},{2,26},{3,30},{4,25},{5,29},{6,27},{7,31},{8,16},{9,... | collective-permute-start | bytes 436232 | tf_op jit(solution)/shard_map/ppermute | solution.py:347
  7.8 13.2 %collective-permute-start.1 = (bf16[568,128]{1,0:T(8,128)(2,1)S(1)}, bf16[568,128]{1,0:T(8,128)(2,1)S(1)}, u32[]{:S(2)}, u32[]{:S(2)}) collective-permute-start(bf16[568,128]{1,0:T(8,128)(2,1)S(1)} %get-tuple-element.24), channel_id=1, source_target_pairs={{0,16},{1,20},{2,18},{3,22},{4,17},{5,21},{6,19},{7,23},{8,24},{9,... | collective-permute-start | bytes 436232 | tf_op jit(solution)/shard_map/ppermute | solution.py:347
  7.8 13.3 %collective-permute-start.2 = (bf16[568,128]{1,0:T(8,128)(2,1)S(1)}, bf16[568,128]{1,0:T(8,128)(2,1)S(1)}, u32[]{:S(2)}, u32[]{:S(2)}) collective-permute-start(bf16[568,128]{1,0:T(8,128)(2,1)S(1)} %get-tuple-element.25), channel_id=1, source_target_pairs={{0,8},{1,12},{2,10},{3,14},{4,9},{5,13},{6,11},{7,15},{8,0},{9,4},... | collective-permute-start | bytes 436232 | tf_op jit(solution)/shard_map/ppermute | solution.py:347
  8.4 13.2 %collective-permute-start.3 = (bf16[568,128]{1,0:T(8,128)(2,1)S(1)}, bf16[568,128]{1,0:T(8,128)(2,1)S(1)}, u32[]{:S(2)}, u32[]{:S(2)}) collective-permute-start(bf16[568,128]{1,0:T(8,128)(2,1)S(1)} %get-tuple-element.26), channel_id=1, source_target_pairs={{0,0},{1,4},{2,2},{3,6},{4,1},{5,5},{6,3},{7,7},{8,8},{9,12},{10,1... | collective-permute-start | bytes 436232 | tf_op jit(solution)/shard_map/ppermute | solution.py:347
  12.1 9.6 %collective-permute-start.4 = (bf16[512,128]{1,0:T(8,128)(2,1)S(1)}, bf16[512,128]{1,0:T(8,128)(2,1)S(1)}, u32[]{:S(2)}, u32[]{:S(2)}) collective-permute-start(bf16[512,128]{1,0:T(8,128)(2,1)S(1)} %slice.24), channel_id=1, source_target_pairs={{0,1},{1,0},{2,3},{3,2},{4,5},{5,4},{6,7},{7,6},{8,9},{9,8},{10,11... | collective-permute-start | bytes 393224 | tf_op jit(solution)/shard_map/ppermute | solution.py:351
  20.9 1.4 %collective-permute-start.5 = (bf16[512,128]{1,0:T(8,128)(2,1)S(1)}, bf16[512,128]{1,0:T(8,128)(2,1)S(1)}, u32[]{:S(2)}, u32[]{:S(2)}) collective-permute-start(bf16[512,128]{1,0:T(8,128)(2,1)S(1)} %slice.25), channel_id=1, source_target_pairs={{0,1},{1,0},{2,3},{3,2},{4,5},{5,4},{6,7},{7,6},{8,9},{9,8},{10,11... | collective-permute-start | bytes 393224 | tf_op jit(solution)/shard_map/ppermute | solution.py:351
  21.1 1.5 %collective-permute-start.6 = (bf16[512,128]{1,0:T(8,128)(2,1)S(1)}, bf16[512,128]{1,0:T(8,128)(2,1)S(1)}, u32[]{:S(2)}, u32[]{:S(2)}) collective-permute-start(bf16[512,128]{1,0:T(8,128)(2,1)S(1)} %slice.26), channel_id=1, source_target_pairs={{0,1},{1,0},{2,3},{3,2},{4,5},{5,4},{6,7},{7,6},{8,9},{9,8},{10,11... | collective-permute-start | bytes 393224 | tf_op jit(solution)/shard_map/ppermute | solution.py:351
  21.6 1.4 %collective-permute-start.7 = (bf16[512,128]{1,0:T(8,128)(2,1)S(1)}, bf16[512,128]{1,0:T(8,128)(2,1)S(1)}, u32[]{:S(2)}, u32[]{:S(2)}) collective-permute-start(bf16[512,128]{1,0:T(8,128)(2,1)S(1)} %slice.27), channel_id=1, source_target_pairs={{0,1},{1,0},{2,3},{3,2},{4,5},{5,4},{6,7},{7,6},{8,9},{9,8},{10,11... | collective-permute-start | bytes 393224 | tf_op jit(solution)/shard_map/ppermute | solution.py:351
  24.2 21.2 %copy-start = (bf16[4,4,2048]{2,1,0:T(4,128)(2,1)S(1)}, bf16[4,4,2048]{2,1,0:T(4,128)(2,1)}, u32[]{:S(2)}) copy-start(bf16[4,4,2048]{2,1,0:T(4,128)(2,1)} %param.10) | copy-start | bytes 196612
  24.3 4.8 %collective-permute-start.8 = (bf16[16,128]{1,0:T(8,128)(2,1)S(1)}, bf16[16,128]{1,0:T(8,128)(2,1)S(1)}, u32[]{:S(2)}, u32[]{:S(2)}) collective-permute-start(bf16[16,128]{1,0:T(8,128)(2,1)S(1)} %get-tuple-element.36), channel_id=1, source_target_pairs={{0,16},{1,20},{2,18},{3,22},{4,17},{5,21},{6,19},{7,23},{8,24},{9,... | collective-permute-start | bytes 12296 | tf_op jit(solution)/shard_map/ppermute | solution.py:347
  24.3 5.5 %collective-permute-start.9 = (bf16[16,128]{1,0:T(8,128)(2,1)S(1)}, bf16[16,128]{1,0:T(8,128)(2,1)S(1)}, u32[]{:S(2)}, u32[]{:S(2)}) collective-permute-start(bf16[16,128]{1,0:T(8,128)(2,1)S(1)} %get-tuple-element.37), channel_id=1, source_target_pairs={{0,24},{1,28},{2,26},{3,30},{4,25},{5,29},{6,27},{7,31},{8,16},{9,... | collective-permute-start | bytes 12296 | tf_op jit(solution)/shard_map/ppermute | solution.py:347
  29.8 2.0 %collective-permute-start.10 = (bf16[528,128]{1,0:T(8,128)(2,1)S(1)}, bf16[528,128]{1,0:T(8,128)(2,1)S(1)}, u32[]{:S(2)}, u32[]{:S(2)}) collective-permute-start(bf16[528,128]{1,0:T(8,128)(2,1)S(1)} %get-tuple-element.38), channel_id=1, source_target_pairs={{0,0},{1,4},{2,2},{3,6},{4,1},{5,5},{6,3},{7,7},{8,8},{9,12},{10,1... | collective-permute-start | bytes 405512 | tf_op jit(solution)/shard_map/ppermute | solution.py:347
  30.5 5.1 %collective-permute-start.11 = (bf16[528,128]{1,0:T(8,128)(2,1)S(1)}, bf16[528,128]{1,0:T(8,128)(2,1)S(1)}, u32[]{:S(2)}, u32[]{:S(2)}) collective-permute-start(bf16[528,128]{1,0:T(8,128)(2,1)S(1)} %get-tuple-element.39), channel_id=1, source_target_pairs={{0,8},{1,12},{2,10},{3,14},{4,9},{5,13},{6,11},{7,15},{8,0},{9,4},... | collective-permute-start | bytes 405512 | tf_op jit(solution)/shard_map/ppermute | solution.py:347
  37.6 6.3 %collective-permute-start.12 = (f32[16,2048]{1,0:T(8,128)S(1)}, f32[16,2048]{1,0:T(8,128)S(1)}, u32[]{:S(2)}, u32[]{:S(2)}) collective-permute-start(f32[16,2048]{1,0:T(8,128)S(1)} %fusion.2), channel_id=1, source_target_pairs={{0,1},{1,0},{2,3},{3,2},{4,5},{5,4},{6,7},{7,6},{8,9},{9,8},{10,11... | collective-permute-start | bytes 393224 | tf_op jit(solution)/shard_map/ppermute | solution.py:382
  41.3 8.2 %collective-permute-start.14 = (bf16[512,128]{1,0:T(8,128)(2,1)S(1)}, bf16[512,128]{1,0:T(8,128)(2,1)S(1)}, u32[]{:S(2)}, u32[]{:S(2)}) collective-permute-start(bf16[512,128]{1,0:T(8,128)(2,1)S(1)} %get-tuple-element.42), channel_id=1, source_target_pairs={{0,24},{1,28},{2,26},{3,30},{4,25},{5,29},{6,27},{7,31},{8,16},{9,... | collective-permute-start | bytes 393224 | tf_op jit(solution)/shard_map/ppermute | solution.py:347
  43.8 12.8 %collective-permute-start.15 = (bf16[512,128]{1,0:T(8,128)(2,1)S(1)}, bf16[512,128]{1,0:T(8,128)(2,1)S(1)}, u32[]{:S(2)}, u32[]{:S(2)}) collective-permute-start(bf16[512,128]{1,0:T(8,128)(2,1)S(1)} %get-tuple-element.43), channel_id=1, source_target_pairs={{0,16},{1,20},{2,18},{3,22},{4,17},{5,21},{6,19},{7,23},{8,24},{9,... | collective-permute-start | bytes 393224 | tf_op jit(solution)/shard_map/ppermute | solution.py:347
  43.9 13.6 %collective-permute-start.13 = (bf16[16,2048]{1,0:T(8,128)(2,1)S(1)}, bf16[16,2048]{1,0:T(8,128)(2,1)S(1)}, u32[]{:S(2)}, u32[]{:S(2)}) collective-permute-start(bf16[16,2048]{1,0:T(8,128)(2,1)S(1)} %add_convert_fusion.1), channel_id=1, source_target_pairs={{0,2},{1,3},{2,0},{3,1},{4,6},{5,7},{6,4},{7,5},{8,10},{9,11},{10,... | collective-permute-start | bytes 196616 | tf_op jit(solution)/shard_map/ppermute | solution.py:384

commit v3 on v2

--- a/solution.py
+++ b/solution.py
@@ -334,7 +334,6 @@
 
     both = ("req", "head")
     sibling = [(i, i ^ 1) for i in range(n_head)]
-    across = [(i, (i + 2) % n_head) for i in range(n_head)]
 
     def swap(value, s):
         pairs = [
@@ -379,9 +378,12 @@
         flat = lax.dynamic_update_slice(flat, rows[s], (0, (z ^ s) * head_size))
     new_state = place(back, local_reqs)
     part = jnp.dot(flat, out_weight, preferred_element_type=F32)
-    part = part + lax.ppermute(part, "head", sibling)
     part = part.astype(BF16)
-    part = part.astype(F32) + lax.ppermute(part, "head", across).astype(F32)
+    parts = [part] + [
+        lax.ppermute(part, "head", [(i, i ^ k) for i in range(n_head)]) for k in range(1, n_head)
+    ]
+    parts = [value.astype(F32) for value in parts]
+    part = (parts[0] + parts[1]) + (parts[2] + parts[3])
     mixed = (resid.reshape(-1, width).astype(F32) + part).astype(BF16).reshape(resid.shape)
     return (mixed, new_state)
 

time: 58.5 us -> 49.8 us (0.85)
  waiting for transfers between devices: 25.1 us -> 15.1 us
  starting transfers between devices: 21.6 us -> 22.7 us
    ppermute x10, waiting for transfers between devices: 23.8 us -> 11.2 us  [swap(): return lax.ppermute(value, both, pairs)]
    ppermute x2 -> x3, waiting for transfers between devices: 0.01 us -> 2.53 us  [swapped_body(): lax.ppermute(part, 'head', [(i, i ^ k) for i in range(n_head)])]
    ppermute x2 -> x3, starting transfers between devices: 5.32 us -> 6.64 us  [swapped_body(): lax.ppermute(part, 'head', [(i, i ^ k) for i in range(n_head)])]
  transfers between devices with their start and end apart: 16 -> 17, of which waited for: 9 -> 10; matrix products, arithmetic and copies ran while one was open for 3% -> 7% of each run, Pallas kernels for 5% -> 6%
where the time goes in v3:
time: 49.8 us; the launch traced here: 49.4 us
  starting transfers between devices  22.7 us (46%)
  waiting for transfers between devices  15.1 us (30%)
  Pallas kernels  6.39 us (13%)
  matrix products  1.98 us (4%)
  other arithmetic  1.52 us (3%)
  local copies, waits for them, and re-layouts  0.9 us (2%)
  between operations  0.82 us (2%)
    ppermute x10, starting transfers between devices, swap(): return lax.ppermute(value, both, pairs)  13.2 us
    ppermute x10, waiting for transfers between devices, swap(): return lax.ppermute(value, both, pairs)  11.2 us
    ppermute x3, starting transfers between devices, swapped_body(): lax.ppermute(part, 'head', [(i, i ^ k) for i in range(n_head)])  6.64 us
    ppermute x4, starting transfers between devices, swapped_body(): lax.ppermute(own[s][:state_rows], 'head', sibling)  2.82 us
    ppermute x3, waiting for transfers between devices, swapped_body(): lax.ppermute(part, 'head', [(i, i ^ k) for i in range(n_head)])  2.53 us
    pallas_call x1, Pallas kernels, middle_states(): pl.pallas_call(functools.partial(states_kernel, blocks, reqs, steps, apar...  2.21 us
    pallas_call x1, Pallas kernels, pack(): pl.pallas_call(functools.partial(pack_kernel, blocks, taps), out_shape=[V...  2.01 us
    dot_general x1, matrix products, swapped_body(): part = jnp.dot(flat, out_weight, preferred_element_type=F32)  1.98 us
  transfers between devices with their start and end apart: 17, of which 10 were waited for; matrix products, arithmetic and copies ran while one was open for 7% of the time, Pallas kernels for 6%

profile of v3, /device:TPU:0, one launch (start us, length us, event | category | flops | bytes accessed | tf_op | source)
XLA Modules:
  0.0 49.4 jit_solution(12228008887022943871)
XLA Ops:
  0.6 2.0 %pack.1 = (bf16[568,128]{1,0:T(8,128)(2,1)S(1)}, bf16[568,128]{1,0:T(8,128)(2,1)S(1)}, bf16[568,128]{1,0:T(8,128)(2,1)S(1)}, bf16[568,128]{1,0:T(8,128)(2,1)S(1)}) custom-call(s32[32]{0:T(128)} %lens_ref.1, bf16[4,3,4,512]{3,2,1,0:T(4,128)(2,1)} %bitcast.7, bf16[3,3,4,512]{3,2,1,0:T(4,128)(2,1)} %bitcast.8, bf16[3,4,512]{2,1,0:T(4,128)(2,1)} %bitcast.9, ...), custom_call_target="tpu_custom_call" | custom-call | tf_op jit(solution)/shard_map/pack/pallas_call | solution.py:140
  2.6 5.1 %collective-permute-start = (bf16[568,128]{1,0:T(8,128)(2,1)S(1)}, bf16[568,128]{1,0:T(8,128)(2,1)S(1)}, u32[]{:S(2)}, u32[]{:S(2)}) collective-permute-start(bf16[568,128]{1,0:T(8,128)(2,1)S(1)} %get-tuple-element.23), channel_id=1, source_target_pairs={{0,24},{1,28},{2,26},{3,30},{4,25},{5,29},{6,27},{7,31},{8,16},{9,... | collective-permute-start | bytes 436232 | tf_op jit(solution)/shard_map/ppermute | solution.py:346
  7.8 0.6 %collective-permute-start.2 = (bf16[568,128]{1,0:T(8,128)(2,1)S(1)}, bf16[568,128]{1,0:T(8,128)(2,1)S(1)}, u32[]{:S(2)}, u32[]{:S(2)}) collective-permute-start(bf16[568,128]{1,0:T(8,128)(2,1)S(1)} %get-tuple-element.25), channel_id=1, source_target_pairs={{0,8},{1,12},{2,10},{3,14},{4,9},{5,13},{6,11},{7,15},{8,0},{9,4},... | collective-permute-start | bytes 436232 | tf_op jit(solution)/shard_map/ppermute | solution.py:346
  8.4 0.7 %collective-permute-start.3 = (bf16[568,128]{1,0:T(8,128)(2,1)S(1)}, bf16[568,128]{1,0:T(8,128)(2,1)S(1)}, u32[]{:S(2)}, u32[]{:S(2)}) collective-permute-start(bf16[568,128]{1,0:T(8,128)(2,1)S(1)} %get-tuple-element.26), channel_id=1, source_target_pairs={{0,0},{1,4},{2,2},{3,6},{4,1},{5,5},{6,3},{7,7},{8,8},{9,12},{10,1... | collective-permute-start | bytes 436232 | tf_op jit(solution)/shard_map/ppermute | solution.py:346
  9.2 0.1 add.83
  9.3 0.9 %select_reduce_fusion = (s32[16]{0:T(128)S(1)}, s32[16]{0:T(128)S(1)}) fusion(s32[32]{0:T(128)} %lens_ref.1, s32[16]{0:T(128)S(1)} %add.83, s32[32]{0:T(128)} %param.15), kind=kLoop, calls=%fused_computation.2 | loop fusion | flops 3040 | bytes 448 | tf_op jit(solution)/shard_map/reduce_sum | solution.py:360
  10.1 0.5 %fusion.index_ref = s32[16]{0:T(128)} fusion(s32[16]{0:T(128)S(1)} %get-tuple-element.45, s32[]{:T(128)S(6)} %select_n.48, s32[]{:T(128)S(6)} %select_n.49), kind=kLoop, calls=%fused_computation.22 | loop fusion | flops 704 | bytes 136 | tf_op jit(solution)/shard_map/add | solution.py:359
  10.7 1.4 %collective-permute-done.refs_0_ = bf16[568,128]{1,0:T(8,128)(2,1)S(1)} collective-permute-done((bf16[568,128]{1,0:T(8,128)(2,1)S(1)}, bf16[568,128]{1,0:T(8,128)(2,1)S(1)}, u32[]{:S(2)}, u32[]{:S(2)}) %collective-permute-start) | collective-permute-done | bytes 145440 | tf_op jit(solution)/shard_map/ppermute | solution.py:346
  12.1 2.1 %collective-permute-start.4 = (bf16[512,128]{1,0:T(8,128)(2,1)S(1)}, bf16[512,128]{1,0:T(8,128)(2,1)S(1)}, u32[]{:S(2)}, u32[]{:S(2)}) collective-permute-start(bf16[512,128]{1,0:T(8,128)(2,1)S(1)} %slice.24), channel_id=1, source_target_pairs={{0,1},{1,0},{2,3},{3,2},{4,5},{5,4},{6,7},{7,6},{8,9},{9,8},{10,11... | collective-permute-start | bytes 393224 | tf_op jit(solution)/shard_map/ppermute | solution.py:350
  14.2 6.7 %collective-permute-done.1.refs_1_ = bf16[568,128]{1,0:T(8,128)(2,1)S(1)} collective-permute-done((bf16[568,128]{1,0:T(8,128)(2,1)S(1)}, bf16[568,128]{1,0:T(8,128)(2,1)S(1)}, u32[]{:S(2)}, u32[]{:S(2)}) %collective-permute-start.1) | collective-permute-done | bytes 145440 | tf_op jit(solution)/shard_map/ppermute | solution.py:346
  21.1 0.6 %collective-permute-start.6 = (bf16[512,128]{1,0:T(8,128)(2,1)S(1)}, bf16[512,128]{1,0:T(8,128)(2,1)S(1)}, u32[]{:S(2)}, u32[]{:S(2)}) collective-permute-start(bf16[512,128]{1,0:T(8,128)(2,1)S(1)} %slice.26), channel_id=1, source_target_pairs={{0,1},{1,0},{2,3},{3,2},{4,5},{5,4},{6,7},{7,6},{8,9},{9,8},{10,11... | collective-permute-start | bytes 393224 | tf_op jit(solution)/shard_map/ppermute | solution.py:350
  21.6 0.1 collective-permute-start.7
  21.7 0.6 %collective-permute-done.5.refs_5_ = bf16[512,128]{1,0:T(8,128)(2,1)S(1)} collective-permute-done((bf16[512,128]{1,0:T(8,128)(2,1)S(1)}, bf16[512,128]{1,0:T(8,128)(2,1)S(1)}, u32[]{:S(2)}, u32[]{:S(2)}) %collective-permute-start.5) | collective-permute-done | bytes 131104 | tf_op jit(solution)/shard_map/ppermute | solution.py:350
  22.4 0.2 collective-permute-done.6.refs_6_
  22.6 0.4 collective-permute-done.7.refs_7_
  23.1 1.3 %rows.1 = (bf16[16,128]{1,0:T(8,128)(2,1)S(1)}, bf16[16,128]{1,0:T(8,128)(2,1)S(1)}, bf16[16,128]{1,0:T(8,128)(2,1)S(1)}, bf16[16,128]{1,0:T(8,128)(2,1)S(1)}, b...) custom-call(s32[16]{0:T(128)} %fusion.index_ref, ...), custom_call_target="tpu_custom_call" | custom-call | tf_op jit(solution)/shard_map/rows/pallas_call | solution.py:287
  24.5 2.5 %collective-permute-start.9 = (bf16[16,128]{1,0:T(8,128)(2,1)S(1)}, bf16[16,128]{1,0:T(8,128)(2,1)S(1)}, u32[]{:S(2)}, u32[]{:S(2)}) collective-permute-start(bf16[16,128]{1,0:T(8,128)(2,1)S(1)} %get-tuple-element.37), channel_id=1, source_target_pairs={{0,24},{1,28},{2,26},{3,30},{4,25},{5,29},{6,27},{7,31},{8,16},{9,... | collective-permute-start | bytes 12296 | tf_op jit(solution)/shard_map/ppermute | solution.py:346
  27.0 2.2 %states.1 = (bf16[528,128]{1,0:T(8,128)(2,1)S(1)}, bf16[528,128]{1,0:T(8,128)(2,1)S(1)}, bf16[512,128]{1,0:T(8,128)(2,1)S(1)}, bf16[512,128]{1,0:T(8,128)(2,1)S(1)}) custom-call(s32[16]{0:T(128)} %fusion.index_ref, bf16[32,128,128]{2,1,0:T(8,128)(2,1)S(1)} %get-tuple-element.27.pool, f32[128,128]{1,0:T(8,128)S(1)} %get-tuple-element.28.turned_ref, ...), custom_call_target="tpu_custom_call" | custom-call | tf_op jit(solution)/shard_map/states/pallas_call | solution.py:314
  29.2 0.7 %collective-permute-done.9 = bf16[16,128]{1,0:T(8,128)(2,1)S(1)} collective-permute-done((bf16[16,128]{1,0:T(8,128)(2,1)S(1)}, bf16[16,128]{1,0:T(8,128)(2,1)S(1)}, u32[]{:S(2)}, u32[]{:S(2)}) %collective-permute-start.9) | collective-permute-done | bytes 4128 | tf_op jit(solution)/shard_map/ppermute | solution.py:346
  29.9 0.7 %collective-permute-start.10 = (bf16[528,128]{1,0:T(8,128)(2,1)S(1)}, bf16[528,128]{1,0:T(8,128)(2,1)S(1)}, u32[]{:S(2)}, u32[]{:S(2)}) collective-permute-start(bf16[528,128]{1,0:T(8,128)(2,1)S(1)} %get-tuple-element.38), channel_id=1, source_target_pairs={{0,0},{1,4},{2,2},{3,6},{4,1},{5,5},{6,3},{7,7},{8,8},{9,12},{10,1... | collective-permute-start | bytes 405512 | tf_op jit(solution)/shard_map/ppermute | solution.py:346
  30.6 1.3 %collective-permute-start.11 = (bf16[528,128]{1,0:T(8,128)(2,1)S(1)}, bf16[528,128]{1,0:T(8,128)(2,1)S(1)}, u32[]{:S(2)}, u32[]{:S(2)}) collective-permute-start(bf16[528,128]{1,0:T(8,128)(2,1)S(1)} %get-tuple-element.39), channel_id=1, source_target_pairs={{0,8},{1,12},{2,10},{3,14},{4,9},{5,13},{6,11},{7,15},{8,0},{9,4},... | collective-permute-start | bytes 405512 | tf_op jit(solution)/shard_map/ppermute | solution.py:346
  31.9 1.5 %collective-permute-start.15 = (bf16[512,128]{1,0:T(8,128)(2,1)S(1)}, bf16[512,128]{1,0:T(8,128)(2,1)S(1)}, u32[]{:S(2)}, u32[]{:S(2)}) collective-permute-start(bf16[512,128]{1,0:T(8,128)(2,1)S(1)} %get-tuple-element.42), channel_id=1, source_target_pairs={{0,24},{1,28},{2,26},{3,30},{4,25},{5,29},{6,27},{7,31},{8,16},{9,... | collective-permute-start | bytes 393224 | tf_op jit(solution)/shard_map/ppermute | solution.py:346
  33.4 0.8 %collective-permute-start.16 = (bf16[512,128]{1,0:T(8,128)(2,1)S(1)}, bf16[512,128]{1,0:T(8,128)(2,1)S(1)}, u32[]{:S(2)}, u32[]{:S(2)}) collective-permute-start(bf16[512,128]{1,0:T(8,128)(2,1)S(1)} %get-tuple-element.43), channel_id=1, source_target_pairs={{0,16},{1,20},{2,18},{3,22},{4,17},{5,21},{6,19},{7,23},{8,24},{9,... | collective-permute-start | bytes 393224 | tf_op jit(solution)/shard_map/ppermute | solution.py:346
  34.2 1.5 %collective-permute-done.11.refs_2_ = bf16[528,128]{1,0:T(8,128)(2,1)S(1)} collective-permute-done((bf16[528,128]{1,0:T(8,128)(2,1)S(1)}, bf16[528,128]{1,0:T(8,128)(2,1)S(1)}, u32[]{:S(2)}, u32[]{:S(2)}) %collective-permute-start.11) | collective-permute-done | bytes 135200 | tf_op jit(solution)/shard_map/ppermute | solution.py:346
  35.7 2.0 %convolution_convert_fusion = bf16[16,2048]{1,0:T(8,128)(2,1)S(1)} fusion(bf16[16,512]{1,0:T(8,128)(2,1)S(1)} %constant_dynamic-update-slice_fusion.1, bf16[512,2048]{1,0:T(8,128)(2,1)} %param.19), kind=kOutput, calls=%fused_computation | convolution fusion | flops 33587200 | bytes 2179072 | tf_op jit(solution)/shard_map/dot_general | solution.py:380
  37.7 5.1 %collective-permute-start.12 = (bf16[16,2048]{1,0:T(8,128)(2,1)S(1)}, bf16[16,2048]{1,0:T(8,128)(2,1)S(1)}, u32[]{:S(2)}, u32[]{:S(2)}) collective-permute-start(bf16[16,2048]{1,0:T(8,128)(2,1)S(1)} %convolution_convert_fusion), channel_id=1, source_target_pairs={{0,1},{1,0},{2,3},{3,2},{4,5},{5,4},{6,7},{7,6},{8,9},{9,8},{10,11... | collective-permute-start | bytes 196616 | tf_op jit(solution)/shard_map/ppermute | solution.py:383
  42.8 1.5 %collective-permute-start.13 = (bf16[16,2048]{1,0:T(8,128)(2,1)S(1)}, bf16[16,2048]{1,0:T(8,128)(2,1)S(1)}, u32[]{:S(2)}, u32[]{:S(2)}) collective-permute-start(bf16[16,2048]{1,0:T(8,128)(2,1)S(1)} %convolution_convert_fusion), channel_id=1, source_target_pairs={{0,2},{1,3},{2,0},{3,1},{4,6},{5,7},{6,4},{7,5},{8,10},{9,11},{10,... | collective-permute-start | bytes 196616 | tf_op jit(solution)/shard_map/ppermute | solution.py:383
  44.4 0.9 %collective-permute-done.16.refs_1_ = bf16[512,128]{1,0:T(8,128)(2,1)S(1)} collective-permute-done((bf16[512,128]{1,0:T(8,128)(2,1)S(1)}, bf16[512,128]{1,0:T(8,128)(2,1)S(1)}, u32[]{:S(2)}, u32[]{:S(2)}) %collective-permute-start.16) | collective-permute-done | bytes 131104 | tf_op jit(solution)/shard_map/ppermute | solution.py:346
  45.2 0.9 %place.1 = bf16[4,4,128,128]{3,2,1,0:T(8,128)(2,1)} custom-call(bf16[512,128]{1,0:T(8,128)(2,1)S(1)} %collective-permute-done.15.refs_0_, bf16[512,128]{1,0:T(8,128)(2,1)S(1)} %collective-permute-done.16.refs_1_, bf16[528,128]{1,0:T(8,128)(2,1)S(1)} %collective-permute-done.11.refs_2_, bf16[528,128]{1,0:T(8,128)(2,1)S(1)} %collective-permute-done.10.refs_3_), custom_call_target="tpu_custom_call" | custom-call | tf_op jit(solution)/shard_map/place/pallas_call | solution.py:266
  46.2 0.9 %collective-permute-done.13 = bf16[16,2048]{1,0:T(8,128)(2,1)S(1)} collective-permute-done((bf16[16,2048]{1,0:T(8,128)(2,1)S(1)}, bf16[16,2048]{1,0:T(8,128)(2,1)S(1)}, u32[]{:S(2)}, u32[]{:S(2)}) %collective-permute-start.13) | collective-permute-done | bytes 65568 | tf_op jit(solution)/shard_map/ppermute | solution.py:383
  47.1 1.6 %collective-permute-done.14 = bf16[16,2048]{1,0:T(8,128)(2,1)S(1)} collective-permute-done((bf16[16,2048]{1,0:T(8,128)(2,1)S(1)}, bf16[16,2048]{1,0:T(8,128)(2,1)S(1)}, u32[]{:S(2)}, u32[]{:S(2)}) %collective-permute-start.14) | collective-permute-done | bytes 65568 | tf_op jit(solution)/shard_map/ppermute | solution.py:383
  48.7 0.7 %reshape.45 = bf16[4,4,2048]{2,1,0:T(4,128)(2,1)} reshape(bf16[16,2048]{1,0:T(8,128)(2,1)S(1)} %add_convert_fusion) | data formatting | bytes 131072 | tf_op jit(solution)/shard_map/reshape | solution.py:387
  (28 shorter events, 0.4 us)
Async XLA Ops:
  2.6 9.4 %collective-permute-start = (bf16[568,128]{1,0:T(8,128)(2,1)S(1)}, bf16[568,128]{1,0:T(8,128)(2,1)S(1)}, u32[]{:S(2)}, u32[]{:S(2)}) collective-permute-start(bf16[568,128]{1,0:T(8,128)(2,1)S(1)} %get-tuple-element.23), channel_id=1, source_target_pairs={{0,24},{1,28},{2,26},{3,30},{4,25},{5,29},{6,27},{7,31},{8,16},{9,... | collective-permute-start | bytes 436232 | tf_op jit(solution)/shard_map/ppermute | solution.py:346
  7.8 13.2 %collective-permute-start.1 = (bf16[568,128]{1,0:T(8,128)(2,1)S(1)}, bf16[568,128]{1,0:T(8,128)(2,1)S(1)}, u32[]{:S(2)}, u32[]{:S(2)}) collective-permute-start(bf16[568,128]{1,0:T(8,128)(2,1)S(1)} %get-tuple-element.24), channel_id=1, source_target_pairs={{0,16},{1,20},{2,18},{3,22},{4,17},{5,21},{6,19},{7,23},{8,24},{9,... | collective-permute-start | bytes 436232 | tf_op jit(solution)/shard_map/ppermute | solution.py:346
  7.8 13.3 %collective-permute-start.2 = (bf16[568,128]{1,0:T(8,128)(2,1)S(1)}, bf16[568,128]{1,0:T(8,128)(2,1)S(1)}, u32[]{:S(2)}, u32[]{:S(2)}) collective-permute-start(bf16[568,128]{1,0:T(8,128)(2,1)S(1)} %get-tuple-element.25), channel_id=1, source_target_pairs={{0,8},{1,12},{2,10},{3,14},{4,9},{5,13},{6,11},{7,15},{8,0},{9,4},... | collective-permute-start | bytes 436232 | tf_op jit(solution)/shard_map/ppermute | solution.py:346
  8.4 13.2 %collective-permute-start.3 = (bf16[568,128]{1,0:T(8,128)(2,1)S(1)}, bf16[568,128]{1,0:T(8,128)(2,1)S(1)}, u32[]{:S(2)}, u32[]{:S(2)}) collective-permute-start(bf16[568,128]{1,0:T(8,128)(2,1)S(1)} %get-tuple-element.26), channel_id=1, source_target_pairs={{0,0},{1,4},{2,2},{3,6},{4,1},{5,5},{6,3},{7,7},{8,8},{9,12},{10,1... | collective-permute-start | bytes 436232 | tf_op jit(solution)/shard_map/ppermute | solution.py:346
  12.1 9.6 %collective-permute-start.4 = (bf16[512,128]{1,0:T(8,128)(2,1)S(1)}, bf16[512,128]{1,0:T(8,128)(2,1)S(1)}, u32[]{:S(2)}, u32[]{:S(2)}) collective-permute-start(bf16[512,128]{1,0:T(8,128)(2,1)S(1)} %slice.24), channel_id=1, source_target_pairs={{0,1},{1,0},{2,3},{3,2},{4,5},{5,4},{6,7},{7,6},{8,9},{9,8},{10,11... | collective-permute-start | bytes 393224 | tf_op jit(solution)/shard_map/ppermute | solution.py:350
  20.9 1.4 %collective-permute-start.5 = (bf16[512,128]{1,0:T(8,128)(2,1)S(1)}, bf16[512,128]{1,0:T(8,128)(2,1)S(1)}, u32[]{:S(2)}, u32[]{:S(2)}) collective-permute-start(bf16[512,128]{1,0:T(8,128)(2,1)S(1)} %slice.25), channel_id=1, source_target_pairs={{0,1},{1,0},{2,3},{3,2},{4,5},{5,4},{6,7},{7,6},{8,9},{9,8},{10,11... | collective-permute-start | bytes 393224 | tf_op jit(solution)/shard_map/ppermute | solution.py:350
  21.1 1.5 %collective-permute-start.6 = (bf16[512,128]{1,0:T(8,128)(2,1)S(1)}, bf16[512,128]{1,0:T(8,128)(2,1)S(1)}, u32[]{:S(2)}, u32[]{:S(2)}) collective-permute-start(bf16[512,128]{1,0:T(8,128)(2,1)S(1)} %slice.26), channel_id=1, source_target_pairs={{0,1},{1,0},{2,3},{3,2},{4,5},{5,4},{6,7},{7,6},{8,9},{9,8},{10,11... | collective-permute-start | bytes 393224 | tf_op jit(solution)/shard_map/ppermute | solution.py:350
  21.6 1.4 %collective-permute-start.7 = (bf16[512,128]{1,0:T(8,128)(2,1)S(1)}, bf16[512,128]{1,0:T(8,128)(2,1)S(1)}, u32[]{:S(2)}, u32[]{:S(2)}) collective-permute-start(bf16[512,128]{1,0:T(8,128)(2,1)S(1)} %slice.27), channel_id=1, source_target_pairs={{0,1},{1,0},{2,3},{3,2},{4,5},{5,4},{6,7},{7,6},{8,9},{9,8},{10,11... | collective-permute-start | bytes 393224 | tf_op jit(solution)/shard_map/ppermute | solution.py:350
  23.1 21.2 %copy-start = (bf16[4,4,2048]{2,1,0:T(4,128)(2,1)S(1)}, bf16[4,4,2048]{2,1,0:T(4,128)(2,1)}, u32[]{:S(2)}) copy-start(bf16[4,4,2048]{2,1,0:T(4,128)(2,1)} %param.10) | copy-start | bytes 196612
  24.4 4.8 %collective-permute-start.8 = (bf16[16,128]{1,0:T(8,128)(2,1)S(1)}, bf16[16,128]{1,0:T(8,128)(2,1)S(1)}, u32[]{:S(2)}, u32[]{:S(2)}) collective-permute-start(bf16[16,128]{1,0:T(8,128)(2,1)S(1)} %get-tuple-element.36), channel_id=1, source_target_pairs={{0,16},{1,20},{2,18},{3,22},{4,17},{5,21},{6,19},{7,23},{8,24},{9,... | collective-permute-start | bytes 12296 | tf_op jit(solution)/shard_map/ppermute | solution.py:346
  24.5 5.5 %collective-permute-start.9 = (bf16[16,128]{1,0:T(8,128)(2,1)S(1)}, bf16[16,128]{1,0:T(8,128)(2,1)S(1)}, u32[]{:S(2)}, u32[]{:S(2)}) collective-permute-start(bf16[16,128]{1,0:T(8,128)(2,1)S(1)} %get-tuple-element.37), channel_id=1, source_target_pairs={{0,24},{1,28},{2,26},{3,30},{4,25},{5,29},{6,27},{7,31},{8,16},{9,... | collective-permute-start | bytes 12296 | tf_op jit(solution)/shard_map/ppermute | solution.py:346
  29.9 4.2 %collective-permute-start.10 = (bf16[528,128]{1,0:T(8,128)(2,1)S(1)}, bf16[528,128]{1,0:T(8,128)(2,1)S(1)}, u32[]{:S(2)}, u32[]{:S(2)}) collective-permute-start(bf16[528,128]{1,0:T(8,128)(2,1)S(1)} %get-tuple-element.38), channel_id=1, source_target_pairs={{0,0},{1,4},{2,2},{3,6},{4,1},{5,5},{6,3},{7,7},{8,8},{9,12},{10,1... | collective-permute-start | bytes 405512 | tf_op jit(solution)/shard_map/ppermute | solution.py:346
  30.6 5.1 %collective-permute-start.11 = (bf16[528,128]{1,0:T(8,128)(2,1)S(1)}, bf16[528,128]{1,0:T(8,128)(2,1)S(1)}, u32[]{:S(2)}, u32[]{:S(2)}) collective-permute-start(bf16[528,128]{1,0:T(8,128)(2,1)S(1)} %get-tuple-element.39), channel_id=1, source_target_pairs={{0,8},{1,12},{2,10},{3,14},{4,9},{5,13},{6,11},{7,15},{8,0},{9,4},... | collective-permute-start | bytes 405512 | tf_op jit(solution)/shard_map/ppermute | solution.py:346
  31.9 12.5 %collective-permute-start.15 = (bf16[512,128]{1,0:T(8,128)(2,1)S(1)}, bf16[512,128]{1,0:T(8,128)(2,1)S(1)}, u32[]{:S(2)}, u32[]{:S(2)}) collective-permute-start(bf16[512,128]{1,0:T(8,128)(2,1)S(1)} %get-tuple-element.42), channel_id=1, source_target_pairs={{0,24},{1,28},{2,26},{3,30},{4,25},{5,29},{6,27},{7,31},{8,16},{9,... | collective-permute-start | bytes 393224 | tf_op jit(solution)/shard_map/ppermute | solution.py:346
  33.4 11.8 %collective-permute-start.16 = (bf16[512,128]{1,0:T(8,128)(2,1)S(1)}, bf16[512,128]{1,0:T(8,128)(2,1)S(1)}, u32[]{:S(2)}, u32[]{:S(2)}) collective-permute-start(bf16[512,128]{1,0:T(8,128)(2,1)S(1)} %get-tuple-element.43), channel_id=1, source_target_pairs={{0,16},{1,20},{2,18},{3,22},{4,17},{5,21},{6,19},{7,23},{8,24},{9,... | collective-permute-start | bytes 393224 | tf_op jit(solution)/shard_map/ppermute | solution.py:346
  37.7 8.5 %collective-permute-start.12 = (bf16[16,2048]{1,0:T(8,128)(2,1)S(1)}, bf16[16,2048]{1,0:T(8,128)(2,1)S(1)}, u32[]{:S(2)}, u32[]{:S(2)}) collective-permute-start(bf16[16,2048]{1,0:T(8,128)(2,1)S(1)} %convolution_convert_fusion), channel_id=1, source_target_pairs={{0,1},{1,0},{2,3},{3,2},{4,5},{5,4},{6,7},{7,6},{8,9},{9,8},{10,11... | collective-permute-start | bytes 196616 | tf_op jit(solution)/shard_map/ppermute | solution.py:383
  42.8 4.3 %collective-permute-start.13 = (bf16[16,2048]{1,0:T(8,128)(2,1)S(1)}, bf16[16,2048]{1,0:T(8,128)(2,1)S(1)}, u32[]{:S(2)}, u32[]{:S(2)}) collective-permute-start(bf16[16,2048]{1,0:T(8,128)(2,1)S(1)} %convolution_convert_fusion), channel_id=1, source_target_pairs={{0,2},{1,3},{2,0},{3,1},{4,6},{5,7},{6,4},{7,5},{8,10},{9,11},{10,... | collective-permute-start | bytes 196616 | tf_op jit(solution)/shard_map/ppermute | solution.py:383
  44.3 4.4 %collective-permute-start.14 = (bf16[16,2048]{1,0:T(8,128)(2,1)S(1)}, bf16[16,2048]{1,0:T(8,128)(2,1)S(1)}, u32[]{:S(2)}, u32[]{:S(2)}) collective-permute-start(bf16[16,2048]{1,0:T(8,128)(2,1)S(1)} %convolution_convert_fusion), channel_id=1, source_target_pairs={{0,3},{1,2},{2,1},{3,0},{4,7},{5,6},{6,5},{7,4},{8,11},{9,10},{10,... | collective-permute-start | bytes 196616 | tf_op jit(solution)/shard_map/ppermute | solution.py:383

commit v4 on v3

--- a/solution.py
+++ b/solution.py
@@ -10,6 +10,7 @@
 BF16 = jnp.bfloat16
 F32 = jnp.float32
 VMEM = pltpu.VMEM
+PARAMS = pltpu.CompilerParams(vmem_limit_bytes=16 * 2**20)
 
 
 def convolve(proj, conv_cache, conv_weight, lens):
@@ -103,14 +104,16 @@
         old = [cache_ref[j, p].astype(F32) for j in range(past)]
         for r in range(reqs):
             length = lens_ref[req * reqs + r]
+            own = p * reqs + r
             for j in range(past):
                 seen = (length >= past - j).astype(F32)
-                joined[j : j + 1, :] = old[j][r : r + 1, :] * seen
-            joined[past : past + steps, :] = proj_ref[r, p].astype(F32)
-            total = joined[past : past + steps, :] * weight[0:1, :]
+                joined[own, j : j + 1, :] = old[j][r : r + 1, :] * seen
+            joined[own, past : past + steps, :] = proj_ref[r, p].astype(F32)
+            total = joined[own, past : past + steps, :] * weight[0:1, :]
             for tap in range(1, taps):
-                total = total + joined[past - tap : past - tap + steps, :] * weight[tap : tap + 1, :]
-            at = (p * reqs + r) * steps
+                begin = past - tap
+                total = total + joined[own, begin : begin + steps, :] * weight[tap : tap + 1, :]
+            at = own * steps
             conv[at : at + steps, :] = total / (1.0 + jnp.exp(-total))
 
     count = 3 * reqs * steps
@@ -145,7 +148,7 @@
         + [pl.BlockSpec(memory_space=pl.ANY)],
         out_specs=[spec] * blocks,
         scratch_shapes=[
-            VMEM((taps - 1 + steps + 1, width), F32),
+            VMEM((3 * reqs, taps + steps, width), F32),
             VMEM((3 * reqs * steps, width), F32),
             VMEM((extra, head_size), F32),
             pltpu.SemaphoreType.DMA((blocks * reqs,)),
@@ -164,11 +167,11 @@
 
 def rows_kernel(blocks, reqs, steps, index_ref, *refs):
     own = refs[:blocks][::-1]
-    sib = refs[blocks : 2 * blocks][::-1]
+    sib = refs[blocks : 2 * blocks]
     live_ref = refs[2 * blocks]
     normed_out = refs[2 * blocks + 1 : 3 * blocks + 1]
-    pool, turned, values = refs[3 * blocks + 1 : 3 * blocks + 4]
-    flat, gathered, columns, lefts, local_out, state_out = refs[3 * blocks + 4 :]
+    pool, turned, lasting, values = refs[3 * blocks + 1 : 3 * blocks + 5]
+    flat, gathered, columns, lefts, local_out, state_out = refs[3 * blocks + 5 :]
     count = blocks * reqs
     head_size = pool.shape[-1]
     rows = reqs * head_size
@@ -199,7 +202,6 @@
         weights = [w * keep[t] for w in weights] + [1.0 - keep[t]]
         decay = decay * keep[t]
         lefts[pl.ds(t * count, count), :] = query[t] * decay
-        values[pl.ds(t * count, count), :] = inputs[t]
         out = jnp.zeros_like(query[t])
         for earlier in range(t + 1):
             score = jnp.sum(query[t] * weights[earlier], axis=-1, keepdims=True)
@@ -219,58 +221,108 @@
 
     columns[...] = jnp.zeros_like(columns)
     columns[pl.ds(0, count), :] = decay
-    for t in range(steps):
-        columns[pl.ds((1 + t) * count, count), :] = weights[t]
     turned[...] = columns[...].T
-
-
-def states_kernel(blocks, reqs, steps, apart, index_ref, pool, turned_ref, values, *refs):
+    for s in range(blocks):
+        for t in range(steps):
+            here = pl.ds((s * steps + t) * reqs, reqs)
+            lasting[here, :] = weights[t][s * reqs : (s + 1) * reqs, :]
+            values[here, :] = inputs[t][s * reqs : (s + 1) * reqs, :]
+
+
+def states_kernel(blocks, reqs, steps, apart, index_ref, pool, turned_ref, lasting, values, *refs):
     riders = refs[: blocks - len(apart)]
     outs = refs[blocks - len(apart) :]
     head_size = pool.shape[-1]
-    count = blocks * reqs
     turned = turned_ref[...]
-    for i in range(count):
-        current = turned[:, i : i + 1] * pool[index_ref[i]].astype(F32)
-        for t in range(steps):
-            column = (1 + t) * count + i
-            value = values[t * count + i : t * count + i + 1, :]
-            current = current + turned[:, column : column + 1] * value
-        row = i % reqs * head_size
-        outs[i // reqs][row : row + head_size, :] = current.astype(BF16)
+    of_req = lax.broadcasted_iota(jnp.int32, (steps * reqs, head_size), 0) % reqs
+    for s in range(blocks):
+        here = slice(s * steps * reqs, (s + 1) * steps * reqs)
+        left = lasting[here, :]
+        high = left.astype(BF16)
+        low = (left - high.astype(F32)).astype(BF16)
+        value = values[here, :]
+        spread = [jnp.where(of_req == r, value, 0.0).astype(BF16) for r in range(reqs)]
+        spread = jnp.concatenate(spread, axis=1)
+        added = lax.dot_general(
+            jnp.concatenate([high, low], axis=0),
+            jnp.concatenate([spread, spread], axis=0),
+            (((0,), (0,)), ((), ())),
+            preferred_element_type=F32,
+        )
+        for r in range(reqs):
+            i = s * reqs + r
+            span = slice(r * head_size, (r + 1) * head_size)
+            current = turned[:, i : i + 1] * pool[index_ref[i]].astype(F32) + added[:, span]
+            outs[s][span, :] = current.astype(BF16)
     for k, s in enumerate(s for s in range(blocks) if s not in apart):
         outs[s][reqs * head_size :, :] = riders[k][...]
 
 
-def place_kernel(blocks, *refs):
-    parts, out, sems = refs[:blocks], refs[blocks], refs[blocks + 1]
+def project_kernel(blocks, *refs):
+    parts, weight, out, left = refs[:blocks], refs[blocks], refs[blocks + 1], refs[blocks + 2]
+    rows, head_size = out.shape[0], parts[0].shape[-1]
+    z = lax.axis_index("req") // 2
+    for s in range(blocks):
+        lanes = pl.ds(pl.multiple_of((z ^ s) * head_size, head_size), head_size)
+        left[:, lanes] = parts[s][parts[s].shape[0] - rows :, :]
+    out[...] = jnp.dot(left[...], weight[...], preferred_element_type=F32).astype(BF16)
+
+
+def project(parts, weight, rows):
+    spec = pl.BlockSpec(memory_space=VMEM)
+    return pl.pallas_call(
+        functools.partial(project_kernel, len(parts)),
+        out_shape=VMEM((rows, weight.shape[1]), BF16),
+        in_specs=[spec] * (len(parts) + 1),
+        out_specs=spec,
+        scratch_shapes=[VMEM((rows, weight.shape[0]), BF16)],
+        name="project",
+        compiler_params=PARAMS,
+    )(*on_chip(*parts, weight))
+
+
+def finish_kernel(blocks, terms, *refs):
+    parts = refs[:blocks][::-1]
+    resid = refs[blocks]
+    added = refs[blocks + 1 : blocks + 1 + terms]
+    mixed, out, sems = refs[blocks + 1 + terms :]
     reqs, _, head_size, _ = out.shape
     z = lax.axis_index("req") // 2
     copies = []
     for s in range(blocks):
         for r in range(reqs):
             copy = pltpu.make_async_copy(
-                parts[blocks - 1 - s].at[pl.ds(r * head_size, head_size), :],
+                parts[s].at[pl.ds(r * head_size, head_size), :],
                 out.at[r, z ^ s],
                 sems.at[s * reqs + r],
             )
             copy.start()
             copies.append(copy)
+    total = [value[...].astype(F32) for value in added]
+    total = (total[0] + total[1]) + (total[2] + total[3])
+    steps = total.shape[0] // reqs
+    for r in range(reqs):
+        mixed[r] = (resid[r].astype(F32) + total[r * steps : (r + 1) * steps, :]).astype(BF16)
     for copy in copies:
         copy.wait()
 
 
-def place(back, reqs):
+def finish(back, resid, added, reqs):
     blocks = len(back)
     head_size = back[0].shape[-1]
+    spec = pl.BlockSpec(memory_space=VMEM)
     return pl.pallas_call(
-        functools.partial(place_kernel, blocks),
-        out_shape=jax.ShapeDtypeStruct((reqs, blocks, head_size, head_size), BF16),
-        in_specs=[pl.BlockSpec(memory_space=VMEM)] * blocks,
-        out_specs=pl.BlockSpec(memory_space=pl.ANY),
+        functools.partial(finish_kernel, blocks, len(added)),
+        out_shape=[
+            jax.ShapeDtypeStruct(resid.shape, BF16),
+            jax.ShapeDtypeStruct((reqs, blocks, head_size, head_size), BF16),
+        ],
+        in_specs=[spec] * (blocks + 1 + len(added)),
+        out_specs=[spec, pl.BlockSpec(memory_space=pl.ANY)],
         scratch_shapes=[pltpu.SemaphoreType.DMA((blocks * reqs,))],
-        name="place",
-    )(*on_chip(*back[::-1]))
+        name="finish",
+        compiler_params=PARAMS,
+    )(*on_chip(*back[::-1], resid, *added))
 
 
 def on_chip(*arrays):
@@ -282,7 +334,7 @@
     count = blocks * reqs
     head_size = own[0].shape[-1]
     extra = own[0].shape[0] - reqs * head_size
-    columns = -(-count * (1 + steps) // 128) * 128
+    columns = -(-count // 128) * 128
     spec = pl.BlockSpec(memory_space=VMEM)
     outs = pl.pallas_call(
         functools.partial(rows_kernel, blocks, reqs, steps),
@@ -291,9 +343,10 @@
             VMEM((2 * count, head_size, head_size), BF16),
             VMEM((head_size, columns), F32),
             VMEM((steps * count, head_size), F32),
+            VMEM((steps * count, head_size), F32),
         ],
         in_specs=[pl.BlockSpec(memory_space=pltpu.SMEM)] + [spec] * (2 * blocks + 1),
-        out_specs=[spec] * (blocks + 3),
+        out_specs=[spec] * (blocks + 4),
         scratch_shapes=[
             VMEM((extra, head_size), F32),
             VMEM((3 * steps, count, head_size), F32),
@@ -303,7 +356,8 @@
             VMEM((steps * count, head_size), F32),
         ],
         name="rows",
-    )(index, *on_chip(*own[::-1], *sib[::-1], live))
+        compiler_params=PARAMS,
+    )(index, *on_chip(*own[::-1], *sib, live))
     return outs[:blocks], outs[blocks:]
 
 
@@ -314,9 +368,10 @@
     return pl.pallas_call(
         functools.partial(states_kernel, blocks, reqs, steps, apart),
         out_shape=[VMEM((r, head_size), BF16) for r in rows],
-        in_specs=[pl.BlockSpec(memory_space=pltpu.SMEM)] + [spec] * (3 + len(riders)),
+        in_specs=[pl.BlockSpec(memory_space=pltpu.SMEM)] + [spec] * (4 + len(riders)),
         out_specs=[spec] * blocks,
         name="states",
+        compiler_params=PARAMS,
     )(index, *on_chip(*kept, *riders))
 
 
@@ -347,7 +402,12 @@
 
     packs = pack(lengths, proj, conv_cache, conv_weight, forget_bias, norm_gain, old_state)
     own = [swap(packs[s], s) for s in range(blocks)]
-    sib = [lax.ppermute(own[s][:state_rows], "head", sibling) for s in range(blocks)]
+    near, far = range(blocks // 2), range(blocks // 2, blocks)
+    sib = [lax.ppermute(own[s][:state_rows], "head", sibling) for s in near]
+    held = lax.optimization_barrier((*sib, *[own[s] for s in far]))
+    sib = list(held[: len(near)])
+    own = own[: len(near)] + list(held[len(near) :])
+    sib += [lax.ppermute(own[s][:state_rows], "head", sibling) for s in far]
 
     zs = z ^ jnp.arange(blocks, dtype=jnp.int32)
     slots = ((zs * 2 + core) * local_reqs)[:, None] + jnp.arange(local_reqs, dtype=jnp.int32)[None, :]
@@ -371,21 +431,12 @@
         rows[s] = value
     back = [swap(states[s], s) for s in range(blocks)]
 
-    flat = jnp.zeros((local_reqs * steps, blocks * head_size), BF16)
-    for s in range(blocks):
-        if s not in apart:
-            rows[s] = back[s][state_rows:]
-        flat = lax.dynamic_update_slice(flat, rows[s], (0, (z ^ s) * head_size))
-    new_state = place(back, local_reqs)
-    part = jnp.dot(flat, out_weight, preferred_element_type=F32)
-    part = part.astype(BF16)
-    parts = [part] + [
+    rows = [rows[s] if s in apart else back[s] for s in range(blocks)]
+    part = project(rows, out_weight, local_reqs * steps)
+    added = [part] + [
         lax.ppermute(part, "head", [(i, i ^ k) for i in range(n_head)]) for k in range(1, n_head)
     ]
-    parts = [value.astype(F32) for value in parts]
-    part = (parts[0] + parts[1]) + (parts[2] + parts[3])
-    mixed = (resid.reshape(-1, width).astype(F32) + part).astype(BF16).reshape(resid.shape)
-    return (mixed, new_state)
+    return tuple(finish(back, resid, added, local_reqs))
 
 
 def solution(mesh):

time: 49.8 us -> 50.6 us (1.016)
  starting transfers between devices: 22.7 us -> 27.4 us
  matrix products: 1.98 us -> 0 us
  local copies, waits for them, and re-layouts: 0.9 us -> 0.21 us
  other arithmetic: 1.52 us -> 0.96 us
    ppermute x4, starting transfers between devices: 2.82 us -> 6.89 us  [the longest x2 3.62 us: swapped_body(): sib = [lax.ppermute(own[s][:state_rows], 'head', sibling) for s in near]]
    ppermute x3, waiting for transfers between devices: 2.53 us -> 0.01 us  [swapped_body(): lax.ppermute(part, 'head', [(i, i ^ k) for i in range(n_head)])]
    ppermute x10, waiting for transfers between devices: 11.2 us -> 13.7 us  [swap(): return lax.ppermute(value, both, pairs)]
    dot_general x1 -> x0, matrix products: 1.98 us -> none  [swapped_body(): part = jnp.dot(flat, out_weight, preferred_element_type=F32)]
    ppermute x10, starting transfers between devices: 13.2 us -> 15.1 us  [swap(): return lax.ppermute(value, both, pairs)]
    ppermute x3, starting transfers between devices: 6.64 us -> 5.42 us  [swapped_body(): lax.ppermute(part, 'head', [(i, i ^ k) for i in range(n_head)])]
    pallas_call x1, Pallas kernels: 2.21 us -> 0.99 us  [middle_states(): pl.pallas_call(functools.partial(states_kernel, blocks, reqs, steps, apar...]
    pallas_call x1 -> x2, Pallas kernels: 0.91 us -> 1.94 us  [the longest x1 1.56 us: finish(): pl.pallas_call(functools.partial(finish_kernel, blocks, len(added)), out_...]
  transfers between devices with their start and end apart: 17 -> 17, of which waited for: 10 -> 6; matrix products, arithmetic and copies ran while one was open for 7% -> 2% of each run, Pallas kernels for 6% -> 3%
where the time goes in v4:
time: 50.6 us; the launch traced here: 50.4 us
  starting transfers between devices  27.4 us (54%)
  waiting for transfers between devices  15 us (30%)
  Pallas kernels  6.09 us (12%)
  other arithmetic  0.96 us (2%)
  between operations  0.75 us (1%)
    ppermute x10, starting transfers between devices, swap(): return lax.ppermute(value, both, pairs)  15.1 us
    ppermute x10, waiting for transfers between devices, swap(): return lax.ppermute(value, both, pairs)  13.7 us
    ppermute x3, starting transfers between devices, swapped_body(): lax.ppermute(part, 'head', [(i, i ^ k) for i in range(n_head)])  5.42 us
    ppermute x2, starting transfers between devices, swapped_body(): sib = [lax.ppermute(own[s][:state_rows], 'head', sibling) for s in near]  3.62 us
    ppermute x2, starting transfers between devices, swapped_body(): sib += [lax.ppermute(own[s][:state_rows], 'head', sibling) for s in far]  3.27 us
    pallas_call x1, Pallas kernels, pack(): pl.pallas_call(functools.partial(pack_kernel, blocks, taps), out_shape=[V...  2.15 us
    pallas_call x1, Pallas kernels, finish(): pl.pallas_call(functools.partial(finish_kernel, blocks, len(added)), out_...  1.56 us
    ppermute x2, waiting for transfers between devices, swapped_body(): sib += [lax.ppermute(own[s][:state_rows], 'head', sibling) for s in far]  1.27 us
  transfers between devices with their start and end apart: 17, of which 6 were waited for; matrix products, arithmetic and copies ran while one was open for 2% of the time, Pallas kernels for 3%

profile of v4, /device:TPU:0, one launch (start us, length us, event | category | flops | bytes accessed | tf_op | source)
XLA Modules:
  0.0 50.4 jit_solution(12390678897346348506)
XLA Ops:
  0.6 2.1 %pack.1 = (bf16[568,128]{1,0:T(8,128)(2,1)S(1)}, bf16[568,128]{1,0:T(8,128)(2,1)S(1)}, bf16[568,128]{1,0:T(8,128)(2,1)S(1)}, bf16[568,128]{1,0:T(8,128)(2,1)S(1)}) custom-call(s32[32]{0:T(128)} %lens_ref.1, bf16[4,3,4,512]{3,2,1,0:T(4,128)(2,1)} %bitcast.5, bf16[3,3,4,512]{3,2,1,0:T(4,128)(2,1)} %bitcast.6, bf16[3,4,512]{2,1,0:T(4,128)(2,1)} %bitcast.7, ...), custom_call_target="tpu_custom_call" | custom-call | tf_op jit(solution)/shard_map/pack/pallas_call | solution.py:143
  2.8 0.7 %collective-permute-start = (bf16[568,128]{1,0:T(8,128)(2,1)S(1)}, bf16[568,128]{1,0:T(8,128)(2,1)S(1)}, u32[]{:S(2)}, u32[]{:S(2)}) collective-permute-start(bf16[568,128]{1,0:T(8,128)(2,1)S(1)} %get-tuple-element.28), channel_id=1, source_target_pairs={{0,0},{1,4},{2,2},{3,6},{4,1},{5,5},{6,3},{7,7},{8,8},{9,12},{10,1... | collective-permute-start | bytes 436232 | tf_op jit(solution)/shard_map/ppermute | solution.py:401
  3.5 3.1 %collective-permute-start.2 = (bf16[568,128]{1,0:T(8,128)(2,1)S(1)}, bf16[568,128]{1,0:T(8,128)(2,1)S(1)}, u32[]{:S(2)}, u32[]{:S(2)}) collective-permute-start(bf16[568,128]{1,0:T(8,128)(2,1)S(1)} %get-tuple-element.29), channel_id=1, source_target_pairs={{0,8},{1,12},{2,10},{3,14},{4,9},{5,13},{6,11},{7,15},{8,0},{9,4},... | collective-permute-start | bytes 436232 | tf_op jit(solution)/shard_map/ppermute | solution.py:401
  6.6 2.6 %collective-permute-start.4 = (bf16[568,128]{1,0:T(8,128)(2,1)S(1)}, bf16[568,128]{1,0:T(8,128)(2,1)S(1)}, u32[]{:S(2)}, u32[]{:S(2)}) collective-permute-start(bf16[568,128]{1,0:T(8,128)(2,1)S(1)} %get-tuple-element.30), channel_id=1, source_target_pairs={{0,16},{1,20},{2,18},{3,22},{4,17},{5,21},{6,19},{7,23},{8,24},{9,... | collective-permute-start | bytes 436232 | tf_op jit(solution)/shard_map/ppermute | solution.py:401
  9.2 0.0 collective-permute-start.5
  9.2 0.1 iota_add_fusion
  9.2 0.1 add.59
  9.3 0.9 %select_reduce_fusion = (s32[16]{0:T(128)S(1)}, s32[16]{0:T(128)S(1)}) fusion(s32[32]{0:T(128)} %lens_ref.1, s32[16]{0:T(128)S(1)} %add.59, s32[32]{0:T(128)} %param.15), kind=kLoop, calls=%fused_computation | loop fusion | flops 3040 | bytes 448 | tf_op jit(solution)/shard_map/reduce_sum | solution.py:420
  10.2 0.0 collective-permute-done.refs_3_
  10.2 3.5 %collective-permute-start.1 = (bf16[512,128]{1,0:T(8,128)(2,1)S(1)}, bf16[512,128]{1,0:T(8,128)(2,1)S(1)}, u32[]{:S(2)}, u32[]{:S(2)}) collective-permute-start(bf16[512,128]{1,0:T(8,128)(2,1)S(1)} %slice.16), channel_id=1, source_target_pairs={{0,1},{1,0},{2,3},{3,2},{4,5},{5,4},{6,7},{7,6},{8,9},{9,8},{10,11... | collective-permute-start | bytes 393224 | tf_op jit(solution)/shard_map/ppermute | solution.py:406
  13.7 0.1 collective-permute-start.3
  13.9 4.3 %collective-permute-done.5.refs_0_ = bf16[568,128]{1,0:T(8,128)(2,1)S(1)} collective-permute-done((bf16[568,128]{1,0:T(8,128)(2,1)S(1)}, bf16[568,128]{1,0:T(8,128)(2,1)S(1)}, u32[]{:S(2)}, u32[]{:S(2)}) %collective-permute-start.5) | collective-permute-done | bytes 145440 | tf_op jit(solution)/shard_map/ppermute | solution.py:401
  18.2 3.2 %collective-permute-start.6 = (bf16[512,128]{1,0:T(8,128)(2,1)S(1)}, bf16[512,128]{1,0:T(8,128)(2,1)S(1)}, u32[]{:S(2)}, u32[]{:S(2)}) collective-permute-start(bf16[512,128]{1,0:T(8,128)(2,1)S(1)} %slice.14), channel_id=1, source_target_pairs={{0,1},{1,0},{2,3},{3,2},{4,5},{5,4},{6,7},{7,6},{8,9},{9,8},{10,11... | collective-permute-start | bytes 393224 | tf_op jit(solution)/shard_map/ppermute | solution.py:410
  21.4 0.1 collective-permute-start.7
  21.5 0.9 %collective-permute-done.6.refs_6_ = bf16[512,128]{1,0:T(8,128)(2,1)S(1)} collective-permute-done((bf16[512,128]{1,0:T(8,128)(2,1)S(1)}, bf16[512,128]{1,0:T(8,128)(2,1)S(1)}, u32[]{:S(2)}, u32[]{:S(2)}) %collective-permute-start.6) | collective-permute-done | bytes 131104 | tf_op jit(solution)/shard_map/ppermute | solution.py:410
  22.4 0.4 collective-permute-done.7.refs_7_
  22.7 0.1 broadcast_in_dim.35.refs_8_
  22.8 1.0 %rows.1 = (bf16[16,128]{1,0:T(8,128)(2,1)S(1)}, bf16[16,128]{1,0:T(8,128)(2,1)S(1)}, bf16[16,128]{1,0:T(8,128)(2,1)S(1)}, bf16[16,128]{1,0:T(8,128)(2,1)S(1)}, b...) custom-call(s32[16]{0:T(128)S(1)} %fusion.index_ref, ...), custom_call_target="tpu_custom_call" | custom-call | tf_op jit(solution)/shard_map/rows/pallas_call | solution.py:339
  23.8 0.0 copy-start.1
  23.8 3.2 %collective-permute-start.8 = (bf16[16,128]{1,0:T(8,128)(2,1)S(1)}, bf16[16,128]{1,0:T(8,128)(2,1)S(1)}, u32[]{:S(2)}, u32[]{:S(2)}) collective-permute-start(bf16[16,128]{1,0:T(8,128)(2,1)S(1)} %get-tuple-element.46), channel_id=1, source_target_pairs={{0,16},{1,20},{2,18},{3,22},{4,17},{5,21},{6,19},{7,23},{8,24},{9,... | collective-permute-start | bytes 12296 | tf_op jit(solution)/shard_map/ppermute | solution.py:401
  27.1 1.3 %collective-permute-start.9 = (bf16[16,128]{1,0:T(8,128)(2,1)S(1)}, bf16[16,128]{1,0:T(8,128)(2,1)S(1)}, u32[]{:S(2)}, u32[]{:S(2)}) collective-permute-start(bf16[16,128]{1,0:T(8,128)(2,1)S(1)} %get-tuple-element.47), channel_id=1, source_target_pairs={{0,24},{1,28},{2,26},{3,30},{4,25},{5,29},{6,27},{7,31},{8,16},{9,... | collective-permute-start | bytes 12296 | tf_op jit(solution)/shard_map/ppermute | solution.py:401
  28.4 1.0 %states.1 = (bf16[528,128]{1,0:T(8,128)(2,1)S(1)}, bf16[528,128]{1,0:T(8,128)(2,1)S(1)}, bf16[512,128]{1,0:T(8,128)(2,1)S(1)}, bf16[512,128]{1,0:T(8,128)(2,1)S(1)}) custom-call(s32[16]{0:T(128)S(1)} %fusion.index_ref, bf16[32,128,128]{2,1,0:T(8,128)(2,1)S(1)} %get-tuple-element.36.pool, f32[128,128]{1,0:T(8,128)S(1)} %get-tuple-element.37.turned_ref, ...), custom_call_target="tpu_custom_call" | custom-call | tf_op jit(solution)/shard_map/states/pallas_call | solution.py:368
  29.4 3.1 %collective-permute-done.9.refs_3_ = bf16[16,128]{1,0:T(8,128)(2,1)S(1)} collective-permute-done((bf16[16,128]{1,0:T(8,128)(2,1)S(1)}, bf16[16,128]{1,0:T(8,128)(2,1)S(1)}, u32[]{:S(2)}, u32[]{:S(2)}) %collective-permute-start.9) | collective-permute-done | bytes 4128 | tf_op jit(solution)/shard_map/ppermute | solution.py:401
  32.5 0.7 %collective-permute-start.13 = (bf16[528,128]{1,0:T(8,128)(2,1)S(1)}, bf16[528,128]{1,0:T(8,128)(2,1)S(1)}, u32[]{:S(2)}, u32[]{:S(2)}) collective-permute-start(bf16[528,128]{1,0:T(8,128)(2,1)S(1)} %get-tuple-element.51), channel_id=1, source_target_pairs={{0,0},{1,4},{2,2},{3,6},{4,1},{5,5},{6,3},{7,7},{8,8},{9,12},{10,1... | collective-permute-start | bytes 405512 | tf_op jit(solution)/shard_map/ppermute | solution.py:401
  33.1 1.4 %collective-permute-start.10 = (bf16[512,128]{1,0:T(8,128)(2,1)S(1)}, bf16[512,128]{1,0:T(8,128)(2,1)S(1)}, u32[]{:S(2)}, u32[]{:S(2)}) collective-permute-start(bf16[512,128]{1,0:T(8,128)(2,1)S(1)} %get-tuple-element.48), channel_id=1, source_target_pairs={{0,24},{1,28},{2,26},{3,30},{4,25},{5,29},{6,27},{7,31},{8,16},{9,... | collective-permute-start | bytes 393224 | tf_op jit(solution)/shard_map/ppermute | solution.py:401
  34.5 2.2 %collective-permute-start.11 = (bf16[512,128]{1,0:T(8,128)(2,1)S(1)}, bf16[512,128]{1,0:T(8,128)(2,1)S(1)}, u32[]{:S(2)}, u32[]{:S(2)}) collective-permute-start(bf16[512,128]{1,0:T(8,128)(2,1)S(1)} %get-tuple-element.49), channel_id=1, source_target_pairs={{0,16},{1,20},{2,18},{3,22},{4,17},{5,21},{6,19},{7,23},{8,24},{9,... | collective-permute-start | bytes 393224 | tf_op jit(solution)/shard_map/ppermute | solution.py:401
  36.7 1.9 %collective-permute-done.12.refs_1_.refs_2_ = bf16[528,128]{1,0:T(8,128)(2,1)S(1)} collective-permute-done((bf16[528,128]{1,0:T(8,128)(2,1)S(1)}, bf16[528,128]{1,0:T(8,128)(2,1)S(1)}, u32[]{:S(2)}, u32[]{:S(2)}) %collective-permute-start.12) | collective-permute-done | bytes 135200 | tf_op jit(solution)/shard_map/ppermute | solution.py:401
  38.6 0.4 project.1.refs_5_
  39.0 4.9 %collective-permute-start.16 = (bf16[16,2048]{1,0:T(8,128)(2,1)S(1)}, bf16[16,2048]{1,0:T(8,128)(2,1)S(1)}, u32[]{:S(2)}, u32[]{:S(2)}) collective-permute-start(bf16[16,2048]{1,0:T(8,128)(2,1)S(1)} %project.1.refs_5_), channel_id=1, source_target_pairs={{0,3},{1,2},{2,1},{3,0},{4,7},{5,6},{6,5},{7,4},{8,11},{9,10},{10,... | collective-permute-start | bytes 196616 | tf_op jit(solution)/shard_map/ppermute | solution.py:437
  43.9 0.5 %collective-permute-start.15 = (bf16[16,2048]{1,0:T(8,128)(2,1)S(1)}, bf16[16,2048]{1,0:T(8,128)(2,1)S(1)}, u32[]{:S(2)}, u32[]{:S(2)}) collective-permute-start(bf16[16,2048]{1,0:T(8,128)(2,1)S(1)} %project.1.refs_5_), channel_id=1, source_target_pairs={{0,2},{1,3},{2,0},{3,1},{4,6},{5,7},{6,4},{7,5},{8,10},{9,11},{10,... | collective-permute-start | bytes 196616 | tf_op jit(solution)/shard_map/ppermute | solution.py:437
  44.4 4.5 %collective-permute-done.11.refs_1_ = bf16[512,128]{1,0:T(8,128)(2,1)S(1)} collective-permute-done((bf16[512,128]{1,0:T(8,128)(2,1)S(1)}, bf16[512,128]{1,0:T(8,128)(2,1)S(1)}, u32[]{:S(2)}, u32[]{:S(2)}) %collective-permute-start.11) | collective-permute-done | bytes 131104 | tf_op jit(solution)/shard_map/ppermute | solution.py:401
  48.9 1.6 %finish.1 = (bf16[4,4,2048]{2,1,0:T(4,128)(2,1)}, bf16[4,4,128,128]{3,2,1,0:T(8,128)(2,1)}) custom-call(bf16[512,128]{1,0:T(8,128)(2,1)S(1)} %collective-permute-done.10.refs_0_, bf16[512,128]{1,0:T(8,128)(2,1)S(1)} %collective-permute-done.11.refs_1_, bf16[528,128]{1,0:T(8,128)(2,1)S(1)} %collective-permute-done.12.refs_1_.refs_2_, ...), custom_call_target="tpu_custom_call" | custom-call | tf_op jit(solution)/shard_map/finish/pallas_call | solution.py:314
  (22 shorter events, 0.1 us)
Async XLA Ops:
  0.6 37.9 %copy-start = (bf16[512,2048]{1,0:T(8,128)(2,1)S(1)}, bf16[512,2048]{1,0:T(8,128)(2,1)}, u32[]{:S(2)}) copy-start(bf16[512,2048]{1,0:T(8,128)(2,1)} %refs_4_.2) | copy-start | bytes 6291460
  2.8 7.4 %collective-permute-start = (bf16[568,128]{1,0:T(8,128)(2,1)S(1)}, bf16[568,128]{1,0:T(8,128)(2,1)S(1)}, u32[]{:S(2)}, u32[]{:S(2)}) collective-permute-start(bf16[568,128]{1,0:T(8,128)(2,1)S(1)} %get-tuple-element.28), channel_id=1, source_target_pairs={{0,0},{1,4},{2,2},{3,6},{4,1},{5,5},{6,3},{7,7},{8,8},{9,12},{10,1... | collective-permute-start | bytes 436232 | tf_op jit(solution)/shard_map/ppermute | solution.py:401
  3.5 10.3 %collective-permute-start.2 = (bf16[568,128]{1,0:T(8,128)(2,1)S(1)}, bf16[568,128]{1,0:T(8,128)(2,1)S(1)}, u32[]{:S(2)}, u32[]{:S(2)}) collective-permute-start(bf16[568,128]{1,0:T(8,128)(2,1)S(1)} %get-tuple-element.29), channel_id=1, source_target_pairs={{0,8},{1,12},{2,10},{3,14},{4,9},{5,13},{6,11},{7,15},{8,0},{9,4},... | collective-permute-start | bytes 436232 | tf_op jit(solution)/shard_map/ppermute | solution.py:401
  6.6 7.3 %collective-permute-start.4 = (bf16[568,128]{1,0:T(8,128)(2,1)S(1)}, bf16[568,128]{1,0:T(8,128)(2,1)S(1)}, u32[]{:S(2)}, u32[]{:S(2)}) collective-permute-start(bf16[568,128]{1,0:T(8,128)(2,1)S(1)} %get-tuple-element.30), channel_id=1, source_target_pairs={{0,16},{1,20},{2,18},{3,22},{4,17},{5,21},{6,19},{7,23},{8,24},{9,... | collective-permute-start | bytes 436232 | tf_op jit(solution)/shard_map/ppermute | solution.py:401
  9.2 9.0 %collective-permute-start.5 = (bf16[568,128]{1,0:T(8,128)(2,1)S(1)}, bf16[568,128]{1,0:T(8,128)(2,1)S(1)}, u32[]{:S(2)}, u32[]{:S(2)}) collective-permute-start(bf16[568,128]{1,0:T(8,128)(2,1)S(1)} %get-tuple-element.31), channel_id=1, source_target_pairs={{0,24},{1,28},{2,26},{3,30},{4,25},{5,29},{6,27},{7,31},{8,16},{9,... | collective-permute-start | bytes 436232 | tf_op jit(solution)/shard_map/ppermute | solution.py:401
  10.2 8.0 %collective-permute-start.1 = (bf16[512,128]{1,0:T(8,128)(2,1)S(1)}, bf16[512,128]{1,0:T(8,128)(2,1)S(1)}, u32[]{:S(2)}, u32[]{:S(2)}) collective-permute-start(bf16[512,128]{1,0:T(8,128)(2,1)S(1)} %slice.16), channel_id=1, source_target_pairs={{0,1},{1,0},{2,3},{3,2},{4,5},{5,4},{6,7},{7,6},{8,9},{9,8},{10,11... | collective-permute-start | bytes 393224 | tf_op jit(solution)/shard_map/ppermute | solution.py:406
  13.7 4.4 %collective-permute-start.3 = (bf16[512,128]{1,0:T(8,128)(2,1)S(1)}, bf16[512,128]{1,0:T(8,128)(2,1)S(1)}, u32[]{:S(2)}, u32[]{:S(2)}) collective-permute-start(bf16[512,128]{1,0:T(8,128)(2,1)S(1)} %slice.17), channel_id=1, source_target_pairs={{0,1},{1,0},{2,3},{3,2},{4,5},{5,4},{6,7},{7,6},{8,9},{9,8},{10,11... | collective-permute-start | bytes 393224 | tf_op jit(solution)/shard_map/ppermute | solution.py:406
  18.2 4.2 %collective-permute-start.6 = (bf16[512,128]{1,0:T(8,128)(2,1)S(1)}, bf16[512,128]{1,0:T(8,128)(2,1)S(1)}, u32[]{:S(2)}, u32[]{:S(2)}) collective-permute-start(bf16[512,128]{1,0:T(8,128)(2,1)S(1)} %slice.14), channel_id=1, source_target_pairs={{0,1},{1,0},{2,3},{3,2},{4,5},{5,4},{6,7},{7,6},{8,9},{9,8},{10,11... | collective-permute-start | bytes 393224 | tf_op jit(solution)/shard_map/ppermute | solution.py:410
  21.4 1.3 %collective-permute-start.7 = (bf16[512,128]{1,0:T(8,128)(2,1)S(1)}, bf16[512,128]{1,0:T(8,128)(2,1)S(1)}, u32[]{:S(2)}, u32[]{:S(2)}) collective-permute-start(bf16[512,128]{1,0:T(8,128)(2,1)S(1)} %slice.15), channel_id=1, source_target_pairs={{0,1},{1,0},{2,3},{3,2},{4,5},{5,4},{6,7},{7,6},{8,9},{9,8},{10,11... | collective-permute-start | bytes 393224 | tf_op jit(solution)/shard_map/ppermute | solution.py:410
  23.8 25.0 %copy-start.1 = (bf16[4,4,2048]{2,1,0:T(4,128)(2,1)S(1)}, bf16[4,4,2048]{2,1,0:T(4,128)(2,1)}, u32[]{:S(2)}) copy-start(bf16[4,4,2048]{2,1,0:T(4,128)(2,1)} %refs_4_.3) | copy-start | bytes 196612
  23.8 5.5 %collective-permute-start.8 = (bf16[16,128]{1,0:T(8,128)(2,1)S(1)}, bf16[16,128]{1,0:T(8,128)(2,1)S(1)}, u32[]{:S(2)}, u32[]{:S(2)}) collective-permute-start(bf16[16,128]{1,0:T(8,128)(2,1)S(1)} %get-tuple-element.46), channel_id=1, source_target_pairs={{0,16},{1,20},{2,18},{3,22},{4,17},{5,21},{6,19},{7,23},{8,24},{9,... | collective-permute-start | bytes 12296 | tf_op jit(solution)/shard_map/ppermute | solution.py:401
  27.1 5.4 %collective-permute-start.9 = (bf16[16,128]{1,0:T(8,128)(2,1)S(1)}, bf16[16,128]{1,0:T(8,128)(2,1)S(1)}, u32[]{:S(2)}, u32[]{:S(2)}) collective-permute-start(bf16[16,128]{1,0:T(8,128)(2,1)S(1)} %get-tuple-element.47), channel_id=1, source_target_pairs={{0,24},{1,28},{2,26},{3,30},{4,25},{5,29},{6,27},{7,31},{8,16},{9,... | collective-permute-start | bytes 12296 | tf_op jit(solution)/shard_map/ppermute | solution.py:401
  32.5 6.1 %collective-permute-start.12 = (bf16[528,128]{1,0:T(8,128)(2,1)S(1)}, bf16[528,128]{1,0:T(8,128)(2,1)S(1)}, u32[]{:S(2)}, u32[]{:S(2)}) collective-permute-start(bf16[528,128]{1,0:T(8,128)(2,1)S(1)} %get-tuple-element.50), channel_id=1, source_target_pairs={{0,8},{1,12},{2,10},{3,14},{4,9},{5,13},{6,11},{7,15},{8,0},{9,4},... | collective-permute-start | bytes 405512 | tf_op jit(solution)/shard_map/ppermute | solution.py:401
  32.5 6.1 %collective-permute-start.13 = (bf16[528,128]{1,0:T(8,128)(2,1)S(1)}, bf16[528,128]{1,0:T(8,128)(2,1)S(1)}, u32[]{:S(2)}, u32[]{:S(2)}) collective-permute-start(bf16[528,128]{1,0:T(8,128)(2,1)S(1)} %get-tuple-element.51), channel_id=1, source_target_pairs={{0,0},{1,4},{2,2},{3,6},{4,1},{5,5},{6,3},{7,7},{8,8},{9,12},{10,1... | collective-permute-start | bytes 405512 | tf_op jit(solution)/shard_map/ppermute | solution.py:401
  33.1 11.2 %collective-permute-start.10 = (bf16[512,128]{1,0:T(8,128)(2,1)S(1)}, bf16[512,128]{1,0:T(8,128)(2,1)S(1)}, u32[]{:S(2)}, u32[]{:S(2)}) collective-permute-start(bf16[512,128]{1,0:T(8,128)(2,1)S(1)} %get-tuple-element.48), channel_id=1, source_target_pairs={{0,24},{1,28},{2,26},{3,30},{4,25},{5,29},{6,27},{7,31},{8,16},{9,... | collective-permute-start | bytes 393224 | tf_op jit(solution)/shard_map/ppermute | solution.py:401
  34.5 14.3 %collective-permute-start.11 = (bf16[512,128]{1,0:T(8,128)(2,1)S(1)}, bf16[512,128]{1,0:T(8,128)(2,1)S(1)}, u32[]{:S(2)}, u32[]{:S(2)}) collective-permute-start(bf16[512,128]{1,0:T(8,128)(2,1)S(1)} %get-tuple-element.49), channel_id=1, source_target_pairs={{0,16},{1,20},{2,18},{3,22},{4,17},{5,21},{6,19},{7,23},{8,24},{9,... | collective-permute-start | bytes 393224 | tf_op jit(solution)/shard_map/ppermute | solution.py:401
  39.0 9.9 %collective-permute-start.16 = (bf16[16,2048]{1,0:T(8,128)(2,1)S(1)}, bf16[16,2048]{1,0:T(8,128)(2,1)S(1)}, u32[]{:S(2)}, u32[]{:S(2)}) collective-permute-start(bf16[16,2048]{1,0:T(8,128)(2,1)S(1)} %project.1.refs_5_), channel_id=1, source_target_pairs={{0,3},{1,2},{2,1},{3,0},{4,7},{5,6},{6,5},{7,4},{8,11},{9,10},{10,... | collective-permute-start | bytes 196616 | tf_op jit(solution)/shard_map/ppermute | solution.py:437
  43.9 5.0 %collective-permute-start.15 = (bf16[16,2048]{1,0:T(8,128)(2,1)S(1)}, bf16[16,2048]{1,0:T(8,128)(2,1)S(1)}, u32[]{:S(2)}, u32[]{:S(2)}) collective-permute-start(bf16[16,2048]{1,0:T(8,128)(2,1)S(1)} %project.1.refs_5_), channel_id=1, source_target_pairs={{0,2},{1,3},{2,0},{3,1},{4,6},{5,7},{6,4},{7,5},{8,10},{9,11},{10,... | collective-permute-start | bytes 196616 | tf_op jit(solution)/shard_map/ppermute | solution.py:437
  44.4 4.5 %collective-permute-start.14 = (bf16[16,2048]{1,0:T(8,128)(2,1)S(1)}, bf16[16,2048]{1,0:T(8,128)(2,1)S(1)}, u32[]{:S(2)}, u32[]{:S(2)}) collective-permute-start(bf16[16,2048]{1,0:T(8,128)(2,1)S(1)} %project.1.refs_5_), channel_id=1, source_target_pairs={{0,1},{1,0},{2,3},{3,2},{4,5},{5,4},{6,7},{7,6},{8,9},{9,8},{10,11... | collective-permute-start | bytes 196616 | tf_op jit(solution)/shard_map/ppermute | solution.py:437

commit v5 on v4

--- a/solution.py
+++ b/solution.py
@@ -78,26 +78,39 @@
     return (mixed, new_state)
 
 
-def pack_kernel(blocks, taps, lens_ref, *refs):
-    proj_ref, cache_ref, weight_ref, bias_ref, gain_ref, state_ref = refs[:6]
+def pack_kernel(blocks, lens_far, *refs):
+    state_ref = refs[0]
+    small = refs[1:6]
     outs = refs[6 : 6 + blocks]
-    joined, conv, tail, sems = refs[6 + blocks :]
-    reqs, _, steps, _ = proj_ref.shape
-    head_size = state_ref.shape[-1]
+    joined, conv, tail, state_sems, small_sems, lens_ref = refs[6 + blocks : 12 + blocks]
+    held = refs[12 + blocks :]
+    reqs, head_size = state_ref.shape[0], state_ref.shape[-1]
     req = lax.axis_index("req")
     z = req // 2
     rows = reqs * head_size
+    fetches = [
+        pltpu.make_async_copy(ref, to, small_sems.at[k])
+        for k, (ref, to) in enumerate(zip((*small, lens_far), (*held, lens_ref)))
+    ]
+    for fetch in fetches:
+        fetch.start()
     copies = []
     for s in range(blocks - 1, -1, -1):
         for r in range(reqs):
             copy = pltpu.make_async_copy(
                 state_ref.at[r, z ^ s],
                 outs[s].at[pl.ds(r * head_size, head_size), :],
-                sems.at[s * reqs + r],
+                state_sems.at[s * reqs + r],
             )
             copy.start()
             copies.append(copy)
-
+    tail[...] = jnp.zeros_like(tail)
+    for fetch in fetches:
+        fetch.wait()
+
+    proj_ref, cache_ref, weight_ref, bias_ref, gain_ref = held
+    steps = proj_ref.shape[2]
+    taps = weight_ref.shape[1]
     past = taps - 1
     for p in range(3):
         weight = weight_ref[p].astype(F32)
@@ -117,7 +130,6 @@
             conv[at : at + steps, :] = total / (1.0 + jnp.exp(-total))
 
     count = 3 * reqs * steps
-    tail[...] = jnp.zeros_like(tail)
     for s in range(blocks):
         head = z ^ s
         lanes = pl.ds(pl.multiple_of(head * head_size, head_size), head_size)
@@ -140,38 +152,40 @@
     extra = 3 * reqs * steps + 6
     extra += -extra % 8
     spec = pl.BlockSpec(memory_space=VMEM)
-    return pl.pallas_call(
-        functools.partial(pack_kernel, blocks, taps),
+    small = (
+        proj.transpose(0, 2, 1, 3),
+        conv_cache.transpose(1, 2, 0, 3),
+        conv_weight.transpose(1, 0, 2),
+        forget_bias.reshape(blocks, head_size),
+        norm_gain.reshape(blocks, head_size),
+    )
+    return pl.pallas_call(
+        functools.partial(pack_kernel, blocks),
         out_shape=[VMEM((reqs * head_size + extra, head_size), BF16)] * blocks,
-        in_specs=[pl.BlockSpec(memory_space=pltpu.SMEM)]
-        + [spec] * 5
-        + [pl.BlockSpec(memory_space=pl.ANY)],
+        in_specs=[pl.BlockSpec(memory_space=pl.ANY)] * 7,
         out_specs=[spec] * blocks,
         scratch_shapes=[
             VMEM((3 * reqs, taps + steps, width), F32),
             VMEM((3 * reqs * steps, width), F32),
             VMEM((extra, head_size), F32),
             pltpu.SemaphoreType.DMA((blocks * reqs,)),
-        ],
+            pltpu.SemaphoreType.DMA((len(small) + 1,)),
+            pltpu.SMEM(lengths.shape, jnp.int32),
+        ]
+        + [VMEM(value.shape, value.dtype) for value in small],
         name="pack",
-    )(
-        lengths,
-        proj.transpose(0, 2, 1, 3),
-        conv_cache.transpose(1, 2, 0, 3),
-        conv_weight.transpose(1, 0, 2),
-        forget_bias.reshape(blocks, head_size),
-        norm_gain.reshape(blocks, head_size),
-        old_state,
-    )
-
-
-def rows_kernel(blocks, reqs, steps, index_ref, *refs):
+    )(lengths, old_state, *small)
+
+
+def middle_kernel(blocks, reqs, steps, index_far, *refs):
     own = refs[:blocks][::-1]
     sib = refs[blocks : 2 * blocks]
     live_ref = refs[2 * blocks]
-    normed_out = refs[2 * blocks + 1 : 3 * blocks + 1]
-    pool, turned, lasting, values = refs[3 * blocks + 1 : 3 * blocks + 5]
-    flat, gathered, columns, lefts, local_out, state_out = refs[3 * blocks + 5 :]
+    outs = refs[2 * blocks + 1 : 3 * blocks + 1]
+    pool, flat, gathered, columns, lefts, lasting, values, heard = refs[3 * blocks + 1 : -2]
+    index_ref, sem = refs[-2:]
+    fetch = pltpu.make_async_copy(index_far, index_ref, sem)
+    fetch.start()
     count = blocks * reqs
     head_size = pool.shape[-1]
     rows = reqs * head_size
@@ -187,7 +201,6 @@
             here = slice(r * head_size, (r + 1) * head_size)
             pool[s * reqs + r] = own[s][here, :]
             pool[(blocks + s) * reqs + r] = sib[s][here, :]
-
     base = 3 * steps * reqs
     bias = flat[base : base + 1, :] + flat[base + 1 : base + 2, :] + flat[base + 2 : base + 3, :]
     gain = flat[base + 3 : base + 4, :] + flat[base + 4 : base + 5, :] + flat[base + 5 : base + 6, :]
@@ -206,34 +219,19 @@
         for earlier in range(t + 1):
             score = jnp.sum(query[t] * weights[earlier], axis=-1, keepdims=True)
             out = out + score * inputs[earlier]
-        local_out[pl.ds(t, count, stride=steps), :] = out
-
-    for i in range(count):
-        left = lefts[pl.ds(i, steps, stride=count), :].astype(BF16)
-        state_out[pl.ds(i * steps, steps), :] = jnp.dot(
-            left, pool[index_ref[i]], preferred_element_type=F32
-        )
-    head_out = state_out[...] + local_out[...]
-    scale = lax.rsqrt(jnp.mean(head_out * head_out, axis=-1, keepdims=True) + 1e-06)
-    normed = (head_out * scale * gain).astype(BF16)
-    for s in range(blocks):
-        normed_out[s][...] = normed[s * reqs * steps : (s + 1) * reqs * steps]
+        heard[pl.ds(t, count, stride=steps), :] = out
 
     columns[...] = jnp.zeros_like(columns)
     columns[pl.ds(0, count), :] = decay
-    turned[...] = columns[...].T
-    for s in range(blocks):
+    turned = columns[...].T
+    for s in range(blocks):
+        mine = slice(s * reqs, (s + 1) * reqs)
         for t in range(steps):
             here = pl.ds((s * steps + t) * reqs, reqs)
-            lasting[here, :] = weights[t][s * reqs : (s + 1) * reqs, :]
-            values[here, :] = inputs[t][s * reqs : (s + 1) * reqs, :]
-
-
-def states_kernel(blocks, reqs, steps, apart, index_ref, pool, turned_ref, lasting, values, *refs):
-    riders = refs[: blocks - len(apart)]
-    outs = refs[blocks - len(apart) :]
-    head_size = pool.shape[-1]
-    turned = turned_ref[...]
+            values[here, :] = inputs[t][mine, :]
+            lasting[here, :] = weights[t][mine, :]
+
+    fetch.wait()
     of_req = lax.broadcasted_iota(jnp.int32, (steps * reqs, head_size), 0) % reqs
     for s in range(blocks):
         here = slice(s * steps * reqs, (s + 1) * steps * reqs)
@@ -251,15 +249,71 @@
         )
         for r in range(reqs):
             i = s * reqs + r
+            old = pool[index_ref[i]]
+            wanted = lefts[pl.ds(i, steps, stride=count), :].astype(BF16)
+            said = jnp.dot(wanted, old, preferred_element_type=F32)
+            heard[pl.ds(i * steps, steps), :] += said
             span = slice(r * head_size, (r + 1) * head_size)
-            current = turned[:, i : i + 1] * pool[index_ref[i]].astype(F32) + added[:, span]
+            current = turned[:, i : i + 1] * old.astype(F32) + added[:, span]
             outs[s][span, :] = current.astype(BF16)
-    for k, s in enumerate(s for s in range(blocks) if s not in apart):
-        outs[s][reqs * head_size :, :] = riders[k][...]
+
+    head_out = heard[...]
+    scale = lax.rsqrt(jnp.mean(head_out * head_out, axis=-1, keepdims=True) + 1e-06)
+    normed = (head_out * scale * gain).astype(BF16)
+    for s in range(blocks):
+        outs[s][rows:, :] = normed[s * reqs * steps : (s + 1) * reqs * steps]
+
+
+def middle(index, own, sib, live, reqs, steps):
+    blocks = len(own)
+    count = blocks * reqs
+    head_size = own[0].shape[-1]
+    extra = own[0].shape[0] - reqs * head_size
+    columns = -(-count // 128) * 128
+    spec = pl.BlockSpec(memory_space=VMEM)
+    table = VMEM((steps * count, head_size), F32)
+    return pl.pallas_call(
+        functools.partial(middle_kernel, blocks, reqs, steps),
+        out_shape=[VMEM((reqs * (head_size + steps), head_size), BF16)] * blocks,
+        in_specs=[pl.BlockSpec(memory_space=pl.ANY)] + [spec] * (2 * blocks + 1),
+        out_specs=[spec] * blocks,
+        scratch_shapes=[
+            VMEM((2 * count, head_size, head_size), BF16),
+            VMEM((extra, head_size), F32),
+            VMEM((3 * steps, count, head_size), F32),
+            VMEM((columns, head_size), F32),
+            table,
+            table,
+            table,
+            table,
+            pltpu.SMEM(index.shape, jnp.int32),
+            pltpu.SemaphoreType.DMA(()),
+        ],
+        name="middle",
+        compiler_params=PARAMS,
+    )(index, *on_chip(*own[::-1], *sib, live))
+
+
+def fetch_kernel(far_ref, out, sem):
+    copy = pltpu.make_async_copy(far_ref, out, sem)
+    copy.start()
+    copy.wait()
+
+
+def fetch(value):
+    return pl.pallas_call(
+        fetch_kernel,
+        out_shape=VMEM(value.shape, value.dtype),
+        in_specs=[pl.BlockSpec(memory_space=pl.ANY)],
+        out_specs=pl.BlockSpec(memory_space=VMEM),
+        scratch_shapes=[pltpu.SemaphoreType.DMA(())],
+        name="fetch",
+        compiler_params=PARAMS,
+    )(pltpu.with_memory_space_constraint(value, pltpu.HBM))
 
 
 def project_kernel(blocks, *refs):
-    parts, weight, out, left = refs[:blocks], refs[blocks], refs[blocks + 1], refs[blocks + 2]
+    parts, weight, out, left = refs[:blocks][::-1], refs[blocks], refs[blocks + 1], refs[blocks + 2]
     rows, head_size = out.shape[0], parts[0].shape[-1]
     z = lax.axis_index("req") // 2
     for s in range(blocks):
@@ -278,14 +332,11 @@
         scratch_shapes=[VMEM((rows, weight.shape[0]), BF16)],
         name="project",
         compiler_params=PARAMS,
-    )(*on_chip(*parts, weight))
-
-
-def finish_kernel(blocks, terms, *refs):
-    parts = refs[:blocks][::-1]
-    resid = refs[blocks]
-    added = refs[blocks + 1 : blocks + 1 + terms]
-    mixed, out, sems = refs[blocks + 1 + terms :]
+    )(*on_chip(*parts[::-1], weight))
+
+
+def place_kernel(blocks, *refs):
+    parts, out, sems = refs[:blocks][::-1], refs[blocks], refs[blocks + 1]
     reqs, _, head_size, _ = out.shape
     z = lax.axis_index("req") // 2
     copies = []
@@ -298,81 +349,47 @@
             )
             copy.start()
             copies.append(copy)
-    total = [value[...].astype(F32) for value in added]
-    total = (total[0] + total[1]) + (total[2] + total[3])
-    steps = total.shape[0] // reqs
-    for r in range(reqs):
-        mixed[r] = (resid[r].astype(F32) + total[r * steps : (r + 1) * steps, :]).astype(BF16)
     for copy in copies:
         copy.wait()
 
 
-def finish(back, resid, added, reqs):
-    blocks = len(back)
-    head_size = back[0].shape[-1]
+def place(back, shape):
+    return pl.pallas_call(
+        functools.partial(place_kernel, len(back)),
+        out_shape=jax.ShapeDtypeStruct(shape, BF16),
+        in_specs=[pl.BlockSpec(memory_space=VMEM)] * len(back),
+        out_specs=pl.BlockSpec(memory_space=pl.ANY),
+        scratch_shapes=[pltpu.SemaphoreType.DMA((len(back) * shape[0],))],
+        name="place",
+        compiler_params=PARAMS,
+    )(*on_chip(*back[::-1]))
+
+
+def add_kernel(resid, *refs):
+    out = refs[-1]
+    total = [value[...].astype(F32) for value in refs[:-1]]
+    while len(total) > 1:
+        total = [total[k] + total[k + 1] for k in range(0, len(total), 2)]
+    reqs = resid.shape[0]
+    steps = total[0].shape[0] // reqs
+    for r in range(reqs):
+        out[r] = (resid[r].astype(F32) + total[0][r * steps : (r + 1) * steps, :]).astype(BF16)
+
+
+def add(resid, terms):
     spec = pl.BlockSpec(memory_space=VMEM)
     return pl.pallas_call(
-        functools.partial(finish_kernel, blocks, len(added)),
-        out_shape=[
-            jax.ShapeDtypeStruct(resid.shape, BF16),
-            jax.ShapeDtypeStruct((reqs, blocks, head_size, head_size), BF16),
-        ],
-        in_specs=[spec] * (blocks + 1 + len(added)),
-        out_specs=[spec, pl.BlockSpec(memory_space=pl.ANY)],
-        scratch_shapes=[pltpu.SemaphoreType.DMA((blocks * reqs,))],
-        name="finish",
+        add_kernel,
+        out_shape=jax.ShapeDtypeStruct(resid.shape, BF16),
+        in_specs=[spec] * (1 + len(terms)),
+        out_specs=spec,
+        name="add",
         compiler_params=PARAMS,
-    )(*on_chip(*back[::-1], resid, *added))
+    )(*on_chip(resid, *terms))
 
 
 def on_chip(*arrays):
     return [pltpu.with_memory_space_constraint(value, VMEM) for value in arrays]
-
-
-def middle_rows(index, own, sib, live, reqs, steps):
-    blocks = len(own)
-    count = blocks * reqs
-    head_size = own[0].shape[-1]
-    extra = own[0].shape[0] - reqs * head_size
-    columns = -(-count // 128) * 128
-    spec = pl.BlockSpec(memory_space=VMEM)
-    outs = pl.pallas_call(
-        functools.partial(rows_kernel, blocks, reqs, steps),
-        out_shape=[VMEM((reqs * steps, head_size), BF16)] * blocks
-        + [
-            VMEM((2 * count, head_size, head_size), BF16),
-            VMEM((head_size, columns), F32),
-            VMEM((steps * count, head_size), F32),
-            VMEM((steps * count, head_size), F32),
-        ],
-        in_specs=[pl.BlockSpec(memory_space=pltpu.SMEM)] + [spec] * (2 * blocks + 1),
-        out_specs=[spec] * (blocks + 4),
-        scratch_shapes=[
-            VMEM((extra, head_size), F32),
-            VMEM((3 * steps, count, head_size), F32),
-            VMEM((columns, head_size), F32),
-            VMEM((steps * count, head_size), F32),
-            VMEM((steps * count, head_size), F32),
-            VMEM((steps * count, head_size), F32),
-        ],
-        name="rows",
-        compiler_params=PARAMS,
-    )(index, *on_chip(*own[::-1], *sib, live))
-    return outs[:blocks], outs[blocks:]
-
-
-def middle_states(index, kept, riders, blocks, reqs, steps, apart):
-    head_size = kept[0].shape[-1]
-    spec = pl.BlockSpec(memory_space=VMEM)
-    rows = [reqs * head_size + (0 if s in apart else reqs * steps) for s in range(blocks)]
-    return pl.pallas_call(
-        functools.partial(states_kernel, blocks, reqs, steps, apart),
-        out_shape=[VMEM((r, head_size), BF16) for r in rows],
-        in_specs=[pl.BlockSpec(memory_space=pltpu.SMEM)] + [spec] * (4 + len(riders)),
-        out_specs=[spec] * blocks,
-        name="states",
-        compiler_params=PARAMS,
-    )(index, *on_chip(*kept, *riders))
 
 
 def swapped_body(
@@ -385,7 +402,6 @@
     own_req = lax.axis_index("req")
     own_head = lax.axis_index("head")
     z, core = own_req // 2, own_head % 2
-    state_rows = local_reqs * head_size
 
     both = ("req", "head")
     sibling = [(i, i ^ 1) for i in range(n_head)]
@@ -403,11 +419,11 @@
     packs = pack(lengths, proj, conv_cache, conv_weight, forget_bias, norm_gain, old_state)
     own = [swap(packs[s], s) for s in range(blocks)]
     near, far = range(blocks // 2), range(blocks // 2, blocks)
-    sib = [lax.ppermute(own[s][:state_rows], "head", sibling) for s in near]
+    sib = [lax.ppermute(own[s], "head", sibling) for s in near]
     held = lax.optimization_barrier((*sib, *[own[s] for s in far]))
     sib = list(held[: len(near)])
     own = own[: len(near)] + list(held[len(near) :])
-    sib += [lax.ppermute(own[s][:state_rows], "head", sibling) for s in far]
+    sib += [lax.ppermute(own[s], "head", sibling) for s in far]
 
     zs = z ^ jnp.arange(blocks, dtype=jnp.int32)
     slots = ((zs * 2 + core) * local_reqs)[:, None] + jnp.arange(local_reqs, dtype=jnp.int32)[None, :]
@@ -420,23 +436,16 @@
     lens = jnp.sum(jnp.where(every == slots[:, None], lengths[None, :], 0), axis=1)
     live = jnp.broadcast_to((lens > 0).astype(F32)[:, None], (slots.shape[0], head_size))
 
-    apart = tuple(range(blocks // 2, blocks))
-    normed, kept = middle_rows(index, own, sib, live, local_reqs, steps)
-    rows = [swap(normed[s], s) if s in apart else None for s in range(blocks)]
-    riders = [normed[s] for s in range(blocks) if s not in apart]
-    states = middle_states(index, kept, riders, blocks, local_reqs, steps, apart)
-    held = lax.optimization_barrier((*states, *[rows[s] for s in apart]))
-    states, far = held[:blocks], held[blocks:]
-    for s, value in zip(apart, far):
-        rows[s] = value
+    states = middle(index, own, sib, live, local_reqs, steps)
     back = [swap(states[s], s) for s in range(blocks)]
-
-    rows = [rows[s] if s in apart else back[s] for s in range(blocks)]
-    part = project(rows, out_weight, local_reqs * steps)
-    added = [part] + [
+    weight, *_ = lax.optimization_barrier((out_weight, *states))
+    part = project(back, fetch(weight), local_reqs * steps)
+    terms = [part] + [
         lax.ppermute(part, "head", [(i, i ^ k) for i in range(n_head)]) for k in range(1, n_head)
     ]
-    return tuple(finish(back, resid, added, local_reqs))
+    held = lax.optimization_barrier((*back, part))
+    new_state = place(held[:blocks], old_state.shape)
+    return add(resid, terms), new_state
 
 
 def solution(mesh):

time: 50.6 us -> 47.5 us (0.939)
  starting transfers between devices: 27.4 us -> 21.3 us
  waiting for transfers between devices: 15 us -> 18 us
    ppermute x10 -> x8, starting transfers between devices: 15.1 us -> 11.5 us  [swap(): return lax.ppermute(value, both, pairs)]
    ppermute x3, waiting for transfers between devices: 0.01 us -> 2.84 us  [swapped_body(): lax.ppermute(part, 'head', [(i, i ^ k) for i in range(n_head)])]
    ppermute x3, starting transfers between devices: 5.42 us -> 2.94 us  [swapped_body(): lax.ppermute(part, 'head', [(i, i ^ k) for i in range(n_head)])]
    pallas_call x4 -> x5, Pallas kernels: 5.71 us -> 5.84 us  [the longest x1 1.6 us: fetch(): pl.pallas_call(fetch_kernel, out_shape=VMEM(value.shape, value.dtype), in...]
    ppermute x10 -> x8, waiting for transfers between devices: 13.7 us -> 13.8 us  [swap(): return lax.ppermute(value, both, pairs)]
  transfers between devices with their start and end apart: 17 -> 15, of which waited for: 6 -> 7; matrix products, arithmetic and copies ran while one was open for 2% -> 2% of each run, Pallas kernels for 3% -> 5%
where the time goes in v5:
time: 47.5 us; the launch traced here: 47.3 us
  starting transfers between devices  21.3 us (45%)
  waiting for transfers between devices  18 us (38%)
  Pallas kernels  6.22 us (13%)
  other arithmetic  0.96 us (2%)
  between operations  0.71 us (1%)
    ppermute x8, waiting for transfers between devices, swap(): return lax.ppermute(value, both, pairs)  13.8 us
    ppermute x8, starting transfers between devices, swap(): return lax.ppermute(value, both, pairs)  11.5 us
    ppermute x2, starting transfers between devices, swapped_body(): sib = [lax.ppermute(own[s], 'head', sibling) for s in near]  3.61 us
    ppermute x2, starting transfers between devices, swapped_body(): sib += [lax.ppermute(own[s], 'head', sibling) for s in far]  3.27 us
    ppermute x3, starting transfers between devices, swapped_body(): lax.ppermute(part, 'head', [(i, i ^ k) for i in range(n_head)])  2.94 us
    ppermute x3, waiting for transfers between devices, swapped_body(): lax.ppermute(part, 'head', [(i, i ^ k) for i in range(n_head)])  2.84 us
    pallas_call x1, Pallas kernels, fetch(): pl.pallas_call(fetch_kernel, out_shape=VMEM(value.shape, value.dtype), in...  1.6 us
    pallas_call x1, Pallas kernels, pack(): pl.pallas_call(functools.partial(pack_kernel, blocks), out_shape=[VMEM((r...  1.47 us
  transfers between devices with their start and end apart: 15, of which 7 were waited for; matrix products, arithmetic and copies ran while one was open for 2% of the time, Pallas kernels for 5%

profile of v5, /device:TPU:0, one launch (start us, length us, event | category | flops | bytes accessed | tf_op | source)
XLA Modules:
  0.0 47.3 jit_solution(2505814202798628312)
XLA Ops:
  0.6 1.5 %pack.1 = (bf16[568,128]{1,0:T(8,128)(2,1)S(1)}, bf16[568,128]{1,0:T(8,128)(2,1)S(1)}, bf16[568,128]{1,0:T(8,128)(2,1)S(1)}, bf16[568,128]{1,0:T(8,128)(2,1)S(1)}) custom-call(s32[32]{0:T(128)} %lens_far.1, bf16[4,4,128,128]{3,2,1,0:T(8,128)(2,1)} %refs_0_.1, bf16[4,3,4,512]{3,2,1,0:T(4,128)(2,1)} %bitcast.5, bf16[3,3,4,512]{3,2,1,0:T(4,128)(2,1)} %bitcast.6, ...), custom_call_target="tpu_custom_call" | custom-call | tf_op jit(solution)/shard_map/pack/pallas_call | solution.py:162
  2.1 0.7 %collective-permute-start = (bf16[568,128]{1,0:T(8,128)(2,1)S(1)}, bf16[568,128]{1,0:T(8,128)(2,1)S(1)}, u32[]{:S(2)}, u32[]{:S(2)}) collective-permute-start(bf16[568,128]{1,0:T(8,128)(2,1)S(1)} %get-tuple-element.19), channel_id=1, source_target_pairs={{0,0},{1,4},{2,2},{3,6},{4,1},{5,5},{6,3},{7,7},{8,8},{9,12},{10,1... | collective-permute-start | bytes 436232 | tf_op jit(solution)/shard_map/ppermute | solution.py:417
  2.8 3.1 %collective-permute-start.2 = (bf16[568,128]{1,0:T(8,128)(2,1)S(1)}, bf16[568,128]{1,0:T(8,128)(2,1)S(1)}, u32[]{:S(2)}, u32[]{:S(2)}) collective-permute-start(bf16[568,128]{1,0:T(8,128)(2,1)S(1)} %get-tuple-element.20), channel_id=1, source_target_pairs={{0,8},{1,12},{2,10},{3,14},{4,9},{5,13},{6,11},{7,15},{8,0},{9,4},... | collective-permute-start | bytes 436232 | tf_op jit(solution)/shard_map/ppermute | solution.py:417
  5.9 2.6 %collective-permute-start.4 = (bf16[568,128]{1,0:T(8,128)(2,1)S(1)}, bf16[568,128]{1,0:T(8,128)(2,1)S(1)}, u32[]{:S(2)}, u32[]{:S(2)}) collective-permute-start(bf16[568,128]{1,0:T(8,128)(2,1)S(1)} %get-tuple-element.21), channel_id=1, source_target_pairs={{0,16},{1,20},{2,18},{3,22},{4,17},{5,21},{6,19},{7,23},{8,24},{9,... | collective-permute-start | bytes 436232 | tf_op jit(solution)/shard_map/ppermute | solution.py:417
  8.5 0.0 collective-permute-start.5
  8.5 0.1 iota_add_fusion
  8.5 0.1 add.60
  8.6 0.9 %select_reduce_fusion = (s32[16]{0:T(128)S(1)}, s32[16]{0:T(128)S(1)}) fusion(s32[32]{0:T(128)} %lens_far.1, s32[16]{0:T(128)S(1)} %add.60, s32[32]{0:T(128)} %param.15), kind=kLoop, calls=%fused_computation | loop fusion | flops 3040 | bytes 448 | tf_op jit(solution)/shard_map/reduce_sum | solution.py:436
  9.5 3.5 %collective-permute-start.1 = (bf16[568,128]{1,0:T(8,128)(2,1)S(1)}, bf16[568,128]{1,0:T(8,128)(2,1)S(1)}, u32[]{:S(2)}, u32[]{:S(2)}) collective-permute-start(bf16[568,128]{1,0:T(8,128)(2,1)S(1)} %collective-permute-done.refs_3_), channel_id=1, source_target_pairs={{0,1},{1,0},{2,3},{3,2},{4,5},{5,4},{6,7},{7,6},{8,9},{9,8},{10,11... | collective-permute-start | bytes 436232 | tf_op jit(solution)/shard_map/ppermute | solution.py:422
  13.0 0.1 collective-permute-start.3
  13.1 4.3 %collective-permute-done.5.refs_0_ = bf16[568,128]{1,0:T(8,128)(2,1)S(1)} collective-permute-done((bf16[568,128]{1,0:T(8,128)(2,1)S(1)}, bf16[568,128]{1,0:T(8,128)(2,1)S(1)}, u32[]{:S(2)}, u32[]{:S(2)}) %collective-permute-start.5) | collective-permute-done | bytes 145440 | tf_op jit(solution)/shard_map/ppermute | solution.py:417
  17.5 3.2 %collective-permute-start.7 = (bf16[568,128]{1,0:T(8,128)(2,1)S(1)}, bf16[568,128]{1,0:T(8,128)(2,1)S(1)}, u32[]{:S(2)}, u32[]{:S(2)}) collective-permute-start(bf16[568,128]{1,0:T(8,128)(2,1)S(1)} %collective-permute-done.5.refs_0_), channel_id=1, source_target_pairs={{0,1},{1,0},{2,3},{3,2},{4,5},{5,4},{6,7},{7,6},{8,9},{9,8},{10,11... | collective-permute-start | bytes 436232 | tf_op jit(solution)/shard_map/ppermute | solution.py:426
  20.7 0.1 collective-permute-start.6
  20.7 0.9 %collective-permute-done.7.refs_7_ = bf16[568,128]{1,0:T(8,128)(2,1)S(1)} collective-permute-done((bf16[568,128]{1,0:T(8,128)(2,1)S(1)}, bf16[568,128]{1,0:T(8,128)(2,1)S(1)}, u32[]{:S(2)}, u32[]{:S(2)}) %collective-permute-start.7) | collective-permute-done | bytes 145440 | tf_op jit(solution)/shard_map/ppermute | solution.py:426
  21.7 0.4 collective-permute-done.6.refs_6_
  22.0 0.1 broadcast_in_dim.35.refs_8_
  22.1 1.2 %middle.1 = (bf16[528,128]{1,0:T(8,128)(2,1)S(1)}, bf16[528,128]{1,0:T(8,128)(2,1)S(1)}, bf16[528,128]{1,0:T(8,128)(2,1)S(1)}, bf16[528,128]{1,0:T(8,128)(2,1)S(1)}) custom-call(s32[16]{0:T(128)S(1)} %fusion.index_far, bf16[568,128]{1,0:T(8,128)(2,1)S(1)} %collective-permute-done.5.refs_0_, bf16[568,128]{1,0:T(8,128)(2,1)S(1)} %collective-permute-done.4.refs_1_, ...), custom_call_target="tpu_custom_call" | custom-call | tf_op jit(solution)/shard_map/middle/pallas_call | solution.py:275
  23.3 2.6 %collective-permute-start.8 = (bf16[528,128]{1,0:T(8,128)(2,1)S(1)}, bf16[528,128]{1,0:T(8,128)(2,1)S(1)}, u32[]{:S(2)}, u32[]{:S(2)}) collective-permute-start(bf16[528,128]{1,0:T(8,128)(2,1)S(1)} %get-tuple-element.27), channel_id=1, source_target_pairs={{0,24},{1,28},{2,26},{3,30},{4,25},{5,29},{6,27},{7,31},{8,16},{9,... | collective-permute-start | bytes 405512 | tf_op jit(solution)/shard_map/ppermute | solution.py:417
  25.8 1.0 %collective-permute-start.9 = (bf16[528,128]{1,0:T(8,128)(2,1)S(1)}, bf16[528,128]{1,0:T(8,128)(2,1)S(1)}, u32[]{:S(2)}, u32[]{:S(2)}) collective-permute-start(bf16[528,128]{1,0:T(8,128)(2,1)S(1)} %get-tuple-element.28), channel_id=1, source_target_pairs={{0,16},{1,20},{2,18},{3,22},{4,17},{5,21},{6,19},{7,23},{8,24},{9,... | collective-permute-start | bytes 405512 | tf_op jit(solution)/shard_map/ppermute | solution.py:417
  26.8 0.9 %collective-permute-start.10 = (bf16[528,128]{1,0:T(8,128)(2,1)S(1)}, bf16[528,128]{1,0:T(8,128)(2,1)S(1)}, u32[]{:S(2)}, u32[]{:S(2)}) collective-permute-start(bf16[528,128]{1,0:T(8,128)(2,1)S(1)} %get-tuple-element.29), channel_id=1, source_target_pairs={{0,8},{1,12},{2,10},{3,14},{4,9},{5,13},{6,11},{7,15},{8,0},{9,4},... | collective-permute-start | bytes 405512 | tf_op jit(solution)/shard_map/ppermute | solution.py:417
  27.7 0.7 %collective-permute-start.11 = (bf16[528,128]{1,0:T(8,128)(2,1)S(1)}, bf16[528,128]{1,0:T(8,128)(2,1)S(1)}, u32[]{:S(2)}, u32[]{:S(2)}) collective-permute-start(bf16[528,128]{1,0:T(8,128)(2,1)S(1)} %get-tuple-element.30), channel_id=1, source_target_pairs={{0,0},{1,4},{2,2},{3,6},{4,1},{5,5},{6,3},{7,7},{8,8},{9,12},{10,1... | collective-permute-start | bytes 405512 | tf_op jit(solution)/shard_map/ppermute | solution.py:417
  28.4 1.6 %fetch.1.refs_4_ = bf16[512,2048]{1,0:T(8,128)(2,1)S(1)} custom-call(bf16[512,2048]{1,0:T(8,128)(2,1)} %far_ref), custom_call_target="tpu_custom_call" | custom-call | tf_op jit(solution)/shard_map/fetch/pallas_call | solution.py:304
  30.0 0.0 copy-start
  30.0 0.4 collective-permute-done.8.refs_0_
  30.5 9.1 %collective-permute-done.9.refs_1_ = bf16[528,128]{1,0:T(8,128)(2,1)S(1)} collective-permute-done((bf16[528,128]{1,0:T(8,128)(2,1)S(1)}, bf16[528,128]{1,0:T(8,128)(2,1)S(1)}, u32[]{:S(2)}, u32[]{:S(2)}) %collective-permute-start.9) | collective-permute-done | bytes 135200 | tf_op jit(solution)/shard_map/ppermute | solution.py:417
  39.5 0.4 project.1.refs_0_
  39.9 2.4 %collective-permute-start.14 = (bf16[16,2048]{1,0:T(8,128)(2,1)S(1)}, bf16[16,2048]{1,0:T(8,128)(2,1)S(1)}, u32[]{:S(2)}, u32[]{:S(2)}) collective-permute-start(bf16[16,2048]{1,0:T(8,128)(2,1)S(1)} %project.1.refs_0_), channel_id=1, source_target_pairs={{0,3},{1,2},{2,1},{3,0},{4,7},{5,6},{6,5},{7,4},{8,11},{9,10},{10,... | collective-permute-start | bytes 196616 | tf_op jit(solution)/shard_map/ppermute | solution.py:444
  42.3 0.5 %collective-permute-start.13 = (bf16[16,2048]{1,0:T(8,128)(2,1)S(1)}, bf16[16,2048]{1,0:T(8,128)(2,1)S(1)}, u32[]{:S(2)}, u32[]{:S(2)}) collective-permute-start(bf16[16,2048]{1,0:T(8,128)(2,1)S(1)} %project.1.refs_0_), channel_id=1, source_target_pairs={{0,2},{1,3},{2,0},{3,1},{4,6},{5,7},{6,4},{7,5},{8,10},{9,11},{10,... | collective-permute-start | bytes 196616 | tf_op jit(solution)/shard_map/ppermute | solution.py:444
  42.8 0.9 %place.1 = bf16[4,4,128,128]{3,2,1,0:T(8,128)(2,1)} custom-call(bf16[528,128]{1,0:T(8,128)(2,1)S(1)} %collective-permute-done.8.refs_0_, bf16[528,128]{1,0:T(8,128)(2,1)S(1)} %collective-permute-done.9.refs_1_, bf16[528,128]{1,0:T(8,128)(2,1)S(1)} %collective-permute-done.10.refs_2_, bf16[528,128]{1,0:T(8,128)(2,1)S(1)} %collective-permute-done.11.refs_3_), custom_call_target="tpu_custom_call" | custom-call | tf_op jit(solution)/shard_map/place/pallas_call | solution.py:357
  43.8 0.5 %collective-permute-done.14.refs_3_ = bf16[16,2048]{1,0:T(8,128)(2,1)S(1)} collective-permute-done((bf16[16,2048]{1,0:T(8,128)(2,1)S(1)}, bf16[16,2048]{1,0:T(8,128)(2,1)S(1)}, u32[]{:S(2)}, u32[]{:S(2)}) %collective-permute-start.14) | collective-permute-done | bytes 65568 | tf_op jit(solution)/shard_map/ppermute | solution.py:444
  44.3 2.3 %collective-permute-done.13.refs_2_ = bf16[16,2048]{1,0:T(8,128)(2,1)S(1)} collective-permute-done((bf16[16,2048]{1,0:T(8,128)(2,1)S(1)}, bf16[16,2048]{1,0:T(8,128)(2,1)S(1)}, u32[]{:S(2)}, u32[]{:S(2)}) %collective-permute-start.13) | collective-permute-done | bytes 65568 | tf_op jit(solution)/shard_map/ppermute | solution.py:444
  46.6 0.7 %add.84 = bf16[4,4,2048]{2,1,0:T(4,128)(2,1)} custom-call(bf16[4,4,2048]{2,1,0:T(4,128)(2,1)S(1)} %copy-done, bf16[16,2048]{1,0:T(8,128)(2,1)S(1)} %project.1.refs_0_, bf16[16,2048]{1,0:T(8,128)(2,1)S(1)} %collective-permute-done.12.refs_1_, bf16[16,2048]{1,0:T(8,128)(2,1)S(1)} %collective-permute-done.13.refs_2_, ...), custom_call_target="tpu_custom_call" | custom-call | tf_op jit(solution)/shard_map/add/pallas_call | solution.py:381
  (13 shorter events, 0.1 us)
Async XLA Ops:
  2.1 7.4 %collective-permute-start = (bf16[568,128]{1,0:T(8,128)(2,1)S(1)}, bf16[568,128]{1,0:T(8,128)(2,1)S(1)}, u32[]{:S(2)}, u32[]{:S(2)}) collective-permute-start(bf16[568,128]{1,0:T(8,128)(2,1)S(1)} %get-tuple-element.19), channel_id=1, source_target_pairs={{0,0},{1,4},{2,2},{3,6},{4,1},{5,5},{6,3},{7,7},{8,8},{9,12},{10,1... | collective-permute-start | bytes 436232 | tf_op jit(solution)/shard_map/ppermute | solution.py:417
  2.8 10.2 %collective-permute-start.2 = (bf16[568,128]{1,0:T(8,128)(2,1)S(1)}, bf16[568,128]{1,0:T(8,128)(2,1)S(1)}, u32[]{:S(2)}, u32[]{:S(2)}) collective-permute-start(bf16[568,128]{1,0:T(8,128)(2,1)S(1)} %get-tuple-element.20), channel_id=1, source_target_pairs={{0,8},{1,12},{2,10},{3,14},{4,9},{5,13},{6,11},{7,15},{8,0},{9,4},... | collective-permute-start | bytes 436232 | tf_op jit(solution)/shard_map/ppermute | solution.py:417
  5.9 7.3 %collective-permute-start.4 = (bf16[568,128]{1,0:T(8,128)(2,1)S(1)}, bf16[568,128]{1,0:T(8,128)(2,1)S(1)}, u32[]{:S(2)}, u32[]{:S(2)}) collective-permute-start(bf16[568,128]{1,0:T(8,128)(2,1)S(1)} %get-tuple-element.21), channel_id=1, source_target_pairs={{0,16},{1,20},{2,18},{3,22},{4,17},{5,21},{6,19},{7,23},{8,24},{9,... | collective-permute-start | bytes 436232 | tf_op jit(solution)/shard_map/ppermute | solution.py:417
  8.5 9.0 %collective-permute-start.5 = (bf16[568,128]{1,0:T(8,128)(2,1)S(1)}, bf16[568,128]{1,0:T(8,128)(2,1)S(1)}, u32[]{:S(2)}, u32[]{:S(2)}) collective-permute-start(bf16[568,128]{1,0:T(8,128)(2,1)S(1)} %get-tuple-element.22), channel_id=1, source_target_pairs={{0,24},{1,28},{2,26},{3,30},{4,25},{5,29},{6,27},{7,31},{8,16},{9,... | collective-permute-start | bytes 436232 | tf_op jit(solution)/shard_map/ppermute | solution.py:417
  9.5 8.0 %collective-permute-start.1 = (bf16[568,128]{1,0:T(8,128)(2,1)S(1)}, bf16[568,128]{1,0:T(8,128)(2,1)S(1)}, u32[]{:S(2)}, u32[]{:S(2)}) collective-permute-start(bf16[568,128]{1,0:T(8,128)(2,1)S(1)} %collective-permute-done.refs_3_), channel_id=1, source_target_pairs={{0,1},{1,0},{2,3},{3,2},{4,5},{5,4},{6,7},{7,6},{8,9},{9,8},{10,11... | collective-permute-start | bytes 436232 | tf_op jit(solution)/shard_map/ppermute | solution.py:422
  13.0 4.4 %collective-permute-start.3 = (bf16[568,128]{1,0:T(8,128)(2,1)S(1)}, bf16[568,128]{1,0:T(8,128)(2,1)S(1)}, u32[]{:S(2)}, u32[]{:S(2)}) collective-permute-start(bf16[568,128]{1,0:T(8,128)(2,1)S(1)} %collective-permute-done.2.refs_2_), channel_id=1, source_target_pairs={{0,1},{1,0},{2,3},{3,2},{4,5},{5,4},{6,7},{7,6},{8,9},{9,8},{10,11... | collective-permute-start | bytes 436232 | tf_op jit(solution)/shard_map/ppermute | solution.py:422
  17.5 4.2 %collective-permute-start.7 = (bf16[568,128]{1,0:T(8,128)(2,1)S(1)}, bf16[568,128]{1,0:T(8,128)(2,1)S(1)}, u32[]{:S(2)}, u32[]{:S(2)}) collective-permute-start(bf16[568,128]{1,0:T(8,128)(2,1)S(1)} %collective-permute-done.5.refs_0_), channel_id=1, source_target_pairs={{0,1},{1,0},{2,3},{3,2},{4,5},{5,4},{6,7},{7,6},{8,9},{9,8},{10,11... | collective-permute-start | bytes 436232 | tf_op jit(solution)/shard_map/ppermute | solution.py:426
  20.7 1.4 %collective-permute-start.6 = (bf16[568,128]{1,0:T(8,128)(2,1)S(1)}, bf16[568,128]{1,0:T(8,128)(2,1)S(1)}, u32[]{:S(2)}, u32[]{:S(2)}) collective-permute-start(bf16[568,128]{1,0:T(8,128)(2,1)S(1)} %collective-permute-done.4.refs_1_), channel_id=1, source_target_pairs={{0,1},{1,0},{2,3},{3,2},{4,5},{5,4},{6,7},{7,6},{8,9},{9,8},{10,11... | collective-permute-start | bytes 436232 | tf_op jit(solution)/shard_map/ppermute | solution.py:426
  23.3 7.2 %collective-permute-start.8 = (bf16[528,128]{1,0:T(8,128)(2,1)S(1)}, bf16[528,128]{1,0:T(8,128)(2,1)S(1)}, u32[]{:S(2)}, u32[]{:S(2)}) collective-permute-start(bf16[528,128]{1,0:T(8,128)(2,1)S(1)} %get-tuple-element.27), channel_id=1, source_target_pairs={{0,24},{1,28},{2,26},{3,30},{4,25},{5,29},{6,27},{7,31},{8,16},{9,... | collective-permute-start | bytes 405512 | tf_op jit(solution)/shard_map/ppermute | solution.py:417
  25.8 13.7 %collective-permute-start.9 = (bf16[528,128]{1,0:T(8,128)(2,1)S(1)}, bf16[528,128]{1,0:T(8,128)(2,1)S(1)}, u32[]{:S(2)}, u32[]{:S(2)}) collective-permute-start(bf16[528,128]{1,0:T(8,128)(2,1)S(1)} %get-tuple-element.28), channel_id=1, source_target_pairs={{0,16},{1,20},{2,18},{3,22},{4,17},{5,21},{6,19},{7,23},{8,24},{9,... | collective-permute-start | bytes 405512 | tf_op jit(solution)/shard_map/ppermute | solution.py:417
  26.8 12.7 %collective-permute-start.10 = (bf16[528,128]{1,0:T(8,128)(2,1)S(1)}, bf16[528,128]{1,0:T(8,128)(2,1)S(1)}, u32[]{:S(2)}, u32[]{:S(2)}) collective-permute-start(bf16[528,128]{1,0:T(8,128)(2,1)S(1)} %get-tuple-element.29), channel_id=1, source_target_pairs={{0,8},{1,12},{2,10},{3,14},{4,9},{5,13},{6,11},{7,15},{8,0},{9,4},... | collective-permute-start | bytes 405512 | tf_op jit(solution)/shard_map/ppermute | solution.py:417
  27.7 11.8 %collective-permute-start.11 = (bf16[528,128]{1,0:T(8,128)(2,1)S(1)}, bf16[528,128]{1,0:T(8,128)(2,1)S(1)}, u32[]{:S(2)}, u32[]{:S(2)}) collective-permute-start(bf16[528,128]{1,0:T(8,128)(2,1)S(1)} %get-tuple-element.30), channel_id=1, source_target_pairs={{0,0},{1,4},{2,2},{3,6},{4,1},{5,5},{6,3},{7,7},{8,8},{9,12},{10,1... | collective-permute-start | bytes 405512 | tf_op jit(solution)/shard_map/ppermute | solution.py:417
  30.0 16.6 %copy-start = (bf16[4,4,2048]{2,1,0:T(4,128)(2,1)S(1)}, bf16[4,4,2048]{2,1,0:T(4,128)(2,1)}, u32[]{:S(2)}) copy-start(bf16[4,4,2048]{2,1,0:T(4,128)(2,1)} %resid.1) | copy-start | bytes 196612
  39.9 4.4 %collective-permute-start.14 = (bf16[16,2048]{1,0:T(8,128)(2,1)S(1)}, bf16[16,2048]{1,0:T(8,128)(2,1)S(1)}, u32[]{:S(2)}, u32[]{:S(2)}) collective-permute-start(bf16[16,2048]{1,0:T(8,128)(2,1)S(1)} %project.1.refs_0_), channel_id=1, source_target_pairs={{0,3},{1,2},{2,1},{3,0},{4,7},{5,6},{6,5},{7,4},{8,11},{9,10},{10,... | collective-permute-start | bytes 196616 | tf_op jit(solution)/shard_map/ppermute | solution.py:444
  42.3 4.3 %collective-permute-start.13 = (bf16[16,2048]{1,0:T(8,128)(2,1)S(1)}, bf16[16,2048]{1,0:T(8,128)(2,1)S(1)}, u32[]{:S(2)}, u32[]{:S(2)}) collective-permute-start(bf16[16,2048]{1,0:T(8,128)(2,1)S(1)} %project.1.refs_0_), channel_id=1, source_target_pairs={{0,2},{1,3},{2,0},{3,1},{4,6},{5,7},{6,4},{7,5},{8,10},{9,11},{10,... | collective-permute-start | bytes 196616 | tf_op jit(solution)/shard_map/ppermute | solution.py:444
  42.8 3.8 %collective-permute-start.12 = (bf16[16,2048]{1,0:T(8,128)(2,1)S(1)}, bf16[16,2048]{1,0:T(8,128)(2,1)S(1)}, u32[]{:S(2)}, u32[]{:S(2)}) collective-permute-start(bf16[16,2048]{1,0:T(8,128)(2,1)S(1)} %project.1.refs_0_), channel_id=1, source_target_pairs={{0,1},{1,0},{2,3},{3,2},{4,5},{5,4},{6,7},{7,6},{8,9},{9,8},{10,11... | collective-permute-start | bytes 196616 | tf_op jit(solution)/shard_map/ppermute | solution.py:444

commit v6 on v5

--- a/solution.py
+++ b/solution.py
@@ -178,8 +178,8 @@
 
 
 def middle_kernel(blocks, reqs, steps, index_far, *refs):
-    own = refs[:blocks][::-1]
-    sib = refs[blocks : 2 * blocks]
+    own = in_order(refs[:blocks], order_out(blocks))
+    sib = in_order(refs[blocks : 2 * blocks], order_out(blocks))
     live_ref = refs[2 * blocks]
     outs = refs[2 * blocks + 1 : 3 * blocks + 1]
     pool, flat, gathered, columns, lefts, lasting, values, heard = refs[3 * blocks + 1 : -2]
@@ -291,7 +291,7 @@
         ],
         name="middle",
         compiler_params=PARAMS,
-    )(index, *on_chip(*own[::-1], *sib, live))
+    )(index, *on_chip(*[own[s] for s in order_out(blocks)], *[sib[s] for s in order_out(blocks)], live))
 
 
 def fetch_kernel(far_ref, out, sem):
@@ -313,7 +313,7 @@
 
 
 def project_kernel(blocks, *refs):
-    parts, weight, out, left = refs[:blocks][::-1], refs[blocks], refs[blocks + 1], refs[blocks + 2]
+    parts, weight, out, left = in_order(refs[:blocks], order_back(blocks)), refs[blocks], refs[blocks + 1], refs[blocks + 2]
     rows, head_size = out.shape[0], parts[0].shape[-1]
     z = lax.axis_index("req") // 2
     for s in range(blocks):
@@ -332,11 +332,11 @@
         scratch_shapes=[VMEM((rows, weight.shape[0]), BF16)],
         name="project",
         compiler_params=PARAMS,
-    )(*on_chip(*parts[::-1], weight))
+    )(*on_chip(*[parts[s] for s in order_back(len(parts))], weight))
 
 
 def place_kernel(blocks, *refs):
-    parts, out, sems = refs[:blocks][::-1], refs[blocks], refs[blocks + 1]
+    parts, out, sems = in_order(refs[:blocks], order_back(blocks)), refs[blocks], refs[blocks + 1]
     reqs, _, head_size, _ = out.shape
     z = lax.axis_index("req") // 2
     copies = []
@@ -362,7 +362,7 @@
         scratch_shapes=[pltpu.SemaphoreType.DMA((len(back) * shape[0],))],
         name="place",
         compiler_params=PARAMS,
-    )(*on_chip(*back[::-1]))
+    )(*on_chip(*[back[s] for s in order_back(len(back))]))
 
 
 def add_kernel(resid, *refs):
@@ -386,6 +386,19 @@
         name="add",
         compiler_params=PARAMS,
     )(*on_chip(resid, *terms))
+
+
+def order_out(blocks):
+    half = blocks // 2
+    return (blocks - 1, *range(half - 1, -1, -1), *range(half, blocks - 1))
+
+
+def order_back(blocks):
+    return tuple(range(blocks - 1, -1, -1))
+
+
+def in_order(refs, order):
+    return [refs[order.index(s)] for s in range(len(refs))]
 
 
 def on_chip(*arrays):
@@ -418,12 +431,7 @@
 
     packs = pack(lengths, proj, conv_cache, conv_weight, forget_bias, norm_gain, old_state)
     own = [swap(packs[s], s) for s in range(blocks)]
-    near, far = range(blocks // 2), range(blocks // 2, blocks)
-    sib = [lax.ppermute(own[s], "head", sibling) for s in near]
-    held = lax.optimization_barrier((*sib, *[own[s] for s in far]))
-    sib = list(held[: len(near)])
-    own = own[: len(near)] + list(held[len(near) :])
-    sib += [lax.ppermute(own[s], "head", sibling) for s in far]
+    sib = [lax.ppermute(own[s], "head", sibling) for s in range(blocks)]
 
     zs = z ^ jnp.arange(blocks, dtype=jnp.int32)
     slots = ((zs * 2 + core) * local_reqs)[:, None] + jnp.arange(local_reqs, dtype=jnp.int32)[None, :]

time: 47.5 us -> 44.3 us (0.933)
  starting transfers between devices: 21.3 us -> 15.7 us
  waiting for transfers between devices: 18 us -> 20.3 us
    ppermute x4, starting transfers between devices: 6.88 us -> 2.24 us  [swapped_body(): sib = [lax.ppermute(own[s], 'head', sibling) for s in range(blocks)]]
    ppermute x8, waiting for transfers between devices: 13.8 us -> 16.1 us  [swap(): return lax.ppermute(value, both, pairs)]
    ppermute x3, starting transfers between devices: 2.94 us -> 1.88 us  [swapped_body(): lax.ppermute(part, 'head', [(i, i ^ k) for i in range(n_head)])]
  transfers between devices with their start and end apart: 15 -> 15, of which waited for: 7 -> 8; matrix products, arithmetic and copies ran while one was open for 2% -> 2% of each run, Pallas kernels for 5% -> 6%
where the time goes in v6:
time: 44.3 us; the launch traced here: 44.1 us
  waiting for transfers between devices  20.3 us (46%)
  starting transfers between devices  15.7 us (35%)
  Pallas kernels  6.22 us (14%)
  other arithmetic  0.96 us (2%)
  between operations  0.72 us (2%)
    ppermute x8, waiting for transfers between devices, swap(): return lax.ppermute(value, both, pairs)  16.1 us
    ppermute x8, starting transfers between devices, swap(): return lax.ppermute(value, both, pairs)  11.6 us
    ppermute x3, waiting for transfers between devices, swapped_body(): lax.ppermute(part, 'head', [(i, i ^ k) for i in range(n_head)])  3.02 us
    ppermute x4, starting transfers between devices, swapped_body(): sib = [lax.ppermute(own[s], 'head', sibling) for s in range(blocks)]  2.24 us
    ppermute x3, starting transfers between devices, swapped_body(): lax.ppermute(part, 'head', [(i, i ^ k) for i in range(n_head)])  1.88 us
    pallas_call x1, Pallas kernels, fetch(): pl.pallas_call(fetch_kernel, out_shape=VMEM(value.shape, value.dtype), in...  1.6 us
    pallas_call x1, Pallas kernels, pack(): pl.pallas_call(functools.partial(pack_kernel, blocks), out_shape=[VMEM((r...  1.47 us
    ppermute x4, waiting for transfers between devices, swapped_body(): sib = [lax.ppermute(own[s], 'head', sibling) for s in range(blocks)]  1.24 us
  transfers between devices with their start and end apart: 15, of which 8 were waited for; matrix products, arithmetic and copies ran while one was open for 2% of the time, Pallas kernels for 6%

profile of v6, /device:TPU:0, one launch (start us, length us, event | category | flops | bytes accessed | tf_op | source)
XLA Modules:
  0.0 44.1 jit_solution(2840658083352160316)
XLA Ops:
  0.6 1.5 %pack.1 = (bf16[568,128]{1,0:T(8,128)(2,1)S(1)}, bf16[568,128]{1,0:T(8,128)(2,1)S(1)}, bf16[568,128]{1,0:T(8,128)(2,1)S(1)}, bf16[568,128]{1,0:T(8,128)(2,1)S(1)}) custom-call(s32[32]{0:T(128)} %lens_far.1, bf16[4,4,128,128]{3,2,1,0:T(8,128)(2,1)} %refs_0_.1, bf16[4,3,4,512]{3,2,1,0:T(4,128)(2,1)} %bitcast.5, bf16[3,3,4,512]{3,2,1,0:T(4,128)(2,1)} %bitcast.6, ...), custom_call_target="tpu_custom_call" | custom-call | tf_op jit(solution)/shard_map/pack/pallas_call | solution.py:162
  2.1 5.1 %collective-permute-start = (bf16[568,128]{1,0:T(8,128)(2,1)S(1)}, bf16[568,128]{1,0:T(8,128)(2,1)S(1)}, u32[]{:S(2)}, u32[]{:S(2)}) collective-permute-start(bf16[568,128]{1,0:T(8,128)(2,1)S(1)} %get-tuple-element.15), channel_id=1, source_target_pairs={{0,24},{1,28},{2,26},{3,30},{4,25},{5,29},{6,27},{7,31},{8,16},{9,... | collective-permute-start | bytes 436232 | tf_op jit(solution)/shard_map/ppermute | solution.py:430
  7.2 0.7 %collective-permute-start.2 = (bf16[568,128]{1,0:T(8,128)(2,1)S(1)}, bf16[568,128]{1,0:T(8,128)(2,1)S(1)}, u32[]{:S(2)}, u32[]{:S(2)}) collective-permute-start(bf16[568,128]{1,0:T(8,128)(2,1)S(1)} %get-tuple-element.17), channel_id=1, source_target_pairs={{0,0},{1,4},{2,2},{3,6},{4,1},{5,5},{6,3},{7,7},{8,8},{9,12},{10,1... | collective-permute-start | bytes 436232 | tf_op jit(solution)/shard_map/ppermute | solution.py:430
  7.9 0.7 %collective-permute-start.3 = (bf16[568,128]{1,0:T(8,128)(2,1)S(1)}, bf16[568,128]{1,0:T(8,128)(2,1)S(1)}, u32[]{:S(2)}, u32[]{:S(2)}) collective-permute-start(bf16[568,128]{1,0:T(8,128)(2,1)S(1)} %get-tuple-element.18), channel_id=1, source_target_pairs={{0,16},{1,20},{2,18},{3,22},{4,17},{5,21},{6,19},{7,23},{8,24},{9,... | collective-permute-start | bytes 436232 | tf_op jit(solution)/shard_map/ppermute | solution.py:430
  8.6 0.1 iota_add_fusion
  8.7 0.1 add.60
  8.8 0.9 %select_reduce_fusion = (s32[16]{0:T(128)S(1)}, s32[16]{0:T(128)S(1)}) fusion(s32[32]{0:T(128)} %lens_far.1, s32[16]{0:T(128)S(1)} %add.60, s32[32]{0:T(128)} %param.15), kind=kLoop, calls=%fused_computation | loop fusion | flops 3040 | bytes 448 | tf_op jit(solution)/shard_map/reduce_sum | solution.py:444
  9.6 1.9 %collective-permute-done.refs_0_ = bf16[568,128]{1,0:T(8,128)(2,1)S(1)} collective-permute-done((bf16[568,128]{1,0:T(8,128)(2,1)S(1)}, bf16[568,128]{1,0:T(8,128)(2,1)S(1)}, u32[]{:S(2)}, u32[]{:S(2)}) %collective-permute-start) | collective-permute-done | bytes 145440 | tf_op jit(solution)/shard_map/ppermute | solution.py:430
  11.6 1.6 %collective-permute-start.4 = (bf16[568,128]{1,0:T(8,128)(2,1)S(1)}, bf16[568,128]{1,0:T(8,128)(2,1)S(1)}, u32[]{:S(2)}, u32[]{:S(2)}) collective-permute-start(bf16[568,128]{1,0:T(8,128)(2,1)S(1)} %collective-permute-done.refs_0_), channel_id=1, source_target_pairs={{0,1},{1,0},{2,3},{3,2},{4,5},{5,4},{6,7},{7,6},{8,9},{9,8},{10,11... | collective-permute-start | bytes 436232 | tf_op jit(solution)/shard_map/ppermute | solution.py:434
  13.2 2.6 %collective-permute-done.1.refs_1_ = bf16[568,128]{1,0:T(8,128)(2,1)S(1)} collective-permute-done((bf16[568,128]{1,0:T(8,128)(2,1)S(1)}, bf16[568,128]{1,0:T(8,128)(2,1)S(1)}, u32[]{:S(2)}, u32[]{:S(2)}) %collective-permute-start.1) | collective-permute-done | bytes 145440 | tf_op jit(solution)/shard_map/ppermute | solution.py:430
  15.8 0.5 %collective-permute-start.5 = (bf16[568,128]{1,0:T(8,128)(2,1)S(1)}, bf16[568,128]{1,0:T(8,128)(2,1)S(1)}, u32[]{:S(2)}, u32[]{:S(2)}) collective-permute-start(bf16[568,128]{1,0:T(8,128)(2,1)S(1)} %collective-permute-done.1.refs_1_), channel_id=1, source_target_pairs={{0,1},{1,0},{2,3},{3,2},{4,5},{5,4},{6,7},{7,6},{8,9},{9,8},{10,11... | collective-permute-start | bytes 436232 | tf_op jit(solution)/shard_map/ppermute | solution.py:434
  16.3 0.0 collective-permute-start.6
  16.3 3.8 %collective-permute-done.3.refs_3_ = bf16[568,128]{1,0:T(8,128)(2,1)S(1)} collective-permute-done((bf16[568,128]{1,0:T(8,128)(2,1)S(1)}, bf16[568,128]{1,0:T(8,128)(2,1)S(1)}, u32[]{:S(2)}, u32[]{:S(2)}) %collective-permute-start.3) | collective-permute-done | bytes 145440 | tf_op jit(solution)/shard_map/ppermute | solution.py:430
  20.2 0.1 collective-permute-start.7
  20.3 1.2 %collective-permute-done.7.refs_7_ = bf16[568,128]{1,0:T(8,128)(2,1)S(1)} collective-permute-done((bf16[568,128]{1,0:T(8,128)(2,1)S(1)}, bf16[568,128]{1,0:T(8,128)(2,1)S(1)}, u32[]{:S(2)}, u32[]{:S(2)}) %collective-permute-start.7) | collective-permute-done | bytes 145440 | tf_op jit(solution)/shard_map/ppermute | solution.py:434
  21.5 0.1 broadcast_in_dim.35.refs_8_
  21.6 1.2 %middle.1 = (bf16[528,128]{1,0:T(8,128)(2,1)S(1)}, bf16[528,128]{1,0:T(8,128)(2,1)S(1)}, bf16[528,128]{1,0:T(8,128)(2,1)S(1)}, bf16[528,128]{1,0:T(8,128)(2,1)S(1)}) custom-call(s32[16]{0:T(128)S(1)} %fusion.index_far, bf16[568,128]{1,0:T(8,128)(2,1)S(1)} %collective-permute-done.refs_0_, bf16[568,128]{1,0:T(8,128)(2,1)S(1)} %collective-permute-done.1.refs_1_, ...), custom_call_target="tpu_custom_call" | custom-call | tf_op jit(solution)/shard_map/middle/pallas_call | solution.py:275
  22.8 2.8 %collective-permute-start.8 = (bf16[528,128]{1,0:T(8,128)(2,1)S(1)}, bf16[528,128]{1,0:T(8,128)(2,1)S(1)}, u32[]{:S(2)}, u32[]{:S(2)}) collective-permute-start(bf16[528,128]{1,0:T(8,128)(2,1)S(1)} %get-tuple-element.19), channel_id=1, source_target_pairs={{0,24},{1,28},{2,26},{3,30},{4,25},{5,29},{6,27},{7,31},{8,16},{9,... | collective-permute-start | bytes 405512 | tf_op jit(solution)/shard_map/ppermute | solution.py:430
  25.6 1.6 %collective-permute-start.10 = (bf16[528,128]{1,0:T(8,128)(2,1)S(1)}, bf16[528,128]{1,0:T(8,128)(2,1)S(1)}, u32[]{:S(2)}, u32[]{:S(2)}) collective-permute-start(bf16[528,128]{1,0:T(8,128)(2,1)S(1)} %get-tuple-element.21), channel_id=1, source_target_pairs={{0,8},{1,12},{2,10},{3,14},{4,9},{5,13},{6,11},{7,15},{8,0},{9,4},... | collective-permute-start | bytes 405512 | tf_op jit(solution)/shard_map/ppermute | solution.py:430
  27.2 0.7 %collective-permute-start.11 = (bf16[528,128]{1,0:T(8,128)(2,1)S(1)}, bf16[528,128]{1,0:T(8,128)(2,1)S(1)}, u32[]{:S(2)}, u32[]{:S(2)}) collective-permute-start(bf16[528,128]{1,0:T(8,128)(2,1)S(1)} %get-tuple-element.22), channel_id=1, source_target_pairs={{0,0},{1,4},{2,2},{3,6},{4,1},{5,5},{6,3},{7,7},{8,8},{9,12},{10,1... | collective-permute-start | bytes 405512 | tf_op jit(solution)/shard_map/ppermute | solution.py:430
  27.9 1.6 %fetch.1.refs_4_ = bf16[512,2048]{1,0:T(8,128)(2,1)S(1)} custom-call(bf16[512,2048]{1,0:T(8,128)(2,1)} %far_ref), custom_call_target="tpu_custom_call" | custom-call | tf_op jit(solution)/shard_map/fetch/pallas_call | solution.py:304
  29.5 0.0 copy-start
  29.5 1.0 %collective-permute-done.8.refs_0_ = bf16[528,128]{1,0:T(8,128)(2,1)S(1)} collective-permute-done((bf16[528,128]{1,0:T(8,128)(2,1)S(1)}, bf16[528,128]{1,0:T(8,128)(2,1)S(1)}, u32[]{:S(2)}, u32[]{:S(2)}) %collective-permute-start.8) | collective-permute-done | bytes 135200 | tf_op jit(solution)/shard_map/ppermute | solution.py:430
  30.5 6.7 %collective-permute-done.9.refs_1_ = bf16[528,128]{1,0:T(8,128)(2,1)S(1)} collective-permute-done((bf16[528,128]{1,0:T(8,128)(2,1)S(1)}, bf16[528,128]{1,0:T(8,128)(2,1)S(1)}, u32[]{:S(2)}, u32[]{:S(2)}) %collective-permute-start.9) | collective-permute-done | bytes 135200 | tf_op jit(solution)/shard_map/ppermute | solution.py:430
  37.2 0.4 project.1.refs_0_
  37.6 1.3 %collective-permute-start.14 = (bf16[16,2048]{1,0:T(8,128)(2,1)S(1)}, bf16[16,2048]{1,0:T(8,128)(2,1)S(1)}, u32[]{:S(2)}, u32[]{:S(2)}) collective-permute-start(bf16[16,2048]{1,0:T(8,128)(2,1)S(1)} %project.1.refs_0_), channel_id=1, source_target_pairs={{0,3},{1,2},{2,1},{3,0},{4,7},{5,6},{6,5},{7,4},{8,11},{9,10},{10,... | collective-permute-start | bytes 196616 | tf_op jit(solution)/shard_map/ppermute | solution.py:452
  38.9 0.5 %collective-permute-start.13 = (bf16[16,2048]{1,0:T(8,128)(2,1)S(1)}, bf16[16,2048]{1,0:T(8,128)(2,1)S(1)}, u32[]{:S(2)}, u32[]{:S(2)}) collective-permute-start(bf16[16,2048]{1,0:T(8,128)(2,1)S(1)} %project.1.refs_0_), channel_id=1, source_target_pairs={{0,2},{1,3},{2,0},{3,1},{4,6},{5,7},{6,4},{7,5},{8,10},{9,11},{10,... | collective-permute-start | bytes 196616 | tf_op jit(solution)/shard_map/ppermute | solution.py:452
  39.4 0.1 collective-permute-start.12
  39.5 0.9 %place.1 = bf16[4,4,128,128]{3,2,1,0:T(8,128)(2,1)} custom-call(bf16[528,128]{1,0:T(8,128)(2,1)S(1)} %collective-permute-done.8.refs_0_, bf16[528,128]{1,0:T(8,128)(2,1)S(1)} %collective-permute-done.9.refs_1_, bf16[528,128]{1,0:T(8,128)(2,1)S(1)} %collective-permute-done.10.refs_2_, bf16[528,128]{1,0:T(8,128)(2,1)S(1)} %collective-permute-done.11.refs_3_), custom_call_target="tpu_custom_call" | custom-call | tf_op jit(solution)/shard_map/place/pallas_call | solution.py:357
  40.4 1.3 %collective-permute-done.14.refs_3_ = bf16[16,2048]{1,0:T(8,128)(2,1)S(1)} collective-permute-done((bf16[16,2048]{1,0:T(8,128)(2,1)S(1)}, bf16[16,2048]{1,0:T(8,128)(2,1)S(1)}, u32[]{:S(2)}, u32[]{:S(2)}) %collective-permute-start.14) | collective-permute-done | bytes 65568 | tf_op jit(solution)/shard_map/ppermute | solution.py:452
  41.7 1.7 %collective-permute-done.13.refs_2_ = bf16[16,2048]{1,0:T(8,128)(2,1)S(1)} collective-permute-done((bf16[16,2048]{1,0:T(8,128)(2,1)S(1)}, bf16[16,2048]{1,0:T(8,128)(2,1)S(1)}, u32[]{:S(2)}, u32[]{:S(2)}) %collective-permute-start.13) | collective-permute-done | bytes 65568 | tf_op jit(solution)/shard_map/ppermute | solution.py:452
  43.4 0.7 %add.84 = bf16[4,4,2048]{2,1,0:T(4,128)(2,1)} custom-call(bf16[4,4,2048]{2,1,0:T(4,128)(2,1)S(1)} %copy-done, bf16[16,2048]{1,0:T(8,128)(2,1)S(1)} %project.1.refs_0_, bf16[16,2048]{1,0:T(8,128)(2,1)S(1)} %collective-permute-done.12.refs_1_, bf16[16,2048]{1,0:T(8,128)(2,1)S(1)} %collective-permute-done.13.refs_2_, ...), custom_call_target="tpu_custom_call" | custom-call | tf_op jit(solution)/shard_map/add/pallas_call | solution.py:381
  (13 shorter events, 0.1 us)
Async XLA Ops:
  2.1 9.5 %collective-permute-start = (bf16[568,128]{1,0:T(8,128)(2,1)S(1)}, bf16[568,128]{1,0:T(8,128)(2,1)S(1)}, u32[]{:S(2)}, u32[]{:S(2)}) collective-permute-start(bf16[568,128]{1,0:T(8,128)(2,1)S(1)} %get-tuple-element.15), channel_id=1, source_target_pairs={{0,24},{1,28},{2,26},{3,30},{4,25},{5,29},{6,27},{7,31},{8,16},{9,... | collective-permute-start | bytes 436232 | tf_op jit(solution)/shard_map/ppermute | solution.py:430
  7.2 8.6 %collective-permute-start.1 = (bf16[568,128]{1,0:T(8,128)(2,1)S(1)}, bf16[568,128]{1,0:T(8,128)(2,1)S(1)}, u32[]{:S(2)}, u32[]{:S(2)}) collective-permute-start(bf16[568,128]{1,0:T(8,128)(2,1)S(1)} %get-tuple-element.16), channel_id=1, source_target_pairs={{0,8},{1,12},{2,10},{3,14},{4,9},{5,13},{6,11},{7,15},{8,0},{9,4},... | collective-permute-start | bytes 436232 | tf_op jit(solution)/shard_map/ppermute | solution.py:430
  7.2 9.1 %collective-permute-start.2 = (bf16[568,128]{1,0:T(8,128)(2,1)S(1)}, bf16[568,128]{1,0:T(8,128)(2,1)S(1)}, u32[]{:S(2)}, u32[]{:S(2)}) collective-permute-start(bf16[568,128]{1,0:T(8,128)(2,1)S(1)} %get-tuple-element.17), channel_id=1, source_target_pairs={{0,0},{1,4},{2,2},{3,6},{4,1},{5,5},{6,3},{7,7},{8,8},{9,12},{10,1... | collective-permute-start | bytes 436232 | tf_op jit(solution)/shard_map/ppermute | solution.py:430
  7.9 12.3 %collective-permute-start.3 = (bf16[568,128]{1,0:T(8,128)(2,1)S(1)}, bf16[568,128]{1,0:T(8,128)(2,1)S(1)}, u32[]{:S(2)}, u32[]{:S(2)}) collective-permute-start(bf16[568,128]{1,0:T(8,128)(2,1)S(1)} %get-tuple-element.18), channel_id=1, source_target_pairs={{0,16},{1,20},{2,18},{3,22},{4,17},{5,21},{6,19},{7,23},{8,24},{9,... | collective-permute-start | bytes 436232 | tf_op jit(solution)/shard_map/ppermute | solution.py:430
  11.6 8.7 %collective-permute-start.4 = (bf16[568,128]{1,0:T(8,128)(2,1)S(1)}, bf16[568,128]{1,0:T(8,128)(2,1)S(1)}, u32[]{:S(2)}, u32[]{:S(2)}) collective-permute-start(bf16[568,128]{1,0:T(8,128)(2,1)S(1)} %collective-permute-done.refs_0_), channel_id=1, source_target_pairs={{0,1},{1,0},{2,3},{3,2},{4,5},{5,4},{6,7},{7,6},{8,9},{9,8},{10,11... | collective-permute-start | bytes 436232 | tf_op jit(solution)/shard_map/ppermute | solution.py:434
  15.8 4.5 %collective-permute-start.5 = (bf16[568,128]{1,0:T(8,128)(2,1)S(1)}, bf16[568,128]{1,0:T(8,128)(2,1)S(1)}, u32[]{:S(2)}, u32[]{:S(2)}) collective-permute-start(bf16[568,128]{1,0:T(8,128)(2,1)S(1)} %collective-permute-done.1.refs_1_), channel_id=1, source_target_pairs={{0,1},{1,0},{2,3},{3,2},{4,5},{5,4},{6,7},{7,6},{8,9},{9,8},{10,11... | collective-permute-start | bytes 436232 | tf_op jit(solution)/shard_map/ppermute | solution.py:434
  16.3 4.0 %collective-permute-start.6 = (bf16[568,128]{1,0:T(8,128)(2,1)S(1)}, bf16[568,128]{1,0:T(8,128)(2,1)S(1)}, u32[]{:S(2)}, u32[]{:S(2)}) collective-permute-start(bf16[568,128]{1,0:T(8,128)(2,1)S(1)} %collective-permute-done.2.refs_2_), channel_id=1, source_target_pairs={{0,1},{1,0},{2,3},{3,2},{4,5},{5,4},{6,7},{7,6},{8,9},{9,8},{10,11... | collective-permute-start | bytes 436232 | tf_op jit(solution)/shard_map/ppermute | solution.py:434
  20.2 1.4 %collective-permute-start.7 = (bf16[568,128]{1,0:T(8,128)(2,1)S(1)}, bf16[568,128]{1,0:T(8,128)(2,1)S(1)}, u32[]{:S(2)}, u32[]{:S(2)}) collective-permute-start(bf16[568,128]{1,0:T(8,128)(2,1)S(1)} %collective-permute-done.3.refs_3_), channel_id=1, source_target_pairs={{0,1},{1,0},{2,3},{3,2},{4,5},{5,4},{6,7},{7,6},{8,9},{9,8},{10,11... | collective-permute-start | bytes 436232 | tf_op jit(solution)/shard_map/ppermute | solution.py:434
  22.8 7.7 %collective-permute-start.8 = (bf16[528,128]{1,0:T(8,128)(2,1)S(1)}, bf16[528,128]{1,0:T(8,128)(2,1)S(1)}, u32[]{:S(2)}, u32[]{:S(2)}) collective-permute-start(bf16[528,128]{1,0:T(8,128)(2,1)S(1)} %get-tuple-element.19), channel_id=1, source_target_pairs={{0,24},{1,28},{2,26},{3,30},{4,25},{5,29},{6,27},{7,31},{8,16},{9,... | collective-permute-start | bytes 405512 | tf_op jit(solution)/shard_map/ppermute | solution.py:430
  25.6 11.6 %collective-permute-start.9 = (bf16[528,128]{1,0:T(8,128)(2,1)S(1)}, bf16[528,128]{1,0:T(8,128)(2,1)S(1)}, u32[]{:S(2)}, u32[]{:S(2)}) collective-permute-start(bf16[528,128]{1,0:T(8,128)(2,1)S(1)} %get-tuple-element.20), channel_id=1, source_target_pairs={{0,16},{1,20},{2,18},{3,22},{4,17},{5,21},{6,19},{7,23},{8,24},{9,... | collective-permute-start | bytes 405512 | tf_op jit(solution)/shard_map/ppermute | solution.py:430
  25.6 11.6 %collective-permute-start.10 = (bf16[528,128]{1,0:T(8,128)(2,1)S(1)}, bf16[528,128]{1,0:T(8,128)(2,1)S(1)}, u32[]{:S(2)}, u32[]{:S(2)}) collective-permute-start(bf16[528,128]{1,0:T(8,128)(2,1)S(1)} %get-tuple-element.21), channel_id=1, source_target_pairs={{0,8},{1,12},{2,10},{3,14},{4,9},{5,13},{6,11},{7,15},{8,0},{9,4},... | collective-permute-start | bytes 405512 | tf_op jit(solution)/shard_map/ppermute | solution.py:430
  27.2 10.0 %collective-permute-start.11 = (bf16[528,128]{1,0:T(8,128)(2,1)S(1)}, bf16[528,128]{1,0:T(8,128)(2,1)S(1)}, u32[]{:S(2)}, u32[]{:S(2)}) collective-permute-start(bf16[528,128]{1,0:T(8,128)(2,1)S(1)} %get-tuple-element.22), channel_id=1, source_target_pairs={{0,0},{1,4},{2,2},{3,6},{4,1},{5,5},{6,3},{7,7},{8,8},{9,12},{10,1... | collective-permute-start | bytes 405512 | tf_op jit(solution)/shard_map/ppermute | solution.py:430
  29.5 13.9 %copy-start = (bf16[4,4,2048]{2,1,0:T(4,128)(2,1)S(1)}, bf16[4,4,2048]{2,1,0:T(4,128)(2,1)}, u32[]{:S(2)}) copy-start(bf16[4,4,2048]{2,1,0:T(4,128)(2,1)} %resid.1) | copy-start | bytes 196612
  37.6 4.1 %collective-permute-start.14 = (bf16[16,2048]{1,0:T(8,128)(2,1)S(1)}, bf16[16,2048]{1,0:T(8,128)(2,1)S(1)}, u32[]{:S(2)}, u32[]{:S(2)}) collective-permute-start(bf16[16,2048]{1,0:T(8,128)(2,1)S(1)} %project.1.refs_0_), channel_id=1, source_target_pairs={{0,3},{1,2},{2,1},{3,0},{4,7},{5,6},{6,5},{7,4},{8,11},{9,10},{10,... | collective-permute-start | bytes 196616 | tf_op jit(solution)/shard_map/ppermute | solution.py:452
  38.9 4.5 %collective-permute-start.13 = (bf16[16,2048]{1,0:T(8,128)(2,1)S(1)}, bf16[16,2048]{1,0:T(8,128)(2,1)S(1)}, u32[]{:S(2)}, u32[]{:S(2)}) collective-permute-start(bf16[16,2048]{1,0:T(8,128)(2,1)S(1)} %project.1.refs_0_), channel_id=1, source_target_pairs={{0,2},{1,3},{2,0},{3,1},{4,6},{5,7},{6,4},{7,5},{8,10},{9,11},{10,... | collective-permute-start | bytes 196616 | tf_op jit(solution)/shard_map/ppermute | solution.py:452
  39.4 4.0 %collective-permute-start.12 = (bf16[16,2048]{1,0:T(8,128)(2,1)S(1)}, bf16[16,2048]{1,0:T(8,128)(2,1)S(1)}, u32[]{:S(2)}, u32[]{:S(2)}) collective-permute-start(bf16[16,2048]{1,0:T(8,128)(2,1)S(1)} %project.1.refs_0_), channel_id=1, source_target_pairs={{0,1},{1,0},{2,3},{3,2},{4,5},{5,4},{6,7},{7,6},{8,9},{9,8},{10,11... | collective-permute-start | bytes 196616 | tf_op jit(solution)/shard_map/ppermute | solution.py:452

commit v7 on v6

--- a/solution.py
+++ b/solution.py
@@ -78,40 +78,51 @@
     return (mixed, new_state)
 
 
-def pack_kernel(blocks, lens_far, *refs):
-    state_ref = refs[0]
-    small = refs[1:6]
-    outs = refs[6 : 6 + blocks]
-    joined, conv, tail, state_sems, small_sems, lens_ref = refs[6 + blocks : 12 + blocks]
-    held = refs[12 + blocks :]
+def pack_kernel(blocks, state_ref, *refs):
+    outs, sems = refs[:blocks], refs[blocks]
     reqs, head_size = state_ref.shape[0], state_ref.shape[-1]
-    req = lax.axis_index("req")
-    z = req // 2
-    rows = reqs * head_size
-    fetches = [
-        pltpu.make_async_copy(ref, to, small_sems.at[k])
-        for k, (ref, to) in enumerate(zip((*small, lens_far), (*held, lens_ref)))
-    ]
-    for fetch in fetches:
-        fetch.start()
+    z = lax.axis_index("req") // 2
     copies = []
     for s in range(blocks - 1, -1, -1):
         for r in range(reqs):
             copy = pltpu.make_async_copy(
                 state_ref.at[r, z ^ s],
                 outs[s].at[pl.ds(r * head_size, head_size), :],
-                state_sems.at[s * reqs + r],
+                sems.at[s * reqs + r],
             )
             copy.start()
             copies.append(copy)
-    tail[...] = jnp.zeros_like(tail)
-    for fetch in fetches:
-        fetch.wait()
-
-    proj_ref, cache_ref, weight_ref, bias_ref, gain_ref = held
-    steps = proj_ref.shape[2]
+    for copy in copies:
+        copy.wait()
+
+
+def pack(old_state):
+    reqs, blocks, head_size, _ = old_state.shape
+    return pl.pallas_call(
+        functools.partial(pack_kernel, blocks),
+        out_shape=[VMEM((reqs * head_size, head_size), BF16)] * blocks,
+        in_specs=[pl.BlockSpec(memory_space=pl.ANY)],
+        out_specs=[pl.BlockSpec(memory_space=VMEM)] * blocks,
+        scratch_shapes=[pltpu.SemaphoreType.DMA((blocks * reqs,))],
+        name="pack",
+    )(old_state)
+
+
+def prepare_kernel(blocks, lens_ref, *refs):
+    proj_ref, cache_ref, weight_ref, bias_ref = refs[:4]
+    turned, lefts, lasting, values, heard = refs[4:9]
+    joined, conv, flat, columns = refs[9:]
+    reqs, _, steps, _ = proj_ref.shape
+    head_size = turned.shape[0]
+    req = lax.axis_index("req")
+    z = req // 2
     taps = weight_ref.shape[1]
     past = taps - 1
+    row = lax.broadcasted_iota(jnp.int32, (reqs, head_size), 0)
+    live = jnp.zeros((reqs, head_size), F32)
+    for r in range(reqs):
+        live = jnp.where(row == r, (lens_ref[req * reqs + r] > 0).astype(F32), live)
+
     for p in range(3):
         weight = weight_ref[p].astype(F32)
         old = [cache_ref[j, p].astype(F32) for j in range(past)]
@@ -129,109 +140,131 @@
             at = own * steps
             conv[at : at + steps, :] = total / (1.0 + jnp.exp(-total))
 
-    count = 3 * reqs * steps
+    columns[...] = jnp.zeros_like(columns)
     for s in range(blocks):
         head = z ^ s
         lanes = pl.ds(pl.multiple_of(head * head_size, head_size), head_size)
-        tail[0:count, :] = conv[:, lanes]
-        for k, ref in enumerate((bias_ref, gain_ref)):
-            rest = ref[pl.ds(head, 1), :]
-            for piece in range(3):
-                value = rest.astype(BF16).astype(F32)
-                tail[count + 3 * k + piece : count + 3 * k + piece + 1, :] = value
-                rest = rest - value
-        outs[s][rows:, :] = tail[...].astype(BF16)
-    for copy in copies:
-        copy.wait()
-
-
-def pack(lengths, proj, conv_cache, conv_weight, forget_bias, norm_gain, old_state):
-    reqs, blocks, head_size, _ = old_state.shape
+        flat[...] = conv[:, lanes].astype(BF16).astype(F32)
+        parts = [
+            [flat[pl.ds(p * reqs * steps + t, reqs, stride=steps), :] for t in range(steps)]
+            for p in range(3)
+        ]
+        query, inputs = parts[0], parts[2]
+        bias = bias_ref[pl.ds(head, 1), :]
+        keep = [jax.nn.sigmoid(gate + bias) for gate in parts[1]]
+        base = s * steps * reqs
+        weights = []
+        decay = live
+        for t in range(steps):
+            weights = [w * keep[t] for w in weights] + [1.0 - keep[t]]
+            decay = decay * keep[t]
+            lefts[pl.ds(base + t * reqs, reqs), :] = query[t] * decay
+            values[pl.ds(base + t * reqs, reqs), :] = inputs[t]
+            out = jnp.zeros_like(query[t])
+            for earlier in range(t + 1):
+                score = jnp.sum(query[t] * weights[earlier], axis=-1, keepdims=True)
+                out = out + score * inputs[earlier]
+            heard[pl.ds(base + t, reqs, stride=steps), :] = out
+        for t in range(steps):
+            lasting[pl.ds(base + t * reqs, reqs), :] = weights[t]
+        columns[pl.ds(s * reqs, reqs), :] = decay
+    turned[...] = columns[...].T
+
+
+def prepare(lengths, proj, conv_cache, conv_weight, forget_bias, blocks, head_size):
+    reqs, steps, _, width = proj.shape
     taps = conv_weight.shape[0]
-    steps, width = proj.shape[1], proj.shape[-1]
-    extra = 3 * reqs * steps + 6
-    extra += -extra % 8
+    columns = -(-blocks * reqs // 128) * 128
     spec = pl.BlockSpec(memory_space=VMEM)
-    small = (
+    table = VMEM((blocks * steps * reqs, head_size), F32)
+    return pl.pallas_call(
+        functools.partial(prepare_kernel, blocks),
+        out_shape=[VMEM((head_size, columns), F32)] + [table] * 4,
+        in_specs=[pl.BlockSpec(memory_space=pltpu.SMEM)] + [spec] * 4,
+        out_specs=[spec] * 5,
+        scratch_shapes=[
+            VMEM((3 * reqs, taps + steps, width), F32),
+            VMEM((3 * reqs * steps, width), F32),
+            VMEM((3 * reqs * steps, head_size), F32),
+            VMEM((columns, head_size), F32),
+        ],
+        name="prepare",
+    )(
+        lengths,
         proj.transpose(0, 2, 1, 3),
         conv_cache.transpose(1, 2, 0, 3),
         conv_weight.transpose(1, 0, 2),
         forget_bias.reshape(blocks, head_size),
-        norm_gain.reshape(blocks, head_size),
     )
-    return pl.pallas_call(
-        functools.partial(pack_kernel, blocks),
-        out_shape=[VMEM((reqs * head_size + extra, head_size), BF16)] * blocks,
-        in_specs=[pl.BlockSpec(memory_space=pl.ANY)] * 7,
-        out_specs=[spec] * blocks,
-        scratch_shapes=[
-            VMEM((3 * reqs, taps + steps, width), F32),
-            VMEM((3 * reqs * steps, width), F32),
-            VMEM((extra, head_size), F32),
-            pltpu.SemaphoreType.DMA((blocks * reqs,)),
-            pltpu.SemaphoreType.DMA((len(small) + 1,)),
-            pltpu.SMEM(lengths.shape, jnp.int32),
-        ]
-        + [VMEM(value.shape, value.dtype) for value in small],
-        name="pack",
-    )(lengths, old_state, *small)
-
-
-def middle_kernel(blocks, reqs, steps, index_far, *refs):
+
+
+def route_kernel(blocks, index_far, *refs):
     own = in_order(refs[:blocks], order_out(blocks))
     sib = in_order(refs[blocks : 2 * blocks], order_out(blocks))
-    live_ref = refs[2 * blocks]
-    outs = refs[2 * blocks + 1 : 3 * blocks + 1]
-    pool, flat, gathered, columns, lefts, lasting, values, heard = refs[3 * blocks + 1 : -2]
-    index_ref, sem = refs[-2:]
+    outs = refs[2 * blocks : 3 * blocks]
+    pool, index_ref, sem = refs[3 * blocks :]
     fetch = pltpu.make_async_copy(index_far, index_ref, sem)
     fetch.start()
-    count = blocks * reqs
     head_size = pool.shape[-1]
-    rows = reqs * head_size
-
+    reqs = outs[0].shape[0] // head_size
     for s in range(blocks):
-        flat[...] = own[s][rows:, :].astype(F32)
-        for part in range(3):
-            for t in range(steps):
-                gathered[part * steps + t, pl.ds(s * reqs, reqs), :] = flat[
-                    pl.ds(part * reqs * steps + t, reqs, stride=steps), :
-                ]
         for r in range(reqs):
             here = slice(r * head_size, (r + 1) * head_size)
             pool[s * reqs + r] = own[s][here, :]
             pool[(blocks + s) * reqs + r] = sib[s][here, :]
-    base = 3 * steps * reqs
-    bias = flat[base : base + 1, :] + flat[base + 1 : base + 2, :] + flat[base + 2 : base + 3, :]
-    gain = flat[base + 3 : base + 4, :] + flat[base + 4 : base + 5, :] + flat[base + 5 : base + 6, :]
-    live = live_ref[...]
-    query = [gathered[t] for t in range(steps)]
-    keep = [jax.nn.sigmoid(gathered[steps + t] + bias) for t in range(steps)]
-    inputs = [gathered[2 * steps + t] for t in range(steps)]
-
-    weights = []
-    decay = live
-    for t in range(steps):
-        weights = [w * keep[t] for w in weights] + [1.0 - keep[t]]
-        decay = decay * keep[t]
-        lefts[pl.ds(t * count, count), :] = query[t] * decay
-        out = jnp.zeros_like(query[t])
-        for earlier in range(t + 1):
-            score = jnp.sum(query[t] * weights[earlier], axis=-1, keepdims=True)
-            out = out + score * inputs[earlier]
-        heard[pl.ds(t, count, stride=steps), :] = out
-
-    columns[...] = jnp.zeros_like(columns)
-    columns[pl.ds(0, count), :] = decay
-    turned = columns[...].T
+    fetch.wait()
     for s in range(blocks):
-        mine = slice(s * reqs, (s + 1) * reqs)
-        for t in range(steps):
-            here = pl.ds((s * steps + t) * reqs, reqs)
-            values[here, :] = inputs[t][mine, :]
-            lasting[here, :] = weights[t][mine, :]
-
-    fetch.wait()
+        for r in range(reqs):
+            outs[s][r * head_size : (r + 1) * head_size, :] = pool[index_ref[s * reqs + r]]
+
+
+def route(index, own, sib):
+    blocks = len(own)
+    rows, head_size = own[0].shape
+    spec = pl.BlockSpec(memory_space=VMEM)
+    return pl.pallas_call(
+        functools.partial(route_kernel, blocks),
+        out_shape=[VMEM((rows, head_size), BF16)] * blocks,
+        in_specs=[pl.BlockSpec(memory_space=pl.ANY)] + [spec] * (2 * blocks),
+        out_specs=[spec] * blocks,
+        scratch_shapes=[
+            VMEM((2 * blocks * rows // head_size, head_size, head_size), BF16),
+            pltpu.SMEM(index.shape, jnp.int32),
+            pltpu.SemaphoreType.DMA(()),
+        ],
+        name="route",
+        compiler_params=PARAMS,
+    )(index, *on_chip(*[own[s] for s in order_out(blocks)], *[sib[s] for s in order_out(blocks)]))
+
+
+def fetch_kernel(far_ref, out, sem):
+    copy = pltpu.make_async_copy(far_ref, out, sem)
+    copy.start()
+    copy.wait()
+
+
+def fetch(value):
+    return pl.pallas_call(
+        fetch_kernel,
+        out_shape=VMEM(value.shape, value.dtype),
+        in_specs=[pl.BlockSpec(memory_space=pl.ANY)],
+        out_specs=pl.BlockSpec(memory_space=VMEM),
+        scratch_shapes=[pltpu.SemaphoreType.DMA(())],
+        name="fetch",
+        compiler_params=PARAMS,
+    )(pltpu.with_memory_space_constraint(value, pltpu.HBM))
+
+
+def home_kernel(blocks, reqs, steps, *refs):
+    back = in_order(refs[:blocks], order_back(blocks))
+    turned_ref, lefts, lasting, values, heard_in, gain_ref, weight = refs[blocks : blocks + 7]
+    outs = refs[blocks + 7 : 2 * blocks + 7]
+    part = refs[2 * blocks + 7]
+    heard, normed = refs[2 * blocks + 8 :]
+    head_size = turned_ref.shape[0]
+    z = lax.axis_index("req") // 2
+    turned = turned_ref[...]
+    heard[...] = heard_in[...]
     of_req = lax.broadcasted_iota(jnp.int32, (steps * reqs, head_size), 0) % reqs
     for s in range(blocks):
         here = slice(s * steps * reqs, (s + 1) * steps * reqs)
@@ -249,90 +282,40 @@
         )
         for r in range(reqs):
             i = s * reqs + r
-            old = pool[index_ref[i]]
-            wanted = lefts[pl.ds(i, steps, stride=count), :].astype(BF16)
+            span = slice(r * head_size, (r + 1) * head_size)
+            old = back[s][span, :]
+            wanted = lefts[pl.ds(here.start + r, steps, stride=reqs), :].astype(BF16)
             said = jnp.dot(wanted, old, preferred_element_type=F32)
             heard[pl.ds(i * steps, steps), :] += said
-            span = slice(r * head_size, (r + 1) * head_size)
             current = turned[:, i : i + 1] * old.astype(F32) + added[:, span]
             outs[s][span, :] = current.astype(BF16)
-
-    head_out = heard[...]
-    scale = lax.rsqrt(jnp.mean(head_out * head_out, axis=-1, keepdims=True) + 1e-06)
-    normed = (head_out * scale * gain).astype(BF16)
-    for s in range(blocks):
-        outs[s][rows:, :] = normed[s * reqs * steps : (s + 1) * reqs * steps]
-
-
-def middle(index, own, sib, live, reqs, steps):
-    blocks = len(own)
-    count = blocks * reqs
-    head_size = own[0].shape[-1]
-    extra = own[0].shape[0] - reqs * head_size
-    columns = -(-count // 128) * 128
+        head_out = heard[here, :]
+        scale = lax.rsqrt(jnp.mean(head_out * head_out, axis=-1, keepdims=True) + 1e-06)
+        gain = gain_ref[pl.ds(z ^ s, 1), :]
+        lanes = pl.ds(pl.multiple_of((z ^ s) * head_size, head_size), head_size)
+        normed[:, lanes] = (head_out * scale * gain).astype(BF16)
+    part[...] = jnp.dot(normed[...], weight[...], preferred_element_type=F32).astype(BF16)
+
+
+def home(back, prepared, norm_gain, weight, reqs, steps):
+    blocks = len(back)
+    head_size = back[0].shape[-1]
     spec = pl.BlockSpec(memory_space=VMEM)
-    table = VMEM((steps * count, head_size), F32)
-    return pl.pallas_call(
-        functools.partial(middle_kernel, blocks, reqs, steps),
-        out_shape=[VMEM((reqs * (head_size + steps), head_size), BF16)] * blocks,
-        in_specs=[pl.BlockSpec(memory_space=pl.ANY)] + [spec] * (2 * blocks + 1),
-        out_specs=[spec] * blocks,
+    gain = norm_gain.reshape(blocks, head_size)
+    *states, part = pl.pallas_call(
+        functools.partial(home_kernel, blocks, reqs, steps),
+        out_shape=[VMEM(back[0].shape, BF16)] * blocks
+        + [VMEM((reqs * steps, weight.shape[1]), BF16)],
+        in_specs=[spec] * (blocks + 7),
+        out_specs=[spec] * (blocks + 1),
         scratch_shapes=[
-            VMEM((2 * count, head_size, head_size), BF16),
-            VMEM((extra, head_size), F32),
-            VMEM((3 * steps, count, head_size), F32),
-            VMEM((columns, head_size), F32),
-            table,
-            table,
-            table,
-            table,
-            pltpu.SMEM(index.shape, jnp.int32),
-            pltpu.SemaphoreType.DMA(()),
+            VMEM((blocks * reqs * steps, head_size), F32),
+            VMEM((reqs * steps, weight.shape[0]), BF16),
         ],
-        name="middle",
+        name="home",
         compiler_params=PARAMS,
-    )(index, *on_chip(*[own[s] for s in order_out(blocks)], *[sib[s] for s in order_out(blocks)], live))
-
-
-def fetch_kernel(far_ref, out, sem):
-    copy = pltpu.make_async_copy(far_ref, out, sem)
-    copy.start()
-    copy.wait()
-
-
-def fetch(value):
-    return pl.pallas_call(
-        fetch_kernel,
-        out_shape=VMEM(value.shape, value.dtype),
-        in_specs=[pl.BlockSpec(memory_space=pl.ANY)],
-        out_specs=pl.BlockSpec(memory_space=VMEM),
-        scratch_shapes=[pltpu.SemaphoreType.DMA(())],
-        name="fetch",
-        compiler_params=PARAMS,
-    )(pltpu.with_memory_space_constraint(value, pltpu.HBM))
-
-
-def project_kernel(blocks, *refs):
-    parts, weight, out, left = in_order(refs[:blocks], order_back(blocks)), refs[blocks], refs[blocks + 1], refs[blocks + 2]
-    rows, head_size = out.shape[0], parts[0].shape[-1]
-    z = lax.axis_index("req") // 2
-    for s in range(blocks):
-        lanes = pl.ds(pl.multiple_of((z ^ s) * head_size, head_size), head_size)
-        left[:, lanes] = parts[s][parts[s].shape[0] - rows :, :]
-    out[...] = jnp.dot(left[...], weight[...], preferred_element_type=F32).astype(BF16)
-
-
-def project(parts, weight, rows):
-    spec = pl.BlockSpec(memory_space=VMEM)
-    return pl.pallas_call(
-        functools.partial(project_kernel, len(parts)),
-        out_shape=VMEM((rows, weight.shape[1]), BF16),
-        in_specs=[spec] * (len(parts) + 1),
-        out_specs=spec,
-        scratch_shapes=[VMEM((rows, weight.shape[0]), BF16)],
-        name="project",
-        compiler_params=PARAMS,
-    )(*on_chip(*[parts[s] for s in order_back(len(parts))], weight))
+    )(*on_chip(*[back[s] for s in order_back(blocks)], *prepared, gain, weight))
+    return states, part
 
 
 def place_kernel(blocks, *refs):
@@ -429,8 +412,12 @@
         ]
         return lax.ppermute(value, both, pairs)
 
-    packs = pack(lengths, proj, conv_cache, conv_weight, forget_bias, norm_gain, old_state)
+    packs = pack(old_state)
     own = [swap(packs[s], s) for s in range(blocks)]
+    proj, conv_cache, conv_weight, forget_bias, norm_gain, *_ = lax.optimization_barrier(
+        (proj, conv_cache, conv_weight, forget_bias, norm_gain, *packs)
+    )
+    prepared = prepare(lengths, proj, conv_cache, conv_weight, forget_bias, blocks, head_size)
     sib = [lax.ppermute(own[s], "head", sibling) for s in range(blocks)]
 
     zs = z ^ jnp.arange(blocks, dtype=jnp.int32)
@@ -441,17 +428,15 @@
     device, pos = source // local_reqs, source % local_reqs
     away = (device % 2 != core).astype(jnp.int32)
     index = (away * blocks + ((device // 2) ^ z)) * local_reqs + pos
-    lens = jnp.sum(jnp.where(every == slots[:, None], lengths[None, :], 0), axis=1)
-    live = jnp.broadcast_to((lens > 0).astype(F32)[:, None], (slots.shape[0], head_size))
-
-    states = middle(index, own, sib, live, local_reqs, steps)
-    back = [swap(states[s], s) for s in range(blocks)]
-    weight, *_ = lax.optimization_barrier((out_weight, *states))
-    part = project(back, fetch(weight), local_reqs * steps)
+
+    routed = route(index, own, sib)
+    back = [swap(routed[s], s) for s in range(blocks)]
+    weight, *_ = lax.optimization_barrier((out_weight, *routed))
+    states, part = home(back, prepared, norm_gain, fetch(weight), local_reqs, steps)
     terms = [part] + [
         lax.ppermute(part, "head", [(i, i ^ k) for i in range(n_head)]) for k in range(1, n_head)
     ]
-    held = lax.optimization_barrier((*back, part))
+    held = lax.optimization_barrier((*states, part))
     new_state = place(held[:blocks], old_state.shape)
     return add(resid, terms), new_state
 

time: 44.3 us -> 42.8 us (0.966)
  waiting for transfers between devices: 20.3 us -> 17.4 us
  Pallas kernels: 6.22 us -> 7.13 us
    ppermute x8, waiting for transfers between devices: 16.1 us -> 13.1 us  [swap(): return lax.ppermute(value, both, pairs)]
    pallas_call x2 -> x3, Pallas kernels: 1.54 us -> 2.76 us  [the longest x1 1.25 us: prepare(): pl.pallas_call(functools.partial(prepare_kernel, blocks), out_shape=[VMEM...]
  transfers between devices with their start and end apart: 15 -> 15, of which waited for: 8 -> 7; matrix products, arithmetic and copies ran while one was open for 2% -> 2% of each run, Pallas kernels for 6% -> 9%
where the time goes in v7:
time: 42.8 us; the launch traced here: 42.4 us
  waiting for transfers between devices  17.4 us (41%)
  starting transfers between devices  16.1 us (38%)
  Pallas kernels  7.13 us (17%)
  other arithmetic  0.94 us (2%)
  between operations  0.75 us (2%)
    ppermute x8, waiting for transfers between devices, swap(): return lax.ppermute(value, both, pairs)  13.1 us
    ppermute x8, starting transfers between devices, swap(): return lax.ppermute(value, both, pairs)  11.6 us
    ppermute x3, waiting for transfers between devices, swapped_body(): lax.ppermute(part, 'head', [(i, i ^ k) for i in range(n_head)])  3.02 us
    ppermute x4, starting transfers between devices, swapped_body(): sib = [lax.ppermute(own[s], 'head', sibling) for s in range(blocks)]  2.62 us
    ppermute x3, starting transfers between devices, swapped_body(): lax.ppermute(part, 'head', [(i, i ^ k) for i in range(n_head)])  1.87 us
    pallas_call x1, Pallas kernels, fetch(): pl.pallas_call(fetch_kernel, out_shape=VMEM(value.shape, value.dtype), in...  1.61 us
    ppermute x4, waiting for transfers between devices, swapped_body(): sib = [lax.ppermute(own[s], 'head', sibling) for s in range(blocks)]  1.3 us
    pallas_call x1, Pallas kernels, prepare(): pl.pallas_call(functools.partial(prepare_kernel, blocks), out_shape=[VMEM...  1.25 us
  transfers between devices with their start and end apart: 15, of which 7 were waited for; matrix products, arithmetic and copies ran while one was open for 2% of the time, Pallas kernels for 9%

profile of v7, /device:TPU:0, one launch (start us, length us, event | category | flops | bytes accessed | tf_op | source)
XLA Modules:
  0.0 42.4 jit_solution(6169958962549557468)
XLA Ops:
  0.6 1.2 %pack.1 = (bf16[512,128]{1,0:T(8,128)(2,1)S(1)}, bf16[512,128]{1,0:T(8,128)(2,1)S(1)}, bf16[512,128]{1,0:T(8,128)(2,1)S(1)}, bf16[512,128]{1,0:T(8,128)(2,1)S(1)}) custom-call(bf16[4,4,128,128]{3,2,1,0:T(8,128)(2,1)} %state_ref.1), custom_call_target="tpu_custom_call" | custom-call | tf_op jit(solution)/shard_map/pack/pallas_call | solution.py:101
  1.8 5.1 %collective-permute-start = (bf16[512,128]{1,0:T(8,128)(2,1)S(1)}, bf16[512,128]{1,0:T(8,128)(2,1)S(1)}, u32[]{:S(2)}, u32[]{:S(2)}) collective-permute-start(bf16[512,128]{1,0:T(8,128)(2,1)S(1)} %get-tuple-element.34), channel_id=1, source_target_pairs={{0,24},{1,28},{2,26},{3,30},{4,25},{5,29},{6,27},{7,31},{8,16},{9,... | collective-permute-start | bytes 393224 | tf_op jit(solution)/shard_map/ppermute | solution.py:413
  6.9 0.7 %collective-permute-start.2 = (bf16[512,128]{1,0:T(8,128)(2,1)S(1)}, bf16[512,128]{1,0:T(8,128)(2,1)S(1)}, u32[]{:S(2)}, u32[]{:S(2)}) collective-permute-start(bf16[512,128]{1,0:T(8,128)(2,1)S(1)} %get-tuple-element.36), channel_id=1, source_target_pairs={{0,0},{1,4},{2,2},{3,6},{4,1},{5,5},{6,3},{7,7},{8,8},{9,12},{10,1... | collective-permute-start | bytes 393224 | tf_op jit(solution)/shard_map/ppermute | solution.py:413
  7.6 0.7 %collective-permute-start.3 = (bf16[512,128]{1,0:T(8,128)(2,1)S(1)}, bf16[512,128]{1,0:T(8,128)(2,1)S(1)}, u32[]{:S(2)}, u32[]{:S(2)}) collective-permute-start(bf16[512,128]{1,0:T(8,128)(2,1)S(1)} %get-tuple-element.37), channel_id=1, source_target_pairs={{0,16},{1,20},{2,18},{3,22},{4,17},{5,21},{6,19},{7,23},{8,24},{9,... | collective-permute-start | bytes 393224 | tf_op jit(solution)/shard_map/ppermute | solution.py:413
  8.3 0.1 iota_add_fusion
  8.4 0.1 add.60
  8.4 0.8 %select_reduce_fusion = s32[16]{0:T(128)S(1)} fusion(s32[32]{0:T(128)} %param.15, s32[16]{0:T(128)S(1)} %add.60), kind=kLoop, calls=%fused_computation | loop fusion | flops 1520 | bytes 256 | tf_op jit(solution)/shard_map/reduce_sum | solution.py:427
  9.3 1.6 %collective-permute-done.refs_0_ = bf16[512,128]{1,0:T(8,128)(2,1)S(1)} collective-permute-done((bf16[512,128]{1,0:T(8,128)(2,1)S(1)}, bf16[512,128]{1,0:T(8,128)(2,1)S(1)}, u32[]{:S(2)}, u32[]{:S(2)}) %collective-permute-start) | collective-permute-done | bytes 131104 | tf_op jit(solution)/shard_map/ppermute | solution.py:413
  10.9 1.9 %collective-permute-start.4 = (bf16[512,128]{1,0:T(8,128)(2,1)S(1)}, bf16[512,128]{1,0:T(8,128)(2,1)S(1)}, u32[]{:S(2)}, u32[]{:S(2)}) collective-permute-start(bf16[512,128]{1,0:T(8,128)(2,1)S(1)} %collective-permute-done.refs_0_), channel_id=1, source_target_pairs={{0,1},{1,0},{2,3},{3,2},{4,5},{5,4},{6,7},{7,6},{8,9},{9,8},{10,11... | collective-permute-start | bytes 393224 | tf_op jit(solution)/shard_map/ppermute | solution.py:421
  12.8 2.1 %collective-permute-done.1.refs_1_ = bf16[512,128]{1,0:T(8,128)(2,1)S(1)} collective-permute-done((bf16[512,128]{1,0:T(8,128)(2,1)S(1)}, bf16[512,128]{1,0:T(8,128)(2,1)S(1)}, u32[]{:S(2)}, u32[]{:S(2)}) %collective-permute-start.1) | collective-permute-done | bytes 131104 | tf_op jit(solution)/shard_map/ppermute | solution.py:413
  14.9 0.5 %collective-permute-start.5 = (bf16[512,128]{1,0:T(8,128)(2,1)S(1)}, bf16[512,128]{1,0:T(8,128)(2,1)S(1)}, u32[]{:S(2)}, u32[]{:S(2)}) collective-permute-start(bf16[512,128]{1,0:T(8,128)(2,1)S(1)} %collective-permute-done.1.refs_1_), channel_id=1, source_target_pairs={{0,1},{1,0},{2,3},{3,2},{4,5},{5,4},{6,7},{7,6},{8,9},{9,8},{10,11... | collective-permute-start | bytes 393224 | tf_op jit(solution)/shard_map/ppermute | solution.py:421
  15.3 0.0 collective-permute-done.2.refs_2_
  15.4 0.3 collective-permute-start.6
  15.6 2.7 %collective-permute-done.3.refs_3_ = bf16[512,128]{1,0:T(8,128)(2,1)S(1)} collective-permute-done((bf16[512,128]{1,0:T(8,128)(2,1)S(1)}, bf16[512,128]{1,0:T(8,128)(2,1)S(1)}, u32[]{:S(2)}, u32[]{:S(2)}) %collective-permute-start.3) | collective-permute-done | bytes 131104 | tf_op jit(solution)/shard_map/ppermute | solution.py:413
  18.4 1.3 %collective-permute-done.7.refs_7_ = bf16[512,128]{1,0:T(8,128)(2,1)S(1)} collective-permute-done((bf16[512,128]{1,0:T(8,128)(2,1)S(1)}, bf16[512,128]{1,0:T(8,128)(2,1)S(1)}, u32[]{:S(2)}, u32[]{:S(2)}) %collective-permute-start.7) | collective-permute-done | bytes 131104 | tf_op jit(solution)/shard_map/ppermute | solution.py:421
  19.7 0.6 %route.1 = (bf16[512,128]{1,0:T(8,128)(2,1)S(1)}, bf16[512,128]{1,0:T(8,128)(2,1)S(1)}, bf16[512,128]{1,0:T(8,128)(2,1)S(1)}, bf16[512,128]{1,0:T(8,128)(2,1)S(1)}) custom-call(s32[16]{0:T(128)S(1)} %fusion.index_far, bf16[512,128]{1,0:T(8,128)(2,1)S(1)} %collective-permute-done.refs_0_, bf16[512,128]{1,0:T(8,128)(2,1)S(1)} %collective-permute-done.1.refs_1_, ...), custom_call_target="tpu_custom_call" | custom-call | tf_op jit(solution)/shard_map/route/pallas_call | solution.py:225
  20.3 2.9 %collective-permute-start.8 = (bf16[512,128]{1,0:T(8,128)(2,1)S(1)}, bf16[512,128]{1,0:T(8,128)(2,1)S(1)}, u32[]{:S(2)}, u32[]{:S(2)}) collective-permute-start(bf16[512,128]{1,0:T(8,128)(2,1)S(1)} %get-tuple-element.38), channel_id=1, source_target_pairs={{0,24},{1,28},{2,26},{3,30},{4,25},{5,29},{6,27},{7,31},{8,16},{9,... | collective-permute-start | bytes 393224 | tf_op jit(solution)/shard_map/ppermute | solution.py:413
  23.2 1.6 %collective-permute-start.10 = (bf16[512,128]{1,0:T(8,128)(2,1)S(1)}, bf16[512,128]{1,0:T(8,128)(2,1)S(1)}, u32[]{:S(2)}, u32[]{:S(2)}) collective-permute-start(bf16[512,128]{1,0:T(8,128)(2,1)S(1)} %get-tuple-element.40), channel_id=1, source_target_pairs={{0,8},{1,12},{2,10},{3,14},{4,9},{5,13},{6,11},{7,15},{8,0},{9,4},... | collective-permute-start | bytes 393224 | tf_op jit(solution)/shard_map/ppermute | solution.py:413
  24.7 0.7 %collective-permute-start.11 = (bf16[512,128]{1,0:T(8,128)(2,1)S(1)}, bf16[512,128]{1,0:T(8,128)(2,1)S(1)}, u32[]{:S(2)}, u32[]{:S(2)}) collective-permute-start(bf16[512,128]{1,0:T(8,128)(2,1)S(1)} %get-tuple-element.41), channel_id=1, source_target_pairs={{0,0},{1,4},{2,2},{3,6},{4,1},{5,5},{6,3},{7,7},{8,8},{9,12},{10,1... | collective-permute-start | bytes 393224 | tf_op jit(solution)/shard_map/ppermute | solution.py:413
  25.4 1.3 %prepare.1 = (f32[128,128]{1,0:T(8,128)S(1)}, f32[64,128]{1,0:T(8,128)S(1)}, f32[64,128]{1,0:T(8,128)S(1)}, f32[64,128]{1,0:T(8,128)S(1)}, f32[64,128]{1,0:T(8,128)S(1)}) custom-call(s32[32]{0:T(128)} %lens_ref.1, bf16[4,3,4,512]{3,2,1,0:T(4,128)(2,1)} %bitcast.6, bf16[3,3,4,512]{3,2,1,0:T(4,128)(2,1)} %bitcast.7, bf16[3,4,512]{2,1,0:T(4,128)(2,1)} %bitcast.8, ...), custom_call_target="tpu_custom_call" | custom-call | tf_op jit(solution)/shard_map/prepare/pallas_call | solution.py:180
  26.7 0.0 copy-start.1
  26.7 1.6 %fetch.1.refs_10_ = bf16[512,2048]{1,0:T(8,128)(2,1)S(1)} custom-call(bf16[512,2048]{1,0:T(8,128)(2,1)} %far_ref), custom_call_target="tpu_custom_call" | custom-call | tf_op jit(solution)/shard_map/fetch/pallas_call | solution.py:247
  28.3 0.0 copy-start
  28.3 6.7 %collective-permute-done.9.refs_1_ = bf16[512,128]{1,0:T(8,128)(2,1)S(1)} collective-permute-done((bf16[512,128]{1,0:T(8,128)(2,1)S(1)}, bf16[512,128]{1,0:T(8,128)(2,1)S(1)}, u32[]{:S(2)}, u32[]{:S(2)}) %collective-permute-start.9) | collective-permute-done | bytes 131104 | tf_op jit(solution)/shard_map/ppermute | solution.py:413
  35.0 0.9 %home.1 = (bf16[512,128]{1,0:T(8,128)(2,1)S(1)}, bf16[512,128]{1,0:T(8,128)(2,1)S(1)}, bf16[512,128]{1,0:T(8,128)(2,1)S(1)}, bf16[512,128]{1,0:T(8,128)(2,1)S(1)}, bf16[16,2048]{1,0:T(8,128)(2,1)S(1)}) custom-call(bf16[512,128]{1,0:T(8,128)(2,1)S(1)} %collective-permute-done.8.refs_0_, bf16[512,128]{1,0:T(8,128)(2,1)S(1)} %collective-permute-done.9.refs_1_, ...), custom_call_target="tpu_custom_call" | custom-call | tf_op jit(solution)/shard_map/home/pallas_call | solution.py:305
  35.9 1.0 %collective-permute-start.14 = (bf16[16,2048]{1,0:T(8,128)(2,1)S(1)}, bf16[16,2048]{1,0:T(8,128)(2,1)S(1)}, u32[]{:S(2)}, u32[]{:S(2)}) collective-permute-start(bf16[16,2048]{1,0:T(8,128)(2,1)S(1)} %get-tuple-element.53.refs_0_), channel_id=1, source_target_pairs={{0,3},{1,2},{2,1},{3,0},{4,7},{5,6},{6,5},{7,4},{8,11},{9,10},{10,... | collective-permute-start | bytes 196616 | tf_op jit(solution)/shard_map/ppermute | solution.py:437
  37.0 0.5 %collective-permute-start.13 = (bf16[16,2048]{1,0:T(8,128)(2,1)S(1)}, bf16[16,2048]{1,0:T(8,128)(2,1)S(1)}, u32[]{:S(2)}, u32[]{:S(2)}) collective-permute-start(bf16[16,2048]{1,0:T(8,128)(2,1)S(1)} %get-tuple-element.53.refs_0_), channel_id=1, source_target_pairs={{0,2},{1,3},{2,0},{3,1},{4,6},{5,7},{6,4},{7,5},{8,10},{9,11},{10,... | collective-permute-start | bytes 196616 | tf_op jit(solution)/shard_map/ppermute | solution.py:437
  37.5 0.3 collective-permute-start.12
  37.8 0.9 %place.1 = bf16[4,4,128,128]{3,2,1,0:T(8,128)(2,1)} custom-call(bf16[512,128]{1,0:T(8,128)(2,1)S(1)} %get-tuple-element.58.refs_0_, bf16[512,128]{1,0:T(8,128)(2,1)S(1)} %get-tuple-element.59.refs_1_, bf16[512,128]{1,0:T(8,128)(2,1)S(1)} %get-tuple-element.60.refs_2_, bf16[512,128]{1,0:T(8,128)(2,1)S(1)} %get-tuple-element.61.refs_3_), custom_call_target="tpu_custom_call" | custom-call | tf_op jit(solution)/shard_map/place/pallas_call | solution.py:340
  38.7 1.5 %collective-permute-done.14.refs_3_ = bf16[16,2048]{1,0:T(8,128)(2,1)S(1)} collective-permute-done((bf16[16,2048]{1,0:T(8,128)(2,1)S(1)}, bf16[16,2048]{1,0:T(8,128)(2,1)S(1)}, u32[]{:S(2)}, u32[]{:S(2)}) %collective-permute-start.14) | collective-permute-done | bytes 65568 | tf_op jit(solution)/shard_map/ppermute | solution.py:437
  40.2 1.5 %collective-permute-done.13.refs_2_ = bf16[16,2048]{1,0:T(8,128)(2,1)S(1)} collective-permute-done((bf16[16,2048]{1,0:T(8,128)(2,1)S(1)}, bf16[16,2048]{1,0:T(8,128)(2,1)S(1)}, u32[]{:S(2)}, u32[]{:S(2)}) %collective-permute-start.13) | collective-permute-done | bytes 65568 | tf_op jit(solution)/shard_map/ppermute | solution.py:437
  41.7 0.7 %add.84 = bf16[4,4,2048]{2,1,0:T(4,128)(2,1)} custom-call(bf16[4,4,2048]{2,1,0:T(4,128)(2,1)S(1)} %copy-done, bf16[16,2048]{1,0:T(8,128)(2,1)S(1)} %get-tuple-element.53.refs_0_, bf16[16,2048]{1,0:T(8,128)(2,1)S(1)} %collective-permute-done.12.refs_1_, bf16[16,2048]{1,0:T(8,128)(2,1)S(1)} %collective-permute-done.13.refs_2_, ...), custom_call_target="tpu_custom_call" | custom-call | tf_op jit(solution)/shard_map/add/pallas_call | solution.py:364
  (14 shorter events, 0.1 us)
Async XLA Ops:
  1.8 9.1 %collective-permute-start = (bf16[512,128]{1,0:T(8,128)(2,1)S(1)}, bf16[512,128]{1,0:T(8,128)(2,1)S(1)}, u32[]{:S(2)}, u32[]{:S(2)}) collective-permute-start(bf16[512,128]{1,0:T(8,128)(2,1)S(1)} %get-tuple-element.34), channel_id=1, source_target_pairs={{0,24},{1,28},{2,26},{3,30},{4,25},{5,29},{6,27},{7,31},{8,16},{9,... | collective-permute-start | bytes 393224 | tf_op jit(solution)/shard_map/ppermute | solution.py:413
  6.9 8.0 %collective-permute-start.1 = (bf16[512,128]{1,0:T(8,128)(2,1)S(1)}, bf16[512,128]{1,0:T(8,128)(2,1)S(1)}, u32[]{:S(2)}, u32[]{:S(2)}) collective-permute-start(bf16[512,128]{1,0:T(8,128)(2,1)S(1)} %get-tuple-element.35), channel_id=1, source_target_pairs={{0,8},{1,12},{2,10},{3,14},{4,9},{5,13},{6,11},{7,15},{8,0},{9,4},... | collective-permute-start | bytes 393224 | tf_op jit(solution)/shard_map/ppermute | solution.py:413
  6.9 8.4 %collective-permute-start.2 = (bf16[512,128]{1,0:T(8,128)(2,1)S(1)}, bf16[512,128]{1,0:T(8,128)(2,1)S(1)}, u32[]{:S(2)}, u32[]{:S(2)}) collective-permute-start(bf16[512,128]{1,0:T(8,128)(2,1)S(1)} %get-tuple-element.36), channel_id=1, source_target_pairs={{0,0},{1,4},{2,2},{3,6},{4,1},{5,5},{6,3},{7,7},{8,8},{9,12},{10,1... | collective-permute-start | bytes 393224 | tf_op jit(solution)/shard_map/ppermute | solution.py:413
  7.6 10.8 %collective-permute-start.3 = (bf16[512,128]{1,0:T(8,128)(2,1)S(1)}, bf16[512,128]{1,0:T(8,128)(2,1)S(1)}, u32[]{:S(2)}, u32[]{:S(2)}) collective-permute-start(bf16[512,128]{1,0:T(8,128)(2,1)S(1)} %get-tuple-element.37), channel_id=1, source_target_pairs={{0,16},{1,20},{2,18},{3,22},{4,17},{5,21},{6,19},{7,23},{8,24},{9,... | collective-permute-start | bytes 393224 | tf_op jit(solution)/shard_map/ppermute | solution.py:413
  10.9 7.5 %collective-permute-start.4 = (bf16[512,128]{1,0:T(8,128)(2,1)S(1)}, bf16[512,128]{1,0:T(8,128)(2,1)S(1)}, u32[]{:S(2)}, u32[]{:S(2)}) collective-permute-start(bf16[512,128]{1,0:T(8,128)(2,1)S(1)} %collective-permute-done.refs_0_), channel_id=1, source_target_pairs={{0,1},{1,0},{2,3},{3,2},{4,5},{5,4},{6,7},{7,6},{8,9},{9,8},{10,11... | collective-permute-start | bytes 393224 | tf_op jit(solution)/shard_map/ppermute | solution.py:421
  14.9 3.5 %collective-permute-start.5 = (bf16[512,128]{1,0:T(8,128)(2,1)S(1)}, bf16[512,128]{1,0:T(8,128)(2,1)S(1)}, u32[]{:S(2)}, u32[]{:S(2)}) collective-permute-start(bf16[512,128]{1,0:T(8,128)(2,1)S(1)} %collective-permute-done.1.refs_1_), channel_id=1, source_target_pairs={{0,1},{1,0},{2,3},{3,2},{4,5},{5,4},{6,7},{7,6},{8,9},{9,8},{10,11... | collective-permute-start | bytes 393224 | tf_op jit(solution)/shard_map/ppermute | solution.py:421
  15.4 3.0 %collective-permute-start.6 = (bf16[512,128]{1,0:T(8,128)(2,1)S(1)}, bf16[512,128]{1,0:T(8,128)(2,1)S(1)}, u32[]{:S(2)}, u32[]{:S(2)}) collective-permute-start(bf16[512,128]{1,0:T(8,128)(2,1)S(1)} %collective-permute-done.2.refs_2_), channel_id=1, source_target_pairs={{0,1},{1,0},{2,3},{3,2},{4,5},{5,4},{6,7},{7,6},{8,9},{9,8},{10,11... | collective-permute-start | bytes 393224 | tf_op jit(solution)/shard_map/ppermute | solution.py:421
  18.3 1.3 %collective-permute-start.7 = (bf16[512,128]{1,0:T(8,128)(2,1)S(1)}, bf16[512,128]{1,0:T(8,128)(2,1)S(1)}, u32[]{:S(2)}, u32[]{:S(2)}) collective-permute-start(bf16[512,128]{1,0:T(8,128)(2,1)S(1)} %collective-permute-done.3.refs_3_), channel_id=1, source_target_pairs={{0,1},{1,0},{2,3},{3,2},{4,5},{5,4},{6,7},{7,6},{8,9},{9,8},{10,11... | collective-permute-start | bytes 393224 | tf_op jit(solution)/shard_map/ppermute | solution.py:421
  20.3 8.0 %collective-permute-start.8 = (bf16[512,128]{1,0:T(8,128)(2,1)S(1)}, bf16[512,128]{1,0:T(8,128)(2,1)S(1)}, u32[]{:S(2)}, u32[]{:S(2)}) collective-permute-start(bf16[512,128]{1,0:T(8,128)(2,1)S(1)} %get-tuple-element.38), channel_id=1, source_target_pairs={{0,24},{1,28},{2,26},{3,30},{4,25},{5,29},{6,27},{7,31},{8,16},{9,... | collective-permute-start | bytes 393224 | tf_op jit(solution)/shard_map/ppermute | solution.py:413
  23.2 11.8 %collective-permute-start.9 = (bf16[512,128]{1,0:T(8,128)(2,1)S(1)}, bf16[512,128]{1,0:T(8,128)(2,1)S(1)}, u32[]{:S(2)}, u32[]{:S(2)}) collective-permute-start(bf16[512,128]{1,0:T(8,128)(2,1)S(1)} %get-tuple-element.39), channel_id=1, source_target_pairs={{0,16},{1,20},{2,18},{3,22},{4,17},{5,21},{6,19},{7,23},{8,24},{9,... | collective-permute-start | bytes 393224 | tf_op jit(solution)/shard_map/ppermute | solution.py:413
  23.2 11.8 %collective-permute-start.10 = (bf16[512,128]{1,0:T(8,128)(2,1)S(1)}, bf16[512,128]{1,0:T(8,128)(2,1)S(1)}, u32[]{:S(2)}, u32[]{:S(2)}) collective-permute-start(bf16[512,128]{1,0:T(8,128)(2,1)S(1)} %get-tuple-element.40), channel_id=1, source_target_pairs={{0,8},{1,12},{2,10},{3,14},{4,9},{5,13},{6,11},{7,15},{8,0},{9,4},... | collective-permute-start | bytes 393224 | tf_op jit(solution)/shard_map/ppermute | solution.py:413
  24.7 10.3 %collective-permute-start.11 = (bf16[512,128]{1,0:T(8,128)(2,1)S(1)}, bf16[512,128]{1,0:T(8,128)(2,1)S(1)}, u32[]{:S(2)}, u32[]{:S(2)}) collective-permute-start(bf16[512,128]{1,0:T(8,128)(2,1)S(1)} %get-tuple-element.41), channel_id=1, source_target_pairs={{0,0},{1,4},{2,2},{3,6},{4,1},{5,5},{6,3},{7,7},{8,8},{9,12},{10,1... | collective-permute-start | bytes 393224 | tf_op jit(solution)/shard_map/ppermute | solution.py:413
  26.7 8.3 %copy-start.1 = (f32[512]{0:T(512)S(1)}, f32[512]{0:T(512)}, u32[]{:S(2)}) copy-start(f32[512]{0:T(512)} %param.18) | copy-start | bytes 6148
  28.3 13.5 %copy-start = (bf16[4,4,2048]{2,1,0:T(4,128)(2,1)S(1)}, bf16[4,4,2048]{2,1,0:T(4,128)(2,1)}, u32[]{:S(2)}) copy-start(bf16[4,4,2048]{2,1,0:T(4,128)(2,1)} %resid.1) | copy-start | bytes 196612
  35.9 4.3 %collective-permute-start.14 = (bf16[16,2048]{1,0:T(8,128)(2,1)S(1)}, bf16[16,2048]{1,0:T(8,128)(2,1)S(1)}, u32[]{:S(2)}, u32[]{:S(2)}) collective-permute-start(bf16[16,2048]{1,0:T(8,128)(2,1)S(1)} %get-tuple-element.53.refs_0_), channel_id=1, source_target_pairs={{0,3},{1,2},{2,1},{3,0},{4,7},{5,6},{6,5},{7,4},{8,11},{9,10},{10,... | collective-permute-start | bytes 196616 | tf_op jit(solution)/shard_map/ppermute | solution.py:437
  37.0 4.8 %collective-permute-start.13 = (bf16[16,2048]{1,0:T(8,128)(2,1)S(1)}, bf16[16,2048]{1,0:T(8,128)(2,1)S(1)}, u32[]{:S(2)}, u32[]{:S(2)}) collective-permute-start(bf16[16,2048]{1,0:T(8,128)(2,1)S(1)} %get-tuple-element.53.refs_0_), channel_id=1, source_target_pairs={{0,2},{1,3},{2,0},{3,1},{4,6},{5,7},{6,4},{7,5},{8,10},{9,11},{10,... | collective-permute-start | bytes 196616 | tf_op jit(solution)/shard_map/ppermute | solution.py:437
  37.5 4.2 %collective-permute-start.12 = (bf16[16,2048]{1,0:T(8,128)(2,1)S(1)}, bf16[16,2048]{1,0:T(8,128)(2,1)S(1)}, u32[]{:S(2)}, u32[]{:S(2)}) collective-permute-start(bf16[16,2048]{1,0:T(8,128)(2,1)S(1)} %get-tuple-element.53.refs_0_), channel_id=1, source_target_pairs={{0,1},{1,0},{2,3},{3,2},{4,5},{5,4},{6,7},{7,6},{8,9},{9,8},{10,11... | collective-permute-start | bytes 196616 | tf_op jit(solution)/shard_map/ppermute | solution.py:437

commit v8 on v7

--- a/solution.py
+++ b/solution.py
@@ -257,15 +257,57 @@
 
 def home_kernel(blocks, reqs, steps, *refs):
     back = in_order(refs[:blocks], order_back(blocks))
-    turned_ref, lefts, lasting, values, heard_in, gain_ref, weight = refs[blocks : blocks + 7]
-    outs = refs[blocks + 7 : 2 * blocks + 7]
-    part = refs[2 * blocks + 7]
-    heard, normed = refs[2 * blocks + 8 :]
+    kept, lefts, heard_in, gain_ref, weight, part, heard, normed = refs[blocks:]
+    stayed = lax.axis_index("req") % 2 == lax.axis_index("head") % 2
+    head_size = gain_ref.shape[-1]
+    z = lax.axis_index("req") // 2
+    heard[...] = heard_in[...]
+    for s in range(blocks):
+        here = slice(s * steps * reqs, (s + 1) * steps * reqs)
+        for r in range(reqs):
+            span = slice(r * head_size, (r + 1) * head_size)
+            old = back[s][span, :]
+            if s == 0:
+                old = jnp.where(stayed, kept[span, :], old)
+            wanted = lefts[pl.ds(here.start + r, steps, stride=reqs), :].astype(BF16)
+            said = jnp.dot(wanted, old, preferred_element_type=F32)
+            heard[pl.ds((s * reqs + r) * steps, steps), :] += said
+        head_out = heard[here, :]
+        scale = lax.rsqrt(jnp.mean(head_out * head_out, axis=-1, keepdims=True) + 1e-06)
+        gain = gain_ref[pl.ds(z ^ s, 1), :]
+        lanes = pl.ds(pl.multiple_of((z ^ s) * head_size, head_size), head_size)
+        normed[:, lanes] = (head_out * scale * gain).astype(BF16)
+    part[...] = jnp.dot(normed[...], weight[...], preferred_element_type=F32).astype(BF16)
+
+
+def home(back, kept, lefts, heard, norm_gain, weight, reqs, steps):
+    blocks = len(back)
+    head_size = back[0].shape[-1]
+    spec = pl.BlockSpec(memory_space=VMEM)
+    gain = norm_gain.reshape(blocks, head_size)
+    return pl.pallas_call(
+        functools.partial(home_kernel, blocks, reqs, steps),
+        out_shape=VMEM((reqs * steps, weight.shape[1]), BF16),
+        in_specs=[spec] * (blocks + 5),
+        out_specs=spec,
+        scratch_shapes=[
+            VMEM((blocks * reqs * steps, head_size), F32),
+            VMEM((reqs * steps, weight.shape[0]), BF16),
+        ],
+        name="home",
+        compiler_params=PARAMS,
+    )(*on_chip(*[back[s] for s in order_back(blocks)], kept, lefts, heard, gain, weight))
+
+
+def place_kernel(blocks, reqs, steps, *refs):
+    back = in_order(refs[:blocks], order_back(blocks))
+    kept, turned_ref, lasting, values, out, fresh, sems = refs[blocks:]
+    stayed = lax.axis_index("req") % 2 == lax.axis_index("head") % 2
     head_size = turned_ref.shape[0]
     z = lax.axis_index("req") // 2
     turned = turned_ref[...]
-    heard[...] = heard_in[...]
     of_req = lax.broadcasted_iota(jnp.int32, (steps * reqs, head_size), 0) % reqs
+    copies = []
     for s in range(blocks):
         here = slice(s * steps * reqs, (s + 1) * steps * reqs)
         left = lasting[here, :]
@@ -284,68 +326,31 @@
             i = s * reqs + r
             span = slice(r * head_size, (r + 1) * head_size)
             old = back[s][span, :]
-            wanted = lefts[pl.ds(here.start + r, steps, stride=reqs), :].astype(BF16)
-            said = jnp.dot(wanted, old, preferred_element_type=F32)
-            heard[pl.ds(i * steps, steps), :] += said
+            if s == 0:
+                old = jnp.where(stayed, kept[span, :], old)
             current = turned[:, i : i + 1] * old.astype(F32) + added[:, span]
-            outs[s][span, :] = current.astype(BF16)
-        head_out = heard[here, :]
-        scale = lax.rsqrt(jnp.mean(head_out * head_out, axis=-1, keepdims=True) + 1e-06)
-        gain = gain_ref[pl.ds(z ^ s, 1), :]
-        lanes = pl.ds(pl.multiple_of((z ^ s) * head_size, head_size), head_size)
-        normed[:, lanes] = (head_out * scale * gain).astype(BF16)
-    part[...] = jnp.dot(normed[...], weight[...], preferred_element_type=F32).astype(BF16)
-
-
-def home(back, prepared, norm_gain, weight, reqs, steps):
-    blocks = len(back)
-    head_size = back[0].shape[-1]
-    spec = pl.BlockSpec(memory_space=VMEM)
-    gain = norm_gain.reshape(blocks, head_size)
-    *states, part = pl.pallas_call(
-        functools.partial(home_kernel, blocks, reqs, steps),
-        out_shape=[VMEM(back[0].shape, BF16)] * blocks
-        + [VMEM((reqs * steps, weight.shape[1]), BF16)],
-        in_specs=[spec] * (blocks + 7),
-        out_specs=[spec] * (blocks + 1),
-        scratch_shapes=[
-            VMEM((blocks * reqs * steps, head_size), F32),
-            VMEM((reqs * steps, weight.shape[0]), BF16),
-        ],
-        name="home",
-        compiler_params=PARAMS,
-    )(*on_chip(*[back[s] for s in order_back(blocks)], *prepared, gain, weight))
-    return states, part
-
-
-def place_kernel(blocks, *refs):
-    parts, out, sems = in_order(refs[:blocks], order_back(blocks)), refs[blocks], refs[blocks + 1]
-    reqs, _, head_size, _ = out.shape
-    z = lax.axis_index("req") // 2
-    copies = []
-    for s in range(blocks):
-        for r in range(reqs):
-            copy = pltpu.make_async_copy(
-                parts[s].at[pl.ds(r * head_size, head_size), :],
-                out.at[r, z ^ s],
-                sems.at[s * reqs + r],
-            )
+            fresh[i] = current.astype(BF16)
+            copy = pltpu.make_async_copy(fresh.at[i], out.at[r, z ^ s], sems.at[i])
             copy.start()
             copies.append(copy)
     for copy in copies:
         copy.wait()
 
 
-def place(back, shape):
-    return pl.pallas_call(
-        functools.partial(place_kernel, len(back)),
+def place(back, kept, turned, lasting, values, shape, steps):
+    reqs, blocks, head_size, _ = shape
+    return pl.pallas_call(
+        functools.partial(place_kernel, blocks, reqs, steps),
         out_shape=jax.ShapeDtypeStruct(shape, BF16),
-        in_specs=[pl.BlockSpec(memory_space=VMEM)] * len(back),
+        in_specs=[pl.BlockSpec(memory_space=VMEM)] * (blocks + 4),
         out_specs=pl.BlockSpec(memory_space=pl.ANY),
-        scratch_shapes=[pltpu.SemaphoreType.DMA((len(back) * shape[0],))],
+        scratch_shapes=[
+            VMEM((blocks * reqs, head_size, head_size), BF16),
+            pltpu.SemaphoreType.DMA((blocks * reqs,)),
+        ],
         name="place",
         compiler_params=PARAMS,
-    )(*on_chip(*[back[s] for s in order_back(len(back))]))
+    )(*on_chip(*[back[s] for s in order_back(blocks)], kept, turned, lasting, values))
 
 
 def add_kernel(resid, *refs):
@@ -402,14 +407,15 @@
     both = ("req", "head")
     sibling = [(i, i ^ 1) for i in range(n_head)]
 
-    def swap(value, s):
-        pairs = [
-            ((a * 2 + b) * n_head + y * 2 + c, ((a ^ s) * 2 + c) * n_head + y * 2 + b)
-            for a in range(blocks)
-            for b in range(2)
-            for y in range(n_head // 2)
-            for c in range(2)
-        ]
+    def swap(value, s, cross=False):
+        pairs = []
+        for a in range(blocks):
+            for b in range(2):
+                for y in range(n_head // 2):
+                    for c in range(2):
+                        to = (b ^ 1, c ^ 1) if cross else (c, b)
+                        here = (a * 2 + b) * n_head + y * 2 + c
+                        pairs.append((here, ((a ^ s) * 2 + to[0]) * n_head + y * 2 + to[1]))
         return lax.ppermute(value, both, pairs)
 
     packs = pack(old_state)
@@ -430,14 +436,16 @@
     index = (away * blocks + ((device // 2) ^ z)) * local_reqs + pos
 
     routed = route(index, own, sib)
-    back = [swap(routed[s], s) for s in range(blocks)]
+    back = [swap(routed[s], s, cross=s == 0) for s in range(blocks)]
     weight, *_ = lax.optimization_barrier((out_weight, *routed))
-    states, part = home(back, prepared, norm_gain, fetch(weight), local_reqs, steps)
+    turned, lefts, lasting, values, heard = prepared
+    weight = fetch(weight)
+    part = home(back, routed[0], lefts, heard, norm_gain, weight, local_reqs, steps)
     terms = [part] + [
         lax.ppermute(part, "head", [(i, i ^ k) for i in range(n_head)]) for k in range(1, n_head)
     ]
-    held = lax.optimization_barrier((*states, part))
-    new_state = place(held[:blocks], old_state.shape)
+    *back, part = lax.optimization_barrier((*back, part))
+    new_state = place(back, routed[0], turned, lasting, values, old_state.shape, steps)
     return add(resid, terms), new_state
 
 
@@ -457,10 +465,9 @@
     out_specs = (P("req", None, None), P("req", "head", None, None))
 
     def body(*args):
-        heads = args[7].shape[1]
-        swapped = (
-            mesh.shape["req"] == 2 * heads and heads & (heads - 1) == 0 and mesh.shape["head"] == 4
-        )
+        heads, parts = args[7].shape[1], mesh.shape["head"]
+        swapped = mesh.shape["req"] == 2 * heads and heads & (heads - 1) == 0
+        swapped = swapped and parts > 1 and parts & (parts - 1) == 0
         return (swapped_body if swapped else generic_body)(*args)
 
     return jax.shard_map(body, mesh=mesh, in_specs=in_specs, out_specs=out_specs, check_vma=False)

time: 42.8 us -> 42.6 us (level)
  waiting for transfers between devices: 17.4 us -> 16.7 us
  starting transfers between devices: 16.1 us -> 16.6 us
    ppermute x8, starting transfers between devices: 11.6 us -> 12.1 us  [swap(): return lax.ppermute(value, both, pairs)]
    ppermute x8, waiting for transfers between devices: 13.1 us -> 12.7 us  [swap(): return lax.ppermute(value, both, pairs)]
  transfers between devices with their start and end apart: 15 -> 15, of which waited for: 7 -> 7; matrix products, arithmetic and copies ran while one was open for 2% -> 2% of each run, Pallas kernels for 9% -> 10%
where the time goes in v8:
time: 42.6 us; the launch traced here: 42.2 us
  waiting for transfers between devices  16.7 us (39%)
  starting transfers between devices  16.6 us (39%)
  Pallas kernels  7.21 us (17%)
  other arithmetic  0.94 us (2%)
  between operations  0.74 us (2%)
    ppermute x8, waiting for transfers between devices, swap(): return lax.ppermute(value, both, pairs)  12.7 us
    ppermute x8, starting transfers between devices, swap(): return lax.ppermute(value, both, pairs)  12.1 us
    ppermute x3, waiting for transfers between devices, swapped_body(): lax.ppermute(part, 'head', [(i, i ^ k) for i in range(n_head)])  2.73 us
    ppermute x4, starting transfers between devices, swapped_body(): sib = [lax.ppermute(own[s], 'head', sibling) for s in range(blocks)]  2.62 us
    ppermute x3, starting transfers between devices, swapped_body(): lax.ppermute(part, 'head', [(i, i ^ k) for i in range(n_head)])  1.87 us
    pallas_call x1, Pallas kernels, fetch(): pl.pallas_call(fetch_kernel, out_shape=VMEM(value.shape, value.dtype), in...  1.61 us
    ppermute x4, waiting for transfers between devices, swapped_body(): sib = [lax.ppermute(own[s], 'head', sibling) for s in range(blocks)]  1.3 us
    pallas_call x1, Pallas kernels, prepare(): pl.pallas_call(functools.partial(prepare_kernel, blocks), out_shape=[VMEM...  1.25 us
  transfers between devices with their start and end apart: 15, of which 7 were waited for; matrix products, arithmetic and copies ran while one was open for 2% of the time, Pallas kernels for 10%

profile of v8, /device:TPU:0, one launch (start us, length us, event | category | flops | bytes accessed | tf_op | source)
XLA Modules:
  0.0 42.2 jit_solution(16455223497897098626)
XLA Ops:
  0.6 1.2 %pack.1 = (bf16[512,128]{1,0:T(8,128)(2,1)S(1)}, bf16[512,128]{1,0:T(8,128)(2,1)S(1)}, bf16[512,128]{1,0:T(8,128)(2,1)S(1)}, bf16[512,128]{1,0:T(8,128)(2,1)S(1)}) custom-call(bf16[4,4,128,128]{3,2,1,0:T(8,128)(2,1)} %state_ref.1), custom_call_target="tpu_custom_call" | custom-call | tf_op jit(solution)/shard_map/pack/pallas_call | solution.py:101
  1.8 5.1 %collective-permute-start = (bf16[512,128]{1,0:T(8,128)(2,1)S(1)}, bf16[512,128]{1,0:T(8,128)(2,1)S(1)}, u32[]{:S(2)}, u32[]{:S(2)}) collective-permute-start(bf16[512,128]{1,0:T(8,128)(2,1)S(1)} %get-tuple-element.25), channel_id=1, source_target_pairs={{0,24},{1,28},{2,26},{3,30},{4,25},{5,29},{6,27},{7,31},{8,16},{9,... | collective-permute-start | bytes 393224 | tf_op jit(solution)/shard_map/ppermute | solution.py:419
  6.9 0.7 %collective-permute-start.2 = (bf16[512,128]{1,0:T(8,128)(2,1)S(1)}, bf16[512,128]{1,0:T(8,128)(2,1)S(1)}, u32[]{:S(2)}, u32[]{:S(2)}) collective-permute-start(bf16[512,128]{1,0:T(8,128)(2,1)S(1)} %get-tuple-element.27), channel_id=1, source_target_pairs={{0,0},{1,4},{2,2},{3,6},{4,1},{5,5},{6,3},{7,7},{8,8},{9,12},{10,1... | collective-permute-start | bytes 393224 | tf_op jit(solution)/shard_map/ppermute | solution.py:419
  7.6 0.7 %collective-permute-start.3 = (bf16[512,128]{1,0:T(8,128)(2,1)S(1)}, bf16[512,128]{1,0:T(8,128)(2,1)S(1)}, u32[]{:S(2)}, u32[]{:S(2)}) collective-permute-start(bf16[512,128]{1,0:T(8,128)(2,1)S(1)} %get-tuple-element.28), channel_id=1, source_target_pairs={{0,16},{1,20},{2,18},{3,22},{4,17},{5,21},{6,19},{7,23},{8,24},{9,... | collective-permute-start | bytes 393224 | tf_op jit(solution)/shard_map/ppermute | solution.py:419
  8.3 0.1 iota_add_fusion
  8.4 0.1 add.60
  8.4 0.8 %select_reduce_fusion = s32[16]{0:T(128)S(1)} fusion(s32[32]{0:T(128)} %param.15, s32[16]{0:T(128)S(1)} %add.60), kind=kLoop, calls=%fused_computation | loop fusion | flops 1520 | bytes 256 | tf_op jit(solution)/shard_map/reduce_sum | solution.py:433
  9.3 1.6 %collective-permute-done.refs_0_ = bf16[512,128]{1,0:T(8,128)(2,1)S(1)} collective-permute-done((bf16[512,128]{1,0:T(8,128)(2,1)S(1)}, bf16[512,128]{1,0:T(8,128)(2,1)S(1)}, u32[]{:S(2)}, u32[]{:S(2)}) %collective-permute-start) | collective-permute-done | bytes 131104 | tf_op jit(solution)/shard_map/ppermute | solution.py:419
  10.9 1.9 %collective-permute-start.4 = (bf16[512,128]{1,0:T(8,128)(2,1)S(1)}, bf16[512,128]{1,0:T(8,128)(2,1)S(1)}, u32[]{:S(2)}, u32[]{:S(2)}) collective-permute-start(bf16[512,128]{1,0:T(8,128)(2,1)S(1)} %collective-permute-done.refs_0_), channel_id=1, source_target_pairs={{0,1},{1,0},{2,3},{3,2},{4,5},{5,4},{6,7},{7,6},{8,9},{9,8},{10,11... | collective-permute-start | bytes 393224 | tf_op jit(solution)/shard_map/ppermute | solution.py:427
  12.8 2.1 %collective-permute-done.1.refs_1_ = bf16[512,128]{1,0:T(8,128)(2,1)S(1)} collective-permute-done((bf16[512,128]{1,0:T(8,128)(2,1)S(1)}, bf16[512,128]{1,0:T(8,128)(2,1)S(1)}, u32[]{:S(2)}, u32[]{:S(2)}) %collective-permute-start.1) | collective-permute-done | bytes 131104 | tf_op jit(solution)/shard_map/ppermute | solution.py:419
  14.9 0.5 %collective-permute-start.5 = (bf16[512,128]{1,0:T(8,128)(2,1)S(1)}, bf16[512,128]{1,0:T(8,128)(2,1)S(1)}, u32[]{:S(2)}, u32[]{:S(2)}) collective-permute-start(bf16[512,128]{1,0:T(8,128)(2,1)S(1)} %collective-permute-done.1.refs_1_), channel_id=1, source_target_pairs={{0,1},{1,0},{2,3},{3,2},{4,5},{5,4},{6,7},{7,6},{8,9},{9,8},{10,11... | collective-permute-start | bytes 393224 | tf_op jit(solution)/shard_map/ppermute | solution.py:427
  15.3 0.0 collective-permute-done.2.refs_2_
  15.4 0.3 collective-permute-start.6
  15.6 2.7 %collective-permute-done.3.refs_3_ = bf16[512,128]{1,0:T(8,128)(2,1)S(1)} collective-permute-done((bf16[512,128]{1,0:T(8,128)(2,1)S(1)}, bf16[512,128]{1,0:T(8,128)(2,1)S(1)}, u32[]{:S(2)}, u32[]{:S(2)}) %collective-permute-start.3) | collective-permute-done | bytes 131104 | tf_op jit(solution)/shard_map/ppermute | solution.py:419
  18.4 1.3 %collective-permute-done.7.refs_7_ = bf16[512,128]{1,0:T(8,128)(2,1)S(1)} collective-permute-done((bf16[512,128]{1,0:T(8,128)(2,1)S(1)}, bf16[512,128]{1,0:T(8,128)(2,1)S(1)}, u32[]{:S(2)}, u32[]{:S(2)}) %collective-permute-start.7) | collective-permute-done | bytes 131104 | tf_op jit(solution)/shard_map/ppermute | solution.py:427
  19.7 0.6 %route.1 = (bf16[512,128]{1,0:T(8,128)(2,1)S(1)}, bf16[512,128]{1,0:T(8,128)(2,1)S(1)}, bf16[512,128]{1,0:T(8,128)(2,1)S(1)}, bf16[512,128]{1,0:T(8,128)(2,1)S(1)}) custom-call(s32[16]{0:T(128)S(1)} %fusion.index_far, bf16[512,128]{1,0:T(8,128)(2,1)S(1)} %collective-permute-done.refs_0_, bf16[512,128]{1,0:T(8,128)(2,1)S(1)} %collective-permute-done.1.refs_1_, ...), custom_call_target="tpu_custom_call" | custom-call | tf_op jit(solution)/shard_map/route/pallas_call | solution.py:225
  20.3 2.9 %collective-permute-start.8 = (bf16[512,128]{1,0:T(8,128)(2,1)S(1)}, bf16[512,128]{1,0:T(8,128)(2,1)S(1)}, u32[]{:S(2)}, u32[]{:S(2)}) collective-permute-start(bf16[512,128]{1,0:T(8,128)(2,1)S(1)} %get-tuple-element.29), channel_id=1, source_target_pairs={{0,24},{1,28},{2,26},{3,30},{4,25},{5,29},{6,27},{7,31},{8,16},{9,... | collective-permute-start | bytes 393224 | tf_op jit(solution)/shard_map/ppermute | solution.py:419
  23.2 1.6 %collective-permute-start.10 = (bf16[512,128]{1,0:T(8,128)(2,1)S(1)}, bf16[512,128]{1,0:T(8,128)(2,1)S(1)}, u32[]{:S(2)}, u32[]{:S(2)}) collective-permute-start(bf16[512,128]{1,0:T(8,128)(2,1)S(1)} %get-tuple-element.31), channel_id=1, source_target_pairs={{0,8},{1,12},{2,10},{3,14},{4,9},{5,13},{6,11},{7,15},{8,0},{9,4},... | collective-permute-start | bytes 393224 | tf_op jit(solution)/shard_map/ppermute | solution.py:419
  24.7 1.2 %collective-permute-start.11 = (bf16[512,128]{1,0:T(8,128)(2,1)S(1)}, bf16[512,128]{1,0:T(8,128)(2,1)S(1)}, u32[]{:S(2)}, u32[]{:S(2)}) collective-permute-start(bf16[512,128]{1,0:T(8,128)(2,1)S(1)} %get-tuple-element.32.refs_4_), channel_id=1, source_target_pairs={{0,5},{1,4},{2,7},{3,6},{4,1},{5,0},{6,3},{7,2},{8,13},{9,12},{10,... | collective-permute-start | bytes 393224 | tf_op jit(solution)/shard_map/ppermute | solution.py:419
  25.9 1.2 %prepare.1 = (f32[128,128]{1,0:T(8,128)S(1)}, f32[64,128]{1,0:T(8,128)S(1)}, f32[64,128]{1,0:T(8,128)S(1)}, f32[64,128]{1,0:T(8,128)S(1)}, f32[64,128]{1,0:T(8,128)S(1)}) custom-call(s32[32]{0:T(128)} %lens_ref.1, bf16[4,3,4,512]{3,2,1,0:T(4,128)(2,1)} %bitcast.6, bf16[3,3,4,512]{3,2,1,0:T(4,128)(2,1)} %bitcast.7, bf16[3,4,512]{2,1,0:T(4,128)(2,1)} %bitcast.8, ...), custom_call_target="tpu_custom_call" | custom-call | tf_op jit(solution)/shard_map/prepare/pallas_call | solution.py:180
  27.1 0.0 copy-start.1
  27.1 1.6 %fetch.1.refs_8_ = bf16[512,2048]{1,0:T(8,128)(2,1)S(1)} custom-call(bf16[512,2048]{1,0:T(8,128)(2,1)} %far_ref), custom_call_target="tpu_custom_call" | custom-call | tf_op jit(solution)/shard_map/fetch/pallas_call | solution.py:247
  28.8 6.2 %collective-permute-done.9.refs_1_ = bf16[512,128]{1,0:T(8,128)(2,1)S(1)} collective-permute-done((bf16[512,128]{1,0:T(8,128)(2,1)S(1)}, bf16[512,128]{1,0:T(8,128)(2,1)S(1)}, u32[]{:S(2)}, u32[]{:S(2)}) %collective-permute-start.9) | collective-permute-done | bytes 131104 | tf_op jit(solution)/shard_map/ppermute | solution.py:419
  35.0 0.0 copy-start
  35.0 0.7 %home.1.refs_0_ = bf16[16,2048]{1,0:T(8,128)(2,1)S(1)} custom-call(bf16[512,128]{1,0:T(8,128)(2,1)S(1)} %collective-permute-done.8.refs_0_, bf16[512,128]{1,0:T(8,128)(2,1)S(1)} %collective-permute-done.9.refs_1_, bf16[512,128]{1,0:T(8,128)(2,1)S(1)} %collective-permute-done.10.refs_2_, bf16[512,128]{1,0:T(8,128)(2,1)S(1)} %collective-permute-done.11.refs_3_, ...), custom_call_target="tpu_custom_call" | custom-call | tf_op jit(solution)/shard_map/home/pallas_call | solution.py:288
  35.7 1.0 %collective-permute-start.14 = (bf16[16,2048]{1,0:T(8,128)(2,1)S(1)}, bf16[16,2048]{1,0:T(8,128)(2,1)S(1)}, u32[]{:S(2)}, u32[]{:S(2)}) collective-permute-start(bf16[16,2048]{1,0:T(8,128)(2,1)S(1)} %home.1.refs_0_), channel_id=1, source_target_pairs={{0,3},{1,2},{2,1},{3,0},{4,7},{5,6},{6,5},{7,4},{8,11},{9,10},{10,... | collective-permute-start | bytes 196616 | tf_op jit(solution)/shard_map/ppermute | solution.py:445
  36.8 0.5 %collective-permute-start.13 = (bf16[16,2048]{1,0:T(8,128)(2,1)S(1)}, bf16[16,2048]{1,0:T(8,128)(2,1)S(1)}, u32[]{:S(2)}, u32[]{:S(2)}) collective-permute-start(bf16[16,2048]{1,0:T(8,128)(2,1)S(1)} %home.1.refs_0_), channel_id=1, source_target_pairs={{0,2},{1,3},{2,0},{3,1},{4,6},{5,7},{6,4},{7,5},{8,10},{9,11},{10,... | collective-permute-start | bytes 196616 | tf_op jit(solution)/shard_map/ppermute | solution.py:445
  37.3 0.3 collective-permute-start.12
  37.6 1.2 %place.1 = bf16[4,4,128,128]{3,2,1,0:T(8,128)(2,1)} custom-call(bf16[512,128]{1,0:T(8,128)(2,1)S(1)} %collective-permute-done.8.refs_0_, bf16[512,128]{1,0:T(8,128)(2,1)S(1)} %collective-permute-done.9.refs_1_, bf16[512,128]{1,0:T(8,128)(2,1)S(1)} %collective-permute-done.10.refs_2_, bf16[512,128]{1,0:T(8,128)(2,1)S(1)} %collective-permute-done.11.refs_3_, ...), custom_call_target="tpu_custom_call" | custom-call | tf_op jit(solution)/shard_map/place/pallas_call | solution.py:342
  38.8 1.2 %collective-permute-done.14.refs_3_ = bf16[16,2048]{1,0:T(8,128)(2,1)S(1)} collective-permute-done((bf16[16,2048]{1,0:T(8,128)(2,1)S(1)}, bf16[16,2048]{1,0:T(8,128)(2,1)S(1)}, u32[]{:S(2)}, u32[]{:S(2)}) %collective-permute-start.14) | collective-permute-done | bytes 65568 | tf_op jit(solution)/shard_map/ppermute | solution.py:445
  40.0 1.5 %collective-permute-done.13.refs_2_ = bf16[16,2048]{1,0:T(8,128)(2,1)S(1)} collective-permute-done((bf16[16,2048]{1,0:T(8,128)(2,1)S(1)}, bf16[16,2048]{1,0:T(8,128)(2,1)S(1)}, u32[]{:S(2)}, u32[]{:S(2)}) %collective-permute-start.13) | collective-permute-done | bytes 65568 | tf_op jit(solution)/shard_map/ppermute | solution.py:445
  41.5 0.7 %add.84 = bf16[4,4,2048]{2,1,0:T(4,128)(2,1)} custom-call(bf16[4,4,2048]{2,1,0:T(4,128)(2,1)S(1)} %copy-done, bf16[16,2048]{1,0:T(8,128)(2,1)S(1)} %home.1.refs_0_, bf16[16,2048]{1,0:T(8,128)(2,1)S(1)} %collective-permute-done.12.refs_1_, bf16[16,2048]{1,0:T(8,128)(2,1)S(1)} %collective-permute-done.13.refs_2_, ...), custom_call_target="tpu_custom_call" | custom-call | tf_op jit(solution)/shard_map/add/pallas_call | solution.py:369
  (14 shorter events, 0.1 us)
Async XLA Ops:
  1.8 9.1 %collective-permute-start = (bf16[512,128]{1,0:T(8,128)(2,1)S(1)}, bf16[512,128]{1,0:T(8,128)(2,1)S(1)}, u32[]{:S(2)}, u32[]{:S(2)}) collective-permute-start(bf16[512,128]{1,0:T(8,128)(2,1)S(1)} %get-tuple-element.25), channel_id=1, source_target_pairs={{0,24},{1,28},{2,26},{3,30},{4,25},{5,29},{6,27},{7,31},{8,16},{9,... | collective-permute-start | bytes 393224 | tf_op jit(solution)/shard_map/ppermute | solution.py:419
  6.9 8.0 %collective-permute-start.1 = (bf16[512,128]{1,0:T(8,128)(2,1)S(1)}, bf16[512,128]{1,0:T(8,128)(2,1)S(1)}, u32[]{:S(2)}, u32[]{:S(2)}) collective-permute-start(bf16[512,128]{1,0:T(8,128)(2,1)S(1)} %get-tuple-element.26), channel_id=1, source_target_pairs={{0,8},{1,12},{2,10},{3,14},{4,9},{5,13},{6,11},{7,15},{8,0},{9,4},... | collective-permute-start | bytes 393224 | tf_op jit(solution)/shard_map/ppermute | solution.py:419
  6.9 8.4 %collective-permute-start.2 = (bf16[512,128]{1,0:T(8,128)(2,1)S(1)}, bf16[512,128]{1,0:T(8,128)(2,1)S(1)}, u32[]{:S(2)}, u32[]{:S(2)}) collective-permute-start(bf16[512,128]{1,0:T(8,128)(2,1)S(1)} %get-tuple-element.27), channel_id=1, source_target_pairs={{0,0},{1,4},{2,2},{3,6},{4,1},{5,5},{6,3},{7,7},{8,8},{9,12},{10,1... | collective-permute-start | bytes 393224 | tf_op jit(solution)/shard_map/ppermute | solution.py:419
  7.6 10.8 %collective-permute-start.3 = (bf16[512,128]{1,0:T(8,128)(2,1)S(1)}, bf16[512,128]{1,0:T(8,128)(2,1)S(1)}, u32[]{:S(2)}, u32[]{:S(2)}) collective-permute-start(bf16[512,128]{1,0:T(8,128)(2,1)S(1)} %get-tuple-element.28), channel_id=1, source_target_pairs={{0,16},{1,20},{2,18},{3,22},{4,17},{5,21},{6,19},{7,23},{8,24},{9,... | collective-permute-start | bytes 393224 | tf_op jit(solution)/shard_map/ppermute | solution.py:419
  10.9 7.5 %collective-permute-start.4 = (bf16[512,128]{1,0:T(8,128)(2,1)S(1)}, bf16[512,128]{1,0:T(8,128)(2,1)S(1)}, u32[]{:S(2)}, u32[]{:S(2)}) collective-permute-start(bf16[512,128]{1,0:T(8,128)(2,1)S(1)} %collective-permute-done.refs_0_), channel_id=1, source_target_pairs={{0,1},{1,0},{2,3},{3,2},{4,5},{5,4},{6,7},{7,6},{8,9},{9,8},{10,11... | collective-permute-start | bytes 393224 | tf_op jit(solution)/shard_map/ppermute | solution.py:427
  14.9 3.5 %collective-permute-start.5 = (bf16[512,128]{1,0:T(8,128)(2,1)S(1)}, bf16[512,128]{1,0:T(8,128)(2,1)S(1)}, u32[]{:S(2)}, u32[]{:S(2)}) collective-permute-start(bf16[512,128]{1,0:T(8,128)(2,1)S(1)} %collective-permute-done.1.refs_1_), channel_id=1, source_target_pairs={{0,1},{1,0},{2,3},{3,2},{4,5},{5,4},{6,7},{7,6},{8,9},{9,8},{10,11... | collective-permute-start | bytes 393224 | tf_op jit(solution)/shard_map/ppermute | solution.py:427
  15.4 3.0 %collective-permute-start.6 = (bf16[512,128]{1,0:T(8,128)(2,1)S(1)}, bf16[512,128]{1,0:T(8,128)(2,1)S(1)}, u32[]{:S(2)}, u32[]{:S(2)}) collective-permute-start(bf16[512,128]{1,0:T(8,128)(2,1)S(1)} %collective-permute-done.2.refs_2_), channel_id=1, source_target_pairs={{0,1},{1,0},{2,3},{3,2},{4,5},{5,4},{6,7},{7,6},{8,9},{9,8},{10,11... | collective-permute-start | bytes 393224 | tf_op jit(solution)/shard_map/ppermute | solution.py:427
  18.3 1.3 %collective-permute-start.7 = (bf16[512,128]{1,0:T(8,128)(2,1)S(1)}, bf16[512,128]{1,0:T(8,128)(2,1)S(1)}, u32[]{:S(2)}, u32[]{:S(2)}) collective-permute-start(bf16[512,128]{1,0:T(8,128)(2,1)S(1)} %collective-permute-done.3.refs_3_), channel_id=1, source_target_pairs={{0,1},{1,0},{2,3},{3,2},{4,5},{5,4},{6,7},{7,6},{8,9},{9,8},{10,11... | collective-permute-start | bytes 393224 | tf_op jit(solution)/shard_map/ppermute | solution.py:427
  20.3 8.5 %collective-permute-start.8 = (bf16[512,128]{1,0:T(8,128)(2,1)S(1)}, bf16[512,128]{1,0:T(8,128)(2,1)S(1)}, u32[]{:S(2)}, u32[]{:S(2)}) collective-permute-start(bf16[512,128]{1,0:T(8,128)(2,1)S(1)} %get-tuple-element.29), channel_id=1, source_target_pairs={{0,24},{1,28},{2,26},{3,30},{4,25},{5,29},{6,27},{7,31},{8,16},{9,... | collective-permute-start | bytes 393224 | tf_op jit(solution)/shard_map/ppermute | solution.py:419
  23.2 11.8 %collective-permute-start.9 = (bf16[512,128]{1,0:T(8,128)(2,1)S(1)}, bf16[512,128]{1,0:T(8,128)(2,1)S(1)}, u32[]{:S(2)}, u32[]{:S(2)}) collective-permute-start(bf16[512,128]{1,0:T(8,128)(2,1)S(1)} %get-tuple-element.30), channel_id=1, source_target_pairs={{0,16},{1,20},{2,18},{3,22},{4,17},{5,21},{6,19},{7,23},{8,24},{9,... | collective-permute-start | bytes 393224 | tf_op jit(solution)/shard_map/ppermute | solution.py:419
  23.2 11.8 %collective-permute-start.10 = (bf16[512,128]{1,0:T(8,128)(2,1)S(1)}, bf16[512,128]{1,0:T(8,128)(2,1)S(1)}, u32[]{:S(2)}, u32[]{:S(2)}) collective-permute-start(bf16[512,128]{1,0:T(8,128)(2,1)S(1)} %get-tuple-element.31), channel_id=1, source_target_pairs={{0,8},{1,12},{2,10},{3,14},{4,9},{5,13},{6,11},{7,15},{8,0},{9,4},... | collective-permute-start | bytes 393224 | tf_op jit(solution)/shard_map/ppermute | solution.py:419
  24.7 10.3 %collective-permute-start.11 = (bf16[512,128]{1,0:T(8,128)(2,1)S(1)}, bf16[512,128]{1,0:T(8,128)(2,1)S(1)}, u32[]{:S(2)}, u32[]{:S(2)}) collective-permute-start(bf16[512,128]{1,0:T(8,128)(2,1)S(1)} %get-tuple-element.32.refs_4_), channel_id=1, source_target_pairs={{0,5},{1,4},{2,7},{3,6},{4,1},{5,0},{6,3},{7,2},{8,13},{9,12},{10,... | collective-permute-start | bytes 393224 | tf_op jit(solution)/shard_map/ppermute | solution.py:419
  27.1 7.9 %copy-start.1 = (f32[512]{0:T(512)S(1)}, f32[512]{0:T(512)}, u32[]{:S(2)}) copy-start(f32[512]{0:T(512)} %param.18) | copy-start | bytes 6148
  35.0 6.5 %copy-start = (bf16[4,4,2048]{2,1,0:T(4,128)(2,1)S(1)}, bf16[4,4,2048]{2,1,0:T(4,128)(2,1)}, u32[]{:S(2)}) copy-start(bf16[4,4,2048]{2,1,0:T(4,128)(2,1)} %resid.1) | copy-start | bytes 196612
  35.7 4.3 %collective-permute-start.14 = (bf16[16,2048]{1,0:T(8,128)(2,1)S(1)}, bf16[16,2048]{1,0:T(8,128)(2,1)S(1)}, u32[]{:S(2)}, u32[]{:S(2)}) collective-permute-start(bf16[16,2048]{1,0:T(8,128)(2,1)S(1)} %home.1.refs_0_), channel_id=1, source_target_pairs={{0,3},{1,2},{2,1},{3,0},{4,7},{5,6},{6,5},{7,4},{8,11},{9,10},{10,... | collective-permute-start | bytes 196616 | tf_op jit(solution)/shard_map/ppermute | solution.py:445
  36.8 4.8 %collective-permute-start.13 = (bf16[16,2048]{1,0:T(8,128)(2,1)S(1)}, bf16[16,2048]{1,0:T(8,128)(2,1)S(1)}, u32[]{:S(2)}, u32[]{:S(2)}) collective-permute-start(bf16[16,2048]{1,0:T(8,128)(2,1)S(1)} %home.1.refs_0_), channel_id=1, source_target_pairs={{0,2},{1,3},{2,0},{3,1},{4,6},{5,7},{6,4},{7,5},{8,10},{9,11},{10,... | collective-permute-start | bytes 196616 | tf_op jit(solution)/shard_map/ppermute | solution.py:445
  37.3 4.2 %collective-permute-start.12 = (bf16[16,2048]{1,0:T(8,128)(2,1)S(1)}, bf16[16,2048]{1,0:T(8,128)(2,1)S(1)}, u32[]{:S(2)}, u32[]{:S(2)}) collective-permute-start(bf16[16,2048]{1,0:T(8,128)(2,1)S(1)} %home.1.refs_0_), channel_id=1, source_target_pairs={{0,1},{1,0},{2,3},{3,2},{4,5},{5,4},{6,7},{7,6},{8,9},{9,8},{10,11... | collective-permute-start | bytes 196616 | tf_op jit(solution)/shard_map/ppermute | solution.py:445

commit v9 on v8

--- a/solution.py
+++ b/solution.py
@@ -382,7 +382,7 @@
 
 
 def order_back(blocks):
-    return tuple(range(blocks - 1, -1, -1))
+    return (*range(blocks // 2, blocks), *range(blocks // 2 - 1, -1, -1))
 
 
 def in_order(refs, order):
@@ -441,9 +441,12 @@
     turned, lefts, lasting, values, heard = prepared
     weight = fetch(weight)
     part = home(back, routed[0], lefts, heard, norm_gain, weight, local_reqs, steps)
-    terms = [part] + [
-        lax.ppermute(part, "head", [(i, i ^ k) for i in range(n_head)]) for k in range(1, n_head)
-    ]
+    terms = [part, lax.ppermute(part, "head", sibling)]
+    step = 2
+    while step < n_head:
+        part = (terms[0].astype(F32) + terms[1].astype(F32)).astype(BF16)
+        terms = [part, lax.ppermute(part, "head", [(i, i ^ step) for i in range(n_head)])]
+        step *= 2
     *back, part = lax.optimization_barrier((*back, part))
     new_state = place(back, routed[0], turned, lasting, values, old_state.shape, steps)
     return add(resid, terms), new_state

time: 42.6 us -> 42.2 us (level)
  starting transfers between devices: 16.6 us -> 15.6 us
  waiting for transfers between devices: 16.7 us -> 17.3 us
    ppermute x8, starting transfers between devices: 12.1 us -> 11.2 us  [swap(): return lax.ppermute(value, both, pairs)]
    ppermute x8, waiting for transfers between devices: 12.7 us -> 13.5 us  [swap(): return lax.ppermute(value, both, pairs)]
    ppermute x3 -> x2, waiting for transfers between devices: 2.73 us -> 2.59 us  [the longest x1 1.59 us: swapped_body(): lax.ppermute(part, 'head', [(i, i ^ step) for i in range(n_head)])]
    ppermute x3 -> x2, starting transfers between devices: 1.87 us -> 1.79 us  [the longest x1 1.53 us: swapped_body(): lax.ppermute(part, 'head', [(i, i ^ step) for i in range(n_head)])]
  transfers between devices with their start and end apart: 15 -> 14, of which waited for: 7 -> 8; matrix products, arithmetic and copies ran while one was open for 2% -> 2% of each run, Pallas kernels for 10% -> 10%
where the time goes in v9:
time: 42.2 us; the launch traced here: 41.9 us
  waiting for transfers between devices  17.3 us (41%)
  starting transfers between devices  15.6 us (37%)
  Pallas kernels  7.19 us (17%)
  other arithmetic  0.96 us (2%)
  between operations  0.73 us (2%)
    ppermute x8, waiting for transfers between devices, swap(): return lax.ppermute(value, both, pairs)  13.5 us
    ppermute x8, starting transfers between devices, swap(): return lax.ppermute(value, both, pairs)  11.2 us
    ppermute x4, starting transfers between devices, swapped_body(): sib = [lax.ppermute(own[s], 'head', sibling) for s in range(blocks)]  2.62 us
    pallas_call x1, Pallas kernels, fetch(): pl.pallas_call(fetch_kernel, out_shape=VMEM(value.shape, value.dtype), in...  1.61 us
    ppermute x1, waiting for transfers between devices, swapped_body(): lax.ppermute(part, 'head', [(i, i ^ step) for i in range(n_head)])  1.59 us
    ppermute x1, starting transfers between devices, swapped_body(): lax.ppermute(part, 'head', [(i, i ^ step) for i in range(n_head)])  1.53 us
    ppermute x4, waiting for transfers between devices, swapped_body(): sib = [lax.ppermute(own[s], 'head', sibling) for s in range(blocks)]  1.3 us
    pallas_call x1, Pallas kernels, prepare(): pl.pallas_call(functools.partial(prepare_kernel, blocks), out_shape=[VMEM...  1.25 us
  transfers between devices with their start and end apart: 14, of which 8 were waited for; matrix products, arithmetic and copies ran while one was open for 2% of the time, Pallas kernels for 10%

profile of v9, /device:TPU:0, one launch (start us, length us, event | category | flops | bytes accessed | tf_op | source)
XLA Modules:
  0.0 41.9 jit_solution(16383911623322967610)
XLA Ops:
  0.6 1.2 %pack.1 = (bf16[512,128]{1,0:T(8,128)(2,1)S(1)}, bf16[512,128]{1,0:T(8,128)(2,1)S(1)}, bf16[512,128]{1,0:T(8,128)(2,1)S(1)}, bf16[512,128]{1,0:T(8,128)(2,1)S(1)}) custom-call(bf16[4,4,128,128]{3,2,1,0:T(8,128)(2,1)} %state_ref.1), custom_call_target="tpu_custom_call" | custom-call | tf_op jit(solution)/shard_map/pack/pallas_call | solution.py:101
  1.8 5.1 %collective-permute-start = (bf16[512,128]{1,0:T(8,128)(2,1)S(1)}, bf16[512,128]{1,0:T(8,128)(2,1)S(1)}, u32[]{:S(2)}, u32[]{:S(2)}) collective-permute-start(bf16[512,128]{1,0:T(8,128)(2,1)S(1)} %get-tuple-element.25), channel_id=1, source_target_pairs={{0,24},{1,28},{2,26},{3,30},{4,25},{5,29},{6,27},{7,31},{8,16},{9,... | collective-permute-start | bytes 393224 | tf_op jit(solution)/shard_map/ppermute | solution.py:419
  6.9 0.7 %collective-permute-start.2 = (bf16[512,128]{1,0:T(8,128)(2,1)S(1)}, bf16[512,128]{1,0:T(8,128)(2,1)S(1)}, u32[]{:S(2)}, u32[]{:S(2)}) collective-permute-start(bf16[512,128]{1,0:T(8,128)(2,1)S(1)} %get-tuple-element.27), channel_id=1, source_target_pairs={{0,0},{1,4},{2,2},{3,6},{4,1},{5,5},{6,3},{7,7},{8,8},{9,12},{10,1... | collective-permute-start | bytes 393224 | tf_op jit(solution)/shard_map/ppermute | solution.py:419
  7.6 0.7 %collective-permute-start.3 = (bf16[512,128]{1,0:T(8,128)(2,1)S(1)}, bf16[512,128]{1,0:T(8,128)(2,1)S(1)}, u32[]{:S(2)}, u32[]{:S(2)}) collective-permute-start(bf16[512,128]{1,0:T(8,128)(2,1)S(1)} %get-tuple-element.28), channel_id=1, source_target_pairs={{0,16},{1,20},{2,18},{3,22},{4,17},{5,21},{6,19},{7,23},{8,24},{9,... | collective-permute-start | bytes 393224 | tf_op jit(solution)/shard_map/ppermute | solution.py:419
  8.3 0.1 iota_add_fusion
  8.4 0.1 add.63
  8.4 0.8 %select_reduce_fusion = s32[16]{0:T(128)S(1)} fusion(s32[32]{0:T(128)} %param.15, s32[16]{0:T(128)S(1)} %add.63), kind=kLoop, calls=%fused_computation.1 | loop fusion | flops 1520 | bytes 256 | tf_op jit(solution)/shard_map/reduce_sum | solution.py:433
  9.3 1.6 %collective-permute-done.refs_0_ = bf16[512,128]{1,0:T(8,128)(2,1)S(1)} collective-permute-done((bf16[512,128]{1,0:T(8,128)(2,1)S(1)}, bf16[512,128]{1,0:T(8,128)(2,1)S(1)}, u32[]{:S(2)}, u32[]{:S(2)}) %collective-permute-start) | collective-permute-done | bytes 131104 | tf_op jit(solution)/shard_map/ppermute | solution.py:419
  10.9 1.9 %collective-permute-start.4 = (bf16[512,128]{1,0:T(8,128)(2,1)S(1)}, bf16[512,128]{1,0:T(8,128)(2,1)S(1)}, u32[]{:S(2)}, u32[]{:S(2)}) collective-permute-start(bf16[512,128]{1,0:T(8,128)(2,1)S(1)} %collective-permute-done.refs_0_), channel_id=1, source_target_pairs={{0,1},{1,0},{2,3},{3,2},{4,5},{5,4},{6,7},{7,6},{8,9},{9,8},{10,11... | collective-permute-start | bytes 393224 | tf_op jit(solution)/shard_map/ppermute | solution.py:427
  12.8 2.1 %collective-permute-done.1.refs_1_ = bf16[512,128]{1,0:T(8,128)(2,1)S(1)} collective-permute-done((bf16[512,128]{1,0:T(8,128)(2,1)S(1)}, bf16[512,128]{1,0:T(8,128)(2,1)S(1)}, u32[]{:S(2)}, u32[]{:S(2)}) %collective-permute-start.1) | collective-permute-done | bytes 131104 | tf_op jit(solution)/shard_map/ppermute | solution.py:419
  14.9 0.5 %collective-permute-start.5 = (bf16[512,128]{1,0:T(8,128)(2,1)S(1)}, bf16[512,128]{1,0:T(8,128)(2,1)S(1)}, u32[]{:S(2)}, u32[]{:S(2)}) collective-permute-start(bf16[512,128]{1,0:T(8,128)(2,1)S(1)} %collective-permute-done.1.refs_1_), channel_id=1, source_target_pairs={{0,1},{1,0},{2,3},{3,2},{4,5},{5,4},{6,7},{7,6},{8,9},{9,8},{10,11... | collective-permute-start | bytes 393224 | tf_op jit(solution)/shard_map/ppermute | solution.py:427
  15.3 0.0 collective-permute-done.2.refs_2_
  15.4 0.3 collective-permute-start.6
  15.6 2.7 %collective-permute-done.3.refs_3_ = bf16[512,128]{1,0:T(8,128)(2,1)S(1)} collective-permute-done((bf16[512,128]{1,0:T(8,128)(2,1)S(1)}, bf16[512,128]{1,0:T(8,128)(2,1)S(1)}, u32[]{:S(2)}, u32[]{:S(2)}) %collective-permute-start.3) | collective-permute-done | bytes 131104 | tf_op jit(solution)/shard_map/ppermute | solution.py:419
  18.4 1.3 %collective-permute-done.7.refs_7_ = bf16[512,128]{1,0:T(8,128)(2,1)S(1)} collective-permute-done((bf16[512,128]{1,0:T(8,128)(2,1)S(1)}, bf16[512,128]{1,0:T(8,128)(2,1)S(1)}, u32[]{:S(2)}, u32[]{:S(2)}) %collective-permute-start.7) | collective-permute-done | bytes 131104 | tf_op jit(solution)/shard_map/ppermute | solution.py:427
  19.7 0.6 %route.1 = (bf16[512,128]{1,0:T(8,128)(2,1)S(1)}, bf16[512,128]{1,0:T(8,128)(2,1)S(1)}, bf16[512,128]{1,0:T(8,128)(2,1)S(1)}, bf16[512,128]{1,0:T(8,128)(2,1)S(1)}) custom-call(s32[16]{0:T(128)S(1)} %fusion.index_far, bf16[512,128]{1,0:T(8,128)(2,1)S(1)} %collective-permute-done.refs_0_, bf16[512,128]{1,0:T(8,128)(2,1)S(1)} %collective-permute-done.1.refs_1_, ...), custom_call_target="tpu_custom_call" | custom-call | tf_op jit(solution)/shard_map/route/pallas_call | solution.py:225
  20.3 1.4 %collective-permute-start.8 = (bf16[512,128]{1,0:T(8,128)(2,1)S(1)}, bf16[512,128]{1,0:T(8,128)(2,1)S(1)}, u32[]{:S(2)}, u32[]{:S(2)}) collective-permute-start(bf16[512,128]{1,0:T(8,128)(2,1)S(1)} %get-tuple-element.29), channel_id=1, source_target_pairs={{0,16},{1,20},{2,18},{3,22},{4,17},{5,21},{6,19},{7,23},{8,24},{9,... | collective-permute-start | bytes 393224 | tf_op jit(solution)/shard_map/ppermute | solution.py:419
  21.7 1.6 %collective-permute-start.9 = (bf16[512,128]{1,0:T(8,128)(2,1)S(1)}, bf16[512,128]{1,0:T(8,128)(2,1)S(1)}, u32[]{:S(2)}, u32[]{:S(2)}) collective-permute-start(bf16[512,128]{1,0:T(8,128)(2,1)S(1)} %get-tuple-element.30), channel_id=1, source_target_pairs={{0,24},{1,28},{2,26},{3,30},{4,25},{5,29},{6,27},{7,31},{8,16},{9,... | collective-permute-start | bytes 393224 | tf_op jit(solution)/shard_map/ppermute | solution.py:419
  23.3 0.5 %collective-permute-start.10 = (bf16[512,128]{1,0:T(8,128)(2,1)S(1)}, bf16[512,128]{1,0:T(8,128)(2,1)S(1)}, u32[]{:S(2)}, u32[]{:S(2)}) collective-permute-start(bf16[512,128]{1,0:T(8,128)(2,1)S(1)} %get-tuple-element.31), channel_id=1, source_target_pairs={{0,8},{1,12},{2,10},{3,14},{4,9},{5,13},{6,11},{7,15},{8,0},{9,4},... | collective-permute-start | bytes 393224 | tf_op jit(solution)/shard_map/ppermute | solution.py:419
  23.8 1.2 %collective-permute-start.11 = (bf16[512,128]{1,0:T(8,128)(2,1)S(1)}, bf16[512,128]{1,0:T(8,128)(2,1)S(1)}, u32[]{:S(2)}, u32[]{:S(2)}) collective-permute-start(bf16[512,128]{1,0:T(8,128)(2,1)S(1)} %get-tuple-element.32.refs_4_), channel_id=1, source_target_pairs={{0,5},{1,4},{2,7},{3,6},{4,1},{5,0},{6,3},{7,2},{8,13},{9,12},{10,... | collective-permute-start | bytes 393224 | tf_op jit(solution)/shard_map/ppermute | solution.py:419
  25.0 1.2 %prepare.1 = (f32[128,128]{1,0:T(8,128)S(1)}, f32[64,128]{1,0:T(8,128)S(1)}, f32[64,128]{1,0:T(8,128)S(1)}, f32[64,128]{1,0:T(8,128)S(1)}, f32[64,128]{1,0:T(8,128)S(1)}) custom-call(s32[32]{0:T(128)} %lens_ref.1, bf16[4,3,4,512]{3,2,1,0:T(4,128)(2,1)} %bitcast.6, bf16[3,3,4,512]{3,2,1,0:T(4,128)(2,1)} %bitcast.7, bf16[3,4,512]{2,1,0:T(4,128)(2,1)} %bitcast.8, ...), custom_call_target="tpu_custom_call" | custom-call | tf_op jit(solution)/shard_map/prepare/pallas_call | solution.py:180
  26.2 0.0 copy-start.1
  26.2 1.6 %fetch.1.refs_8_ = bf16[512,2048]{1,0:T(8,128)(2,1)S(1)} custom-call(bf16[512,2048]{1,0:T(8,128)(2,1)} %far_ref), custom_call_target="tpu_custom_call" | custom-call | tf_op jit(solution)/shard_map/fetch/pallas_call | solution.py:247
  27.9 5.2 %collective-permute-done.8.refs_0_ = bf16[512,128]{1,0:T(8,128)(2,1)S(1)} collective-permute-done((bf16[512,128]{1,0:T(8,128)(2,1)S(1)}, bf16[512,128]{1,0:T(8,128)(2,1)S(1)}, u32[]{:S(2)}, u32[]{:S(2)}) %collective-permute-start.8) | collective-permute-done | bytes 131104 | tf_op jit(solution)/shard_map/ppermute | solution.py:419
  33.1 1.8 %collective-permute-done.10.refs_2_ = bf16[512,128]{1,0:T(8,128)(2,1)S(1)} collective-permute-done((bf16[512,128]{1,0:T(8,128)(2,1)S(1)}, bf16[512,128]{1,0:T(8,128)(2,1)S(1)}, u32[]{:S(2)}, u32[]{:S(2)}) %collective-permute-start.10) | collective-permute-done | bytes 131104 | tf_op jit(solution)/shard_map/ppermute | solution.py:419
  34.9 0.7 %home.1 = bf16[16,2048]{1,0:T(8,128)(2,1)S(1)} custom-call(bf16[512,128]{1,0:T(8,128)(2,1)S(1)} %collective-permute-done.8.refs_0_, bf16[512,128]{1,0:T(8,128)(2,1)S(1)} %collective-permute-done.9.refs_1_, bf16[512,128]{1,0:T(8,128)(2,1)S(1)} %collective-permute-done.10.refs_2_, bf16[512,128]{1,0:T(8,128)(2,1)S(1)} %collective-permute-done.11.refs_3_, ...), custom_call_target="tpu_custom_call" | custom-call | tf_op jit(solution)/shard_map/home/pallas_call | solution.py:288
  35.6 0.3 collective-permute-start.12
  35.9 1.0 %collective-permute-done.12 = bf16[16,2048]{1,0:T(8,128)(2,1)S(1)} collective-permute-done((bf16[16,2048]{1,0:T(8,128)(2,1)S(1)}, bf16[16,2048]{1,0:T(8,128)(2,1)S(1)}, u32[]{:S(2)}, u32[]{:S(2)}) %collective-permute-start.12) | collective-permute-done | bytes 65568 | tf_op jit(solution)/shard_map/ppermute | solution.py:444
  36.9 1.5 %collective-permute-start.13 = (bf16[16,2048]{1,0:T(8,128)(2,1)S(1)}, bf16[16,2048]{1,0:T(8,128)(2,1)S(1)}, u32[]{:S(2)}, u32[]{:S(2)}) collective-permute-start(bf16[16,2048]{1,0:T(8,128)(2,1)S(1)} %add_convert_fusion.refs_0_), channel_id=1, source_target_pairs={{0,2},{1,3},{2,0},{3,1},{4,6},{5,7},{6,4},{7,5},{8,10},{9,11},{10,... | collective-permute-start | bytes 196616 | tf_op jit(solution)/shard_map/ppermute | solution.py:448
  38.4 1.2 %place.1 = bf16[4,4,128,128]{3,2,1,0:T(8,128)(2,1)} custom-call(bf16[512,128]{1,0:T(8,128)(2,1)S(1)} %collective-permute-done.8.refs_0_, bf16[512,128]{1,0:T(8,128)(2,1)S(1)} %collective-permute-done.9.refs_1_, bf16[512,128]{1,0:T(8,128)(2,1)S(1)} %collective-permute-done.10.refs_2_, bf16[512,128]{1,0:T(8,128)(2,1)S(1)} %collective-permute-done.11.refs_3_, ...), custom_call_target="tpu_custom_call" | custom-call | tf_op jit(solution)/shard_map/place/pallas_call | solution.py:342
  39.6 1.6 %collective-permute-done.13.refs_1_ = bf16[16,2048]{1,0:T(8,128)(2,1)S(1)} collective-permute-done((bf16[16,2048]{1,0:T(8,128)(2,1)S(1)}, bf16[16,2048]{1,0:T(8,128)(2,1)S(1)}, u32[]{:S(2)}, u32[]{:S(2)}) %collective-permute-start.13) | collective-permute-done | bytes 65568 | tf_op jit(solution)/shard_map/ppermute | solution.py:448
  41.2 0.7 %add.89 = bf16[4,4,2048]{2,1,0:T(4,128)(2,1)} custom-call(bf16[4,4,2048]{2,1,0:T(4,128)(2,1)S(1)} %copy-done, bf16[16,2048]{1,0:T(8,128)(2,1)S(1)} %add_convert_fusion.refs_0_, bf16[16,2048]{1,0:T(8,128)(2,1)S(1)} %collective-permute-done.13.refs_1_), custom_call_target="tpu_custom_call" | custom-call | tf_op jit(solution)/shard_map/add/pallas_call | solution.py:369
  (13 shorter events, 0.1 us)
Async XLA Ops:
  1.8 9.1 %collective-permute-start = (bf16[512,128]{1,0:T(8,128)(2,1)S(1)}, bf16[512,128]{1,0:T(8,128)(2,1)S(1)}, u32[]{:S(2)}, u32[]{:S(2)}) collective-permute-start(bf16[512,128]{1,0:T(8,128)(2,1)S(1)} %get-tuple-element.25), channel_id=1, source_target_pairs={{0,24},{1,28},{2,26},{3,30},{4,25},{5,29},{6,27},{7,31},{8,16},{9,... | collective-permute-start | bytes 393224 | tf_op jit(solution)/shard_map/ppermute | solution.py:419
  6.9 8.0 %collective-permute-start.1 = (bf16[512,128]{1,0:T(8,128)(2,1)S(1)}, bf16[512,128]{1,0:T(8,128)(2,1)S(1)}, u32[]{:S(2)}, u32[]{:S(2)}) collective-permute-start(bf16[512,128]{1,0:T(8,128)(2,1)S(1)} %get-tuple-element.26), channel_id=1, source_target_pairs={{0,8},{1,12},{2,10},{3,14},{4,9},{5,13},{6,11},{7,15},{8,0},{9,4},... | collective-permute-start | bytes 393224 | tf_op jit(solution)/shard_map/ppermute | solution.py:419
  6.9 8.4 %collective-permute-start.2 = (bf16[512,128]{1,0:T(8,128)(2,1)S(1)}, bf16[512,128]{1,0:T(8,128)(2,1)S(1)}, u32[]{:S(2)}, u32[]{:S(2)}) collective-permute-start(bf16[512,128]{1,0:T(8,128)(2,1)S(1)} %get-tuple-element.27), channel_id=1, source_target_pairs={{0,0},{1,4},{2,2},{3,6},{4,1},{5,5},{6,3},{7,7},{8,8},{9,12},{10,1... | collective-permute-start | bytes 393224 | tf_op jit(solution)/shard_map/ppermute | solution.py:419
  7.6 10.8 %collective-permute-start.3 = (bf16[512,128]{1,0:T(8,128)(2,1)S(1)}, bf16[512,128]{1,0:T(8,128)(2,1)S(1)}, u32[]{:S(2)}, u32[]{:S(2)}) collective-permute-start(bf16[512,128]{1,0:T(8,128)(2,1)S(1)} %get-tuple-element.28), channel_id=1, source_target_pairs={{0,16},{1,20},{2,18},{3,22},{4,17},{5,21},{6,19},{7,23},{8,24},{9,... | collective-permute-start | bytes 393224 | tf_op jit(solution)/shard_map/ppermute | solution.py:419
  10.9 7.5 %collective-permute-start.4 = (bf16[512,128]{1,0:T(8,128)(2,1)S(1)}, bf16[512,128]{1,0:T(8,128)(2,1)S(1)}, u32[]{:S(2)}, u32[]{:S(2)}) collective-permute-start(bf16[512,128]{1,0:T(8,128)(2,1)S(1)} %collective-permute-done.refs_0_), channel_id=1, source_target_pairs={{0,1},{1,0},{2,3},{3,2},{4,5},{5,4},{6,7},{7,6},{8,9},{9,8},{10,11... | collective-permute-start | bytes 393224 | tf_op jit(solution)/shard_map/ppermute | solution.py:427
  14.9 3.5 %collective-permute-start.5 = (bf16[512,128]{1,0:T(8,128)(2,1)S(1)}, bf16[512,128]{1,0:T(8,128)(2,1)S(1)}, u32[]{:S(2)}, u32[]{:S(2)}) collective-permute-start(bf16[512,128]{1,0:T(8,128)(2,1)S(1)} %collective-permute-done.1.refs_1_), channel_id=1, source_target_pairs={{0,1},{1,0},{2,3},{3,2},{4,5},{5,4},{6,7},{7,6},{8,9},{9,8},{10,11... | collective-permute-start | bytes 393224 | tf_op jit(solution)/shard_map/ppermute | solution.py:427
  15.4 3.0 %collective-permute-start.6 = (bf16[512,128]{1,0:T(8,128)(2,1)S(1)}, bf16[512,128]{1,0:T(8,128)(2,1)S(1)}, u32[]{:S(2)}, u32[]{:S(2)}) collective-permute-start(bf16[512,128]{1,0:T(8,128)(2,1)S(1)} %collective-permute-done.2.refs_2_), channel_id=1, source_target_pairs={{0,1},{1,0},{2,3},{3,2},{4,5},{5,4},{6,7},{7,6},{8,9},{9,8},{10,11... | collective-permute-start | bytes 393224 | tf_op jit(solution)/shard_map/ppermute | solution.py:427
  18.3 1.3 %collective-permute-start.7 = (bf16[512,128]{1,0:T(8,128)(2,1)S(1)}, bf16[512,128]{1,0:T(8,128)(2,1)S(1)}, u32[]{:S(2)}, u32[]{:S(2)}) collective-permute-start(bf16[512,128]{1,0:T(8,128)(2,1)S(1)} %collective-permute-done.3.refs_3_), channel_id=1, source_target_pairs={{0,1},{1,0},{2,3},{3,2},{4,5},{5,4},{6,7},{7,6},{8,9},{9,8},{10,11... | collective-permute-start | bytes 393224 | tf_op jit(solution)/shard_map/ppermute | solution.py:427
  20.3 12.8 %collective-permute-start.8 = (bf16[512,128]{1,0:T(8,128)(2,1)S(1)}, bf16[512,128]{1,0:T(8,128)(2,1)S(1)}, u32[]{:S(2)}, u32[]{:S(2)}) collective-permute-start(bf16[512,128]{1,0:T(8,128)(2,1)S(1)} %get-tuple-element.29), channel_id=1, source_target_pairs={{0,16},{1,20},{2,18},{3,22},{4,17},{5,21},{6,19},{7,23},{8,24},{9,... | collective-permute-start | bytes 393224 | tf_op jit(solution)/shard_map/ppermute | solution.py:419
  21.7 11.4 %collective-permute-start.9 = (bf16[512,128]{1,0:T(8,128)(2,1)S(1)}, bf16[512,128]{1,0:T(8,128)(2,1)S(1)}, u32[]{:S(2)}, u32[]{:S(2)}) collective-permute-start(bf16[512,128]{1,0:T(8,128)(2,1)S(1)} %get-tuple-element.30), channel_id=1, source_target_pairs={{0,24},{1,28},{2,26},{3,30},{4,25},{5,29},{6,27},{7,31},{8,16},{9,... | collective-permute-start | bytes 393224 | tf_op jit(solution)/shard_map/ppermute | solution.py:419
  23.3 11.6 %collective-permute-start.10 = (bf16[512,128]{1,0:T(8,128)(2,1)S(1)}, bf16[512,128]{1,0:T(8,128)(2,1)S(1)}, u32[]{:S(2)}, u32[]{:S(2)}) collective-permute-start(bf16[512,128]{1,0:T(8,128)(2,1)S(1)} %get-tuple-element.31), channel_id=1, source_target_pairs={{0,8},{1,12},{2,10},{3,14},{4,9},{5,13},{6,11},{7,15},{8,0},{9,4},... | collective-permute-start | bytes 393224 | tf_op jit(solution)/shard_map/ppermute | solution.py:419
  23.8 11.1 %collective-permute-start.11 = (bf16[512,128]{1,0:T(8,128)(2,1)S(1)}, bf16[512,128]{1,0:T(8,128)(2,1)S(1)}, u32[]{:S(2)}, u32[]{:S(2)}) collective-permute-start(bf16[512,128]{1,0:T(8,128)(2,1)S(1)} %get-tuple-element.32.refs_4_), channel_id=1, source_target_pairs={{0,5},{1,4},{2,7},{3,6},{4,1},{5,0},{6,3},{7,2},{8,13},{9,12},{10,... | collective-permute-start | bytes 393224 | tf_op jit(solution)/shard_map/ppermute | solution.py:419
  26.2 8.7 %copy-start.1 = (f32[512]{0:T(512)S(1)}, f32[512]{0:T(512)}, u32[]{:S(2)}) copy-start(f32[512]{0:T(512)} %param.18) | copy-start | bytes 6148
  34.9 6.3 %copy-start = (bf16[4,4,2048]{2,1,0:T(4,128)(2,1)S(1)}, bf16[4,4,2048]{2,1,0:T(4,128)(2,1)}, u32[]{:S(2)}) copy-start(bf16[4,4,2048]{2,1,0:T(4,128)(2,1)} %resid.1) | copy-start | bytes 196612
  35.6 1.3 %collective-permute-start.12 = (bf16[16,2048]{1,0:T(8,128)(2,1)S(1)}, bf16[16,2048]{1,0:T(8,128)(2,1)S(1)}, u32[]{:S(2)}, u32[]{:S(2)}) collective-permute-start(bf16[16,2048]{1,0:T(8,128)(2,1)S(1)} %home.1), channel_id=1, source_target_pairs={{0,1},{1,0},{2,3},{3,2},{4,5},{5,4},{6,7},{7,6},{8,9},{9,8},{10,11... | collective-permute-start | bytes 196616 | tf_op jit(solution)/shard_map/ppermute | solution.py:444
  36.9 4.3 %collective-permute-start.13 = (bf16[16,2048]{1,0:T(8,128)(2,1)S(1)}, bf16[16,2048]{1,0:T(8,128)(2,1)S(1)}, u32[]{:S(2)}, u32[]{:S(2)}) collective-permute-start(bf16[16,2048]{1,0:T(8,128)(2,1)S(1)} %add_convert_fusion.refs_0_), channel_id=1, source_target_pairs={{0,2},{1,3},{2,0},{3,1},{4,6},{5,7},{6,4},{7,5},{8,10},{9,11},{10,... | collective-permute-start | bytes 196616 | tf_op jit(solution)/shard_map/ppermute | solution.py:448

commit v10 on v9

--- a/solution.py
+++ b/solution.py
@@ -441,12 +441,13 @@
     turned, lefts, lasting, values, heard = prepared
     weight = fetch(weight)
     part = home(back, routed[0], lefts, heard, norm_gain, weight, local_reqs, steps)
-    terms = [part, lax.ppermute(part, "head", sibling)]
-    step = 2
-    while step < n_head:
+    step = n_head // 2
+    terms = [part, lax.ppermute(part, "head", [(i, i ^ step) for i in range(n_head)])]
+    while step > 1:
+        step //= 2
         part = (terms[0].astype(F32) + terms[1].astype(F32)).astype(BF16)
         terms = [part, lax.ppermute(part, "head", [(i, i ^ step) for i in range(n_head)])]
-        step *= 2
+
     *back, part = lax.optimization_barrier((*back, part))
     new_state = place(back, routed[0], turned, lasting, values, old_state.shape, steps)
     return add(resid, terms), new_state

time: 42.2 us -> 42.3 us (level)
    ppermute x1 -> x2, waiting for transfers between devices: 1.59 us -> 2.83 us  [swapped_body(): lax.ppermute(part, 'head', [(i, i ^ step) for i in range(n_head)])]
    ppermute x1 -> x0, waiting for transfers between devices: 1 us -> none  [swapped_body(): terms = [part, lax.ppermute(part, 'head', sibling)]]
    ppermute x1 -> x2, starting transfers between devices: 1.53 us -> 1.55 us  [swapped_body(): lax.ppermute(part, 'head', [(i, i ^ step) for i in range(n_head)])]
  transfers between devices with their start and end apart: 14 -> 14, of which waited for: 8 -> 7; matrix products, arithmetic and copies ran while one was open for 2% -> 2% of each run, Pallas kernels for 10% -> 10%
where the time goes in v10:
time: 42.3 us; the launch traced here: 41.9 us
  waiting for transfers between devices  17.6 us (42%)
  starting transfers between devices  15.4 us (36%)
  Pallas kernels  7.19 us (17%)
  other arithmetic  0.96 us (2%)
  between operations  0.73 us (2%)
    ppermute x8, waiting for transfers between devices, swap(): return lax.ppermute(value, both, pairs)  13.5 us
    ppermute x8, starting transfers between devices, swap(): return lax.ppermute(value, both, pairs)  11.2 us
    ppermute x2, waiting for transfers between devices, swapped_body(): lax.ppermute(part, 'head', [(i, i ^ step) for i in range(n_head)])  2.83 us
    ppermute x4, starting transfers between devices, swapped_body(): sib = [lax.ppermute(own[s], 'head', sibling) for s in range(blocks)]  2.62 us
    pallas_call x1, Pallas kernels, fetch(): pl.pallas_call(fetch_kernel, out_shape=VMEM(value.shape, value.dtype), in...  1.61 us
    ppermute x2, starting transfers between devices, swapped_body(): lax.ppermute(part, 'head', [(i, i ^ step) for i in range(n_head)])  1.55 us
    ppermute x4, waiting for transfers between devices, swapped_body(): sib = [lax.ppermute(own[s], 'head', sibling) for s in range(blocks)]  1.3 us
    pallas_call x1, Pallas kernels, prepare(): pl.pallas_call(functools.partial(prepare_kernel, blocks), out_shape=[VMEM...  1.25 us
  transfers between devices with their start and end apart: 14, of which 7 were waited for; matrix products, arithmetic and copies ran while one was open for 2% of the time, Pallas kernels for 10%

profile of v10, /device:TPU:0, one launch (start us, length us, event | category | flops | bytes accessed | tf_op | source)
XLA Modules:
  0.0 41.9 jit_solution(1435855911421893371)
XLA Ops:
  0.6 1.2 %pack.1 = (bf16[512,128]{1,0:T(8,128)(2,1)S(1)}, bf16[512,128]{1,0:T(8,128)(2,1)S(1)}, bf16[512,128]{1,0:T(8,128)(2,1)S(1)}, bf16[512,128]{1,0:T(8,128)(2,1)S(1)}) custom-call(bf16[4,4,128,128]{3,2,1,0:T(8,128)(2,1)} %state_ref.1), custom_call_target="tpu_custom_call" | custom-call | tf_op jit(solution)/shard_map/pack/pallas_call | solution.py:101
  1.8 5.1 %collective-permute-start = (bf16[512,128]{1,0:T(8,128)(2,1)S(1)}, bf16[512,128]{1,0:T(8,128)(2,1)S(1)}, u32[]{:S(2)}, u32[]{:S(2)}) collective-permute-start(bf16[512,128]{1,0:T(8,128)(2,1)S(1)} %get-tuple-element.25), channel_id=1, source_target_pairs={{0,24},{1,28},{2,26},{3,30},{4,25},{5,29},{6,27},{7,31},{8,16},{9,... | collective-permute-start | bytes 393224 | tf_op jit(solution)/shard_map/ppermute | solution.py:419
  6.9 0.0 collective-permute-start.1
  6.9 0.7 %collective-permute-start.2 = (bf16[512,128]{1,0:T(8,128)(2,1)S(1)}, bf16[512,128]{1,0:T(8,128)(2,1)S(1)}, u32[]{:S(2)}, u32[]{:S(2)}) collective-permute-start(bf16[512,128]{1,0:T(8,128)(2,1)S(1)} %get-tuple-element.27), channel_id=1, source_target_pairs={{0,0},{1,4},{2,2},{3,6},{4,1},{5,5},{6,3},{7,7},{8,8},{9,12},{10,1... | collective-permute-start | bytes 393224 | tf_op jit(solution)/shard_map/ppermute | solution.py:419
  7.6 0.7 %collective-permute-start.3 = (bf16[512,128]{1,0:T(8,128)(2,1)S(1)}, bf16[512,128]{1,0:T(8,128)(2,1)S(1)}, u32[]{:S(2)}, u32[]{:S(2)}) collective-permute-start(bf16[512,128]{1,0:T(8,128)(2,1)S(1)} %get-tuple-element.28), channel_id=1, source_target_pairs={{0,16},{1,20},{2,18},{3,22},{4,17},{5,21},{6,19},{7,23},{8,24},{9,... | collective-permute-start | bytes 393224 | tf_op jit(solution)/shard_map/ppermute | solution.py:419
  8.3 0.1 iota_add_fusion
  8.4 0.1 add.63
  8.4 0.8 %select_reduce_fusion = s32[16]{0:T(128)S(1)} fusion(s32[32]{0:T(128)} %param.15, s32[16]{0:T(128)S(1)} %add.63), kind=kLoop, calls=%fused_computation.1 | loop fusion | flops 1520 | bytes 256 | tf_op jit(solution)/shard_map/reduce_sum | solution.py:433
  9.3 1.6 %collective-permute-done.refs_0_ = bf16[512,128]{1,0:T(8,128)(2,1)S(1)} collective-permute-done((bf16[512,128]{1,0:T(8,128)(2,1)S(1)}, bf16[512,128]{1,0:T(8,128)(2,1)S(1)}, u32[]{:S(2)}, u32[]{:S(2)}) %collective-permute-start) | collective-permute-done | bytes 131104 | tf_op jit(solution)/shard_map/ppermute | solution.py:419
  10.9 1.9 %collective-permute-start.4 = (bf16[512,128]{1,0:T(8,128)(2,1)S(1)}, bf16[512,128]{1,0:T(8,128)(2,1)S(1)}, u32[]{:S(2)}, u32[]{:S(2)}) collective-permute-start(bf16[512,128]{1,0:T(8,128)(2,1)S(1)} %collective-permute-done.refs_0_), channel_id=1, source_target_pairs={{0,1},{1,0},{2,3},{3,2},{4,5},{5,4},{6,7},{7,6},{8,9},{9,8},{10,11... | collective-permute-start | bytes 393224 | tf_op jit(solution)/shard_map/ppermute | solution.py:427
  12.8 2.1 %collective-permute-done.1.refs_1_ = bf16[512,128]{1,0:T(8,128)(2,1)S(1)} collective-permute-done((bf16[512,128]{1,0:T(8,128)(2,1)S(1)}, bf16[512,128]{1,0:T(8,128)(2,1)S(1)}, u32[]{:S(2)}, u32[]{:S(2)}) %collective-permute-start.1) | collective-permute-done | bytes 131104 | tf_op jit(solution)/shard_map/ppermute | solution.py:419
  14.9 0.5 %collective-permute-start.5 = (bf16[512,128]{1,0:T(8,128)(2,1)S(1)}, bf16[512,128]{1,0:T(8,128)(2,1)S(1)}, u32[]{:S(2)}, u32[]{:S(2)}) collective-permute-start(bf16[512,128]{1,0:T(8,128)(2,1)S(1)} %collective-permute-done.1.refs_1_), channel_id=1, source_target_pairs={{0,1},{1,0},{2,3},{3,2},{4,5},{5,4},{6,7},{7,6},{8,9},{9,8},{10,11... | collective-permute-start | bytes 393224 | tf_op jit(solution)/shard_map/ppermute | solution.py:427
  15.4 0.3 collective-permute-start.6
  15.6 2.7 %collective-permute-done.3.refs_3_ = bf16[512,128]{1,0:T(8,128)(2,1)S(1)} collective-permute-done((bf16[512,128]{1,0:T(8,128)(2,1)S(1)}, bf16[512,128]{1,0:T(8,128)(2,1)S(1)}, u32[]{:S(2)}, u32[]{:S(2)}) %collective-permute-start.3) | collective-permute-done | bytes 131104 | tf_op jit(solution)/shard_map/ppermute | solution.py:419
  18.4 1.3 %collective-permute-done.7.refs_7_ = bf16[512,128]{1,0:T(8,128)(2,1)S(1)} collective-permute-done((bf16[512,128]{1,0:T(8,128)(2,1)S(1)}, bf16[512,128]{1,0:T(8,128)(2,1)S(1)}, u32[]{:S(2)}, u32[]{:S(2)}) %collective-permute-start.7) | collective-permute-done | bytes 131104 | tf_op jit(solution)/shard_map/ppermute | solution.py:427
  19.7 0.6 %route.1 = (bf16[512,128]{1,0:T(8,128)(2,1)S(1)}, bf16[512,128]{1,0:T(8,128)(2,1)S(1)}, bf16[512,128]{1,0:T(8,128)(2,1)S(1)}, bf16[512,128]{1,0:T(8,128)(2,1)S(1)}) custom-call(s32[16]{0:T(128)S(1)} %fusion.index_far, bf16[512,128]{1,0:T(8,128)(2,1)S(1)} %collective-permute-done.refs_0_, bf16[512,128]{1,0:T(8,128)(2,1)S(1)} %collective-permute-done.1.refs_1_, ...), custom_call_target="tpu_custom_call" | custom-call | tf_op jit(solution)/shard_map/route/pallas_call | solution.py:225
  20.3 1.4 %collective-permute-start.8 = (bf16[512,128]{1,0:T(8,128)(2,1)S(1)}, bf16[512,128]{1,0:T(8,128)(2,1)S(1)}, u32[]{:S(2)}, u32[]{:S(2)}) collective-permute-start(bf16[512,128]{1,0:T(8,128)(2,1)S(1)} %get-tuple-element.29), channel_id=1, source_target_pairs={{0,16},{1,20},{2,18},{3,22},{4,17},{5,21},{6,19},{7,23},{8,24},{9,... | collective-permute-start | bytes 393224 | tf_op jit(solution)/shard_map/ppermute | solution.py:419
  21.7 1.6 %collective-permute-start.9 = (bf16[512,128]{1,0:T(8,128)(2,1)S(1)}, bf16[512,128]{1,0:T(8,128)(2,1)S(1)}, u32[]{:S(2)}, u32[]{:S(2)}) collective-permute-start(bf16[512,128]{1,0:T(8,128)(2,1)S(1)} %get-tuple-element.30), channel_id=1, source_target_pairs={{0,24},{1,28},{2,26},{3,30},{4,25},{5,29},{6,27},{7,31},{8,16},{9,... | collective-permute-start | bytes 393224 | tf_op jit(solution)/shard_map/ppermute | solution.py:419
  23.3 0.5 %collective-permute-start.10 = (bf16[512,128]{1,0:T(8,128)(2,1)S(1)}, bf16[512,128]{1,0:T(8,128)(2,1)S(1)}, u32[]{:S(2)}, u32[]{:S(2)}) collective-permute-start(bf16[512,128]{1,0:T(8,128)(2,1)S(1)} %get-tuple-element.31), channel_id=1, source_target_pairs={{0,8},{1,12},{2,10},{3,14},{4,9},{5,13},{6,11},{7,15},{8,0},{9,4},... | collective-permute-start | bytes 393224 | tf_op jit(solution)/shard_map/ppermute | solution.py:419
  23.8 1.2 %collective-permute-start.11 = (bf16[512,128]{1,0:T(8,128)(2,1)S(1)}, bf16[512,128]{1,0:T(8,128)(2,1)S(1)}, u32[]{:S(2)}, u32[]{:S(2)}) collective-permute-start(bf16[512,128]{1,0:T(8,128)(2,1)S(1)} %get-tuple-element.32.refs_4_), channel_id=1, source_target_pairs={{0,5},{1,4},{2,7},{3,6},{4,1},{5,0},{6,3},{7,2},{8,13},{9,12},{10,... | collective-permute-start | bytes 393224 | tf_op jit(solution)/shard_map/ppermute | solution.py:419
  25.0 1.2 %prepare.1 = (f32[128,128]{1,0:T(8,128)S(1)}, f32[64,128]{1,0:T(8,128)S(1)}, f32[64,128]{1,0:T(8,128)S(1)}, f32[64,128]{1,0:T(8,128)S(1)}, f32[64,128]{1,0:T(8,128)S(1)}) custom-call(s32[32]{0:T(128)} %lens_ref.1, bf16[4,3,4,512]{3,2,1,0:T(4,128)(2,1)} %bitcast.6, bf16[3,3,4,512]{3,2,1,0:T(4,128)(2,1)} %bitcast.7, bf16[3,4,512]{2,1,0:T(4,128)(2,1)} %bitcast.8, ...), custom_call_target="tpu_custom_call" | custom-call | tf_op jit(solution)/shard_map/prepare/pallas_call | solution.py:180
  26.2 0.0 copy-start.1
  26.2 1.6 %fetch.1.refs_8_ = bf16[512,2048]{1,0:T(8,128)(2,1)S(1)} custom-call(bf16[512,2048]{1,0:T(8,128)(2,1)} %far_ref), custom_call_target="tpu_custom_call" | custom-call | tf_op jit(solution)/shard_map/fetch/pallas_call | solution.py:247
  27.9 5.2 %collective-permute-done.8.refs_0_ = bf16[512,128]{1,0:T(8,128)(2,1)S(1)} collective-permute-done((bf16[512,128]{1,0:T(8,128)(2,1)S(1)}, bf16[512,128]{1,0:T(8,128)(2,1)S(1)}, u32[]{:S(2)}, u32[]{:S(2)}) %collective-permute-start.8) | collective-permute-done | bytes 131104 | tf_op jit(solution)/shard_map/ppermute | solution.py:419
  33.1 1.8 %collective-permute-done.10.refs_2_ = bf16[512,128]{1,0:T(8,128)(2,1)S(1)} collective-permute-done((bf16[512,128]{1,0:T(8,128)(2,1)S(1)}, bf16[512,128]{1,0:T(8,128)(2,1)S(1)}, u32[]{:S(2)}, u32[]{:S(2)}) %collective-permute-start.10) | collective-permute-done | bytes 131104 | tf_op jit(solution)/shard_map/ppermute | solution.py:419
  34.9 0.7 %home.1 = bf16[16,2048]{1,0:T(8,128)(2,1)S(1)} custom-call(bf16[512,128]{1,0:T(8,128)(2,1)S(1)} %collective-permute-done.8.refs_0_, bf16[512,128]{1,0:T(8,128)(2,1)S(1)} %collective-permute-done.9.refs_1_, bf16[512,128]{1,0:T(8,128)(2,1)S(1)} %collective-permute-done.10.refs_2_, bf16[512,128]{1,0:T(8,128)(2,1)S(1)} %collective-permute-done.11.refs_3_, ...), custom_call_target="tpu_custom_call" | custom-call | tf_op jit(solution)/shard_map/home/pallas_call | solution.py:288
  35.6 1.5 %collective-permute-start.12 = (bf16[16,2048]{1,0:T(8,128)(2,1)S(1)}, bf16[16,2048]{1,0:T(8,128)(2,1)S(1)}, u32[]{:S(2)}, u32[]{:S(2)}) collective-permute-start(bf16[16,2048]{1,0:T(8,128)(2,1)S(1)} %home.1), channel_id=1, source_target_pairs={{0,2},{1,3},{2,0},{3,1},{4,6},{5,7},{6,4},{7,5},{8,10},{9,11},{10,... | collective-permute-start | bytes 196616 | tf_op jit(solution)/shard_map/ppermute | solution.py:445
  37.1 2.8 %collective-permute-done.12 = bf16[16,2048]{1,0:T(8,128)(2,1)S(1)} collective-permute-done((bf16[16,2048]{1,0:T(8,128)(2,1)S(1)}, bf16[16,2048]{1,0:T(8,128)(2,1)S(1)}, u32[]{:S(2)}, u32[]{:S(2)}) %collective-permute-start.12) | collective-permute-done | bytes 65568 | tf_op jit(solution)/shard_map/ppermute | solution.py:445
  39.9 0.1 collective-permute-start.13
  40.0 1.2 %place.1 = bf16[4,4,128,128]{3,2,1,0:T(8,128)(2,1)} custom-call(bf16[512,128]{1,0:T(8,128)(2,1)S(1)} %collective-permute-done.8.refs_0_, bf16[512,128]{1,0:T(8,128)(2,1)S(1)} %collective-permute-done.9.refs_1_, bf16[512,128]{1,0:T(8,128)(2,1)S(1)} %collective-permute-done.10.refs_2_, bf16[512,128]{1,0:T(8,128)(2,1)S(1)} %collective-permute-done.11.refs_3_, ...), custom_call_target="tpu_custom_call" | custom-call | tf_op jit(solution)/shard_map/place/pallas_call | solution.py:342
  41.2 0.0 collective-permute-done.13.refs_1_
  41.2 0.7 %add.89 = bf16[4,4,2048]{2,1,0:T(4,128)(2,1)} custom-call(bf16[4,4,2048]{2,1,0:T(4,128)(2,1)S(1)} %copy-done, bf16[16,2048]{1,0:T(8,128)(2,1)S(1)} %add_convert_fusion.refs_0_, bf16[16,2048]{1,0:T(8,128)(2,1)S(1)} %collective-permute-done.13.refs_1_), custom_call_target="tpu_custom_call" | custom-call | tf_op jit(solution)/shard_map/add/pallas_call | solution.py:369
  (13 shorter events, 0.1 us)
Async XLA Ops:
  1.8 9.1 %collective-permute-start = (bf16[512,128]{1,0:T(8,128)(2,1)S(1)}, bf16[512,128]{1,0:T(8,128)(2,1)S(1)}, u32[]{:S(2)}, u32[]{:S(2)}) collective-permute-start(bf16[512,128]{1,0:T(8,128)(2,1)S(1)} %get-tuple-element.25), channel_id=1, source_target_pairs={{0,24},{1,28},{2,26},{3,30},{4,25},{5,29},{6,27},{7,31},{8,16},{9,... | collective-permute-start | bytes 393224 | tf_op jit(solution)/shard_map/ppermute | solution.py:419
  6.9 8.0 %collective-permute-start.1 = (bf16[512,128]{1,0:T(8,128)(2,1)S(1)}, bf16[512,128]{1,0:T(8,128)(2,1)S(1)}, u32[]{:S(2)}, u32[]{:S(2)}) collective-permute-start(bf16[512,128]{1,0:T(8,128)(2,1)S(1)} %get-tuple-element.26), channel_id=1, source_target_pairs={{0,8},{1,12},{2,10},{3,14},{4,9},{5,13},{6,11},{7,15},{8,0},{9,4},... | collective-permute-start | bytes 393224 | tf_op jit(solution)/shard_map/ppermute | solution.py:419
  6.9 8.4 %collective-permute-start.2 = (bf16[512,128]{1,0:T(8,128)(2,1)S(1)}, bf16[512,128]{1,0:T(8,128)(2,1)S(1)}, u32[]{:S(2)}, u32[]{:S(2)}) collective-permute-start(bf16[512,128]{1,0:T(8,128)(2,1)S(1)} %get-tuple-element.27), channel_id=1, source_target_pairs={{0,0},{1,4},{2,2},{3,6},{4,1},{5,5},{6,3},{7,7},{8,8},{9,12},{10,1... | collective-permute-start | bytes 393224 | tf_op jit(solution)/shard_map/ppermute | solution.py:419
  7.6 10.8 %collective-permute-start.3 = (bf16[512,128]{1,0:T(8,128)(2,1)S(1)}, bf16[512,128]{1,0:T(8,128)(2,1)S(1)}, u32[]{:S(2)}, u32[]{:S(2)}) collective-permute-start(bf16[512,128]{1,0:T(8,128)(2,1)S(1)} %get-tuple-element.28), channel_id=1, source_target_pairs={{0,16},{1,20},{2,18},{3,22},{4,17},{5,21},{6,19},{7,23},{8,24},{9,... | collective-permute-start | bytes 393224 | tf_op jit(solution)/shard_map/ppermute | solution.py:419
  10.9 7.5 %collective-permute-start.4 = (bf16[512,128]{1,0:T(8,128)(2,1)S(1)}, bf16[512,128]{1,0:T(8,128)(2,1)S(1)}, u32[]{:S(2)}, u32[]{:S(2)}) collective-permute-start(bf16[512,128]{1,0:T(8,128)(2,1)S(1)} %collective-permute-done.refs_0_), channel_id=1, source_target_pairs={{0,1},{1,0},{2,3},{3,2},{4,5},{5,4},{6,7},{7,6},{8,9},{9,8},{10,11... | collective-permute-start | bytes 393224 | tf_op jit(solution)/shard_map/ppermute | solution.py:427
  14.9 3.5 %collective-permute-start.5 = (bf16[512,128]{1,0:T(8,128)(2,1)S(1)}, bf16[512,128]{1,0:T(8,128)(2,1)S(1)}, u32[]{:S(2)}, u32[]{:S(2)}) collective-permute-start(bf16[512,128]{1,0:T(8,128)(2,1)S(1)} %collective-permute-done.1.refs_1_), channel_id=1, source_target_pairs={{0,1},{1,0},{2,3},{3,2},{4,5},{5,4},{6,7},{7,6},{8,9},{9,8},{10,11... | collective-permute-start | bytes 393224 | tf_op jit(solution)/shard_map/ppermute | solution.py:427
  15.4 3.0 %collective-permute-start.6 = (bf16[512,128]{1,0:T(8,128)(2,1)S(1)}, bf16[512,128]{1,0:T(8,128)(2,1)S(1)}, u32[]{:S(2)}, u32[]{:S(2)}) collective-permute-start(bf16[512,128]{1,0:T(8,128)(2,1)S(1)} %collective-permute-done.2.refs_2_), channel_id=1, source_target_pairs={{0,1},{1,0},{2,3},{3,2},{4,5},{5,4},{6,7},{7,6},{8,9},{9,8},{10,11... | collective-permute-start | bytes 393224 | tf_op jit(solution)/shard_map/ppermute | solution.py:427
  18.3 1.3 %collective-permute-start.7 = (bf16[512,128]{1,0:T(8,128)(2,1)S(1)}, bf16[512,128]{1,0:T(8,128)(2,1)S(1)}, u32[]{:S(2)}, u32[]{:S(2)}) collective-permute-start(bf16[512,128]{1,0:T(8,128)(2,1)S(1)} %collective-permute-done.3.refs_3_), channel_id=1, source_target_pairs={{0,1},{1,0},{2,3},{3,2},{4,5},{5,4},{6,7},{7,6},{8,9},{9,8},{10,11... | collective-permute-start | bytes 393224 | tf_op jit(solution)/shard_map/ppermute | solution.py:427
  20.3 12.8 %collective-permute-start.8 = (bf16[512,128]{1,0:T(8,128)(2,1)S(1)}, bf16[512,128]{1,0:T(8,128)(2,1)S(1)}, u32[]{:S(2)}, u32[]{:S(2)}) collective-permute-start(bf16[512,128]{1,0:T(8,128)(2,1)S(1)} %get-tuple-element.29), channel_id=1, source_target_pairs={{0,16},{1,20},{2,18},{3,22},{4,17},{5,21},{6,19},{7,23},{8,24},{9,... | collective-permute-start | bytes 393224 | tf_op jit(solution)/shard_map/ppermute | solution.py:419
  21.7 11.4 %collective-permute-start.9 = (bf16[512,128]{1,0:T(8,128)(2,1)S(1)}, bf16[512,128]{1,0:T(8,128)(2,1)S(1)}, u32[]{:S(2)}, u32[]{:S(2)}) collective-permute-start(bf16[512,128]{1,0:T(8,128)(2,1)S(1)} %get-tuple-element.30), channel_id=1, source_target_pairs={{0,24},{1,28},{2,26},{3,30},{4,25},{5,29},{6,27},{7,31},{8,16},{9,... | collective-permute-start | bytes 393224 | tf_op jit(solution)/shard_map/ppermute | solution.py:419
  23.3 11.6 %collective-permute-start.10 = (bf16[512,128]{1,0:T(8,128)(2,1)S(1)}, bf16[512,128]{1,0:T(8,128)(2,1)S(1)}, u32[]{:S(2)}, u32[]{:S(2)}) collective-permute-start(bf16[512,128]{1,0:T(8,128)(2,1)S(1)} %get-tuple-element.31), channel_id=1, source_target_pairs={{0,8},{1,12},{2,10},{3,14},{4,9},{5,13},{6,11},{7,15},{8,0},{9,4},... | collective-permute-start | bytes 393224 | tf_op jit(solution)/shard_map/ppermute | solution.py:419
  23.8 11.1 %collective-permute-start.11 = (bf16[512,128]{1,0:T(8,128)(2,1)S(1)}, bf16[512,128]{1,0:T(8,128)(2,1)S(1)}, u32[]{:S(2)}, u32[]{:S(2)}) collective-permute-start(bf16[512,128]{1,0:T(8,128)(2,1)S(1)} %get-tuple-element.32.refs_4_), channel_id=1, source_target_pairs={{0,5},{1,4},{2,7},{3,6},{4,1},{5,0},{6,3},{7,2},{8,13},{9,12},{10,... | collective-permute-start | bytes 393224 | tf_op jit(solution)/shard_map/ppermute | solution.py:419
  26.2 8.7 %copy-start.1 = (f32[512]{0:T(512)S(1)}, f32[512]{0:T(512)}, u32[]{:S(2)}) copy-start(f32[512]{0:T(512)} %param.18) | copy-start | bytes 6148
  34.9 6.3 %copy-start = (bf16[4,4,2048]{2,1,0:T(4,128)(2,1)S(1)}, bf16[4,4,2048]{2,1,0:T(4,128)(2,1)}, u32[]{:S(2)}) copy-start(bf16[4,4,2048]{2,1,0:T(4,128)(2,1)} %resid.1) | copy-start | bytes 196612
  35.6 4.3 %collective-permute-start.12 = (bf16[16,2048]{1,0:T(8,128)(2,1)S(1)}, bf16[16,2048]{1,0:T(8,128)(2,1)S(1)}, u32[]{:S(2)}, u32[]{:S(2)}) collective-permute-start(bf16[16,2048]{1,0:T(8,128)(2,1)S(1)} %home.1), channel_id=1, source_target_pairs={{0,2},{1,3},{2,0},{3,1},{4,6},{5,7},{6,4},{7,5},{8,10},{9,11},{10,... | collective-permute-start | bytes 196616 | tf_op jit(solution)/shard_map/ppermute | solution.py:445
  39.9 1.3 %collective-permute-start.13 = (bf16[16,2048]{1,0:T(8,128)(2,1)S(1)}, bf16[16,2048]{1,0:T(8,128)(2,1)S(1)}, u32[]{:S(2)}, u32[]{:S(2)}) collective-permute-start(bf16[16,2048]{1,0:T(8,128)(2,1)S(1)} %add_convert_fusion.refs_0_), channel_id=1, source_target_pairs={{0,1},{1,0},{2,3},{3,2},{4,5},{5,4},{6,7},{7,6},{8,9},{9,8},{10,11... | collective-permute-start | bytes 196616 | tf_op jit(solution)/shard_map/ppermute | solution.py:449

commit v11 on v9

--- a/solution.py
+++ b/solution.py
@@ -419,7 +419,8 @@
         return lax.ppermute(value, both, pairs)
 
     packs = pack(old_state)
-    own = [swap(packs[s], s) for s in range(blocks)]
+    own = [swap(packs[s], s, cross=s == 0) for s in range(blocks)]
+    own[0] = jnp.where(own_req % 2 == core, packs[0], own[0])
     proj, conv_cache, conv_weight, forget_bias, norm_gain, *_ = lax.optimization_barrier(
         (proj, conv_cache, conv_weight, forget_bias, norm_gain, *packs)
     )

time: 42.2 us -> 42.3 us (level)
  waiting for transfers between devices: 17.3 us -> 17.8 us
    ppermute x8, starting transfers between devices: 11.2 us -> 10.3 us  [swap(): return lax.ppermute(value, both, pairs)]
    ppermute x8, waiting for transfers between devices: 13.5 us -> 14 us  [swap(): return lax.ppermute(value, both, pairs)]
  transfers between devices with their start and end apart: 14 -> 14, of which waited for: 8 -> 7; matrix products, arithmetic and copies ran while one was open for 2% -> 2% of each run, Pallas kernels for 10% -> 10%
where the time goes in v11:
time: 42.3 us; the launch traced here: 42 us
  waiting for transfers between devices  17.8 us (42%)
  starting transfers between devices  15.2 us (36%)
  Pallas kernels  7.19 us (17%)
  other arithmetic  0.97 us (2%)
  between operations  0.71 us (2%)
    ppermute x8, waiting for transfers between devices, swap(): return lax.ppermute(value, both, pairs)  14 us
    ppermute x8, starting transfers between devices, swap(): return lax.ppermute(value, both, pairs)  10.3 us
    ppermute x4, starting transfers between devices, swapped_body(): sib = [lax.ppermute(own[s], 'head', sibling) for s in range(blocks)]  2.66 us
    ppermute x1, waiting for transfers between devices, swapped_body(): lax.ppermute(part, 'head', [(i, i ^ step) for i in range(n_head)])  1.62 us
    pallas_call x1, Pallas kernels, fetch(): pl.pallas_call(fetch_kernel, out_shape=VMEM(value.shape, value.dtype), in...  1.61 us
    ppermute x1, starting transfers between devices, swapped_body(): lax.ppermute(part, 'head', [(i, i ^ step) for i in range(n_head)])  1.58 us
    ppermute x4, waiting for transfers between devices, swapped_body(): sib = [lax.ppermute(own[s], 'head', sibling) for s in range(blocks)]  1.31 us
    pallas_call x1, Pallas kernels, prepare(): pl.pallas_call(functools.partial(prepare_kernel, blocks), out_shape=[VMEM...  1.25 us
  transfers between devices with their start and end apart: 14, of which 7 were waited for; matrix products, arithmetic and copies ran while one was open for 2% of the time, Pallas kernels for 10%

profile of v11, /device:TPU:0, one launch (start us, length us, event | category | flops | bytes accessed | tf_op | source)
XLA Modules:
  0.0 42.0 jit_solution(3527199633628620788)
XLA Ops:
  0.6 1.2 %pack.1 = (bf16[512,128]{1,0:T(8,128)(2,1)S(1)}, bf16[512,128]{1,0:T(8,128)(2,1)S(1)}, bf16[512,128]{1,0:T(8,128)(2,1)S(1)}, bf16[512,128]{1,0:T(8,128)(2,1)S(1)}) custom-call(bf16[4,4,128,128]{3,2,1,0:T(8,128)(2,1)} %state_ref.1), custom_call_target="tpu_custom_call" | custom-call | tf_op jit(solution)/shard_map/pack/pallas_call | solution.py:101
  1.8 5.1 %collective-permute-start = (bf16[512,128]{1,0:T(8,128)(2,1)S(1)}, bf16[512,128]{1,0:T(8,128)(2,1)S(1)}, u32[]{:S(2)}, u32[]{:S(2)}) collective-permute-start(bf16[512,128]{1,0:T(8,128)(2,1)S(1)} %get-tuple-element.25), channel_id=1, source_target_pairs={{0,24},{1,28},{2,26},{3,30},{4,25},{5,29},{6,27},{7,31},{8,16},{9,... | collective-permute-start | bytes 393224 | tf_op jit(solution)/shard_map/ppermute | solution.py:419
  6.9 0.0 collective-permute-start.1
  6.9 0.6 %collective-permute-start.3 = (bf16[512,128]{1,0:T(8,128)(2,1)S(1)}, bf16[512,128]{1,0:T(8,128)(2,1)S(1)}, u32[]{:S(2)}, u32[]{:S(2)}) collective-permute-start(bf16[512,128]{1,0:T(8,128)(2,1)S(1)} %get-tuple-element.28), channel_id=1, source_target_pairs={{0,16},{1,20},{2,18},{3,22},{4,17},{5,21},{6,19},{7,23},{8,24},{9,... | collective-permute-start | bytes 393224 | tf_op jit(solution)/shard_map/ppermute | solution.py:419
  7.5 0.4 collective-permute-start.2
  7.9 0.1 iota_add_fusion
  8.0 0.1 add.66
  8.1 0.8 %select_reduce_fusion = s32[16]{0:T(128)S(1)} fusion(s32[32]{0:T(128)} %param.15, s32[16]{0:T(128)S(1)} %add.66), kind=kLoop, calls=%fused_computation.2 | loop fusion | flops 1520 | bytes 256 | tf_op jit(solution)/shard_map/reduce_sum | solution.py:434
  8.9 4.9 %collective-permute-done.2 = bf16[512,128]{1,0:T(8,128)(2,1)S(1)} collective-permute-done((bf16[512,128]{1,0:T(8,128)(2,1)S(1)}, bf16[512,128]{1,0:T(8,128)(2,1)S(1)}, u32[]{:S(2)}, u32[]{:S(2)}) %collective-permute-start.2) | collective-permute-done | bytes 131104 | tf_op jit(solution)/shard_map/ppermute | solution.py:419
  13.9 2.1 %collective-permute-start.6 = (bf16[512,128]{1,0:T(8,128)(2,1)S(1)}, bf16[512,128]{1,0:T(8,128)(2,1)S(1)}, u32[]{:S(2)}, u32[]{:S(2)}) collective-permute-start(bf16[512,128]{1,0:T(8,128)(2,1)S(1)} %broadcast_select_fusion.refs_2_), channel_id=1, source_target_pairs={{0,1},{1,0},{2,3},{3,2},{4,5},{5,4},{6,7},{7,6},{8,9},{9,8},{10,11... | collective-permute-start | bytes 393224 | tf_op jit(solution)/shard_map/ppermute | solution.py:428
  16.0 0.0 collective-permute-done.refs_0_
  16.0 0.1 collective-permute-start.4
  16.1 0.4 %collective-permute-start.5 = (bf16[512,128]{1,0:T(8,128)(2,1)S(1)}, bf16[512,128]{1,0:T(8,128)(2,1)S(1)}, u32[]{:S(2)}, u32[]{:S(2)}) collective-permute-start(bf16[512,128]{1,0:T(8,128)(2,1)S(1)} %collective-permute-done.1.refs_1_), channel_id=1, source_target_pairs={{0,1},{1,0},{2,3},{3,2},{4,5},{5,4},{6,7},{7,6},{8,9},{9,8},{10,11... | collective-permute-start | bytes 393224 | tf_op jit(solution)/shard_map/ppermute | solution.py:428
  16.5 2.3 %collective-permute-done.3.refs_3_ = bf16[512,128]{1,0:T(8,128)(2,1)S(1)} collective-permute-done((bf16[512,128]{1,0:T(8,128)(2,1)S(1)}, bf16[512,128]{1,0:T(8,128)(2,1)S(1)}, u32[]{:S(2)}, u32[]{:S(2)}) %collective-permute-start.3) | collective-permute-done | bytes 131104 | tf_op jit(solution)/shard_map/ppermute | solution.py:419
  18.9 1.3 %collective-permute-done.7.refs_7_ = bf16[512,128]{1,0:T(8,128)(2,1)S(1)} collective-permute-done((bf16[512,128]{1,0:T(8,128)(2,1)S(1)}, bf16[512,128]{1,0:T(8,128)(2,1)S(1)}, u32[]{:S(2)}, u32[]{:S(2)}) %collective-permute-start.7) | collective-permute-done | bytes 131104 | tf_op jit(solution)/shard_map/ppermute | solution.py:428
  20.2 0.6 %route.1 = (bf16[512,128]{1,0:T(8,128)(2,1)S(1)}, bf16[512,128]{1,0:T(8,128)(2,1)S(1)}, bf16[512,128]{1,0:T(8,128)(2,1)S(1)}, bf16[512,128]{1,0:T(8,128)(2,1)S(1)}) custom-call(s32[16]{0:T(128)S(1)} %fusion.index_far, bf16[512,128]{1,0:T(8,128)(2,1)S(1)} %collective-permute-done.refs_0_, bf16[512,128]{1,0:T(8,128)(2,1)S(1)} %collective-permute-done.1.refs_1_, ...), custom_call_target="tpu_custom_call" | custom-call | tf_op jit(solution)/shard_map/route/pallas_call | solution.py:225
  20.8 0.9 %collective-permute-start.8 = (bf16[512,128]{1,0:T(8,128)(2,1)S(1)}, bf16[512,128]{1,0:T(8,128)(2,1)S(1)}, u32[]{:S(2)}, u32[]{:S(2)}) collective-permute-start(bf16[512,128]{1,0:T(8,128)(2,1)S(1)} %get-tuple-element.29), channel_id=1, source_target_pairs={{0,16},{1,20},{2,18},{3,22},{4,17},{5,21},{6,19},{7,23},{8,24},{9,... | collective-permute-start | bytes 393224 | tf_op jit(solution)/shard_map/ppermute | solution.py:419
  21.7 1.7 %collective-permute-start.9 = (bf16[512,128]{1,0:T(8,128)(2,1)S(1)}, bf16[512,128]{1,0:T(8,128)(2,1)S(1)}, u32[]{:S(2)}, u32[]{:S(2)}) collective-permute-start(bf16[512,128]{1,0:T(8,128)(2,1)S(1)} %get-tuple-element.30), channel_id=1, source_target_pairs={{0,24},{1,28},{2,26},{3,30},{4,25},{5,29},{6,27},{7,31},{8,16},{9,... | collective-permute-start | bytes 393224 | tf_op jit(solution)/shard_map/ppermute | solution.py:419
  23.4 0.9 %collective-permute-start.10 = (bf16[512,128]{1,0:T(8,128)(2,1)S(1)}, bf16[512,128]{1,0:T(8,128)(2,1)S(1)}, u32[]{:S(2)}, u32[]{:S(2)}) collective-permute-start(bf16[512,128]{1,0:T(8,128)(2,1)S(1)} %get-tuple-element.31), channel_id=1, source_target_pairs={{0,8},{1,12},{2,10},{3,14},{4,9},{5,13},{6,11},{7,15},{8,0},{9,4},... | collective-permute-start | bytes 393224 | tf_op jit(solution)/shard_map/ppermute | solution.py:419
  24.4 0.6 %collective-permute-start.11 = (bf16[512,128]{1,0:T(8,128)(2,1)S(1)}, bf16[512,128]{1,0:T(8,128)(2,1)S(1)}, u32[]{:S(2)}, u32[]{:S(2)}) collective-permute-start(bf16[512,128]{1,0:T(8,128)(2,1)S(1)} %get-tuple-element.32.refs_4_), channel_id=1, source_target_pairs={{0,5},{1,4},{2,7},{3,6},{4,1},{5,0},{6,3},{7,2},{8,13},{9,12},{10,... | collective-permute-start | bytes 393224 | tf_op jit(solution)/shard_map/ppermute | solution.py:419
  25.0 1.2 %prepare.1 = (f32[128,128]{1,0:T(8,128)S(1)}, f32[64,128]{1,0:T(8,128)S(1)}, f32[64,128]{1,0:T(8,128)S(1)}, f32[64,128]{1,0:T(8,128)S(1)}, f32[64,128]{1,0:T(8,128)S(1)}) custom-call(s32[32]{0:T(128)} %lens_ref.1, bf16[4,3,4,512]{3,2,1,0:T(4,128)(2,1)} %bitcast.6, bf16[3,3,4,512]{3,2,1,0:T(4,128)(2,1)} %bitcast.7, bf16[3,4,512]{2,1,0:T(4,128)(2,1)} %bitcast.8, ...), custom_call_target="tpu_custom_call" | custom-call | tf_op jit(solution)/shard_map/prepare/pallas_call | solution.py:180
  26.2 0.0 copy-start.1
  26.3 1.6 %fetch.1.refs_8_ = bf16[512,2048]{1,0:T(8,128)(2,1)S(1)} custom-call(bf16[512,2048]{1,0:T(8,128)(2,1)} %far_ref), custom_call_target="tpu_custom_call" | custom-call | tf_op jit(solution)/shard_map/fetch/pallas_call | solution.py:247
  27.9 5.6 %collective-permute-done.8.refs_0_ = bf16[512,128]{1,0:T(8,128)(2,1)S(1)} collective-permute-done((bf16[512,128]{1,0:T(8,128)(2,1)S(1)}, bf16[512,128]{1,0:T(8,128)(2,1)S(1)}, u32[]{:S(2)}, u32[]{:S(2)}) %collective-permute-start.8) | collective-permute-done | bytes 131104 | tf_op jit(solution)/shard_map/ppermute | solution.py:419
  33.4 1.1 %collective-permute-done.10.refs_2_ = bf16[512,128]{1,0:T(8,128)(2,1)S(1)} collective-permute-done((bf16[512,128]{1,0:T(8,128)(2,1)S(1)}, bf16[512,128]{1,0:T(8,128)(2,1)S(1)}, u32[]{:S(2)}, u32[]{:S(2)}) %collective-permute-start.10) | collective-permute-done | bytes 131104 | tf_op jit(solution)/shard_map/ppermute | solution.py:419
  34.6 0.7 %home.1 = bf16[16,2048]{1,0:T(8,128)(2,1)S(1)} custom-call(bf16[512,128]{1,0:T(8,128)(2,1)S(1)} %collective-permute-done.8.refs_0_, bf16[512,128]{1,0:T(8,128)(2,1)S(1)} %collective-permute-done.9.refs_1_, bf16[512,128]{1,0:T(8,128)(2,1)S(1)} %collective-permute-done.10.refs_2_, bf16[512,128]{1,0:T(8,128)(2,1)S(1)} %collective-permute-done.11.refs_3_, ...), custom_call_target="tpu_custom_call" | custom-call | tf_op jit(solution)/shard_map/home/pallas_call | solution.py:288
  35.3 0.6 %collective-permute-start.12 = (bf16[16,2048]{1,0:T(8,128)(2,1)S(1)}, bf16[16,2048]{1,0:T(8,128)(2,1)S(1)}, u32[]{:S(2)}, u32[]{:S(2)}) collective-permute-start(bf16[16,2048]{1,0:T(8,128)(2,1)S(1)} %home.1), channel_id=1, source_target_pairs={{0,1},{1,0},{2,3},{3,2},{4,5},{5,4},{6,7},{7,6},{8,9},{9,8},{10,11... | collective-permute-start | bytes 196616 | tf_op jit(solution)/shard_map/ppermute | solution.py:445
  35.9 0.9 %collective-permute-done.12 = bf16[16,2048]{1,0:T(8,128)(2,1)S(1)} collective-permute-done((bf16[16,2048]{1,0:T(8,128)(2,1)S(1)}, bf16[16,2048]{1,0:T(8,128)(2,1)S(1)}, u32[]{:S(2)}, u32[]{:S(2)}) %collective-permute-start.12) | collective-permute-done | bytes 65568 | tf_op jit(solution)/shard_map/ppermute | solution.py:445
  36.9 1.6 %collective-permute-start.13 = (bf16[16,2048]{1,0:T(8,128)(2,1)S(1)}, bf16[16,2048]{1,0:T(8,128)(2,1)S(1)}, u32[]{:S(2)}, u32[]{:S(2)}) collective-permute-start(bf16[16,2048]{1,0:T(8,128)(2,1)S(1)} %add_convert_fusion.refs_0_), channel_id=1, source_target_pairs={{0,2},{1,3},{2,0},{3,1},{4,6},{5,7},{6,4},{7,5},{8,10},{9,11},{10,... | collective-permute-start | bytes 196616 | tf_op jit(solution)/shard_map/ppermute | solution.py:449
  38.4 1.2 %place.1 = bf16[4,4,128,128]{3,2,1,0:T(8,128)(2,1)} custom-call(bf16[512,128]{1,0:T(8,128)(2,1)S(1)} %collective-permute-done.8.refs_0_, bf16[512,128]{1,0:T(8,128)(2,1)S(1)} %collective-permute-done.9.refs_1_, bf16[512,128]{1,0:T(8,128)(2,1)S(1)} %collective-permute-done.10.refs_2_, bf16[512,128]{1,0:T(8,128)(2,1)S(1)} %collective-permute-done.11.refs_3_, ...), custom_call_target="tpu_custom_call" | custom-call | tf_op jit(solution)/shard_map/place/pallas_call | solution.py:342
  39.7 1.6 %collective-permute-done.13.refs_1_ = bf16[16,2048]{1,0:T(8,128)(2,1)S(1)} collective-permute-done((bf16[16,2048]{1,0:T(8,128)(2,1)S(1)}, bf16[16,2048]{1,0:T(8,128)(2,1)S(1)}, u32[]{:S(2)}, u32[]{:S(2)}) %collective-permute-start.13) | collective-permute-done | bytes 65568 | tf_op jit(solution)/shard_map/ppermute | solution.py:449
  41.3 0.7 %add.93 = bf16[4,4,2048]{2,1,0:T(4,128)(2,1)} custom-call(bf16[4,4,2048]{2,1,0:T(4,128)(2,1)S(1)} %copy-done, bf16[16,2048]{1,0:T(8,128)(2,1)S(1)} %add_convert_fusion.refs_0_, bf16[16,2048]{1,0:T(8,128)(2,1)S(1)} %collective-permute-done.13.refs_1_), custom_call_target="tpu_custom_call" | custom-call | tf_op jit(solution)/shard_map/add/pallas_call | solution.py:369
  (14 shorter events, 0.1 us)
Async XLA Ops:
  1.8 14.2 %collective-permute-start = (bf16[512,128]{1,0:T(8,128)(2,1)S(1)}, bf16[512,128]{1,0:T(8,128)(2,1)S(1)}, u32[]{:S(2)}, u32[]{:S(2)}) collective-permute-start(bf16[512,128]{1,0:T(8,128)(2,1)S(1)} %get-tuple-element.25), channel_id=1, source_target_pairs={{0,24},{1,28},{2,26},{3,30},{4,25},{5,29},{6,27},{7,31},{8,16},{9,... | collective-permute-start | bytes 393224 | tf_op jit(solution)/shard_map/ppermute | solution.py:419
  6.9 9.2 %collective-permute-start.1 = (bf16[512,128]{1,0:T(8,128)(2,1)S(1)}, bf16[512,128]{1,0:T(8,128)(2,1)S(1)}, u32[]{:S(2)}, u32[]{:S(2)}) collective-permute-start(bf16[512,128]{1,0:T(8,128)(2,1)S(1)} %get-tuple-element.26), channel_id=1, source_target_pairs={{0,8},{1,12},{2,10},{3,14},{4,9},{5,13},{6,11},{7,15},{8,0},{9,4},... | collective-permute-start | bytes 393224 | tf_op jit(solution)/shard_map/ppermute | solution.py:419
  6.9 11.9 %collective-permute-start.3 = (bf16[512,128]{1,0:T(8,128)(2,1)S(1)}, bf16[512,128]{1,0:T(8,128)(2,1)S(1)}, u32[]{:S(2)}, u32[]{:S(2)}) collective-permute-start(bf16[512,128]{1,0:T(8,128)(2,1)S(1)} %get-tuple-element.28), channel_id=1, source_target_pairs={{0,16},{1,20},{2,18},{3,22},{4,17},{5,21},{6,19},{7,23},{8,24},{9,... | collective-permute-start | bytes 393224 | tf_op jit(solution)/shard_map/ppermute | solution.py:419
  7.5 6.3 %collective-permute-start.2 = (bf16[512,128]{1,0:T(8,128)(2,1)S(1)}, bf16[512,128]{1,0:T(8,128)(2,1)S(1)}, u32[]{:S(2)}, u32[]{:S(2)}) collective-permute-start(bf16[512,128]{1,0:T(8,128)(2,1)S(1)} %get-tuple-element.27), channel_id=1, source_target_pairs={{0,5},{1,4},{2,7},{3,6},{4,1},{5,0},{6,3},{7,2},{8,13},{9,12},{10,... | collective-permute-start | bytes 393224 | tf_op jit(solution)/shard_map/ppermute | solution.py:419
  13.9 6.3 %collective-permute-start.6 = (bf16[512,128]{1,0:T(8,128)(2,1)S(1)}, bf16[512,128]{1,0:T(8,128)(2,1)S(1)}, u32[]{:S(2)}, u32[]{:S(2)}) collective-permute-start(bf16[512,128]{1,0:T(8,128)(2,1)S(1)} %broadcast_select_fusion.refs_2_), channel_id=1, source_target_pairs={{0,1},{1,0},{2,3},{3,2},{4,5},{5,4},{6,7},{7,6},{8,9},{9,8},{10,11... | collective-permute-start | bytes 393224 | tf_op jit(solution)/shard_map/ppermute | solution.py:428
  16.0 2.9 %collective-permute-start.4 = (bf16[512,128]{1,0:T(8,128)(2,1)S(1)}, bf16[512,128]{1,0:T(8,128)(2,1)S(1)}, u32[]{:S(2)}, u32[]{:S(2)}) collective-permute-start(bf16[512,128]{1,0:T(8,128)(2,1)S(1)} %collective-permute-done.refs_0_), channel_id=1, source_target_pairs={{0,1},{1,0},{2,3},{3,2},{4,5},{5,4},{6,7},{7,6},{8,9},{9,8},{10,11... | collective-permute-start | bytes 393224 | tf_op jit(solution)/shard_map/ppermute | solution.py:428
  16.1 2.8 %collective-permute-start.5 = (bf16[512,128]{1,0:T(8,128)(2,1)S(1)}, bf16[512,128]{1,0:T(8,128)(2,1)S(1)}, u32[]{:S(2)}, u32[]{:S(2)}) collective-permute-start(bf16[512,128]{1,0:T(8,128)(2,1)S(1)} %collective-permute-done.1.refs_1_), channel_id=1, source_target_pairs={{0,1},{1,0},{2,3},{3,2},{4,5},{5,4},{6,7},{7,6},{8,9},{9,8},{10,11... | collective-permute-start | bytes 393224 | tf_op jit(solution)/shard_map/ppermute | solution.py:428
  18.9 1.3 %collective-permute-start.7 = (bf16[512,128]{1,0:T(8,128)(2,1)S(1)}, bf16[512,128]{1,0:T(8,128)(2,1)S(1)}, u32[]{:S(2)}, u32[]{:S(2)}) collective-permute-start(bf16[512,128]{1,0:T(8,128)(2,1)S(1)} %collective-permute-done.3.refs_3_), channel_id=1, source_target_pairs={{0,1},{1,0},{2,3},{3,2},{4,5},{5,4},{6,7},{7,6},{8,9},{9,8},{10,11... | collective-permute-start | bytes 393224 | tf_op jit(solution)/shard_map/ppermute | solution.py:428
  20.8 12.6 %collective-permute-start.8 = (bf16[512,128]{1,0:T(8,128)(2,1)S(1)}, bf16[512,128]{1,0:T(8,128)(2,1)S(1)}, u32[]{:S(2)}, u32[]{:S(2)}) collective-permute-start(bf16[512,128]{1,0:T(8,128)(2,1)S(1)} %get-tuple-element.29), channel_id=1, source_target_pairs={{0,16},{1,20},{2,18},{3,22},{4,17},{5,21},{6,19},{7,23},{8,24},{9,... | collective-permute-start | bytes 393224 | tf_op jit(solution)/shard_map/ppermute | solution.py:419
  21.7 11.7 %collective-permute-start.9 = (bf16[512,128]{1,0:T(8,128)(2,1)S(1)}, bf16[512,128]{1,0:T(8,128)(2,1)S(1)}, u32[]{:S(2)}, u32[]{:S(2)}) collective-permute-start(bf16[512,128]{1,0:T(8,128)(2,1)S(1)} %get-tuple-element.30), channel_id=1, source_target_pairs={{0,24},{1,28},{2,26},{3,30},{4,25},{5,29},{6,27},{7,31},{8,16},{9,... | collective-permute-start | bytes 393224 | tf_op jit(solution)/shard_map/ppermute | solution.py:419
  23.4 11.2 %collective-permute-start.10 = (bf16[512,128]{1,0:T(8,128)(2,1)S(1)}, bf16[512,128]{1,0:T(8,128)(2,1)S(1)}, u32[]{:S(2)}, u32[]{:S(2)}) collective-permute-start(bf16[512,128]{1,0:T(8,128)(2,1)S(1)} %get-tuple-element.31), channel_id=1, source_target_pairs={{0,8},{1,12},{2,10},{3,14},{4,9},{5,13},{6,11},{7,15},{8,0},{9,4},... | collective-permute-start | bytes 393224 | tf_op jit(solution)/shard_map/ppermute | solution.py:419
  24.4 10.2 %collective-permute-start.11 = (bf16[512,128]{1,0:T(8,128)(2,1)S(1)}, bf16[512,128]{1,0:T(8,128)(2,1)S(1)}, u32[]{:S(2)}, u32[]{:S(2)}) collective-permute-start(bf16[512,128]{1,0:T(8,128)(2,1)S(1)} %get-tuple-element.32.refs_4_), channel_id=1, source_target_pairs={{0,5},{1,4},{2,7},{3,6},{4,1},{5,0},{6,3},{7,2},{8,13},{9,12},{10,... | collective-permute-start | bytes 393224 | tf_op jit(solution)/shard_map/ppermute | solution.py:419
  26.2 8.3 %copy-start.1 = (f32[512]{0:T(512)S(1)}, f32[512]{0:T(512)}, u32[]{:S(2)}) copy-start(f32[512]{0:T(512)} %param.18) | copy-start | bytes 6148
  34.6 6.7 %copy-start = (bf16[4,4,2048]{2,1,0:T(4,128)(2,1)S(1)}, bf16[4,4,2048]{2,1,0:T(4,128)(2,1)}, u32[]{:S(2)}) copy-start(bf16[4,4,2048]{2,1,0:T(4,128)(2,1)} %resid.1) | copy-start | bytes 196612
  35.3 1.5 %collective-permute-start.12 = (bf16[16,2048]{1,0:T(8,128)(2,1)S(1)}, bf16[16,2048]{1,0:T(8,128)(2,1)S(1)}, u32[]{:S(2)}, u32[]{:S(2)}) collective-permute-start(bf16[16,2048]{1,0:T(8,128)(2,1)S(1)} %home.1), channel_id=1, source_target_pairs={{0,1},{1,0},{2,3},{3,2},{4,5},{5,4},{6,7},{7,6},{8,9},{9,8},{10,11... | collective-permute-start | bytes 196616 | tf_op jit(solution)/shard_map/ppermute | solution.py:445
  36.9 4.4 %collective-permute-start.13 = (bf16[16,2048]{1,0:T(8,128)(2,1)S(1)}, bf16[16,2048]{1,0:T(8,128)(2,1)S(1)}, u32[]{:S(2)}, u32[]{:S(2)}) collective-permute-start(bf16[16,2048]{1,0:T(8,128)(2,1)S(1)} %add_convert_fusion.refs_0_), channel_id=1, source_target_pairs={{0,2},{1,3},{2,0},{3,1},{4,6},{5,7},{6,4},{7,5},{8,10},{9,11},{10,... | collective-permute-start | bytes 196616 | tf_op jit(solution)/shard_map/ppermute | solution.py:449
